TPU v7x, 32 devices: a whole 2x2x4 slice. The times are simulated.
32 devices in a mesh: dp: 8 (over z, x), tensor: 4 (over y, core).
Axes of the slice: x: 2, y: 2, z: 4, core: 2. Of those that a mesh axis runs over, the one named last changes fastest.
Arguments:
- tokens: bfloat16 [8192, 2048], P('dp'), may hold values from -6 to 6
- attn_gain: bfloat16 [2048], P('dp'), may hold values from 0.3984375 to 1.59375
- qkv_weight: bfloat16 [2048, 3, 2048], P('dp', None, 'tensor'), may hold values from -0.125 to 0.125
- out_weight: bfloat16 [2048, 2048], P('dp', 'tensor'), may hold values from -2 to 2
- moe_gain: bfloat16 [2048], P('dp'), may hold values from 0.3984375 to 1.59375
- router_weight: bfloat16 [2048, 4], P('dp'), may hold values from -0.09375 to 0.09375
- expert_weight: bfloat16 [3, 8192, 5632], P(None, 'dp', 'tensor'), may hold values from -0.125 to 0.125
- routes: int32 [8192, 2], P('dp'), may hold values from 0 to 3, all different within a row; in each aligned block of 1024 rows (0 to 1023, 1024 to 2047, ...) at most 768 rows name the same one
- cotangent: bfloat16 [8192, 2048], P('dp'), may hold values from -6 to 6
Outputs:
- layer_out: float32 [8192, 2048], P('dp')
- input_grad: float32 [8192, 2048], P('dp')
- attn_gain_grad: float32 [2048], P('dp')
- qkv_grad: float32 [2048, 3, 2048], P('dp', None, 'tensor')
- out_weight_grad: float32 [2048, 2048], P('dp', 'tensor')
- moe_gain_grad: float32 [2048], P('dp')
- router_grad: float32 [2048, 4], P('dp')
- expert_grad: float32 [3, 8192, 5632], P(None, 'dp', 'tensor')
Inputs may be any that keep to these rules, and one draw needn't show every extreme that they name: `routes`: each row names two different experts; among the rows of one index of dp no expert is named more than 768 times.
All inputs are finite; a program needn't handle non-finite values.
Results may differ from a plain program's by a relative error of at most 0.023.
Values may be sent and summed in bfloat16 or wider, within the bound.
No kernel may reach another device: no remote copies, remote signals or barrier semaphores. Data moves between devices by JAX's collectives and lax.ppermute only.
A program may use at most 384 MiB of HBM per device.

v0:
```python
import math

import jax
import jax.numpy as jnp
from jax import lax
from jax.sharding import PartitionSpec as P

HEAD = 128
EXPERTS = 4
SEQ = 1024
BLOCK = 256
MOST = 768


epsilon = 1e-05
theta_base = 10000.0
masked_out = -1e30


def from_partner(value, axis, distance):
    return lax.ppermute(value, axis, [(i, i ^ 1 << distance) for i in range(lax.axis_size(axis))])


def rotary_tables(length, width):
    half_width = width // 2
    freqs = theta_base ** (-(jnp.arange(half_width, dtype=jnp.float32) * 2.0 / width))
    angles = jnp.arange(length, dtype=jnp.float32)[:, None] * freqs[None, :]
    cosine = jnp.cos(angles)
    sine = jnp.sin(angles)
    return (jnp.concatenate([cosine, cosine], 1), jnp.concatenate([sine, sine], 1))


def rotate(vectors, cosine, sine):
    half_width = vectors.shape[-1] // 2
    turned = jnp.concatenate([-vectors[..., half_width:], vectors[..., :half_width]], -1)
    return vectors * cosine + turned * sine


def block_mask(length):
    blocks = jnp.arange(length, dtype=jnp.int32) // BLOCK
    return blocks[None, :] <= blocks[:, None]


def contract(left, right, left_dim, right_dim):
    return lax.dot_general(
        left, right, (((left_dim,), (right_dim,)), ((), ())), preferred_element_type=jnp.float32
    )


def send_out(buffer):
    return lax.all_to_all(buffer, "dp", split_axis=0, concat_axis=0, tiled=True)


def send_back(buffer):
    return lax.all_to_all(buffer, "dp", split_axis=0, concat_axis=0, tiled=True)


def widen_source(pairs):
    return lax.all_gather(pairs, "tensor", axis=2, tiled=True)


def expert_sum(partial_value):
    return lax.psum_scatter(partial_value, "tensor", scatter_dimension=1, tiled=True)


def group_gather(local, group_count):
    levels = group_count.bit_length() - 1
    position = lax.axis_index("dp")
    gathered = local
    for bit in range(levels):
        partner = from_partner(gathered, "dp", bit)
        upper_side = position // (1 << bit) % 2 == 1
        lower_half = jnp.where(upper_side, partner, gathered)
        upper_half = jnp.where(upper_side, gathered, partner)
        gathered = jnp.concatenate([lower_half, upper_half], axis=1)
    return gathered


def group_reduce(full, group_count):
    levels = group_count.bit_length() - 1
    position = lax.axis_index("dp")
    current = full
    for bit in range(levels - 1, -1, -1):
        middle = current.shape[1] // 2
        upper_side = position // (1 << bit) % 2 == 1
        kept = jnp.where(upper_side, current[:, middle:], current[:, :middle])
        given = jnp.where(upper_side, current[:, :middle], current[:, middle:])
        current = kept + from_partner(given.astype(jnp.bfloat16), "dp", bit).astype(given.dtype)
    return current


def pack(source_rows, index, filled):
    return jnp.where(filled, source_rows[index], jnp.zeros((), source_rows.dtype))


def body(
    tokens,
    attn_gain,
    qkv_weight,
    out_weight,
    moe_gain,
    router_weight,
    expert_weight,
    routes,
    cotangent,
):
    rows = tokens.shape[0]
    width = tokens.shape[1]
    tensor_count = lax.axis_size("tensor")
    dp_count = lax.axis_size("dp")
    group_count = dp_count // EXPERTS
    local_width = width // tensor_count
    head_count = local_width // HEAD
    seq_count = rows // SEQ
    scale = 1.0 / math.sqrt(HEAD)
    qkv_full, out_full, gain_one, gain_two, router_full = (
        lax.all_gather(qkv_weight, "dp", axis=0, tiled=True),
        lax.all_gather(out_weight, "dp", axis=0, tiled=True),
        lax.all_gather(attn_gain, "dp", axis=0, tiled=True),
        lax.all_gather(moe_gain, "dp", axis=0, tiled=True),
        lax.all_gather(router_weight, "dp", axis=0, tiled=True),
    )
    qkv_flat = qkv_full.reshape(width, 3 * local_width)
    gain_first = gain_one.astype(jnp.float32)
    gain_second = gain_two.astype(jnp.float32)
    inputs = tokens.astype(jnp.float32)
    scale_one = lax.rsqrt(jnp.mean(inputs * inputs, axis=1, keepdims=True) + epsilon)
    normed_one = inputs * scale_one
    normed_in = (normed_one * gain_first).astype(jnp.bfloat16)
    qkv = jnp.dot(normed_in, qkv_flat, preferred_element_type=jnp.float32)
    cosine, sine = rotary_tables(SEQ, HEAD)
    cosine = cosine[:, None, :]
    sine = sine[:, None, :]
    allowed = block_mask(SEQ)

    def heads_of(block):
        return block.reshape(seq_count, SEQ, head_count, HEAD)

    query = rotate(heads_of(qkv[:, :local_width]), cosine, sine).astype(jnp.bfloat16)
    keys = rotate(heads_of(qkv[:, local_width : 2 * local_width]), cosine, sine).astype(
        jnp.bfloat16
    )
    values = heads_of(qkv[:, 2 * local_width :]).astype(jnp.bfloat16)

    def scores_of(query_seq, key_seq):
        scores = (
            jnp.einsum("qhd,khd->hqk", query_seq, key_seq, preferred_element_type=jnp.float32)
            * scale
        )
        return jnp.where(allowed[None], scores, masked_out)

    def forward_sequence(operands):
        query_seq, key_seq, value_seq = operands
        scores = scores_of(query_seq, key_seq)
        peak = jnp.max(scores, axis=2, keepdims=True)
        expo = jnp.exp(scores - peak)
        totals = jnp.sum(expo, axis=2, keepdims=True)
        probs = (expo / totals).astype(jnp.bfloat16)
        context_seq = jnp.einsum(
            "hqk,khd->qhd", probs, value_seq, preferred_element_type=jnp.float32
        )
        return (context_seq.astype(jnp.bfloat16), (peak + jnp.log(totals))[:, :, 0])

    context, logsum = lax.map(forward_sequence, (query, keys, values))
    context_rows = context.reshape(rows, local_width)
    attn_part = contract(context_rows, out_full, 1, 1)
    hidden = inputs + lax.psum(attn_part, "tensor")
    scale_two = lax.rsqrt(jnp.mean(hidden * hidden, axis=1, keepdims=True) + epsilon)
    normed_two = hidden * scale_two
    moe_in = (normed_two * gain_second).astype(jnp.bfloat16)
    logits = jnp.dot(moe_in, router_full, preferred_element_type=jnp.float32)
    picked = routes[:, :, None] == jnp.arange(EXPERTS, dtype=jnp.int32)[None, None, :]
    picked_float = picked.astype(jnp.float32)
    chosen = jnp.sum(picked_float * logits[:, None, :], axis=2)
    gates = jax.nn.softmax(chosen, axis=1)
    capacity = MOST // group_count
    picked_int = picked.astype(jnp.int32)
    hits = jnp.sum(picked_int, axis=1)
    earlier = jnp.cumsum(hits, axis=0) - hits
    ranking = jnp.sum(picked_int * earlier[:, None, :], axis=2)
    slot = (routes * group_count + ranking % group_count) * capacity + ranking // group_count
    slot_flat = slot.reshape(-1)
    owner = (
        jnp.zeros((dp_count * capacity,), jnp.int32)
        .at[slot_flat]
        .set(jnp.arange(2 * rows, dtype=jnp.int32) + 1)
    )
    filled = (owner > 0)[:, None]
    source_pair = jnp.maximum(owner - 1, 0)
    arrived = send_out(pack(moe_in, source_pair // 2, filled))
    expert_local = group_gather(expert_weight, group_count)
    gate_weight = expert_local[0]
    up_weight = expert_local[1]
    down_weight = expert_local[2]
    pre_gate = jnp.dot(arrived, gate_weight, preferred_element_type=jnp.float32)
    pre_up = jnp.dot(arrived, up_weight, preferred_element_type=jnp.float32)
    activation = (jax.nn.silu(pre_gate) * pre_up).astype(jnp.bfloat16)
    expert_part = contract(activation, down_weight, 1, 1)
    expert_columns = expert_sum(expert_part).astype(jnp.bfloat16)
    pair_columns = send_back(expert_columns)[slot_flat].reshape(rows, 2, local_width)
    expert_rows = widen_source(pair_columns)
    mixed = jnp.sum(gates[:, :, None] * expert_rows.astype(jnp.float32), axis=1)
    layer_out = hidden + mixed
    grad_out = cotangent.astype(jnp.float32)
    gate_grad = jnp.einsum("td,tkd->tk", cotangent, expert_rows, preferred_element_type=jnp.float32)
    pair_grad = (
        (gates[:, :, None] * grad_out[:, None, :]).astype(jnp.bfloat16).reshape(2 * rows, width)
    )
    arrived_grad = send_out(pack(pair_grad, source_pair, filled))
    act_grad = jnp.dot(arrived_grad, down_weight, preferred_element_type=jnp.float32)
    sigma = jax.nn.sigmoid(pre_gate)
    gate_pre_grad = (act_grad * pre_up * sigma * (1.0 + pre_gate * (1.0 - sigma))).astype(
        jnp.bfloat16
    )
    up_pre_grad = (act_grad * pre_gate * sigma).astype(jnp.bfloat16)
    weight_terms = jnp.stack(
        [
            contract(arrived, gate_pre_grad, 0, 0),
            contract(arrived, up_pre_grad, 0, 0),
            contract(arrived_grad, activation, 0, 0),
        ]
    )
    input_part = contract(gate_pre_grad, gate_weight, 1, 1) + contract(up_pre_grad, up_weight, 1, 1)
    input_columns = expert_sum(input_part).astype(jnp.bfloat16)
    back_pairs = send_back(input_columns)[slot_flat].reshape(rows, 2, local_width)
    input_rows = widen_source(back_pairs)
    expert_grad = group_reduce(weight_terms, group_count)
    weighted = jnp.sum(gates * gate_grad, axis=1, keepdims=True)
    chosen_grad = gates * (gate_grad - weighted)
    logit_grad = jnp.sum(picked_float * chosen_grad[:, :, None], axis=1).astype(jnp.bfloat16)
    router_grad = contract(moe_in, logit_grad, 0, 0)
    moe_grad = contract(logit_grad, router_full, 1, 1) + jnp.sum(
        input_rows.astype(jnp.float32), axis=1
    )
    scaled_grad = moe_grad * gain_second
    moe_gain_grad = jnp.sum(moe_grad * normed_two, axis=0)
    hidden_grad = grad_out + scale_two * (
        scaled_grad - normed_two * jnp.mean(scaled_grad * normed_two, axis=1, keepdims=True)
    )
    attn_grad = hidden_grad.astype(jnp.bfloat16)
    out_grad = contract(attn_grad, context_rows, 0, 0)
    context_grad = jnp.dot(attn_grad, out_full, preferred_element_type=jnp.float32).astype(
        jnp.bfloat16
    )
    context_grad = heads_of(context_grad)

    def backward_sequence(operands):
        query_seq, key_seq, value_seq, logsum_seq, grad_seq = operands
        scores = scores_of(query_seq, key_seq)
        probs = jnp.exp(scores - logsum_seq[:, :, None])
        rounded = probs.astype(jnp.bfloat16)
        prob_grad = jnp.einsum(
            "qhd,khd->hqk", grad_seq, value_seq, preferred_element_type=jnp.float32
        )
        score_grad = (
            probs * (prob_grad - jnp.sum(probs * prob_grad, axis=2, keepdims=True))
        ).astype(jnp.bfloat16)
        query_grad = (
            jnp.einsum("hqk,khd->qhd", score_grad, key_seq, preferred_element_type=jnp.float32)
            * scale
        )
        key_grad = (
            jnp.einsum("hqk,qhd->khd", score_grad, query_seq, preferred_element_type=jnp.float32)
            * scale
        )
        value_grad = jnp.einsum(
            "hqk,qhd->khd", rounded, grad_seq, preferred_element_type=jnp.float32
        )
        return (
            rotate(query_grad, cosine, -sine).astype(jnp.bfloat16),
            rotate(key_grad, cosine, -sine).astype(jnp.bfloat16),
            value_grad.astype(jnp.bfloat16),
        )

    query_back, key_back, value_back = lax.map(
        backward_sequence, (query, keys, values, logsum, context_grad)
    )
    qkv_grad_rows = jnp.concatenate(
        [
            query_back.reshape(rows, local_width),
            key_back.reshape(rows, local_width),
            value_back.reshape(rows, local_width),
        ],
        axis=1,
    )
    qkv_grad = contract(normed_in, qkv_grad_rows, 0, 0).reshape(width, 3, local_width)
    normed_grad = lax.psum(
        contract(qkv_grad_rows, qkv_flat, 1, 1).astype(jnp.bfloat16), "tensor"
    ).astype(jnp.float32)
    scaled_in = normed_grad * gain_first
    attn_gain_grad = jnp.sum(normed_grad * normed_one, axis=0)
    input_grad = hidden_grad + scale_one * (
        scaled_in - normed_one * jnp.mean(scaled_in * normed_one, axis=1, keepdims=True)
    )
    shards = (
        lax.psum_scatter(
            qkv_grad.astype(jnp.bfloat16), "dp", scatter_dimension=0, tiled=True
        ).astype(jnp.float32),
        lax.psum_scatter(
            out_grad.astype(jnp.bfloat16), "dp", scatter_dimension=0, tiled=True
        ).astype(jnp.float32),
        lax.psum_scatter(
            attn_gain_grad.astype(jnp.bfloat16), "dp", scatter_dimension=0, tiled=True
        ).astype(jnp.float32),
        lax.psum_scatter(
            moe_gain_grad.astype(jnp.bfloat16), "dp", scatter_dimension=0, tiled=True
        ).astype(jnp.float32),
        lax.psum_scatter(
            router_grad.astype(jnp.bfloat16), "dp", scatter_dimension=0, tiled=True
        ).astype(jnp.float32),
    )
    return (
        layer_out,
        input_grad,
        shards[2],
        shards[0],
        shards[1],
        shards[3],
        shards[4],
        expert_grad,
    )


def solution(mesh):
    placed = (
        P("dp", None),
        P("dp"),
        P("dp", None, "tensor"),
        P("dp", "tensor"),
        P("dp"),
        P("dp", None),
        P(None, "dp", "tensor"),
        P("dp", None),
        P("dp", None),
    )
    return jax.shard_map(
        body,
        mesh=mesh,
        in_specs=placed,
        out_specs=(
            P("dp", None),
            P("dp", None),
            P("dp"),
            P("dp", None, "tensor"),
            P("dp", "tensor"),
            P("dp"),
            P("dp", None),
            P(None, "dp", "tensor"),
        ),
        check_vma=False,
    )
```

profile of v0, /device:TPU:0, one launch (start us, length us, event | category | flops | bytes accessed | tf_op | source)
XLA Modules:
  0.0 2411.4 jit_solution(3569148333382426436)
XLA Ops:
  11.0 22.3 all-gather
  39.5 73.8 %all-gather.7.cloned.1.call-done = bf16[2048,3,512]{0,2,1:T(8,128)(2,1)} async-done(((bf16[256,3,512]{0,2,1:T(8,128)(2,1)}), bf16[2048,3,512]{0,2,1:T(8,128)(2,1)}) %all-gather.7.cloned.1.call-update) | async-done | bytes 6291472 | tf_op jit(solution)/shard_map/all_gather | solution.py:117
  170.5 18.1 all-gather.1
  199.7 122.3 %all-reduce.6.cloned.1.call-done = f32[1024,2048]{1,0:T(8,128)} async-done(((f32[1024,2048]{1,0:T(8,128)}), f32[1024,2048]{1,0:T(8,128)}) %all-reduce.6.cloned.1.call-update) | async-done | bytes 8388624 | tf_op jit(solution)/shard_map/psum | solution.py:167
  334.0 26.5 %gather_fusion = bf16[3072,2048]{1,0:T(8,128)(2,1)} fusion(bf16[1024,2048]{1,0:T(8,128)(2,1)} %multiply_convert_fusion.5, s32[3072]{0:T(1024)S(1)} %get-tuple-element.100), kind=kCustom, calls=%fused_computation | custom fusion | bytes 25178112 | tf_op jit(solution)/shard_map/gather | solution.py:93
  379.2 320.0 %collective-permute-done = bf16[3,1024,1408]{2,1,0:T(8,128)(2,1)} collective-permute-done((bf16[3,1024,1408]{2,1,0:T(8,128)(2,1)}, bf16[3,1024,1408]{2,1,0:T(8,128)(2,1)}, u32[]{:S(2)}, u32[]{:S(2)}) %collective-permute-start) | collective-permute-done | bytes 8650784 | tf_op jit(solution)/shard_map/ppermute | solution.py:21
  711.0 25.8 %fusion.80 = f32[3072,1408]{1,0:T(8,128)} fusion(bf16[3072,2048]{1,0:T(8,128)(2,1)} %bitcast.15, bf16[3,1024,1408]{2,1,0:T(8,128)(2,1)} %get-tuple-element.78, bf16[3,1024,1408]{2,1,0:T(8,128)(2,1)} %get-tuple-element.77), kind=kOutput, calls=%fused_computation.177 | convolution fusion | flops 17728274432 | bytes 47185920 | tf_op jit(solution)/shard_map/dot_general | solution.py:195
  736.8 29.6 %multiply_convert_fusion.2 = (bf16[3072,1408]{1,0:T(8,128)(2,1)}, f32[3072,1408]{1,0:T(8,128)}) fusion(f32[3072,1408]{1,0:T(8,128)} %fusion.80, bf16[3072,2048]{1,0:T(8,128)(2,1)} %bitcast.15, bf16[3,1024,1408]{2,1,0:T(8,128)(2,1)} %get-tuple-element.78, bf16[3,1024,1408]{2,1,0:T(8,128)(2,1)} %get-tuple-element.77), kind=kOutput, calls=%fused_computation.14 | convolution fusion | flops 17754226688 | bytes 73138176 | tf_op jit(solution)/shard_map/dot_general | solution.py:196
  766.4 26.2 %fusion.77 = f32[3072,2048]{1,0:T(8,128)} fusion(bf16[3072,1408]{1,0:T(8,128)(2,1)} %get-tuple-element.105, bf16[3,1024,1408]{2,1,0:T(8,128)(2,1)} %get-tuple-element.77, bf16[3,1024,1408]{2,1,0:T(8,128)(2,1)} %get-tuple-element.78), kind=kOutput, calls=%fused_computation.176 | convolution fusion | flops 17728274432 | bytes 51118080 | tf_op jit(solution)/shard_map/dot_general | solution.py:45
  792.7 180.0 %reduce-scatter.8.cloned.1.call-done = f32[3072,512]{1,0:T(8,128)} async-done(((f32[3072,2048]{1,0:T(8,128)}), f32[3072,512]{1,0:T(8,128)}) %reduce-scatter.8.cloned.1.call-update) | async-done | bytes 6291472 | tf_op jit(solution)/shard_map/reduce_scatter | solution.py:63
  983.1 70.6 %all-to-all-done.1 = bf16[8,384,512]{2,1,0:T(8,128)(2,1)S(1)} async-done(((bf16[8,384,512]{2,1,0:T(8,128)(2,1)}), bf16[8,384,512]{2,1,0:T(8,128)(2,1)S(1)}, u32[]{:S(2)}, u32[]{:S(2)}) %all-to-all-start.1) | async-done | bytes 3145760 | tf_op jit(solution)/shard_map/all_to_all | solution.py:55
  1077.7 20.6 mul.360
  1098.3 26.0 %all_gather.25 = bf16[2048,4]{0,1:T(4,128)(2,1)S(1)} all-gather(bf16[256,4]{0,1:T(4,128)(2,1)S(1)} %copy-done.48), channel_id=1, replica_groups=mesh['dp'=8,'tensor'=4] {'dp'}, dimensions={0}, use_global_device_ids=true | all-gather | bytes 18432 | tf_op jit(solution)/shard_map/all_gather | solution.py:121
  1151.2 28.3 %gather_fusion.2 = bf16[3072,2048]{1,0:T(8,128)(2,1)} fusion(bf16[2048,2048]{1,0:T(8,128)(2,1)} %multiply_convert_fusion.4, s32[3072]{0:T(1024)S(1)} %copy-done.39), kind=kCustom, calls=%fused_computation.2 | custom fusion | bytes 25178112 | tf_op jit(solution)/shard_map/gather | solution.py:93
  1185.9 275.4 %all_to_all.42 = bf16[8,384,2048]{2,1,0:T(8,128)(2,1)} all-to-all(bf16[8,384,2048]{2,1,0:T(8,128)(2,1)S(1)} %broadcast_select_fusion), channel_id=1, replica_groups=mesh['dp'=8,'tensor'=4] {'dp'}, dimensions={0} | all-to-all | bytes 25165824 | tf_op jit(solution)/shard_map/all_to_all | solution.py:51
  1461.2 32.2 %multiply_convert_fusion.1 = (bf16[3072,1408]{1,0:T(8,128)(2,1)}, bf16[3072,1408]{1,0:T(8,128)(2,1)}) fusion(f32[3072,1408]{1,0:T(8,128)} %fusion.80, f32[3072,1408]{1,0:T(8,128)} %get-tuple-element.106, bf16[3072,2048]{1,0:T(8,128)(2,1)} %bitcast.151, bf16[3,1024,1408]{2,1,0:T(8,128)(2,1)} %get-tuple-element.77, bf16[3,1024,1408]{2,1,0:T(8,128)(2,1)} %get-tuple-element.78), kind=kOutput, calls=%fused_computation.13 | convolution fusion | flops 17784504320 | bytes 81788928 | tf_op jit(solution)/shard_map/dot_general | solution.py:210
  1493.4 26.2 %fusion.82 = f32[3072,2048]{1,0:T(8,128)} fusion(bf16[3072,1408]{1,0:T(8,128)(2,1)} %get-tuple-element.76, bf16[3,1024,1408]{2,1,0:T(8,128)(2,1)} %get-tuple-element.78, bf16[3,1024,1408]{2,1,0:T(8,128)(2,1)} %get-tuple-element.77), kind=kOutput, calls=%fused_computation.178 | convolution fusion | flops 17728274432 | bytes 51118080 | tf_op jit(solution)/shard_map/dot_general | solution.py:45
  1519.7 29.8 %convolution_add_fusion = f32[3072,2048]{1,0:T(8,128)} fusion(f32[3072,2048]{1,0:T(8,128)} %fusion.82, bf16[3072,1408]{1,0:T(8,128)(2,1)} %get-tuple-element.63, bf16[3,1024,1408]{2,1,0:T(8,128)(2,1)} %get-tuple-element.78, bf16[3,1024,1408]{2,1,0:T(8,128)(2,1)} %get-tuple-element.77), kind=kOutput, calls=%fused_computation.36 | convolution fusion | flops 17734565888 | bytes 76283904 | tf_op jit(solution)/shard_map/dot_general | solution.py:45
  1549.5 178.6 %reduce-scatter.10.cloned.1.call-done = f32[3072,512]{1,0:T(8,128)} async-done(((f32[3072,2048]{1,0:T(8,128)}), f32[3072,512]{1,0:T(8,128)}) %reduce-scatter.10.cloned.1.call-update) | async-done | bytes 6291472 | tf_op jit(solution)/shard_map/reduce_scatter | solution.py:63
  1731.3 76.5 %all_to_all.43 = bf16[8,384,512]{2,1,0:T(8,128)(2,1)S(1)} all-to-all(bf16[8,384,512]{2,1,0:T(8,128)(2,1)S(1)} %bitcast.154), channel_id=1, replica_groups=mesh['dp'=8,'tensor'=4] {'dp'}, dimensions={0} | all-to-all | bytes 6291456 | tf_op jit(solution)/shard_map/all_to_all | solution.py:55
  1825.9 29.0 %multiply_reduce_fusion.1 = f32[1024,2048]{1,0:T(8,128)} fusion(bf16[1024,2,2048]{2,1,0:T(2,128)(2,1)} %all-gather.11.cloned.1.call-done, f32[1024,2]{1,0:T(8,128)S(1)} %copy-done.11), kind=kLoop, calls=%fused_computation.21 | loop fusion | flops 10485760 | bytes 16785408 | tf_op jit(solution)/shard_map/reduce_sum | solution.py:202
  1855.0 26.8 %convolution_bitcast_fusion = f32[1,2048,1408]{2,1,0:T(8,128)} fusion(bf16[3072,2048]{1,0:T(8,128)(2,1)} %bitcast.152, bf16[3072,1408]{1,0:T(8,128)(2,1)} %get-tuple-element.105), kind=kOutput, calls=%fused_computation.41 | convolution fusion | flops 17716740096 | bytes 32768000 | tf_op jit(solution)/shard_map/dot_general | solution.py:45
  1881.8 24.5 %convolution_bitcast_fusion.1 = f32[1,2048,1408]{2,1,0:T(8,128)} fusion(bf16[3072,2048]{1,0:T(8,128)(2,1)} %bitcast.15, bf16[3072,1408]{1,0:T(8,128)(2,1)S(1)} %bitcast.183), kind=kOutput, calls=%fused_computation.42 | convolution fusion | flops 17716740096 | bytes 32768000 | tf_op jit(solution)/shard_map/dot_general | solution.py:45
  1906.3 28.0 %convert_reduce_fusion = f32[1024,2048]{1,0:T(8,128)} fusion(bf16[1024,2,2048]{2,1,0:T(2,128)(2,1)} %all-gather.13.cloned.1.call-done), kind=kLoop, calls=%fused_computation.19 | loop fusion | flops 6291456 | bytes 16777216 | tf_op jit(solution)/shard_map/reduce_sum | solution.py:232
  1944.9 13.0 multiply_add_fusion
  1964.4 14.0 multiply_reduce_fusion
  2026.6 27.2 %convolution_bitcast_fusion.2 = f32[1,2048,1408]{2,1,0:T(8,128)} fusion(bf16[3072,2048]{1,0:T(8,128)(2,1)} %bitcast.15, bf16[3072,1408]{1,0:T(8,128)(2,1)} %get-tuple-element.63), kind=kOutput, calls=%fused_computation.43 | convolution fusion | flops 17716740096 | bytes 32768000 | tf_op jit(solution)/shard_map/dot_general | solution.py:45
  2061.0 23.8 pad_maximum_fusion
  2084.8 15.8 select_convert_fusion
  2122.3 220.8 %collective-permute-done.1 = bf16[3,1024,1408]{2,1,0:T(8,128)(2,1)} collective-permute-done((bf16[3,1024,1408]{2,1,0:T(8,128)(2,1)}, bf16[3,1024,1408]{2,1,0:T(8,128)(2,1)}, u32[]{:S(2)}, u32[]{:S(2)}) %collective-permute-start.1) | collective-permute-done | bytes 8650784 | tf_op jit(solution)/shard_map/ppermute | solution.py:21
  2343.1 20.7 convert_add_fusion
  2368.7 20.6 all-reduce.2
  (258 shorter events, 322.5 us)
Async XLA Ops:
  7.2 106.2 %all-gather.7.cloned.1.call-start = ((), (), s32[]{:S(2)}) async-start(), calls=%async_computation.9 | async-start | bytes 7077888 | tf_op jit(solution)/shard_map/all_gather | solution.py:117
  9.5 153.5 %all-gather.9.cloned.1.call-start = ((), (), s32[]{:S(2)}) async-start(), calls=%async_computation.10 | async-start | bytes 2359296 | tf_op jit(solution)/shard_map/all_gather | solution.py:118
  10.3 311.7 %all-reduce.6.cloned.1.call-start = ((), (), s32[]{:S(2)}) async-start(), calls=%async_computation.11 | async-start | bytes 16777216 | tf_op jit(solution)/shard_map/psum | solution.py:167
  33.3 90.2 %copy-start.33 = (f32[8,1,256]{2,1,0:T(1,128)}, f32[8,1,256]{2,1,0:T(1,128)S(1)}, u32[]{:S(2)}) copy-start(f32[8,1,256]{2,1,0:T(1,128)S(1)} %convert_element_type.199) | copy-start | bytes 24580
  36.5 87.0 %copy-start.40 = (f32[1024]{0:T(1024)}, f32[1024]{0:T(1024)S(1)}, u32[]{:S(2)}) copy-start(f32[1024]{0:T(1024)S(1)} %add_rsqrt_fusion.1) | copy-start | bytes 12292
  188.6 139.3 %copy-start.25 = (f32[8,1,256]{2,1,0:T(1,128)}, f32[8,1,256]{2,1,0:T(1,128)S(1)}, u32[]{:S(2)}) copy-start(f32[8,1,256]{2,1,0:T(1,128)S(1)} %convert_element_type.200) | copy-start | bytes 24580
  199.0 161.5 %copy-start.44 = (pred[8,384]{1,0:T(8,128)(4,1)}, pred[8,384]{1,0:T(8,128)(4,1)S(1)}, u32[]{:S(2)}) copy-start(pred[8,384]{1,0:T(8,128)(4,1)S(1)} %broadcast_in_dim.104) | copy-start | bytes 9220
  371.2 339.8 %all-to-all-start = ((bf16[8,384,2048]{2,1,0:T(8,128)(2,1)}), bf16[8,384,2048]{2,1,0:T(8,128)(2,1)}, u32[]{:S(2)}, u32[]{:S(2)}) async-start(bf16[8,384,2048]{2,1,0:T(8,128)(2,1)} %broadcast_select_fusion.1), calls=%async_computation | async-start | bytes 25165824 | tf_op jit(solution)/shard_map/all_to_all | solution.py:51
  376.7 596.0 %reduce-scatter.8.cloned.1.call-start = ((), (), s32[]{:S(2)}) async-start(), calls=%async_computation.12 | async-start | bytes 31457280 | tf_op jit(solution)/shard_map/reduce_scatter | solution.py:63
  377.1 322.1 %collective-permute-start = (bf16[3,1024,1408]{2,1,0:T(8,128)(2,1)}, bf16[3,1024,1408]{2,1,0:T(8,128)(2,1)}, u32[]{:S(2)}, u32[]{:S(2)}) collective-permute-start(bf16[3,1024,1408]{2,1,0:T(8,128)(2,1)} %param.15), channel_id=1, source_target_pairs={{0,4},{4,0},{8,12},{12,8},{16,20},{20,16},{24,28},{28,24},{1,5},{5... | collective-permute-start | bytes 25952264 | tf_op jit(solution)/shard_map/ppermute | solution.py:21
  792.6 190.5 %copy-start.43 = (s32[2048,1]{0,1:T(1,128)S(1)}, s32[2048,1]{0,1:T(1,128)}, u32[]{:S(2)}) copy-start(s32[2048,1]{0,1:T(1,128)} %copy-done.42) | copy-start | bytes 24580
  977.6 76.2 %all-to-all-start.1 = ((bf16[8,384,512]{2,1,0:T(8,128)(2,1)}), bf16[8,384,512]{2,1,0:T(8,128)(2,1)S(1)}, u32[]{:S(2)}, u32[]{:S(2)}) async-start(bf16[8,384,512]{2,1,0:T(8,128)(2,1)} %bitcast.153), calls=%async_computation.2 | async-start | bytes 6291456 | tf_op jit(solution)/shard_map/all_to_all | solution.py:55
  983.1 145.4 %all-gather.11.cloned.1.call-start = ((), (), s32[]{:S(2)}) async-start(), calls=%async_computation.13 | async-start | bytes 10485760 | tf_op jit(solution)/shard_map/all_gather | solution.py:59
  983.1 79.8 %copy-start.27 = (s32[2048]{0:T(1024)}, s32[2048]{0:T(1024)S(1)}, u32[]{:S(2)}) copy-start(s32[2048]{0:T(1024)S(1)} %broadcast_clamp_fusion) | copy-start | bytes 24580
  1067.1 661.0 %reduce-scatter.10.cloned.1.call-start = ((), (), s32[]{:S(2)}) async-start(), calls=%async_computation.14 | async-start | bytes 31457280 | tf_op jit(solution)/shard_map/reduce_scatter | solution.py:63
  1077.7 50.6 %copy-start.19 = (s32[1024,2]{0,1:T(2,128)S(1)}, s32[1024,2]{0,1:T(2,128)}, u32[]{:S(2)}) copy-start(s32[1024,2]{0,1:T(2,128)} %param.16) | copy-start | bytes 24580
  1151.2 28.3 %copy-start.45 = (pred[8,384]{1,0:T(8,128)(4,1)S(1)}, pred[8,384]{1,0:T(8,128)(4,1)}, u32[]{:S(2)}) copy-start(pred[8,384]{1,0:T(8,128)(4,1)} %copy-done.44) | copy-start | bytes 9220
  1549.4 258.3 %copy-start.28 = (s32[2048]{0:T(1024)S(1)}, s32[2048]{0:T(1024)}, u32[]{:S(2)}) copy-start(s32[2048]{0:T(1024)} %copy-done.27) | copy-start | bytes 24580
  1549.5 356.9 %all-gather.13.cloned.1.call-start = ((), (), s32[]{:S(2)}) async-start(), calls=%async_computation.15 | async-start | bytes 10485760 | tf_op jit(solution)/shard_map/all_gather | solution.py:59
  1821.2 299.5 %reduce-scatter.16.cloned.1.call-start = ((), (), s32[]{:S(2)}) async-start(), calls=%async_computation.19 | async-start | bytes 589824
  1825.9 537.9 %all-reduce.8.cloned.1.call-start = ((), (), s32[]{:S(2)}) async-start(), calls=%async_computation.16 | async-start | bytes 8388608 | tf_op jit(solution)/shard_map/psum | solution.py:287
  1825.9 55.9 %slice-start.8 = ((s8[8650752]{0:T(1024)(128)(4,1)}), s8[262144]{0:T(1024)(128)(4,1)S(1)}, s32[]{:S(2)}) async-start(s8[8650752]{0:T(1024)(128)(4,1)} %bitcast.182), calls=%async_computation.28 | async-start | bytes 524288
  1855.0 26.8 %slice-start.9 = ((s8[8650752]{0:T(1024)(128)(4,1)}), s8[4194304]{0:T(1024)(128)(4,1)S(1)}, s32[]{:S(2)}) async-start(s8[8650752]{0:T(1024)(128)(4,1)} %bitcast.182), calls=%async_computation.29 | async-start | bytes 8388608
  1855.0 26.8 %slice-start.10 = ((s8[8650752]{0:T(1024)(128)(4,1)}), s8[4194304]{0:T(1024)(128)(4,1)S(1)}, s32[]{:S(2)}) async-start(s8[8650752]{0:T(1024)(128)(4,1)} %bitcast.182), calls=%async_computation.30 | async-start | bytes 8388608
  1906.3 28.1 %copy-start.24 = (bf16[2048,4]{0,1:T(4,128)(2,1)S(1)}, bf16[2048,4]{0,1:T(4,128)(2,1)}, u32[]{:S(2)}) copy-start(bf16[2048,4]{0,1:T(4,128)(2,1)} %copy-done.23) | copy-start | bytes 49156
  1906.3 28.1 %copy-start.26 = (f32[8,1,256]{2,1,0:T(1,128)S(1)}, f32[8,1,256]{2,1,0:T(1,128)}, u32[]{:S(2)}) copy-start(f32[8,1,256]{2,1,0:T(1,128)} %copy-done.25) | copy-start | bytes 24580
  1906.3 28.1 %copy-start.38 = (f32[1024]{0:T(1024)S(1)}, f32[1024]{0:T(1024)}, u32[]{:S(2)}) copy-start(f32[1024]{0:T(1024)} %copy-done.37) | copy-start | bytes 12292
  1906.3 38.6 %slice-start.4 = ((s8[8388608]{0:T(1024)(128)(4,1)}), s8[4194304]{0:T(1024)(128)(4,1)S(1)}, s32[]{:S(2)}) async-start(s8[8388608]{0:T(1024)(128)(4,1)} %bitcast.140), calls=%async_computation.24 | async-start | bytes 8388608
  2026.5 373.6 %reduce-scatter.14.cloned.1.call-start = ((), (), s32[]{:S(2)}) async-start(), calls=%async_computation.18 | async-start | bytes 2359296 | tf_op jit(solution)/shard_map/reduce_scatter | solution.py:299
  2026.6 27.2 %copy-start.51 = (bf16[4,128,1024]{2,1,0:T(8,128)(2,1)S(1)}, bf16[4,128,1024]{2,1,0:T(8,128)(2,1)}, u32[]{:S(2)}) copy-start(bf16[4,128,1024]{2,1,0:T(8,128)(2,1)} %copy-done.50) | copy-start | bytes 3145732
  2060.9 341.0 %reduce-scatter.12.cloned.1.call-start = ((), (), s32[]{:S(2)}) async-start(), calls=%async_computation.17 | async-start | bytes 7077888 | tf_op jit(solution)/shard_map/reduce_scatter | solution.py:296
  2100.6 242.5 %collective-permute-start.1 = (bf16[3,1024,1408]{2,1,0:T(8,128)(2,1)}, bf16[3,1024,1408]{2,1,0:T(8,128)(2,1)}, u32[]{:S(2)}, u32[]{:S(2)}) collective-permute-start(bf16[3,1024,1408]{2,1,0:T(8,128)(2,1)} %select_convert_fusion), channel_id=1, source_target_pairs={{0,4},{4,0},{8,12},{12,8},{16,20},{20,16},{24,28},{28,24},{1,5},{5... | collective-permute-start | bytes 25952264 | tf_op jit(solution)/shard_map/ppermute | solution.py:21
  (47 other events, 434.1 us)
Sparse Core Ops, SparseCore 0:
  10.6 102.7 all-gather.6
  115.5 47.4 all-gather.8
  170.6 151.3 all-reduce.5
  792.8 179.8 reduce-scatter.7
  1067.2 57.5 all-gather.10
  1549.6 178.5 reduce-scatter.9
  1821.3 57.4 all-gather.12
  1882.2 61.8 reduce-scatter.15
  2026.7 83.7 all-reduce.7
  2113.9 78.1 reduce-scatter.13
  2195.7 145.1 reduce-scatter.11
where the time goes:
time: 2420 us; the launch traced here: 2410 us
  waiting for transfers between devices  1170 us (48%)
  blocking collectives  439 us (18%)
  matrix products  377 us (16%)
  other arithmetic  243 us (10%)
  local copies, waits for them, and re-layouts  154 us (6%)
    ppermute x2, waiting for transfers between devices, from_partner(): lax.ppermute(value, axis, [(i, i ^ 1 << distance) for i in range(lax.axis...  541 us
    reduce_scatter x2, waiting for transfers between devices, expert_sum(): lax.psum_scatter(partial_value, 'tensor', scatter_dimension=1, tiled=True)  359 us
    all_to_all x1, blocking collectives, send_out(): return lax.all_to_all(buffer, 'dp', split_axis=0, concat_axis=0, tiled=True)  275 us
    dot_general x12, matrix products, contract(): lax.dot_general(left, right, (((left_dim,), (right_dim,)), ((), ())), pre...  206 us
    psum x1, waiting for transfers between devices, body(): hidden = inputs + lax.psum(attn_part, 'tensor')  122 us
    all_to_all x1, blocking collectives, send_back(): return lax.all_to_all(buffer, 'dp', split_axis=0, concat_axis=0, tiled=True)  76.5 us
    all_gather x1, waiting for transfers between devices, body(): lax.all_gather(qkv_weight, 'dp', axis=0, tiled=True)  73.8 us
    all_to_all x1, waiting for transfers between devices, send_back(): return lax.all_to_all(buffer, 'dp', split_axis=0, concat_axis=0, tiled=True)  70.6 us
  transfers between devices with their start and end apart: 15, of which 8 were waited for; matrix products, arithmetic and copies ran while one was open for 18% of the time, Pallas kernels for 0%

commit v1 on v0

v1 whole, which is shorter than its diff:
```python
import math

import jax
import jax.numpy as jnp
from jax import lax
from jax.sharding import PartitionSpec as P

HEAD = 128
EXPERTS = 4
SEQ = 1024
BLOCK = 256
MOST = 768


epsilon = 1e-05
theta_base = 10000.0
masked_out = -1e30
low = jnp.bfloat16
full = jnp.float32


def swap(value, axis, distance):
    return lax.ppermute(value, axis, [(i, i ^ distance) for i in range(lax.axis_size(axis))])


def rotary_tables(length, width):
    half_width = width // 2
    freqs = theta_base ** (-(jnp.arange(half_width, dtype=jnp.float32) * 2.0 / width))
    angles = jnp.arange(length, dtype=jnp.float32)[:, None] * freqs[None, :]
    cosine = jnp.cos(angles)
    sine = jnp.sin(angles)
    return (jnp.concatenate([cosine, cosine], 1), jnp.concatenate([sine, sine], 1))


def rotate(vectors, cosine, sine):
    half_width = vectors.shape[-1] // 2
    turned = jnp.concatenate([-vectors[..., half_width:], vectors[..., :half_width]], -1)
    return vectors * cosine + turned * sine


def block_mask(length):
    blocks = jnp.arange(length, dtype=jnp.int32) // BLOCK
    return blocks[None, :] <= blocks[:, None]


def contract(left, right, left_dim, right_dim):
    return lax.dot_general(
        left, right, (((left_dim,), (right_dim,)), ((), ())), preferred_element_type=jnp.float32
    )


def levels_of(count):
    return count.bit_length() - 1


def side_of(index, bit):
    return (index >> bit) & 1 == 1


def tensor_sum(value):
    for bit in range(levels_of(lax.axis_size("tensor"))):
        value = value + swap(value, "tensor", 1 << bit)
    return value


def all_sum(value):
    for axis in ("tensor", "dp"):
        for bit in range(levels_of(lax.axis_size(axis))):
            value = value + swap(value, axis, 1 << bit)
    return value


def tensor_reduce(part):
    count = lax.axis_size("tensor")
    place = lax.axis_index("tensor")
    size = part.shape[1] // count
    blocks = [part[:, i * size : (i + 1) * size] for i in range(count)]
    for bit in range(levels_of(count)):
        upper = side_of(place, bit)
        kept = [jnp.where(upper, b, a) for a, b in zip(blocks[::2], blocks[1::2])]
        given = [jnp.where(upper, a, b) for a, b in zip(blocks[::2], blocks[1::2])]
        sent = jnp.concatenate([v.astype(low) for v in given], 1)
        came = swap(sent, "tensor", 1 << bit)
        blocks = [
            v.astype(full) + came[:, i * size : (i + 1) * size].astype(full)
            for i, v in enumerate(kept)
        ]
    return blocks[0]


def tensor_gather(own):
    count = lax.axis_size("tensor")
    place = lax.axis_index("tensor")
    size = own.shape[1]
    held = own
    order = list(range(levels_of(count)))[::-1]
    for bit in order:
        came = swap(held, "tensor", 1 << bit)
        upper = side_of(place, bit)
        number = held.shape[1] // size
        mine = [held[:, i * size : (i + 1) * size] for i in range(number)]
        theirs = [came[:, i * size : (i + 1) * size] for i in range(number)]
        pairs = []
        for a, b in zip(mine, theirs):
            pairs.append((jnp.where(upper, b, a), jnp.where(upper, a, b)))
        held = jnp.concatenate([v for pair in pairs for v in pair], 1)
    return held


def near_gather(own):
    held = [own]
    count = lax.axis_size("tensor")
    for bit in range(levels_of(count))[::-1]:
        came = swap(jnp.concatenate(held, 1) if len(held) > 1 else held[0], "tensor", 1 << bit)
        size = own.shape[1]
        theirs = [came[:, i * size : (i + 1) * size] for i in range(len(held))]
        held = [v for pair in zip(held, theirs) for v in pair]
    return jnp.concatenate(held, 1)


def near_reduce(part):
    count = lax.axis_size("tensor")
    size = part.shape[1] // count
    blocks = [part[:, i * size : (i + 1) * size] for i in range(count)]
    for bit in range(levels_of(count)):
        sent = jnp.concatenate([v.astype(low) for v in blocks[1::2]], 1)
        came = swap(sent, "tensor", 1 << bit)
        blocks = [
            v.astype(full) + came[:, i * size : (i + 1) * size].astype(full)
            for i, v in enumerate(blocks[::2])
        ]
    return blocks[0]


def turn_blocks(value, index, number):
    size = value.shape[0] // number
    blocks = [value[i * size : (i + 1) * size] for i in range(number)]
    for bit in range(levels_of(number)):
        upper = side_of(index, bit)
        blocks = [jnp.where(upper, blocks[i ^ (1 << bit)], blocks[i]) for i in range(number)]
    return jnp.concatenate(blocks, 0) if number > 1 else value


def group_gather(local, position, group_count):
    held = local
    for bit in range(levels_of(group_count)):
        partner = swap(held, "dp", 1 << bit)
        upper = side_of(position, bit)
        held = jnp.concatenate(
            [jnp.where(upper, partner, held), jnp.where(upper, held, partner)], axis=0
        )
    return held


def group_reduce(value, position, group_count):
    current = value
    for bit in range(levels_of(group_count))[::-1]:
        middle = current.shape[0] // 2
        upper = side_of(position, bit)
        kept = jnp.where(upper, current[middle:], current[:middle])
        given = jnp.where(upper, current[:middle], current[middle:])
        current = kept.astype(full) + swap(given.astype(low), "dp", 1 << bit).astype(full)
    return current


def body(
    tokens,
    attn_gain,
    qkv_weight,
    out_weight,
    moe_gain,
    router_weight,
    expert_weight,
    routes,
    cotangent,
):
    rows = tokens.shape[0]
    width = tokens.shape[1]
    tensor_count = lax.axis_size("tensor")
    dp_count = lax.axis_size("dp")
    group_count = dp_count // EXPERTS
    size = width // tensor_count
    hidden_size = expert_weight.shape[2]
    head_count = size // HEAD
    scale = 1.0 / math.sqrt(HEAD)
    place = lax.axis_index("tensor")
    index = lax.axis_index("dp")
    expert = index // group_count
    inner = tensor_count // group_count
    position = (index % group_count) ^ (place // inner)
    turn = place % inner

    def own_columns(value):
        return lax.dynamic_slice_in_dim(value, place * size, size, 1)

    extras = jnp.concatenate([router_weight, attn_gain[:, None], moe_gain[:, None]], 1)
    extras = jnp.pad(extras, ((0, 0), (0, 128 - extras.shape[1])))
    first = lax.all_gather(
        jnp.concatenate([qkv_weight.reshape(-1, 3 * size), extras], 1), "dp", axis=0, tiled=True
    )
    qkv_flat = first[:, : 3 * size]
    small = first[:, 3 * size :].T
    router_full = small[:EXPERTS]
    gain_first = small[EXPERTS : EXPERTS + 1].astype(full)
    gain_second = small[EXPERTS + 1 : EXPERTS + 2].astype(full)
    gain_first_own = own_columns(gain_first)
    gain_second_own = own_columns(gain_second)
    router_own = own_columns(router_full)
    out_full = lax.all_gather(out_weight, "dp", axis=0, tiled=True)

    near = jnp.arange(EXPERTS, dtype=jnp.int32) ^ expert
    routes_t = routes.T
    names = jnp.arange(EXPERTS, dtype=jnp.int32)
    hits = jnp.sum((routes_t[None] == names[:, None, None]).astype(jnp.int32), 1)
    rank = jnp.cumsum(hits, axis=1) - hits
    slot = jnp.where(hits > 0, rank, -1)
    slot_near = jnp.take(slot, near, axis=0)
    chosen = (
        jnp.arange(MOST, dtype=jnp.int32)[None, :, None] == slot_near[:, None, :]
    ).astype(low).reshape(EXPERTS * MOST, rows)

    def to_experts(own):
        packed = jnp.dot(chosen, own, preferred_element_type=full).astype(low)
        parts = [packed[s * MOST : (s + 1) * MOST] for s in range(EXPERTS)]
        parts = [parts[0]] + [
            swap(parts[s], "dp", s * group_count) for s in range(1, EXPERTS)
        ]
        return jnp.concatenate([near_gather(v) for v in parts], 0)

    def to_tokens(part):
        parts = []
        for s in range(EXPERTS):
            own = near_reduce(part[s * MOST : (s + 1) * MOST]).astype(low)
            parts.append(own if s == 0 else swap(own, "dp", s * group_count))
        return contract(chosen, jnp.concatenate(parts, 0), 0, 0)

    grad_own = own_columns(cotangent)
    grad_rows = to_experts(grad_own)

    down_local = turn_blocks(expert_weight[2], turn, inner)
    pair_local = turn_blocks(
        jnp.concatenate([expert_weight[0], expert_weight[1]], 1), turn, inner
    )
    down_weight = group_gather(down_local, position, group_count)
    pair_weight = group_gather(pair_local, position, group_count)

    inputs = tokens.astype(full)
    scale_one = lax.rsqrt(jnp.mean(inputs * inputs, axis=1, keepdims=True) + epsilon)
    normed_in = (inputs * scale_one * gain_first).astype(low)
    inputs_own = own_columns(tokens).astype(full)
    qkv = jnp.dot(normed_in, qkv_flat, preferred_element_type=full)
    cosine, sine = rotary_tables(SEQ, HEAD)
    cosine = cosine[:, None, :]
    sine = sine[:, None, :]
    allowed = block_mask(SEQ)

    def heads_of(block):
        return block.reshape(-1, SEQ, head_count, HEAD)

    query = rotate(heads_of(qkv[:, :size]), cosine, sine).astype(low)
    keys = rotate(heads_of(qkv[:, size : 2 * size]), cosine, sine).astype(low)
    values = heads_of(qkv[:, 2 * size :]).astype(low)

    def scores_of(query_seq, key_seq):
        scores = jnp.einsum("qhd,khd->hqk", query_seq, key_seq, preferred_element_type=full) * scale
        return jnp.where(allowed[None], scores, masked_out)

    def forward_sequence(operands):
        query_seq, key_seq, value_seq = operands
        scores = scores_of(query_seq, key_seq)
        peak = jnp.max(scores, axis=2, keepdims=True)
        expo = jnp.exp(scores - peak)
        totals = jnp.sum(expo, axis=2, keepdims=True)
        probs = (expo / totals).astype(low)
        context_seq = jnp.einsum("hqk,khd->qhd", probs, value_seq, preferred_element_type=full)
        return (context_seq.astype(low), (peak + jnp.log(totals))[:, :, 0])

    context, logsum = lax.map(forward_sequence, (query, keys, values))
    context_rows = context.reshape(rows, size)
    attn_part = contract(context_rows, out_full, 1, 1).astype(low)
    hidden = inputs_own + tensor_reduce(attn_part)

    scaled_hidden = (hidden * gain_second_own).astype(low)
    sums = tensor_sum(
        jnp.concatenate(
            [contract(router_own, scaled_hidden, 1, 1), jnp.sum(hidden * hidden, 1)[None]], 0
        )
    )
    scale_two_row = lax.rsqrt(sums[EXPERTS:] / width + epsilon)
    scale_two = scale_two_row.reshape(rows, 1)
    logits = sums[:EXPERTS] * scale_two_row
    normed_two = hidden * scale_two
    moe_in = (normed_two * gain_second_own).astype(low)
    named = hits > 0
    top = jnp.max(jnp.where(named, logits, masked_out), axis=0, keepdims=True)
    weight = jnp.where(named, jnp.exp(logits - top), 0.0)
    gates = weight / jnp.sum(weight, axis=0, keepdims=True)

    def three_parts(value):
        a = value.astype(low)
        b = (value - a.astype(full)).astype(low)
        return [a, b, (value - a.astype(full) - b.astype(full)).astype(low)]

    gates_near = jnp.take(gates, near, axis=0)
    chosen_blocks = chosen.reshape(EXPERTS, MOST, rows)
    gate_parts = jnp.stack(three_parts(gates_near), 1)
    gate_packed = jnp.sum(
        lax.dot_general(
            gate_parts, chosen_blocks, (((2,), (2,)), ((0,), (0,))), preferred_element_type=full
        ),
        1,
    )
    gate_rows = jnp.concatenate(
        [gate_packed[0]]
        + [swap(gate_packed[s], "dp", s * group_count) for s in range(1, EXPERTS)],
        0,
    )[:, None]

    arrived = to_experts(moe_in)

    raw_grad = jnp.dot(grad_rows, down_weight, preferred_element_type=full)
    both = jnp.dot(arrived, pair_weight, preferred_element_type=full)
    pre_gate = both[:, :hidden_size]
    pre_up = both[:, hidden_size:]
    sigma = jax.nn.sigmoid(pre_gate)
    silu = pre_gate * sigma
    act = silu * pre_up
    gate_grad_part = jnp.sum(act * raw_grad, 1)
    activation = (act * gate_rows).astype(low)
    act_grad = raw_grad * gate_rows
    gate_pre_grad = (act_grad * pre_up * sigma * (1.0 + pre_gate * (1.0 - sigma))).astype(low)
    up_pre_grad = (act_grad * silu).astype(low)
    pre_grad = jnp.concatenate([gate_pre_grad, up_pre_grad], 1)

    input_part = contract(pre_grad, pair_weight, 1, 1).astype(low)
    back = to_tokens(input_part)
    gate_grad_rows = tensor_sum(gate_grad_part.reshape(EXPERTS, MOST))
    gate_grad_near = jnp.stack(
        [gate_grad_rows[0]]
        + [swap(gate_grad_rows[s], "dp", s * group_count) for s in range(1, EXPERTS)],
        0,
    )
    expert_part = contract(activation, down_weight, 1, 1).astype(low)
    mixed = to_tokens(expert_part)
    layer_own = hidden + mixed
    layer_out = tensor_gather(layer_own.astype(low)).astype(full)

    pair_terms = contract(arrived, pre_grad, 0, 0).astype(low)
    down_terms = contract(grad_rows, activation, 0, 0).astype(low)
    pair_grad = turn_blocks(group_reduce(pair_terms, position, group_count), turn, inner)
    down_grad = turn_blocks(group_reduce(down_terms, position, group_count), turn, inner)
    expert_grad = jnp.stack([pair_grad[:, :hidden_size], pair_grad[:, hidden_size:], down_grad])

    gate_grad_parts = jnp.stack(three_parts(gate_grad_near), 1)
    gate_grad = jnp.sum(
        lax.dot_general(
            gate_grad_parts, chosen_blocks, (((2,), (1,)), ((0,), (0,))), preferred_element_type=full
        ),
        1,
    )
    gate_grad = jnp.take(gate_grad, near, axis=0)
    weighted = jnp.sum(gates * gate_grad, axis=0, keepdims=True)
    logit_grad = (gates * (gate_grad - weighted)).astype(low)
    router_grad = jnp.dot(logit_grad, moe_in, preferred_element_type=full)
    moe_grad = contract(logit_grad, router_own, 0, 0) + back

    grad_out = grad_own.astype(full)
    scaled_grad = moe_grad * gain_second_own
    moe_gain_grad = jnp.sum(moe_grad * normed_two, axis=0)
    mean_two = tensor_sum(jnp.sum(scaled_grad * normed_two, axis=1)[None]) / width
    hidden_grad = grad_out + scale_two * (scaled_grad - normed_two * mean_two.reshape(rows, 1))
    attn_grad = tensor_gather(hidden_grad.astype(low))
    out_grad = contract(attn_grad, context_rows, 0, 0)
    out_shard = lax.psum_scatter(
        out_grad.astype(low), "dp", scatter_dimension=0, tiled=True
    ).astype(full)
    context_grad = heads_of(jnp.dot(attn_grad, out_full, preferred_element_type=full).astype(low))

    def backward_sequence(operands):
        query_seq, key_seq, value_seq, logsum_seq, grad_seq = operands
        scores = scores_of(query_seq, key_seq)
        probs = jnp.exp(scores - logsum_seq[:, :, None])
        rounded = probs.astype(low)
        prob_grad = jnp.einsum("qhd,khd->hqk", grad_seq, value_seq, preferred_element_type=full)
        score_grad = (
            probs * (prob_grad - jnp.sum(probs * prob_grad, axis=2, keepdims=True))
        ).astype(low)
        query_grad = (
            jnp.einsum("hqk,khd->qhd", score_grad, key_seq, preferred_element_type=full) * scale
        )
        key_grad = (
            jnp.einsum("hqk,qhd->khd", score_grad, query_seq, preferred_element_type=full) * scale
        )
        value_grad = jnp.einsum("hqk,qhd->khd", rounded, grad_seq, preferred_element_type=full)
        return (
            rotate(query_grad, cosine, -sine).astype(low),
            rotate(key_grad, cosine, -sine).astype(low),
            value_grad.astype(low),
        )

    query_back, key_back, value_back = lax.map(
        backward_sequence, (query, keys, values, logsum, context_grad)
    )
    qkv_grad_rows = jnp.concatenate(
        [v.reshape(rows, size) for v in (query_back, key_back, value_back)], axis=1
    )
    qkv_grad = contract(normed_in, qkv_grad_rows, 0, 0).astype(low)
    qkv_shard = lax.psum_scatter(qkv_grad, "dp", scatter_dimension=0, tiled=True).astype(full)
    normed_grad = tensor_reduce(contract(qkv_grad_rows, qkv_flat, 1, 1).astype(low))
    normed_one = inputs_own * scale_one
    scaled_in = normed_grad * gain_first_own
    attn_gain_grad = jnp.sum(normed_grad * normed_one, axis=0)
    mean_one = tensor_sum(jnp.sum(scaled_in * normed_one, axis=1)[None]) / width
    input_own = hidden_grad + scale_one * (scaled_in - normed_one * mean_one.reshape(rows, 1))
    input_grad = tensor_gather(input_own.astype(low)).astype(full)

    mine = jnp.concatenate(
        [router_grad, attn_gain_grad[None], moe_gain_grad[None]], 0
    )
    mine = lax.dynamic_update_slice_in_dim(
        jnp.zeros((mine.shape[0], width), full), mine, place * size, 1
    )
    share = width // dp_count
    mine = lax.dynamic_slice_in_dim(all_sum(mine), index * share, share, 1)
    return (
        layer_out,
        input_grad,
        mine[EXPERTS],
        qkv_shard.reshape(share, 3, size),
        out_shard,
        mine[EXPERTS + 1],
        mine[:EXPERTS].T,
        expert_grad,
    )


def solution(mesh):
    placed = (
        P("dp", None),
        P("dp"),
        P("dp", None, "tensor"),
        P("dp", "tensor"),
        P("dp"),
        P("dp", None),
        P(None, "dp", "tensor"),
        P("dp", None),
        P("dp", None),
    )
    return jax.shard_map(
        body,
        mesh=mesh,
        in_specs=placed,
        out_specs=(
            P("dp", None),
            P("dp", None),
            P("dp"),
            P("dp", None, "tensor"),
            P("dp", "tensor"),
            P("dp"),
            P("dp", None),
            P(None, "dp", "tensor"),
        ),
        check_vma=False,
    )
```

time: 2420 us -> 1530 us (0.63)
  waiting for transfers between devices: 1170 us -> 570 us
  blocking collectives: 439 us -> 0 us
  other arithmetic: 243 us -> 406 us
  starting transfers between devices: 15.4 us -> 124 us
  local copies, waits for them, and re-layouts: 154 us -> 62.5 us
  matrix products: 377 us -> 340 us
    reduce_scatter x4 -> x2, waiting for transfers between devices: 359 us -> 0.01 us  [the longest x1 0.01 us: body(): lax.psum_scatter(out_grad.astype(low), 'dp', scatter_dimension=0, tiled=T...]
    all_to_all x2 -> x0, blocking collectives: 352 us -> none  [the longest x1 275 us: send_out(): return lax.all_to_all(buffer, 'dp', split_axis=0, concat_axis=0, tiled=True)]
    psum x2 -> x0, waiting for transfers between devices: 122 us -> none  [the longest x1 122 us: body(): hidden = inputs + lax.psum(attn_part, 'tensor')]
    ppermute x2 -> x77, starting transfers between devices: 3.4 us -> 123 us  [swap(): lax.ppermute(value, axis, [(i, i ^ distance) for i in range(lax.axis_size...]
    dot_general x0 -> x2, other arithmetic: none -> 99.6 us  [the longest x1 58.1 us: body(): both = jnp.dot(arrived, pair_weight, preferred_element_type=full)]
    concatenate x0 -> x28, other arithmetic: none -> 85.4 us  [the longest x1 47.9 us: to_experts(): return jnp.concatenate([near_gather(v) for v in parts], 0)]
    ppermute x2 -> x77, waiting for transfers between devices: 541 us -> 467 us  [swap(): lax.ppermute(value, axis, [(i, i ^ distance) for i in range(lax.axis_size...]
    gather x4 -> x3, local copies, waits for them, and re-layouts: 73.2 us -> 2.42 us  [the longest x1 1.29 us: body(): slot_near = jnp.take(slot, near, axis=0)]
  transfers between devices with their start and end apart: 15 -> 81, of which waited for: 8 -> 30; matrix products, arithmetic and copies ran while one was open for 18% -> 39% of each run, Pallas kernels for 0% -> 0%
where the time goes in v1:
time: 1530 us; the launch traced here: 1520 us
  waiting for transfers between devices  570 us (37%)
  other arithmetic  406 us (27%)
  matrix products  340 us (22%)
  starting transfers between devices  124 us (8%)
  local copies, waits for them, and re-layouts  62.5 us (4%)
  between operations  15.7 us (1%)
    ppermute x77, waiting for transfers between devices, swap(): lax.ppermute(value, axis, [(i, i ^ distance) for i in range(lax.axis_size...  467 us
    dot_general x12, matrix products, contract(): lax.dot_general(left, right, (((left_dim,), (right_dim,)), ((), ())), pre...  187 us
    ppermute x77, starting transfers between devices, swap(): lax.ppermute(value, axis, [(i, i ^ distance) for i in range(lax.axis_size...  123 us
    all_gather x1, waiting for transfers between devices, body(): lax.all_gather(jnp.concatenate([qkv_weight.reshape(-1, 3 * size), extras]...  102 us
    dot_general x1, other arithmetic, body(): both = jnp.dot(arrived, pair_weight, preferred_element_type=full)  58.1 us
    concatenate x1, other arithmetic, to_experts(): return jnp.concatenate([near_gather(v) for v in parts], 0)  47.9 us
    dot_general x1, matrix products, body(): both = jnp.dot(arrived, pair_weight, preferred_element_type=full)  44.7 us
    dot_general x1, other arithmetic, contract(): lax.dot_general(left, right, (((left_dim,), (right_dim,)), ((), ())), pre...  41.5 us
  transfers between devices with their start and end apart: 81, of which 30 were waited for; matrix products, arithmetic and copies ran while one was open for 39% of the time, Pallas kernels for 0%

profile of v1, /device:TPU:0, one launch (start us, length us, event | category | flops | bytes accessed | tf_op | source)
XLA Modules:
  0.0 1517.8 jit_solution(16066370203128951875)
XLA Ops:
  18.6 102.1 %all-gather.3.cloned.1.call-done = bf16[2048,1664]{0,1:T(8,128)(2,1)} async-done(((bf16[256,1664]{0,1:T(8,128)(2,1)}), bf16[2048,1664]{0,1:T(8,128)(2,1)}) %all-gather.3.cloned.1.call-update) | async-done | bytes 6815760 | tf_op jit(solution)/shard_map/all_gather | solution.py:198
  122.6 10.1 fusion.24
  209.4 14.8 collective-permute-done.1
  257.7 123.5 %collective-permute-done.19 = bf16[1024,1408]{1,0:T(8,128)(2,1)} collective-permute-done((bf16[1024,1408]{1,0:T(8,128)(2,1)}, bf16[1024,1408]{1,0:T(8,128)(2,1)}, u32[]{:S(2)}, u32[]{:S(2)}) %collective-permute-start.19) | collective-permute-done | bytes 2883616 | tf_op jit(solution)/shard_map/ppermute | solution.py:23
  388.0 15.6 %collective-permute-done.12 = bf16[768,512]{0,1:T(8,128)(2,1)} collective-permute-done((bf16[768,512]{0,1:T(8,128)(2,1)S(1)}, bf16[768,512]{0,1:T(8,128)(2,1)}, u32[]{:S(2)}, u32[]{:S(2)}) %collective-permute-start.12) | collective-permute-done | bytes 786464 | tf_op jit(solution)/shard_map/ppermute | solution.py:23
  406.5 14.9 collective-permute-done.35
  422.1 46.7 %collective-permute-done.38 = bf16[768,512]{0,1:T(8,128)(2,1)} collective-permute-done((bf16[768,512]{0,1:T(8,128)(2,1)}, bf16[768,512]{0,1:T(8,128)(2,1)}, u32[]{:S(2)}, u32[]{:S(2)}) %collective-permute-start.38) | collective-permute-done | bytes 786464 | tf_op jit(solution)/shard_map/ppermute | solution.py:23
  491.0 15.4 %collective-permute-done.36 = bf16[768,512]{0,1:T(8,128)(2,1)S(1)} collective-permute-done((bf16[768,512]{0,1:T(8,128)(2,1)}, bf16[768,512]{0,1:T(8,128)(2,1)S(1)}, u32[]{:S(2)}, u32[]{:S(2)}) %collective-permute-start.36) | collective-permute-done | bytes 786464 | tf_op jit(solution)/shard_map/ppermute | solution.py:23
  506.4 16.8 %collective-permute-done.39 = bf16[768,512]{0,1:T(8,128)(2,1)S(1)} collective-permute-done((bf16[768,512]{0,1:T(8,128)(2,1)}, bf16[768,512]{0,1:T(8,128)(2,1)S(1)}, u32[]{:S(2)}, u32[]{:S(2)}) %collective-permute-start.39) | collective-permute-done | bytes 786464 | tf_op jit(solution)/shard_map/ppermute | solution.py:23
  523.2 11.3 broadcast_select_fusion.2
  548.1 58.1 %maximum_maximum_fusion.11 = bf16[3072,2048]{0,1:T(8,128)(2,1)} fusion(bf16[768,512]{0,1:T(8,128)(2,1)} %get-tuple-element.228, bf16[768,512]{0,1:T(8,128)(2,1)S(1)} %collective-permute-done.13, bf16[768,512]{0,1:T(8,128)(2,1)} %get-tuple-element.227, bf16[768,512]{0,1:T(8,128)(2,1)} %collective-permute-done.12, ...), kind=kLoop, calls=%fused_computation.20.clone.1.clone.2 | loop fusion | flops 201326592 | bytes 25165824 | tf_op jit(solution)/shard_map/dot_general | solution.py:322
  606.3 44.7 %fusion.16 = f32[3072,2816]{0,1:T(8,128)} fusion(bf16[1024,2816]{1,0:T(8,128)(2,1)} %get-tuple-element.164, bf16[1024,2816]{1,0:T(8,128)(2,1)} %get-tuple-element.163, bf16[3072,2048]{0,1:T(8,128)(2,1)} %maximum_maximum_fusion.11), kind=kOutput, calls=%fused_computation.47 | convolution fusion | flops 35456548864 | bytes 58720256 | tf_op jit(solution)/shard_map/dot_general | solution.py:322
  659.2 47.9 %maximum_maximum_fusion.1 = bf16[3072,2048]{0,1:T(8,128)(2,1)} fusion(bf16[768,512]{0,1:T(8,128)(2,1)} %get-tuple-element.236, bf16[768,512]{0,1:T(8,128)(2,1)S(1)} %copy-done.52, bf16[768,512]{0,1:T(8,128)(2,1)} %get-tuple-element.235, bf16[768,512]{0,1:T(8,128)(2,1)S(1)} %copy-done.46, bf16[768,512]{0,1:T(8,128)(2,1)} %get-tuple-element.234, ...), kind=kLoop, calls=%fused_computation.21 | loop fusion | flops 201326592 | bytes 25165824 | tf_op jit(solution)/shard_map/concatenate | solution.py:228
  707.1 30.8 %multiply_reduce_fusion = (f32[3072]{0:T(1024)S(1)}, f32[3072,1408]{0,1:T(8,128)}) fusion(f32[3072,2816]{0,1:T(8,128)} %fusion.16, bf16[3072,2048]{0,1:T(8,128)(2,1)} %maximum_maximum_fusion.1, bf16[1024,1408]{1,0:T(8,128)(2,1)} %get-tuple-element.176, bf16[1024,1408]{1,0:T(8,128)(2,1)} %get-tuple-element.175), kind=kOutput, calls=%fused_computation.7 | convolution fusion | flops 17758547968 | bytes 70266880 | tf_op jit(solution)/shard_map/dot_general | solution.py:321
  765.0 27.9 %multiply_convert_fusion.1 = (bf16[3072,1408]{0,1:T(8,128)(2,1)}, bf16[3072,1408]{0,1:T(8,128)(2,1)}, bf16[3072,1408]{0,1:T(8,128)(2,1)}) fusion(f32[3072,2816]{0,1:T(8,128)} %fusion.16, f32[3072,1408]{0,1:T(8,128)} %get-tuple-element.260, f32[3072]{0:T(1024)S(1)} %pad_maximum_fusion.46), kind=kLoop, calls=%fused_computation.6 | loop fusion | flops 73531392 | bytes 77869056 | tf_op jit(solution)/shard_map/convert_element_type | solution.py:331
  792.9 44.2 %convolution_convert_fusion = bf16[3072,2048]{0,1:T(8,128)(2,1)} fusion(bf16[3072,1408]{0,1:T(8,128)(2,1)} %get-tuple-element.127, bf16[3072,1408]{0,1:T(8,128)(2,1)} %get-tuple-element.126, bf16[1024,2816]{1,0:T(8,128)(2,1)} %get-tuple-element.164, bf16[1024,2816]{1,0:T(8,128)(2,1)} %get-tuple-element.163), kind=kOutput, calls=%fused_computation.30 | convolution fusion | flops 35497443328 | bytes 41418752 | tf_op jit(solution)/shard_map/dot_general | solution.py:47
  856.6 41.5 %maximum_maximum_fusion.10 = bf16[3072,2048]{0,1:T(8,128)(2,1)} fusion(bf16[768,512]{0,1:T(8,128)(2,1)} %get-tuple-element.228, bf16[768,512]{0,1:T(8,128)(2,1)S(1)} %copy-done.30, bf16[768,512]{0,1:T(8,128)(2,1)} %get-tuple-element.227, bf16[768,512]{0,1:T(8,128)(2,1)} %collective-permute-done.12, bf16[768,512]{0,1:T(8,128)(2,1)} %get-tuple-element.226, ...), kind=kLoop, calls=%fused_computation.20.clone.clone.2 | loop fusion | flops 201326592 | bytes 25165824 | tf_op jit(solution)/shard_map/dot_general | solution.py:47
  908.1 47.9 %convolution_convert_fusion.1 = bf16[2048,2816]{1,0:T(8,128)(2,1)} fusion(bf16[3072,1408]{0,1:T(8,128)(2,1)} %get-tuple-element.127, bf16[3072,1408]{0,1:T(8,128)(2,1)} %get-tuple-element.126, bf16[3072,2048]{0,1:T(8,128)(2,1)} %maximum_maximum_fusion.10), kind=kOutput, calls=%fused_computation.31 | convolution fusion | flops 35473850368 | bytes 41418752 | tf_op jit(solution)/shard_map/dot_general | solution.py:47
  967.2 23.2 %convolution_convert_fusion.2 = bf16[3072,2048]{0,1:T(8,128)(2,1)S(1)} fusion(bf16[3072,1408]{0,1:T(8,128)(2,1)} %get-tuple-element.128, bf16[1024,1408]{1,0:T(8,128)(2,1)} %get-tuple-element.176, bf16[1024,1408]{1,0:T(8,128)(2,1)S(1)} %copy-done.59), kind=kOutput, calls=%fused_computation.32 | convolution fusion | flops 17734565888 | bytes 27000832 | tf_op jit(solution)/shard_map/dot_general | solution.py:47
  997.0 21.4 %collective-permute-done.56 = bf16[768,512]{0,1:T(8,128)(2,1)} collective-permute-done((bf16[768,512]{0,1:T(8,128)(2,1)}, bf16[768,512]{0,1:T(8,128)(2,1)}, u32[]{:S(2)}, u32[]{:S(2)}) %collective-permute-start.56) | collective-permute-done | bytes 786464 | tf_op jit(solution)/shard_map/ppermute | solution.py:23
  1034.1 24.9 %convolution_convert_fusion.3 = bf16[2048,1408]{1,0:T(8,128)(2,1)S(1)} fusion(bf16[3072,2048]{0,1:T(8,128)(2,1)} %maximum_maximum_fusion.1, bf16[3072,1408]{0,1:T(8,128)(2,1)} %get-tuple-element.128), kind=kOutput, calls=%fused_computation.45 | convolution fusion | flops 17719623680 | bytes 27000832 | tf_op jit(solution)/shard_map/dot_general | solution.py:47
  1110.7 14.5 multiply_reduce_fusion.1
  1127.8 10.4 multiply_convert_fusion.3
  1161.3 11.8 convolution_convert_fusion.4
  1191.0 15.5 %collective-permute-start.24 = (bf16[768,512]{0,1:T(8,128)(2,1)}, bf16[768,512]{0,1:T(8,128)(2,1)}, u32[]{:S(2)}, u32[]{:S(2)}) collective-permute-start(bf16[768,512]{0,1:T(8,128)(2,1)} %get-tuple-element.156), channel_id=1, source_target_pairs={{0,8},{4,12},{8,0},{12,4},{16,24},{20,28},{24,16},{28,20},{1,9},{5... | collective-permute-start | bytes 2359304 | tf_op jit(solution)/shard_map/ppermute | solution.py:23
  1207.4 100.3 %collective-permute-done.76 = bf16[1024,1408]{1,0:T(8,128)(2,1)} collective-permute-done((bf16[1024,1408]{1,0:T(8,128)(2,1)}, bf16[1024,1408]{1,0:T(8,128)(2,1)}, u32[]{:S(2)}, u32[]{:S(2)}) %collective-permute-start.76) | collective-permute-done | bytes 2883616 | tf_op jit(solution)/shard_map/ppermute | solution.py:23
  1312.9 14.8 collective-permute-done.30
  1340.4 19.9 %collective-permute-done.31 = bf16[1024,512]{1,0:T(8,128)(2,1)S(1)} collective-permute-done((bf16[1024,512]{1,0:T(8,128)(2,1)S(1)}, bf16[1024,512]{1,0:T(8,128)(2,1)S(1)}, u32[]{:S(2)}, u32[]{:S(2)}) %collective-permute-start.31) | collective-permute-done | bytes 1048608 | tf_op jit(solution)/shard_map/ppermute | solution.py:23
  1362.1 17.3 %collective-permute-done.65 = bf16[1024,512]{1,0:T(8,128)(2,1)S(1)} collective-permute-done((bf16[1024,512]{1,0:T(8,128)(2,1)S(1)}, bf16[1024,512]{1,0:T(8,128)(2,1)S(1)}, u32[]{:S(2)}, u32[]{:S(2)}) %collective-permute-start.65) | collective-permute-done | bytes 1048608 | tf_op jit(solution)/shard_map/ppermute | solution.py:23
  1383.7 12.3 convert_add_fusion
  1434.5 11.3 pad_maximum_fusion.1
  1445.8 42.9 %collective-permute-start.73 = (f32[6,2048]{1,0:T(8,128)S(1)}, f32[6,2048]{1,0:T(8,128)S(1)}, u32[]{:S(2)}, u32[]{:S(2)}) collective-permute-start(f32[6,2048]{1,0:T(8,128)S(1)} %add.322), channel_id=1, source_target_pairs={{0,8},{4,12},{8,0},{12,4},{16,24},{20,28},{24,16},{28,20},{1,9},{5... | collective-permute-start | bytes 147464 | tf_op jit(solution)/shard_map/ppermute | solution.py:23
  (558 shorter events, 447.3 us)
Async XLA Ops:
  7.2 113.6 %all-gather.3.cloned.1.call-start = ((), (), s32[]{:S(2)}) async-start(), calls=%async_computation.2 | async-start | bytes 7667712 | tf_op jit(solution)/shard_map/all_gather | solution.py:198
  11.6 159.6 %all-gather.5.cloned.1.call-start = ((), (), s32[]{:S(2)}) async-start(), calls=%async_computation.3 | async-start | bytes 2359296 | tf_op jit(solution)/shard_map/all_gather | solution.py:209
  12.4 1488.0 %reduce-scatter.5.cloned.1.call-start = ((), (), s32[]{:S(2)}) async-start(), calls=%async_computation.5 | async-start | bytes 2359296 | tf_op jit(solution)/shard_map/reduce_scatter | solution.py:374
  192.4 291.1 %collective-permute-start.15 = (bf16[1024,2816]{1,0:T(8,128)(2,1)}, bf16[1024,2816]{1,0:T(8,128)(2,1)}, u32[]{:S(2)}, u32[]{:S(2)}) collective-permute-start(bf16[1024,2816]{1,0:T(8,128)(2,1)} %pad_maximum_fusion.9), channel_id=1, source_target_pairs={{0,4},{4,0},{8,12},{12,8},{16,20},{20,16},{24,28},{28,24},{1,5},{5... | collective-permute-start | bytes 17301512 | tf_op jit(solution)/shard_map/ppermute | solution.py:23
  205.2 176.0 %collective-permute-start.19 = (bf16[1024,1408]{1,0:T(8,128)(2,1)}, bf16[1024,1408]{1,0:T(8,128)(2,1)}, u32[]{:S(2)}, u32[]{:S(2)}) collective-permute-start(bf16[1024,1408]{1,0:T(8,128)(2,1)} %pad_maximum_fusion.15), channel_id=1, source_target_pairs={{0,4},{4,0},{8,12},{12,8},{16,20},{20,16},{24,28},{28,24},{1,5},{5... | collective-permute-start | bytes 8650760 | tf_op jit(solution)/shard_map/ppermute | solution.py:23
  248.3 134.7 %collective-permute-start.4 = (bf16[768,512]{0,1:T(8,128)(2,1)S(1)}, bf16[768,512]{0,1:T(8,128)(2,1)S(1)}, u32[]{:S(2)}, u32[]{:S(2)}) collective-permute-start(bf16[768,512]{0,1:T(8,128)(2,1)S(1)} %get-tuple-element.193), channel_id=1, source_target_pairs={{0,2},{1,3},{2,0},{3,1},{4,6},{5,7},{6,4},{7,5},{8,10},{9,11},{10,... | collective-permute-start | bytes 2359304 | tf_op jit(solution)/shard_map/ppermute | solution.py:23
  249.8 135.5 %collective-permute-start.6 = (bf16[768,512]{0,1:T(8,128)(2,1)S(1)}, bf16[768,512]{0,1:T(8,128)(2,1)}, u32[]{:S(2)}, u32[]{:S(2)}) collective-permute-start(bf16[768,512]{0,1:T(8,128)(2,1)S(1)} %get-tuple-element.196), channel_id=1, source_target_pairs={{0,8},{4,12},{8,0},{12,4},{16,24},{20,28},{24,16},{28,20},{1,9},{5... | collective-permute-start | bytes 2359304 | tf_op jit(solution)/shard_map/ppermute | solution.py:23
  249.8 135.9 %collective-permute-start.9 = (bf16[768,512]{0,1:T(8,128)(2,1)S(1)}, bf16[768,512]{0,1:T(8,128)(2,1)}, u32[]{:S(2)}, u32[]{:S(2)}) collective-permute-start(bf16[768,512]{0,1:T(8,128)(2,1)S(1)} %get-tuple-element.195), channel_id=1, source_target_pairs={{0,16},{4,20},{8,24},{12,28},{16,0},{20,4},{24,8},{28,12},{1,17},{... | collective-permute-start | bytes 2359304 | tf_op jit(solution)/shard_map/ppermute | solution.py:23
  385.7 83.1 %collective-permute-start.38 = (bf16[768,512]{0,1:T(8,128)(2,1)}, bf16[768,512]{0,1:T(8,128)(2,1)}, u32[]{:S(2)}, u32[]{:S(2)}) collective-permute-start(bf16[768,512]{0,1:T(8,128)(2,1)} %get-tuple-element.199), channel_id=1, source_target_pairs={{0,16},{4,20},{8,24},{12,28},{16,0},{20,4},{24,8},{28,12},{1,17},{... | collective-permute-start | bytes 2359304 | tf_op jit(solution)/shard_map/ppermute | solution.py:23
  403.6 66.7 %collective-permute-start.7 = (bf16[768,512]{0,1:T(8,128)(2,1)}, bf16[768,512]{0,1:T(8,128)(2,1)}, u32[]{:S(2)}, u32[]{:S(2)}) collective-permute-start(bf16[768,512]{0,1:T(8,128)(2,1)} %collective-permute-done.6), channel_id=1, source_target_pairs={{0,2},{1,3},{2,0},{3,1},{4,6},{5,7},{6,4},{7,5},{8,10},{9,11},{10,... | collective-permute-start | bytes 2359304 | tf_op jit(solution)/shard_map/ppermute | solution.py:23
  406.0 64.9 %collective-permute-start.10 = (bf16[768,512]{0,1:T(8,128)(2,1)}, bf16[768,512]{0,1:T(8,128)(2,1)}, u32[]{:S(2)}, u32[]{:S(2)}) collective-permute-start(bf16[768,512]{0,1:T(8,128)(2,1)} %collective-permute-done.9), channel_id=1, source_target_pairs={{0,2},{1,3},{2,0},{3,1},{4,6},{5,7},{6,4},{7,5},{8,10},{9,11},{10,... | collective-permute-start | bytes 2359304 | tf_op jit(solution)/shard_map/ppermute | solution.py:23
  421.4 62.1 %collective-permute-start.41 = (bf16[768,512]{0,1:T(8,128)(2,1)}, bf16[768,512]{0,1:T(8,128)(2,1)S(1)}, u32[]{:S(2)}, u32[]{:S(2)}) collective-permute-start(bf16[768,512]{0,1:T(8,128)(2,1)} %get-tuple-element.198), channel_id=1, source_target_pairs={{0,24},{4,28},{8,16},{12,20},{16,8},{20,12},{24,0},{28,4},{1,25},{... | collective-permute-start | bytes 2359304 | tf_op jit(solution)/shard_map/ppermute | solution.py:23
  470.9 52.4 %collective-permute-start.39 = (bf16[768,512]{0,1:T(8,128)(2,1)}, bf16[768,512]{0,1:T(8,128)(2,1)S(1)}, u32[]{:S(2)}, u32[]{:S(2)}) collective-permute-start(bf16[768,512]{0,1:T(8,128)(2,1)} %collective-permute-done.38), channel_id=1, source_target_pairs={{0,2},{1,3},{2,0},{3,1},{4,6},{5,7},{6,4},{7,5},{8,10},{9,11},{10,... | collective-permute-start | bytes 2359304 | tf_op jit(solution)/shard_map/ppermute | solution.py:23
  483.5 59.8 %collective-permute-start.5 = (bf16[768,1024]{0,1:T(8,128)(2,1)S(1)}, bf16[768,1024]{0,1:T(8,128)(2,1)S(1)}, u32[]{:S(2)}, u32[]{:S(2)}) collective-permute-start(bf16[768,1024]{0,1:T(8,128)(2,1)S(1)} %pad_maximum_fusion.21), channel_id=1, source_target_pairs={{0,1},{1,0},{2,3},{3,2},{4,5},{5,4},{6,7},{7,6},{8,9},{9,8},{10,11... | collective-permute-start | bytes 4718600 | tf_op jit(solution)/shard_map/ppermute | solution.py:23
  483.6 60.0 %collective-permute-start.34 = (bf16[768,1024]{0,1:T(8,128)(2,1)S(1)}, bf16[768,1024]{0,1:T(8,128)(2,1)S(1)}, u32[]{:S(2)}, u32[]{:S(2)}) collective-permute-start(bf16[768,1024]{0,1:T(8,128)(2,1)S(1)} %pad_maximum_fusion.29), channel_id=1, source_target_pairs={{0,1},{1,0},{2,3},{3,2},{4,5},{5,4},{6,7},{7,6},{8,9},{9,8},{10,11... | collective-permute-start | bytes 4718600 | tf_op jit(solution)/shard_map/ppermute | solution.py:23
  543.2 107.8 %collective-permute-start.37 = (bf16[768,1024]{0,1:T(8,128)(2,1)}, bf16[768,1024]{0,1:T(8,128)(2,1)}, u32[]{:S(2)}, u32[]{:S(2)}) collective-permute-start(bf16[768,1024]{0,1:T(8,128)(2,1)} %pad_maximum_fusion.30), channel_id=1, source_target_pairs={{0,1},{1,0},{2,3},{3,2},{4,5},{5,4},{6,7},{7,6},{8,9},{9,8},{10,11... | collective-permute-start | bytes 4718600 | tf_op jit(solution)/shard_map/ppermute | solution.py:23
  543.6 110.2 %collective-permute-start.40 = (bf16[768,1024]{0,1:T(8,128)(2,1)}, bf16[768,1024]{0,1:T(8,128)(2,1)}, u32[]{:S(2)}, u32[]{:S(2)}) collective-permute-start(bf16[768,1024]{0,1:T(8,128)(2,1)} %pad_maximum_fusion.31), channel_id=1, source_target_pairs={{0,1},{1,0},{2,3},{3,2},{4,5},{5,4},{6,7},{7,6},{8,9},{9,8},{10,11... | collective-permute-start | bytes 4718600 | tf_op jit(solution)/shard_map/ppermute | solution.py:23
  545.2 111.3 %collective-permute-start.43 = (bf16[768,1024]{0,1:T(8,128)(2,1)}, bf16[768,1024]{0,1:T(8,128)(2,1)}, u32[]{:S(2)}, u32[]{:S(2)}) collective-permute-start(bf16[768,1024]{0,1:T(8,128)(2,1)} %pad_maximum_fusion.32), channel_id=1, source_target_pairs={{0,1},{1,0},{2,3},{3,2},{4,5},{5,4},{6,7},{7,6},{8,9},{9,8},{10,11... | collective-permute-start | bytes 4718600 | tf_op jit(solution)/shard_map/ppermute | solution.py:23
  846.3 55.4 %collective-permute-start.51 = (bf16[768,1024]{0,1:T(8,128)(2,1)}, bf16[768,1024]{0,1:T(8,128)(2,1)}, u32[]{:S(2)}, u32[]{:S(2)}) collective-permute-start(bf16[768,1024]{0,1:T(8,128)(2,1)} %pad_maximum_fusion.34), channel_id=1, source_target_pairs={{0,1},{1,0},{2,3},{3,2},{4,5},{5,4},{6,7},{7,6},{8,9},{9,8},{10,11... | collective-permute-start | bytes 4718600 | tf_op jit(solution)/shard_map/ppermute | solution.py:23
  962.8 55.6 %collective-permute-start.56 = (bf16[768,512]{0,1:T(8,128)(2,1)}, bf16[768,512]{0,1:T(8,128)(2,1)}, u32[]{:S(2)}, u32[]{:S(2)}) collective-permute-start(bf16[768,512]{0,1:T(8,128)(2,1)} %get-tuple-element.143), channel_id=1, source_target_pairs={{0,16},{4,20},{8,24},{12,28},{16,0},{20,4},{24,8},{28,12},{1,17},{... | collective-permute-start | bytes 2359304 | tf_op jit(solution)/shard_map/ppermute | solution.py:23
  966.0 52.5 %collective-permute-start.59 = (bf16[768,512]{0,1:T(8,128)(2,1)S(1)}, bf16[768,512]{0,1:T(8,128)(2,1)}, u32[]{:S(2)}, u32[]{:S(2)}) collective-permute-start(bf16[768,512]{0,1:T(8,128)(2,1)S(1)} %get-tuple-element.142), channel_id=1, source_target_pairs={{0,24},{4,28},{8,16},{12,20},{16,8},{20,12},{24,0},{28,4},{1,25},{... | collective-permute-start | bytes 2359304 | tf_op jit(solution)/shard_map/ppermute | solution.py:23
  1079.9 303.8 %collective-permute-start.75 = (bf16[1024,2816]{1,0:T(8,128)(2,1)}, bf16[1024,2816]{1,0:T(8,128)(2,1)}, u32[]{:S(2)}, u32[]{:S(2)}) collective-permute-start(bf16[1024,2816]{1,0:T(8,128)(2,1)} %broadcast_select_fusion), channel_id=1, source_target_pairs={{0,4},{4,0},{8,12},{12,8},{16,20},{20,16},{24,28},{28,24},{1,5},{5... | collective-permute-start | bytes 17301512 | tf_op jit(solution)/shard_map/ppermute | solution.py:23
  1080.9 226.8 %collective-permute-start.76 = (bf16[1024,1408]{1,0:T(8,128)(2,1)}, bf16[1024,1408]{1,0:T(8,128)(2,1)}, u32[]{:S(2)}, u32[]{:S(2)}) collective-permute-start(bf16[1024,1408]{1,0:T(8,128)(2,1)} %broadcast_select_fusion.3), channel_id=1, source_target_pairs={{0,4},{4,0},{8,12},{12,8},{16,20},{20,16},{24,28},{28,24},{1,5},{5... | collective-permute-start | bytes 8650760 | tf_op jit(solution)/shard_map/ppermute | solution.py:23
  1094.3 90.3 %collective-permute-start.23 = (bf16[768,512]{0,1:T(8,128)(2,1)}, bf16[768,512]{0,1:T(8,128)(2,1)}, u32[]{:S(2)}, u32[]{:S(2)}) collective-permute-start(bf16[768,512]{0,1:T(8,128)(2,1)} %get-tuple-element.147), channel_id=1, source_target_pairs={{0,2},{1,3},{2,0},{3,1},{4,6},{5,7},{6,4},{7,5},{8,10},{9,11},{10,... | collective-permute-start | bytes 2359304 | tf_op jit(solution)/shard_map/ppermute | solution.py:23
  1095.8 88.9 %collective-permute-start.26 = (bf16[768,512]{0,1:T(8,128)(2,1)}, bf16[768,512]{0,1:T(8,128)(2,1)}, u32[]{:S(2)}, u32[]{:S(2)}) collective-permute-start(bf16[768,512]{0,1:T(8,128)(2,1)} %get-tuple-element.146), channel_id=1, source_target_pairs={{0,2},{1,3},{2,0},{3,1},{4,6},{5,7},{6,4},{7,5},{8,10},{9,11},{10,... | collective-permute-start | bytes 2359304 | tf_op jit(solution)/shard_map/ppermute | solution.py:23
  1096.4 88.4 %collective-permute-start.29 = (bf16[768,512]{0,1:T(8,128)(2,1)}, bf16[768,512]{0,1:T(8,128)(2,1)}, u32[]{:S(2)}, u32[]{:S(2)}) collective-permute-start(bf16[768,512]{0,1:T(8,128)(2,1)} %get-tuple-element.145), channel_id=1, source_target_pairs={{0,2},{1,3},{2,0},{3,1},{4,6},{5,7},{6,4},{7,5},{8,10},{9,11},{10,... | collective-permute-start | bytes 2359304 | tf_op jit(solution)/shard_map/ppermute | solution.py:23
  1106.0 401.9 %reduce-scatter.3.cloned.1.call-start = ((), (), s32[]{:S(2)}) async-start(), calls=%async_computation.4 | async-start | bytes 7077888 | tf_op jit(solution)/shard_map/reduce_scatter | solution.py:408
  1184.6 150.1 %collective-permute-start.64 = (bf16[1024,1024]{1,0:T(8,128)(2,1)S(1)}, bf16[1024,1024]{1,0:T(8,128)(2,1)S(1)}, u32[]{:S(2)}, u32[]{:S(2)}) collective-permute-start(bf16[1024,1024]{1,0:T(8,128)(2,1)S(1)} %pad_maximum_fusion.19), channel_id=1, source_target_pairs={{0,1},{1,0},{2,3},{3,2},{4,5},{5,4},{6,7},{7,6},{8,9},{9,8},{10,11... | collective-permute-start | bytes 6291464 | tf_op jit(solution)/shard_map/ppermute | solution.py:23
  1191.0 121.9 %collective-permute-start.24 = (bf16[768,512]{0,1:T(8,128)(2,1)}, bf16[768,512]{0,1:T(8,128)(2,1)}, u32[]{:S(2)}, u32[]{:S(2)}) collective-permute-start(bf16[768,512]{0,1:T(8,128)(2,1)} %get-tuple-element.156), channel_id=1, source_target_pairs={{0,8},{4,12},{8,0},{12,4},{16,24},{20,28},{24,16},{28,20},{1,9},{5... | collective-permute-start | bytes 2359304 | tf_op jit(solution)/shard_map/ppermute | solution.py:23
  1206.5 106.4 %collective-permute-start.27 = (bf16[768,512]{0,1:T(8,128)(2,1)}, bf16[768,512]{0,1:T(8,128)(2,1)}, u32[]{:S(2)}, u32[]{:S(2)}) collective-permute-start(bf16[768,512]{0,1:T(8,128)(2,1)} %get-tuple-element.158), channel_id=1, source_target_pairs={{0,16},{4,20},{8,24},{12,28},{16,0},{20,4},{24,8},{28,12},{1,17},{... | collective-permute-start | bytes 2359304 | tf_op jit(solution)/shard_map/ppermute | solution.py:23
  1362.1 126.6 %collective-permute-start.32 = (bf16[1024,1024]{1,0:T(8,128)(2,1)}, bf16[1024,1024]{1,0:T(8,128)(2,1)}, u32[]{:S(2)}, u32[]{:S(2)}) collective-permute-start(bf16[1024,1024]{1,0:T(8,128)(2,1)} %pad_maximum_fusion.17), channel_id=1, source_target_pairs={{0,1},{1,0},{2,3},{3,2},{4,5},{5,4},{6,7},{7,6},{8,9},{9,8},{10,11... | collective-permute-start | bytes 6291464 | tf_op jit(solution)/shard_map/ppermute | solution.py:23
  1434.5 67.7 %collective-permute-start.69 = (bf16[1024,1024]{1,0:T(8,128)(2,1)}, bf16[1024,1024]{1,0:T(8,128)(2,1)}, u32[]{:S(2)}, u32[]{:S(2)}) collective-permute-start(bf16[1024,1024]{1,0:T(8,128)(2,1)} %pad_maximum_fusion.20), channel_id=1, source_target_pairs={{0,1},{1,0},{2,3},{3,2},{4,5},{5,4},{6,7},{7,6},{8,9},{9,8},{10,11... | collective-permute-start | bytes 6291464 | tf_op jit(solution)/shard_map/ppermute | solution.py:23
  (166 other events, 3692.0 us)
Sparse Core Ops, SparseCore 0:
  11.7 108.9 all-gather.2
  122.9 47.4 all-gather.4
  1106.2 90.6 reduce-scatter.4
  1200.3 175.8 reduce-scatter.2

commit v2 on v1

v2 whole, which is shorter than its diff:
```python
import functools
import math

import jax
import jax.numpy as jnp
from jax import lax
from jax.experimental import pallas as pl
from jax.experimental.pallas import tpu as pltpu
from jax.sharding import PartitionSpec as P

HEAD = 128
EXPERTS = 4
SEQ = 1024
BLOCK = 256
MOST = 768


epsilon = 1e-05
theta_base = 10000.0
masked_out = -1e30
low = jnp.bfloat16
full = jnp.float32


def swap(value, axis, distance):
    return lax.ppermute(value, axis, [(i, i ^ distance) for i in range(lax.axis_size(axis))])


def contract(left, right, left_dim, right_dim):
    return lax.dot_general(
        left, right, (((left_dim,), (right_dim,)), ((), ())), preferred_element_type=jnp.float32
    )


def levels_of(count):
    return count.bit_length() - 1


def side_of(index, bit):
    return (index >> bit) & 1 == 1


def tensor_sum(value):
    for bit in range(levels_of(lax.axis_size("tensor"))):
        value = value + swap(value, "tensor", 1 << bit)
    return value


def all_sum(value):
    for axis in ("tensor", "dp"):
        for bit in range(levels_of(lax.axis_size(axis))):
            value = value + swap(value, axis, 1 << bit)
    return value


def tensor_reduce(part):
    count = lax.axis_size("tensor")
    place = lax.axis_index("tensor")
    size = part.shape[1] // count
    blocks = [part[:, i * size : (i + 1) * size] for i in range(count)]
    for bit in range(levels_of(count)):
        upper = side_of(place, bit)
        kept = [jnp.where(upper, b, a) for a, b in zip(blocks[::2], blocks[1::2])]
        given = [jnp.where(upper, a, b) for a, b in zip(blocks[::2], blocks[1::2])]
        sent = jnp.concatenate([v.astype(low) for v in given], 1)
        came = swap(sent, "tensor", 1 << bit)
        blocks = [
            v.astype(full) + came[:, i * size : (i + 1) * size].astype(full)
            for i, v in enumerate(kept)
        ]
    return blocks[0]


def tensor_gather(own):
    count = lax.axis_size("tensor")
    place = lax.axis_index("tensor")
    size = own.shape[1]
    held = own
    order = list(range(levels_of(count)))[::-1]
    for bit in order:
        came = swap(held, "tensor", 1 << bit)
        upper = side_of(place, bit)
        number = held.shape[1] // size
        mine = [held[:, i * size : (i + 1) * size] for i in range(number)]
        theirs = [came[:, i * size : (i + 1) * size] for i in range(number)]
        pairs = []
        for a, b in zip(mine, theirs):
            pairs.append((jnp.where(upper, b, a), jnp.where(upper, a, b)))
        held = jnp.concatenate([v for pair in pairs for v in pair], 1)
    return held


def after(value, *others):
    return lax.optimization_barrier((value, *others))[0]


def rotary_tables():
    half = HEAD // 2
    freqs = theta_base ** (-(jnp.arange(half, dtype=full) * 2.0 / HEAD))
    angles = jnp.arange(SEQ, dtype=full)[:, None] * freqs[None, :]
    cosine = jnp.cos(angles)
    sine = jnp.sin(angles)
    return (jnp.concatenate([cosine, cosine], 1), jnp.concatenate([-sine, sine], 1))


def limits(mib):
    return pltpu.CompilerParams(vmem_limit_bytes=mib << 20)


def cost(flops, moved, powers=0):
    return pl.CostEstimate(flops=int(flops), bytes_accessed=int(moved), transcendentals=int(powers))


def dot_cols(a, b):
    return lax.dot_general(a, b, (((1,), (1,)), ((), ())), preferred_element_type=full)


def dot_rows(a, b):
    return lax.dot_general(a, b, (((0,), (0,)), ((), ())), preferred_element_type=full)


def attention_kernel(scale, q_in, k_in, v_in, cos, sin, out, q_out, k_out, v_out, logs):
    def turned(ref):
        x = ref[...]
        return (x * cos[...] + pltpu.roll(x, HEAD // 2, 1) * sin[...]).astype(low)

    q_out[...] = turned(q_in)
    k_out[...] = turned(k_in)
    v_out[...] = v_in[...].astype(low)
    for block in range(SEQ // BLOCK):
        mine = pl.ds(block * BLOCK, BLOCK)
        seen = pl.ds(0, (block + 1) * BLOCK)
        scores = dot_cols(q_out[mine, :], k_out[seen, :]) * scale
        peak = jnp.max(scores, axis=1, keepdims=True)
        expo = jnp.exp(scores - peak)
        total = jnp.sum(expo, axis=1, keepdims=True)
        probs = (expo / total).astype(low)
        out[mine, :] = jnp.dot(probs, v_out[seen, :], preferred_element_type=full).astype(low)
        logs[0, mine, :] = peak + jnp.log(total)


def attention(qkv, cosine, sine, scale):
    rows = qkv.shape[0]
    size = qkv.shape[1] // 3
    heads = size // HEAD
    block = (SEQ, HEAD)
    table = pl.BlockSpec(block, lambda s, h: (0, 0))
    spec = pl.BlockSpec(block, lambda s, h: (s, h))
    shape = jax.ShapeDtypeStruct((rows, size), low)
    pairs = rows * heads * SEQ * 5 // 8
    return pl.pallas_call(
        functools.partial(attention_kernel, scale),
        grid=(rows // SEQ, heads),
        in_specs=[
            pl.BlockSpec(block, lambda s, h: (s, h)),
            pl.BlockSpec(block, lambda s, h: (s, heads + h)),
            pl.BlockSpec(block, lambda s, h: (s, 2 * heads + h)),
            table,
            table,
        ],
        out_specs=[spec] * 4 + [pl.BlockSpec((1, SEQ, 1), lambda s, h: (h, s, 0))],
        out_shape=[shape] * 4 + [jax.ShapeDtypeStruct((heads, rows, 1), full)],
        compiler_params=limits(48),
        cost_estimate=cost(4 * pairs * HEAD, rows * size * 20, pairs),
        name="attention",
    )(qkv, qkv, qkv, cosine, sine)


def attention_back_kernel(scale, heads, q_in, k_in, v_in, logs, grad, cos, sin, out, dk, dv):
    head = pl.program_id(1)
    dk[...] = jnp.zeros_like(dk)
    dv[...] = jnp.zeros_like(dv)

    def columns(which):
        return pl.ds(pl.multiple_of((which * heads + head) * HEAD, HEAD), HEAD)

    def turned(x, at):
        return (x * cos[at, :] - pltpu.roll(x, HEAD // 2, 1) * sin[at, :]).astype(low)

    for block in range(SEQ // BLOCK):
        mine = pl.ds(block * BLOCK, BLOCK)
        seen = pl.ds(0, (block + 1) * BLOCK)
        query, keys, values, given = q_in[mine, :], k_in[seen, :], v_in[seen, :], grad[mine, :]
        probs = jnp.exp(dot_cols(query, keys) * scale - logs[0, mine, :])
        prob_grad = dot_cols(given, values)
        inner = jnp.sum(probs * prob_grad, axis=1, keepdims=True)
        score_grad = (probs * (prob_grad - inner)).astype(low)
        query_grad = jnp.dot(score_grad, keys, preferred_element_type=full) * scale
        out[mine, columns(0)] = turned(query_grad, mine)
        dk[seen, :] += dot_rows(score_grad, query)
        dv[seen, :] += dot_rows(probs.astype(low), given)
    whole = pl.ds(0, SEQ)
    out[:, columns(1)] = turned(dk[...] * scale, whole)
    out[:, columns(2)] = dv[...].astype(low)


def attention_back(query, keys, values, logs, grad, cosine, sine, scale):
    rows, size = query.shape
    heads = size // HEAD
    block = (SEQ, HEAD)
    table = pl.BlockSpec(block, lambda s, h: (0, 0))
    spec = pl.BlockSpec(block, lambda s, h: (s, h))
    pairs = rows * heads * SEQ * 5 // 8
    return pl.pallas_call(
        functools.partial(attention_back_kernel, scale, heads),
        grid=(rows // SEQ, heads),
        in_specs=[spec] * 3
        + [pl.BlockSpec((1, SEQ, 1), lambda s, h: (h, s, 0)), spec, table, table],
        out_specs=pl.BlockSpec((SEQ, 3 * size), lambda s, h: (s, 0)),
        out_shape=jax.ShapeDtypeStruct((rows, 3 * size), low),
        scratch_shapes=[pltpu.VMEM(block, full)] * 2,
        compiler_params=limits(48),
        cost_estimate=cost(10 * pairs * HEAD, rows * size * 16, pairs),
        name="attention_back",
    )(query, keys, values, logs, grad, cosine, sine)


def expert_kernel(count, carried, *refs):
    blocks, refs = refs[:count], refs[count:]
    pair, raw, gate = refs[:3]
    rows_out, act_out, grad_out, even, odd, gate_grad, held = refs[3 + carried :]
    size = blocks[0].shape[1]
    hidden = raw.shape[1]
    for i, ref in enumerate(blocks):
        held[:, i * size : (i + 1) * size] = ref[...]
    rows_out[...] = held[...]
    both = jnp.dot(held[...], pair[...], preferred_element_type=full)
    pre_gate = both[:, :hidden]
    pre_up = both[:, hidden:]
    sigma = 1.0 / (1.0 + jnp.exp(-pre_gate))
    silu = pre_gate * sigma
    act = silu * pre_up
    back = raw[...].astype(full)
    gate_grad[...] = jnp.sum(act * back, axis=1, keepdims=True)
    act_out[...] = (act * gate[...]).astype(low)
    back = back * gate[...]
    grad_out[:, :hidden] = (back * pre_up * sigma * (1.0 + pre_gate * (1.0 - sigma))).astype(low)
    grad_out[:, hidden:] = (back * silu).astype(low)
    part = dot_cols(grad_out[...], pair[...]).astype(low)
    for i in range(count):
        (odd if i % 2 else even)[:, i // 2 * size : (i // 2 + 1) * size] = part[
            :, i * size : (i + 1) * size
        ]


def expert_pass(step, blocks, pair, raw, gate, carried):
    count = len(blocks)
    size = blocks[0].shape[1]
    width, both = pair.shape
    hidden = both // 2
    total = raw.shape[0]
    tile = 256
    steps = MOST // tile
    here = lambda i: (step * steps + i, 0)
    near = lambda i: (i, 0)
    near_spec = lambda columns: pl.BlockSpec((tile, columns), near)
    here_spec = lambda columns: pl.BlockSpec((tile, columns), here)
    shape = lambda r, c, t=low: jax.ShapeDtypeStruct((r, c), t)
    inputs = [*blocks, pair, raw, gate, *carried]
    return pl.pallas_call(
        functools.partial(expert_kernel, count, len(carried)),
        grid=(steps,),
        in_specs=[near_spec(size)] * count
        + [
            pl.BlockSpec((width, both), lambda i: (0, 0), pipeline_mode=pl.Buffered(1)),
            here_spec(hidden),
            near_spec(1),
        ]
        + [pl.BlockSpec(memory_space=pl.ANY)] * len(carried),
        out_specs=[
            here_spec(width),
            here_spec(hidden),
            here_spec(both),
            near_spec(width // 2),
            near_spec(width // 2),
            near_spec(1),
        ],
        out_shape=[
            shape(total, width),
            shape(total, hidden),
            shape(total, both),
            shape(MOST, width // 2),
            shape(MOST, width // 2),
            shape(MOST, 1, full),
        ],
        scratch_shapes=[pltpu.VMEM((tile, width), low)],
        input_output_aliases={count + 3 + i: i for i in range(len(carried))},
        compiler_params=limits(60),
        cost_estimate=cost(
            4 * MOST * width * both, width * both * 2 + MOST * (width * 8 + hidden * 8), MOST * hidden
        ),
        name="expert",
    )(*inputs)


def expert_grad_kernel(hidden, turn, pair_a, pair_b, down_a, down_b, out):
    which = pl.program_id(0)

    @pl.when(which < 2)
    def _():
        out[0] = (pair_a[...].astype(full) + pair_b[...].astype(full))[:, :hidden]

    @pl.when(which == 2)
    def _():
        out[0] = (down_a[...].astype(full) + down_b[...].astype(full))[:, :hidden]


def expert_grad_sum(turn, pair_a, pair_b, down_a, down_b, hidden, inner):
    rows = pair_a.shape[0]
    padded = pair_a.shape[1] // 2
    tile = 256
    per = rows // inner // tile
    pair_spec = pl.BlockSpec(
        (tile, padded), lambda w, i, turn: (i ^ (turn[0] * per), jnp.minimum(w, 1))
    )
    down_spec = pl.BlockSpec((tile, padded), lambda w, i, turn: (jnp.where(w == 2, i, 0), 0))
    return pl.pallas_call(
        functools.partial(expert_grad_kernel, hidden),
        grid_spec=pltpu.PrefetchScalarGridSpec(
            num_scalar_prefetch=1,
            grid=(3, rows // tile),
            in_specs=[pair_spec, pair_spec, down_spec, down_spec],
            out_specs=pl.BlockSpec((1, tile, hidden), lambda w, i, turn: (w, i, 0)),
        ),
        out_shape=jax.ShapeDtypeStruct((3, rows, hidden), full),
        compiler_params=limits(32),
        cost_estimate=cost(rows * padded * 3, rows * padded * 24),
        name="expert_grad_sum",
    )(turn, pair_a, pair_b, down_a, down_b)


def near_blocks(own):
    held = [own]
    for bit in range(levels_of(lax.axis_size("tensor")))[::-1]:
        theirs = [swap(v, "tensor", 1 << bit) for v in held]
        held = [v for pair in zip(held, theirs) for v in pair]
    return held


def near_reduce(even, odd):
    count = lax.axis_size("tensor")
    number = count // 2
    size = even.shape[1] // number
    came = swap(odd, "tensor", 1)
    for bit in range(1, levels_of(count)):
        blocks = [
            even[:, i * size : (i + 1) * size].astype(full)
            + came[:, i * size : (i + 1) * size].astype(full)
            for i in range(number)
        ]
        sent = [v.astype(low) for v in blocks[1::2]]
        even = jnp.concatenate(blocks[::2], 1)
        came = swap(jnp.concatenate(sent, 1), "tensor", 1 << bit)
        number //= 2
    return (even.astype(full) + came.astype(full)).astype(low)

def turn_blocks(value, index, number):
    size = value.shape[0] // number
    blocks = [value[i * size : (i + 1) * size] for i in range(number)]
    for bit in range(levels_of(number)):
        upper = side_of(index, bit)
        blocks = [jnp.where(upper, blocks[i ^ (1 << bit)], blocks[i]) for i in range(number)]
    return jnp.concatenate(blocks, 0) if number > 1 else value


def group_gather(local, position, group_count):
    held = local
    for bit in range(levels_of(group_count)):
        partner = swap(held, "dp", 1 << bit)
        upper = side_of(position, bit)
        held = jnp.concatenate(
            [jnp.where(upper, partner, held), jnp.where(upper, held, partner)], axis=0
        )
    return held


def group_sum(term, width, position, group_count):
    top = levels_of(group_count) - 1
    half = width // 2
    upper = (position >> top) & 1
    given = term((1 - upper) * half, half)
    came = swap(given, "dp", 1 << top)
    kept = functools.partial(term, upper * half, half)
    return given, came, kept


def group_finish(kept, came, position, group_count):
    for bit in range(levels_of(group_count) - 1)[::-1]:
        current = kept.astype(full) + came.astype(full)
        middle = current.shape[0] // 2
        upper = (position >> bit) & 1
        kept = lax.dynamic_slice_in_dim(current, upper * middle, middle, 0)
        given = lax.dynamic_slice_in_dim(current, (1 - upper) * middle, middle, 0)
        came = swap(given.astype(low), "dp", 1 << bit)
    return kept, came


def body(
    tokens,
    attn_gain,
    qkv_weight,
    out_weight,
    moe_gain,
    router_weight,
    expert_weight,
    routes,
    cotangent,
):
    rows = tokens.shape[0]
    width = tokens.shape[1]
    tensor_count = lax.axis_size("tensor")
    dp_count = lax.axis_size("dp")
    group_count = dp_count // EXPERTS
    size = width // tensor_count
    hidden_size = expert_weight.shape[2]
    padded = -(-hidden_size // 128) * 128
    scale = 1.0 / math.sqrt(HEAD)
    place = lax.axis_index("tensor")
    index = lax.axis_index("dp")
    expert = index // group_count
    member = index % group_count
    inner = tensor_count // group_count
    position = member ^ (place // inner)
    turn = place % inner

    def own_columns(value):
        return lax.dynamic_slice_in_dim(value, place * size, size, 1)

    extras = jnp.concatenate([router_weight, attn_gain[:, None], moe_gain[:, None]], 1)
    extras = jnp.pad(extras, ((0, 0), (0, 128 - extras.shape[1])))
    first = lax.all_gather(
        jnp.concatenate([qkv_weight.reshape(-1, 3 * size), extras], 1), "dp", axis=0, tiled=True
    )
    qkv_flat = first[:, : 3 * size]
    small = first[:, 3 * size :].T
    router_full = small[:EXPERTS]
    gain_first = small[EXPERTS : EXPERTS + 1].astype(full)
    gain_second = small[EXPERTS + 1 : EXPERTS + 2].astype(full)
    gain_first_own = own_columns(gain_first)
    gain_second_own = own_columns(gain_second)
    router_own = own_columns(router_full)
    out_full = lax.all_gather(out_weight, "dp", axis=0, tiled=True)

    near = jnp.arange(EXPERTS, dtype=jnp.int32) ^ expert
    names = jnp.arange(EXPERTS, dtype=jnp.int32)
    hits = jnp.sum((routes.T[None] == names[:, None, None]).astype(jnp.int32), 1)
    rank = jnp.cumsum(hits, axis=1) - hits
    slot_near = jnp.take(jnp.where(hits > 0, rank, -1), near, axis=0)
    places = jnp.arange(MOST, dtype=jnp.int32)[:, None]
    chosen = [(places == slot_near[s][None, :]).astype(low) for s in range(EXPERTS)]

    def packed(own):
        return [jnp.dot(c, own, preferred_element_type=full).astype(low) for c in chosen]

    def exchange(parts):
        return [parts[0]] + [swap(parts[s], "dp", s * group_count) for s in range(1, EXPERTS)]

    def unpacked(parts):
        total = contract(chosen[0], parts[0], 0, 0)
        for c, part in zip(chosen[1:], parts[1:]):
            total = total + contract(c, part, 0, 0)
        return total

    def widened(value):
        return jnp.pad(value, ((0, 0), (0, padded - hidden_size)))

    down_local = widened(expert_weight[2])
    pair_local = turn_blocks(
        jnp.concatenate([widened(expert_weight[0]), widened(expert_weight[1])], 1), turn, inner
    )
    down_weight = lax.optimization_barrier(
        group_gather(after(down_local, first), member, group_count)
    )
    pair_weight = group_gather(after(pair_local, down_weight), position, group_count)

    grad_own = own_columns(cotangent)
    grad_packed = [after(v, first) for v in packed(grad_own)]
    grad_rows = lax.all_gather(
        jnp.concatenate(exchange(grad_packed), 0), "tensor", axis=1, tiled=True
    )

    inputs = tokens.astype(full)
    scale_one = lax.rsqrt(jnp.mean(inputs * inputs, axis=1, keepdims=True) + epsilon)
    normed_in = (inputs * scale_one * gain_first).astype(low)
    inputs_own = own_columns(tokens).astype(full)
    qkv = jnp.dot(normed_in, qkv_flat, preferred_element_type=full)
    cosine, sine = rotary_tables()
    context, query, keys, values, logs = attention(qkv, cosine, sine, scale)
    attn_part = contract(context, out_full, 1, 1).astype(low)
    hidden = after(inputs_own + tensor_reduce(attn_part), down_weight)

    scaled_hidden = (hidden * gain_second_own).astype(low)
    sums = tensor_sum(
        jnp.concatenate(
            [contract(router_own, scaled_hidden, 1, 1), jnp.sum(hidden * hidden, 1)[None]], 0
        )
    )
    scale_two_row = lax.rsqrt(sums[EXPERTS:] / width + epsilon)
    scale_two = scale_two_row.reshape(rows, 1)
    logits = sums[:EXPERTS] * scale_two_row
    normed_two = hidden * scale_two
    moe_in = (normed_two * gain_second_own).astype(low)
    named = hits > 0
    top = jnp.max(jnp.where(named, logits, masked_out), axis=0, keepdims=True)
    weight = jnp.where(named, jnp.exp(logits - top), 0.0)
    gates = weight / jnp.sum(weight, axis=0, keepdims=True)

    def three_parts(value):
        a = value.astype(low)
        b = (value - a.astype(full)).astype(low)
        return jnp.stack([a, b, (value - a.astype(full) - b.astype(full)).astype(low)])

    moe_packed = packed(moe_in)
    arrived = [near_blocks(v) for v in exchange(moe_packed)]

    gates_near = jnp.take(gates, near, axis=0)
    gate_rows = exchange(
        [
            jnp.sum(contract(three_parts(gates_near[s]), chosen[s], 1, 1), 0)
            for s in range(EXPERTS)
        ]
    )

    grad_rows = after(grad_rows, *moe_packed)
    raw = jnp.dot(grad_rows, down_weight, preferred_element_type=full).astype(low)
    carried = ()
    returned = []
    gate_grads = []
    for step in range(EXPERTS):
        moe_rows, activation, pre_grad, even, odd, gate_grad = expert_pass(
            step, arrived[step], pair_weight, raw, gate_rows[step][:, None], carried
        )
        carried = (moe_rows, activation, pre_grad)
        returned.append(near_reduce(even, odd))
        gate_grads.append(gate_grad)
    back = unpacked(exchange(returned))
    gate_grad_rows = tensor_sum(jnp.concatenate(gate_grads, 1).T)
    gate_grad_near = jnp.stack(exchange([gate_grad_rows[s] for s in range(EXPERTS)]))

    def down_term(start, number):
        part = lax.dynamic_slice_in_dim(grad_rows, start, number, 1)
        return contract(part, activation, 0, 0).astype(low)

    def pair_term(start, number):
        part = lax.dynamic_slice_in_dim(moe_rows, start, number, 1)
        return contract(part, pre_grad, 0, 0).astype(low)

    down_given, down_came, down_kept = group_sum(down_term, width, member, group_count)
    pair_given, pair_came, pair_kept = group_sum(pair_term, width, position, group_count)
    expert_part = contract(
        after(activation, down_given, pair_given), down_weight, 1, 1
    ).astype(low)
    expert_own = lax.psum_scatter(expert_part, "tensor", scatter_dimension=1, tiled=True)
    mixed = unpacked(exchange([expert_own[s * MOST : (s + 1) * MOST] for s in range(EXPERTS)]))
    layer_own = hidden + mixed
    layer_out = tensor_gather(layer_own.astype(low)).astype(full)
    down_a, down_b = group_finish(down_kept(), down_came, member, group_count)
    pair_a, pair_b = group_finish(pair_kept(), pair_came, position, group_count)
    expert_grad = expert_grad_sum(
        turn[None].astype(jnp.int32), pair_a, pair_b, down_a, down_b, hidden_size, inner
    )

    gate_grad = jnp.stack(
        [
            jnp.sum(contract(three_parts(gate_grad_near[s]), chosen[s], 1, 0), 0)
            for s in range(EXPERTS)
        ]
    )
    gate_grad = jnp.take(gate_grad, near, axis=0)
    weighted = jnp.sum(gates * gate_grad, axis=0, keepdims=True)
    logit_grad = (gates * (gate_grad - weighted)).astype(low)
    router_grad = jnp.dot(logit_grad, moe_in, preferred_element_type=full)
    moe_grad = contract(logit_grad, router_own, 0, 0) + back

    grad_out = grad_own.astype(full)
    scaled_grad = moe_grad * gain_second_own
    moe_gain_grad = jnp.sum(moe_grad * normed_two, axis=0)
    mean_two = tensor_sum(jnp.sum(scaled_grad * normed_two, axis=1)[None]) / width
    hidden_grad = grad_out + scale_two * (scaled_grad - normed_two * mean_two.reshape(rows, 1))
    attn_grad = tensor_gather(hidden_grad.astype(low))
    out_grad = contract(attn_grad, context, 0, 0)
    out_shard = lax.psum_scatter(
        out_grad.astype(low), "dp", scatter_dimension=0, tiled=True
    ).astype(full)
    context_grad = jnp.dot(attn_grad, out_full, preferred_element_type=full).astype(low)
    qkv_grad_rows = attention_back(query, keys, values, logs, context_grad, cosine, sine, scale)
    qkv_grad = contract(normed_in, qkv_grad_rows, 0, 0).astype(low)
    qkv_shard = lax.psum_scatter(qkv_grad, "dp", scatter_dimension=0, tiled=True).astype(full)
    normed_grad = tensor_reduce(contract(qkv_grad_rows, qkv_flat, 1, 1).astype(low))
    normed_one = inputs_own * scale_one
    scaled_in = normed_grad * gain_first_own
    attn_gain_grad = jnp.sum(normed_grad * normed_one, axis=0)
    mean_one = tensor_sum(jnp.sum(scaled_in * normed_one, axis=1)[None]) / width
    input_own = hidden_grad + scale_one * (scaled_in - normed_one * mean_one.reshape(rows, 1))
    input_grad = tensor_gather(input_own.astype(low)).astype(full)

    mine = jnp.concatenate([router_grad, attn_gain_grad[None], moe_gain_grad[None]], 0)
    mine = lax.dynamic_update_slice_in_dim(
        jnp.zeros((mine.shape[0], width), full), mine, place * size, 1
    )
    share = width // dp_count
    mine = lax.dynamic_slice_in_dim(all_sum(mine), index * share, share, 1)
    return (
        layer_out,
        input_grad,
        mine[EXPERTS],
        qkv_shard.reshape(share, 3, size),
        out_shard,
        mine[EXPERTS + 1],
        mine[:EXPERTS].T,
        expert_grad,
    )


def solution(mesh):
    placed = (
        P("dp", None),
        P("dp"),
        P("dp", None, "tensor"),
        P("dp", "tensor"),
        P("dp"),
        P("dp", None),
        P(None, "dp", "tensor"),
        P("dp", None),
        P("dp", None),
    )
    return jax.shard_map(
        body,
        mesh=mesh,
        in_specs=placed,
        out_specs=(
            P("dp", None),
            P("dp", None),
            P("dp"),
            P("dp", None, "tensor"),
            P("dp", "tensor"),
            P("dp"),
            P("dp", None),
            P(None, "dp", "tensor"),
        ),
        check_vma=False,
    )
```

time: 1530 us -> 1330 us (0.87)
  other arithmetic: 406 us -> 102 us
  Pallas kernels: 0 us -> 143 us
  matrix products: 340 us -> 206 us
  waiting for transfers between devices: 570 us -> 700 us
  local copies, waits for them, and re-layouts: 62.5 us -> 44.7 us
  starting transfers between devices: 124 us -> 108 us
    pallas_call x0 -> x7, Pallas kernels: none -> 143 us  [the longest x4 102 us: expert_pass(): pl.pallas_call(functools.partial(expert_kernel, count, len(carried)), gri...]
    ppermute x77 -> x65, waiting for transfers between devices: 467 us -> 568 us  [swap(): lax.ppermute(value, axis, [(i, i ^ distance) for i in range(lax.axis_size...]
    dot_general x2 -> x0, other arithmetic: 99.6 us -> none  [the longest x1 58.1 us: body(): both = jnp.dot(arrived, pair_weight, preferred_element_type=full)]
    dot_general x12 -> x9, matrix products: 137 us -> 38.4 us  [the longest x1 25.3 us: body(): jnp.dot(grad_rows, down_weight, preferred_element_type=full).astype(low)]
    concatenate x19 -> x4, other arithmetic: 73.9 us -> 16.4 us  [the longest x2 14.3 us: group_gather(): jnp.concatenate([jnp.where(upper, partner, held), jnp.where(upper, held,...]
    convert_element_type x10 -> x9, other arithmetic: 66.8 us -> 12.6 us  [the longest x4 6.04 us: near_reduce(): sent = [v.astype(low) for v in blocks[1::2]]]
    dot_general x12 -> x27, matrix products: 187 us -> 151 us  [contract(): lax.dot_general(left, right, (((left_dim,), (right_dim,)), ((), ())), pre...]
    all_gather x1, waiting for transfers between devices: 0.02 us -> 33.9 us  [body(): out_full = lax.all_gather(out_weight, 'dp', axis=0, tiled=True)]
  transfers between devices with their start and end apart: 81 -> 71, of which waited for: 30 -> 28; matrix products, arithmetic and copies ran while one was open for 39% -> 19% of each run, Pallas kernels for 0% -> 9%
where the time goes in v2:
time: 1330 us; the launch traced here: 1320 us
  waiting for transfers between devices  700 us (53%)
  matrix products  206 us (15%)
  Pallas kernels  143 us (11%)
  starting transfers between devices  108 us (8%)
  other arithmetic  102 us (8%)
  local copies, waits for them, and re-layouts  44.7 us (3%)
  between operations  15.9 us (1%)
    ppermute x65, waiting for transfers between devices, swap(): lax.ppermute(value, axis, [(i, i ^ distance) for i in range(lax.axis_size...  568 us
    dot_general x27, matrix products, contract(): lax.dot_general(left, right, (((left_dim,), (right_dim,)), ((), ())), pre...  151 us
    ppermute x65, starting transfers between devices, swap(): lax.ppermute(value, axis, [(i, i ^ distance) for i in range(lax.axis_size...  107 us
    pallas_call x4, Pallas kernels, expert_pass(): pl.pallas_call(functools.partial(expert_kernel, count, len(carried)), gri...  102 us
    all_gather x1, waiting for transfers between devices, body(): lax.all_gather(jnp.concatenate([qkv_weight.reshape(-1, 3 * size), extras]...  96.8 us
    all_gather x1, waiting for transfers between devices, body(): out_full = lax.all_gather(out_weight, 'dp', axis=0, tiled=True)  33.9 us
  transfers between devices with their start and end apart: 71, of which 28 were waited for; matrix products, arithmetic and copies ran while one was open for 19% of the time, Pallas kernels for 9%

profile of v2, /device:TPU:0, one launch (start us, length us, event | category | flops | bytes accessed | tf_op | source)
XLA Modules:
  0.0 1319.2 jit_solution(8711804204291145195)
XLA Ops:
  23.9 96.8 %all-gather.4.cloned.1.call-done = bf16[2048,1664]{0,1:T(8,128)(2,1)} async-done(((bf16[256,1664]{0,1:T(8,128)(2,1)}), bf16[2048,1664]{0,1:T(8,128)(2,1)}) %all-gather.4.cloned.1.call-update) | async-done | bytes 6815760 | tf_op jit(solution)/shard_map/all_gather | solution.py:431
  124.1 11.8 fusion.19.q_in.k_in.v_in
  135.9 12.5 attention.1
  150.4 33.9 %all-gather.6.cloned.1.call-done = bf16[2048,512]{1,0:T(8,128)(2,1)} async-done(((bf16[256,512]{1,0:T(8,128)(2,1)}), bf16[2048,512]{1,0:T(8,128)(2,1)}) %all-gather.6.cloned.1.call-update) | async-done | bytes 2097168 | tf_op jit(solution)/shard_map/all_gather | solution.py:442
  207.6 18.0 %collective-permute-done.1 = bf16[1024,512]{1,0:T(8,128)(2,1)S(1)} collective-permute-done((bf16[1024,512]{1,0:T(8,128)(2,1)S(1)}, bf16[1024,512]{1,0:T(8,128)(2,1)S(1)}, u32[]{:S(2)}, u32[]{:S(2)}) %collective-permute-start.1) | collective-permute-done | bytes 1048608 | tf_op jit(solution)/shard_map/ppermute | solution.py:26
  246.4 25.7 %collective-permute-done.10 = bf16[768,512]{1,0:T(8,128)(2,1)S(1)} collective-permute-done((bf16[768,512]{1,0:T(8,128)(2,1)S(1)}, bf16[768,512]{1,0:T(8,128)(2,1)S(1)}, u32[]{:S(2)}, u32[]{:S(2)}) %collective-permute-start.10) | collective-permute-done | bytes 786464 | tf_op jit(solution)/shard_map/ppermute | solution.py:26
  272.1 24.6 %collective-permute-done.11 = bf16[768,512]{1,0:T(8,128)(2,1)S(1)} collective-permute-done((bf16[768,512]{1,0:T(8,128)(2,1)S(1)}, bf16[768,512]{1,0:T(8,128)(2,1)S(1)}, u32[]{:S(2)}, u32[]{:S(2)}) %collective-permute-start.11) | collective-permute-done | bytes 786464 | tf_op jit(solution)/shard_map/ppermute | solution.py:26
  315.5 15.8 %collective-permute-start.23 = (f32[768]{0:T(1024)S(1)}, f32[768]{0:T(1024)S(1)}, u32[]{:S(2)}, u32[]{:S(2)}) collective-permute-start(f32[768]{0:T(1024)S(1)} %fusion.104), channel_id=1, source_target_pairs={{0,8},{4,12},{8,0},{12,4},{16,24},{20,28},{24,16},{28,20},{1,9},{5... | collective-permute-start | bytes 9224 | tf_op jit(solution)/shard_map/ppermute | solution.py:26
  355.1 72.6 %collective-permute-done.9 = bf16[1024,2816]{1,0:T(8,128)(2,1)} collective-permute-done((bf16[1024,2816]{1,0:T(8,128)(2,1)}, bf16[1024,2816]{1,0:T(8,128)(2,1)}, u32[]{:S(2)}, u32[]{:S(2)}) %collective-permute-start.9) | collective-permute-done | bytes 5767200 | tf_op jit(solution)/shard_map/ppermute | solution.py:26
  438.7 11.0 pad_maximum_fusion.refs_4_
  449.7 25.3 %convolution_convert_fusion.refs_5_ = bf16[3072,1408]{1,0:T(8,128)(2,1)} fusion(bf16[3072,2048]{1,0:T(8,128)(2,1)} %all-gather.8.cloned.1.call-done, bf16[2048,1408]{1,0:T(8,128)(2,1)} %pad_maximum_fusion.1), kind=kOutput, calls=%fused_computation.4 | convolution fusion | flops 17721065472 | bytes 27000832 | tf_op jit(solution)/shard_map/dot_general | solution.py:525
  477.3 25.4 %expert.4 = (bf16[3072,2048]{1,0:T(8,128)(2,1)}, bf16[3072,1408]{1,0:T(8,128)(2,1)}, bf16[3072,2816]{1,0:T(8,128)(2,1)}, bf16[768,1024]{1,0:T(8,128)(2,1)}, bf16[768,1024]{1,0:T(8,128)(2,1)}, /*index=5*/f32[768,1]{1,0:T(8,128)}) custom-call(bf16[768,512]{1,0:T(8,128)(2,1)} %fusion.89.refs_0_, bf16[768,512]{1,0:T(8,128)(2,1)} %collective-permute-done.24.refs_1_, ...), custom_call_target="tpu_custom_call" | custom-call | flops 17716740096 | bytes 32768000 | tf_op jit(solution)/shard_map/expert/pallas_call | solution.py:260
  512.1 25.7 %expert.5 = (bf16[3072,2048]{1,0:T(8,128)(2,1)}, bf16[3072,1408]{1,0:T(8,128)(2,1)}, bf16[3072,2816]{1,0:T(8,128)(2,1)}, bf16[768,1024]{1,0:T(8,128)(2,1)}, bf16[768,1024]{1,0:T(8,128)(2,1)}, /*index=5*/f32[768,1]{1,0:T(8,128)}) custom-call(bf16[768,512]{1,0:T(8,128)(2,1)} %collective-permute-done.19.refs_, ...), custom_call_target="tpu_custom_call", output_to_operand_aliasing={{0}: (7, {}), {1}: (8, {}), {2}: (9, {})} | custom-call | flops 17716740096 | bytes 32768000 | tf_op jit(solution)/shard_map/expert/pallas_call | solution.py:260
  537.8 25.5 %expert.6 = (bf16[3072,2048]{1,0:T(8,128)(2,1)}, bf16[3072,1408]{1,0:T(8,128)(2,1)}, bf16[3072,2816]{1,0:T(8,128)(2,1)}, bf16[768,1024]{1,0:T(8,128)(2,1)}, bf16[768,1024]{1,0:T(8,128)(2,1)}, /*index=5*/f32[768,1]{1,0:T(8,128)}) custom-call(bf16[768,512]{1,0:T(8,128)(2,1)} %collective-permute-done.14.refs_, ...), custom_call_target="tpu_custom_call", output_to_operand_aliasing={{0}: (7, {}), {1}: (8, {}), {2}: (9, {})} | custom-call | flops 17716740096 | bytes 32768000 | tf_op jit(solution)/shard_map/expert/pallas_call | solution.py:260
  563.3 25.9 %expert.7 = (bf16[3072,2048]{1,0:T(8,128)(2,1)}, bf16[3072,1408]{1,0:T(8,128)(2,1)}, bf16[3072,2816]{1,0:T(8,128)(2,1)}, bf16[768,1024]{1,0:T(8,128)(2,1)}, bf16[768,1024]{1,0:T(8,128)(2,1)}, /*index=5*/f32[768,1]{1,0:T(8,128)}) custom-call(bf16[768,512]{1,0:T(8,128)(2,1)} %collective-permute-done.5.refs_0, ...), custom_call_target="tpu_custom_call", output_to_operand_aliasing={{0}: (7, {}), {1}: (8, {}), {2}: (9, {})} | custom-call | flops 17716740096 | bytes 32768000 | tf_op jit(solution)/shard_map/expert/pallas_call | solution.py:260
  589.2 15.9 %fusion.24 = bf16[1024,1408]{1,0:T(8,128)(2,1)} fusion(bf16[3072,1408]{1,0:T(8,128)(2,1)} %get-tuple-element.68, bf16[3072,2048]{1,0:T(8,128)(2,1)} %all-gather.8.cloned.1.call-done, s32[]{:T(128)S(6)} %select_n.270), kind=kOutput, calls=%fused_computation.36 | convolution fusion | flops 8859811840 | bytes 17825796 | tf_op jit(solution)/shard_map/dot_general | solution.py:30
  605.1 25.0 %fusion.11 = bf16[1024,2816]{1,0:T(8,128)(2,1)} fusion(bf16[3072,2816]{1,0:T(8,128)(2,1)} %get-tuple-element.67, bf16[3072,2048]{1,0:T(8,128)(2,1)S(1)} %copy-done.58, s32[]{:T(128)S(6)} %select_n.271), kind=kOutput, calls=%fused_computation.26 | convolution fusion | flops 17719623680 | bytes 29360132 | tf_op jit(solution)/shard_map/dot_general | solution.py:30
  630.1 23.7 %convolution_convert_fusion.1 = bf16[3072,2048]{1,0:T(8,128)(2,1)} fusion(bf16[3072,1408]{1,0:T(8,128)(2,1)} %get-tuple-element.68, bf16[2048,1408]{1,0:T(8,128)(2,1)S(1)} %bitcast.83), kind=kOutput, calls=%fused_computation.5 | convolution fusion | flops 17723031552 | bytes 27000832 | tf_op jit(solution)/shard_map/dot_general | solution.py:30
  667.6 19.7 %collective-permute-start.34 = (f32[768]{0:T(1024)S(1)}, f32[768]{0:T(1024)S(1)}, u32[]{:S(2)}, u32[]{:S(2)}) collective-permute-start(f32[768]{0:T(1024)S(1)} %get-tuple-element.189), channel_id=1, source_target_pairs={{0,8},{4,12},{8,0},{12,4},{16,24},{20,28},{24,16},{28,20},{1,9},{5... | collective-permute-start | bytes 9224 | tf_op jit(solution)/shard_map/ppermute | solution.py:26
  715.6 28.5 %collective-permute-done.40 = bf16[768,512]{1,0:T(8,128)(2,1)S(1)} collective-permute-done((bf16[768,512]{1,0:T(8,128)(2,1)S(1)}, bf16[768,512]{1,0:T(8,128)(2,1)S(1)}, u32[]{:S(2)}, u32[]{:S(2)}) %collective-permute-start.40) | collective-permute-done | bytes 786464 | tf_op jit(solution)/shard_map/ppermute | solution.py:26
  746.0 31.9 %collective-permute-done.43 = bf16[768,512]{1,0:T(8,128)(2,1)S(1)} collective-permute-done((bf16[768,512]{1,0:T(8,128)(2,1)S(1)}, bf16[768,512]{1,0:T(8,128)(2,1)S(1)}, u32[]{:S(2)}, u32[]{:S(2)}) %collective-permute-start.43) | collective-permute-done | bytes 786464 | tf_op jit(solution)/shard_map/ppermute | solution.py:26
  779.6 31.9 %collective-permute-done.46 = bf16[768,512]{1,0:T(8,128)(2,1)S(1)} collective-permute-done((bf16[768,512]{1,0:T(8,128)(2,1)S(1)}, bf16[768,512]{1,0:T(8,128)(2,1)S(1)}, u32[]{:S(2)}, u32[]{:S(2)}) %collective-permute-start.46) | collective-permute-done | bytes 786464 | tf_op jit(solution)/shard_map/ppermute | solution.py:26
  814.6 22.1 %collective-permute-done.38 = bf16[768,512]{1,0:T(8,128)(2,1)S(1)} collective-permute-done((bf16[768,512]{1,0:T(8,128)(2,1)S(1)}, bf16[768,512]{1,0:T(8,128)(2,1)S(1)}, u32[]{:S(2)}, u32[]{:S(2)}) %collective-permute-start.38) | collective-permute-done | bytes 786464 | tf_op jit(solution)/shard_map/ppermute | solution.py:26
  850.7 23.8 %collective-permute-done.50 = bf16[1024,512]{1,0:T(8,128)(2,1)S(1)} collective-permute-done((bf16[1024,512]{1,0:T(8,128)(2,1)S(1)}, bf16[1024,512]{1,0:T(8,128)(2,1)S(1)}, u32[]{:S(2)}, u32[]{:S(2)}) %collective-permute-start.50) | collective-permute-done | bytes 1048608 | tf_op jit(solution)/shard_map/ppermute | solution.py:26
  891.0 15.5 %attention_back.1 = bf16[1024,1536]{1,0:T(8,128)(2,1)} custom-call(bf16[1024,512]{1,0:T(8,128)(2,1)S(1)} %get-tuple-element.81.q_in, bf16[1024,512]{1,0:T(8,128)(2,1)S(1)} %get-tuple-element.82.k_in, bf16[1024,512]{1,0:T(8,128)(2,1)S(1)} %copy-done.1, f32[4,1024,1]{2,1,0:T(8,128)} %get-tuple-element.84.logs, ...), custom_call_target="tpu_custom_call" | custom-call | flops 3355443200 | bytes 8388608 | tf_op jit(solution)/shard_map/attention_back/pallas_call | solution.py:204
  935.2 24.4 %collective-permute-done.53 = bf16[1024,512]{1,0:T(8,128)(2,1)S(1)} collective-permute-done((bf16[1024,512]{1,0:T(8,128)(2,1)S(1)}, bf16[1024,512]{1,0:T(8,128)(2,1)S(1)}, u32[]{:S(2)}, u32[]{:S(2)}) %collective-permute-start.53) | collective-permute-done | bytes 1048608 | tf_op jit(solution)/shard_map/ppermute | solution.py:26
  979.1 215.7 %collective-permute-done.60 = f32[6,2048]{1,0:T(8,128)S(1)} collective-permute-done((f32[6,2048]{1,0:T(8,128)S(1)}, f32[6,2048]{1,0:T(8,128)S(1)}, u32[]{:S(2)}, u32[]{:S(2)}) %collective-permute-start.60) | collective-permute-done | bytes 49184 | tf_op jit(solution)/shard_map/ppermute | solution.py:26
  1204.0 12.6 collective-permute-done.29
  1219.5 12.3 fusion.27.down_a
  1231.9 16.6 %collective-permute-start.62 = (f32[6,2048]{1,0:T(8,128)S(1)}, f32[6,2048]{1,0:T(8,128)S(1)}, u32[]{:S(2)}, u32[]{:S(2)}) collective-permute-start(f32[6,2048]{1,0:T(8,128)S(1)} %add.253), channel_id=1, source_target_pairs={{0,16},{4,20},{8,24},{12,28},{16,0},{20,4},{24,8},{28,12},{1,17},{... | collective-permute-start | bytes 147464 | tf_op jit(solution)/shard_map/ppermute | solution.py:26
  1253.0 25.3 %fusion.14.pair_a = bf16[1024,2816]{1,0:T(8,128)(2,1)S(1)} fusion(bf16[3072,2816]{1,0:T(8,128)(2,1)} %get-tuple-element.67, bf16[3072,2048]{1,0:T(8,128)(2,1)} %get-tuple-element.66, s32[]{:T(128)S(6)} %select_n.297), kind=kOutput, calls=%fused_computation.27 | convolution fusion | flops 17719623680 | bytes 29360132 | tf_op jit(solution)/shard_map/dot_general | solution.py:30
  1278.3 12.7 expert_grad_sum.1
  (419 shorter events, 295.2 us)
Async XLA Ops:
  7.2 113.6 %all-gather.4.cloned.1.call-start = ((), (), s32[]{:S(2)}) async-start(), calls=%async_computation.3 | async-start | bytes 7667712 | tf_op jit(solution)/shard_map/all_gather | solution.py:431
  11.6 172.7 %all-gather.6.cloned.1.call-start = ((), (), s32[]{:S(2)}) async-start(), calls=%async_computation.4 | async-start | bytes 2359296 | tf_op jit(solution)/shard_map/all_gather | solution.py:442
  12.4 437.3 %all-gather.8.cloned.1.call-start = ((), (), s32[]{:S(2)}) async-start(), calls=%async_computation.5 | async-start | bytes 15728640 | tf_op jit(solution)/shard_map/all_gather | solution.py:478
  120.7 81.2 %collective-permute-start.2 = (bf16[1024,1408]{1,0:T(8,128)(2,1)}, bf16[1024,1408]{1,0:T(8,128)(2,1)}, u32[]{:S(2)}, u32[]{:S(2)}) collective-permute-start(bf16[1024,1408]{1,0:T(8,128)(2,1)} %get-tuple-element.48), channel_id=1, source_target_pairs={{0,4},{4,0},{8,12},{12,8},{16,20},{20,16},{24,28},{28,24},{1,5},{5... | collective-permute-start | bytes 8650760 | tf_op jit(solution)/shard_map/ppermute | solution.py:26
  241.5 55.1 %collective-permute-start.11 = (bf16[768,512]{1,0:T(8,128)(2,1)S(1)}, bf16[768,512]{1,0:T(8,128)(2,1)S(1)}, u32[]{:S(2)}, u32[]{:S(2)}) collective-permute-start(bf16[768,512]{1,0:T(8,128)(2,1)S(1)} %fusion.94), channel_id=1, source_target_pairs={{0,16},{4,20},{8,24},{12,28},{16,0},{20,4},{24,8},{28,12},{1,17},{... | collective-permute-start | bytes 2359304 | tf_op jit(solution)/shard_map/ppermute | solution.py:26
  243.5 53.2 %collective-permute-start.12 = (bf16[768,512]{1,0:T(8,128)(2,1)S(1)}, bf16[768,512]{1,0:T(8,128)(2,1)S(1)}, u32[]{:S(2)}, u32[]{:S(2)}) collective-permute-start(bf16[768,512]{1,0:T(8,128)(2,1)S(1)} %fusion.91), channel_id=1, source_target_pairs={{0,24},{4,28},{8,16},{12,20},{16,8},{20,12},{24,0},{28,4},{1,25},{... | collective-permute-start | bytes 2359304 | tf_op jit(solution)/shard_map/ppermute | solution.py:26
  298.5 670.0 %reduce-scatter.4.cloned.1.call-start = ((), (), s32[]{:S(2)}) async-start(), calls=%async_computation.6 | async-start | bytes 15728640 | tf_op jit(solution)/shard_map/reduce_scatter | solution.py:553
  307.3 120.4 %collective-permute-start.9 = (bf16[1024,2816]{1,0:T(8,128)(2,1)}, bf16[1024,2816]{1,0:T(8,128)(2,1)}, u32[]{:S(2)}, u32[]{:S(2)}) collective-permute-start(bf16[1024,2816]{1,0:T(8,128)(2,1)} %pad_maximum_fusion.2), channel_id=1, source_target_pairs={{0,4},{4,0},{8,12},{12,8},{16,20},{20,16},{24,28},{28,24},{1,5},{5... | collective-permute-start | bytes 17301512 | tf_op jit(solution)/shard_map/ppermute | solution.py:26
  348.1 126.8 %collective-permute-start.24 = (bf16[768,512]{1,0:T(8,128)(2,1)}, bf16[768,512]{1,0:T(8,128)(2,1)}, u32[]{:S(2)}, u32[]{:S(2)}) collective-permute-start(bf16[768,512]{1,0:T(8,128)(2,1)} %fusion.89.refs_0_), channel_id=1, source_target_pairs={{0,1},{1,0},{2,3},{3,2},{4,5},{5,4},{6,7},{7,6},{8,9},{9,8},{10,11... | collective-permute-start | bytes 2359304 | tf_op jit(solution)/shard_map/ppermute | solution.py:26
  350.3 124.6 %collective-permute-start.14 = (bf16[768,512]{1,0:T(8,128)(2,1)}, bf16[768,512]{1,0:T(8,128)(2,1)}, u32[]{:S(2)}, u32[]{:S(2)}) collective-permute-start(bf16[768,512]{1,0:T(8,128)(2,1)} %fusion.95), channel_id=1, source_target_pairs={{0,16},{4,20},{8,24},{12,28},{16,0},{20,4},{24,8},{28,12},{1,17},{... | collective-permute-start | bytes 2359304 | tf_op jit(solution)/shard_map/ppermute | solution.py:26
  353.3 122.3 %collective-permute-start.5 = (bf16[768,512]{1,0:T(8,128)(2,1)}, bf16[768,512]{1,0:T(8,128)(2,1)}, u32[]{:S(2)}, u32[]{:S(2)}) collective-permute-start(bf16[768,512]{1,0:T(8,128)(2,1)} %fusion.90), channel_id=1, source_target_pairs={{0,24},{4,28},{8,16},{12,20},{16,8},{20,12},{24,0},{28,4},{1,25},{... | collective-permute-start | bytes 2359304 | tf_op jit(solution)/shard_map/ppermute | solution.py:26
  355.1 120.7 %collective-permute-start.26 = (bf16[768,512]{1,0:T(8,128)(2,1)}, bf16[768,512]{1,0:T(8,128)(2,1)}, u32[]{:S(2)}, u32[]{:S(2)}) collective-permute-start(bf16[768,512]{1,0:T(8,128)(2,1)} %collective-permute-done.25.refs_2_), channel_id=1, source_target_pairs={{0,1},{1,0},{2,3},{3,2},{4,5},{5,4},{6,7},{7,6},{8,9},{9,8},{10,11... | collective-permute-start | bytes 2359304 | tf_op jit(solution)/shard_map/ppermute | solution.py:26
  427.7 49.5 %collective-permute-start.21 = (bf16[768,512]{1,0:T(8,128)(2,1)}, bf16[768,512]{1,0:T(8,128)(2,1)}, u32[]{:S(2)}, u32[]{:S(2)}) collective-permute-start(bf16[768,512]{1,0:T(8,128)(2,1)} %collective-permute-done.19.refs_0_), channel_id=1, source_target_pairs={{0,2},{1,3},{2,0},{3,1},{4,6},{5,7},{6,4},{7,5},{8,10},{9,11},{10,... | collective-permute-start | bytes 2359304 | tf_op jit(solution)/shard_map/ppermute | solution.py:26
  475.6 62.2 %collective-permute-start.15 = (bf16[768,512]{1,0:T(8,128)(2,1)}, bf16[768,512]{1,0:T(8,128)(2,1)}, u32[]{:S(2)}, u32[]{:S(2)}) collective-permute-start(bf16[768,512]{1,0:T(8,128)(2,1)} %collective-permute-done.14.refs_0_), channel_id=1, source_target_pairs={{0,1},{1,0},{2,3},{3,2},{4,5},{5,4},{6,7},{7,6},{8,9},{9,8},{10,11... | collective-permute-start | bytes 2359304 | tf_op jit(solution)/shard_map/ppermute | solution.py:26
  502.7 60.6 %collective-permute-start.6 = (bf16[768,512]{1,0:T(8,128)(2,1)}, bf16[768,512]{1,0:T(8,128)(2,1)}, u32[]{:S(2)}, u32[]{:S(2)}) collective-permute-start(bf16[768,512]{1,0:T(8,128)(2,1)} %collective-permute-done.5.refs_0_), channel_id=1, source_target_pairs={{0,1},{1,0},{2,3},{3,2},{4,5},{5,4},{6,7},{7,6},{8,9},{9,8},{10,11... | collective-permute-start | bytes 2359304 | tf_op jit(solution)/shard_map/ppermute | solution.py:26
  512.1 51.2 %collective-permute-start.8 = (bf16[768,512]{1,0:T(8,128)(2,1)}, bf16[768,512]{1,0:T(8,128)(2,1)}, u32[]{:S(2)}, u32[]{:S(2)}) collective-permute-start(bf16[768,512]{1,0:T(8,128)(2,1)} %collective-permute-done.7.refs_2_), channel_id=1, source_target_pairs={{0,1},{1,0},{2,3},{3,2},{4,5},{5,4},{6,7},{7,6},{8,9},{9,8},{10,11... | collective-permute-start | bytes 2359304 | tf_op jit(solution)/shard_map/ppermute | solution.py:26
  653.8 638.3 %reduce-scatter.8.cloned.1.call-start = ((), (), s32[]{:S(2)}) async-start(), calls=%async_computation.8 | async-start | bytes 2359296 | tf_op jit(solution)/shard_map/reduce_scatter | solution.py:582
  663.8 48.7 %collective-permute-start.37 = (bf16[768,1024]{1,0:T(8,128)(2,1)}, bf16[768,1024]{1,0:T(8,128)(2,1)}, u32[]{:S(2)}, u32[]{:S(2)}) collective-permute-start(bf16[768,1024]{1,0:T(8,128)(2,1)} %get-tuple-element.74), channel_id=1, source_target_pairs={{0,1},{1,0},{2,3},{3,2},{4,5},{5,4},{6,7},{7,6},{8,9},{9,8},{10,11... | collective-permute-start | bytes 4718600 | tf_op jit(solution)/shard_map/ppermute | solution.py:26
  708.9 69.0 %collective-permute-start.43 = (bf16[768,512]{1,0:T(8,128)(2,1)S(1)}, bf16[768,512]{1,0:T(8,128)(2,1)S(1)}, u32[]{:S(2)}, u32[]{:S(2)}) collective-permute-start(bf16[768,512]{1,0:T(8,128)(2,1)S(1)} %add_convert_fusion.4), channel_id=1, source_target_pairs={{0,2},{1,3},{2,0},{3,1},{4,6},{5,7},{6,4},{7,5},{8,10},{9,11},{10,... | collective-permute-start | bytes 2359304 | tf_op jit(solution)/shard_map/ppermute | solution.py:26
  712.0 99.6 %collective-permute-start.46 = (bf16[768,512]{1,0:T(8,128)(2,1)S(1)}, bf16[768,512]{1,0:T(8,128)(2,1)S(1)}, u32[]{:S(2)}, u32[]{:S(2)}) collective-permute-start(bf16[768,512]{1,0:T(8,128)(2,1)S(1)} %add_convert_fusion.2), channel_id=1, source_target_pairs={{0,2},{1,3},{2,0},{3,1},{4,6},{5,7},{6,4},{7,5},{8,10},{9,11},{10,... | collective-permute-start | bytes 2359304 | tf_op jit(solution)/shard_map/ppermute | solution.py:26
  713.9 122.9 %collective-permute-start.38 = (bf16[768,512]{1,0:T(8,128)(2,1)S(1)}, bf16[768,512]{1,0:T(8,128)(2,1)S(1)}, u32[]{:S(2)}, u32[]{:S(2)}) collective-permute-start(bf16[768,512]{1,0:T(8,128)(2,1)S(1)} %add_convert_fusion.8), channel_id=1, source_target_pairs={{0,2},{1,3},{2,0},{3,1},{4,6},{5,7},{6,4},{7,5},{8,10},{9,11},{10,... | collective-permute-start | bytes 2359304 | tf_op jit(solution)/shard_map/ppermute | solution.py:26
  745.7 93.3 %collective-permute-start.41 = (bf16[768,512]{1,0:T(8,128)(2,1)S(1)}, bf16[768,512]{1,0:T(8,128)(2,1)S(1)}, u32[]{:S(2)}, u32[]{:S(2)}) collective-permute-start(bf16[768,512]{1,0:T(8,128)(2,1)S(1)} %add_convert_fusion.5), channel_id=1, source_target_pairs={{0,8},{4,12},{8,0},{12,4},{16,24},{20,28},{24,16},{28,20},{1,9},{5... | collective-permute-start | bytes 2359304 | tf_op jit(solution)/shard_map/ppermute | solution.py:26
  779.4 60.7 %collective-permute-start.44 = (bf16[768,512]{1,0:T(8,128)(2,1)S(1)}, bf16[768,512]{1,0:T(8,128)(2,1)S(1)}, u32[]{:S(2)}, u32[]{:S(2)}) collective-permute-start(bf16[768,512]{1,0:T(8,128)(2,1)S(1)} %add_convert_fusion.3), channel_id=1, source_target_pairs={{0,16},{4,20},{8,24},{12,28},{16,0},{20,4},{24,8},{28,12},{1,17},{... | collective-permute-start | bytes 2359304 | tf_op jit(solution)/shard_map/ppermute | solution.py:26
  885.7 414.7 %reduce-scatter.6.cloned.1.call-start = ((), (), s32[]{:S(2)}) async-start(), calls=%async_computation.7 | async-start | bytes 7077888 | tf_op jit(solution)/shard_map/reduce_scatter | solution.py:588
  964.2 314.1 %collective-permute-start.63 = (bf16[1024,2816]{1,0:T(8,128)(2,1)}, bf16[1024,2816]{1,0:T(8,128)(2,1)}, u32[]{:S(2)}, u32[]{:S(2)}) collective-permute-start(bf16[1024,2816]{1,0:T(8,128)(2,1)} %fusion.11), channel_id=1, source_target_pairs={{0,4},{4,0},{8,12},{12,8},{16,20},{20,16},{24,28},{28,24},{1,5},{5... | collective-permute-start | bytes 17301512 | tf_op jit(solution)/shard_map/ppermute | solution.py:26
  965.7 312.6 %collective-permute-start.64 = (bf16[1024,1408]{1,0:T(8,128)(2,1)}, bf16[1024,1408]{1,0:T(8,128)(2,1)S(1)}, u32[]{:S(2)}, u32[]{:S(2)}) collective-permute-start(bf16[1024,1408]{1,0:T(8,128)(2,1)} %fusion.24), channel_id=1, source_target_pairs={{0,4},{4,0},{8,12},{12,8},{16,20},{20,16},{24,28},{28,24},{1,5},{5... | collective-permute-start | bytes 8650760 | tf_op jit(solution)/shard_map/ppermute | solution.py:26
  970.4 229.9 %collective-permute-start.27 = (bf16[768,512]{1,0:T(8,128)(2,1)S(1)}, bf16[768,512]{1,0:T(8,128)(2,1)S(1)}, u32[]{:S(2)}, u32[]{:S(2)}) collective-permute-start(bf16[768,512]{1,0:T(8,128)(2,1)S(1)} %get-tuple-element.154), channel_id=1, source_target_pairs={{0,8},{4,12},{8,0},{12,4},{16,24},{20,28},{24,16},{28,20},{1,9},{5... | collective-permute-start | bytes 2359304 | tf_op jit(solution)/shard_map/ppermute | solution.py:26
  973.5 221.2 %collective-permute-start.60 = (f32[6,2048]{1,0:T(8,128)S(1)}, f32[6,2048]{1,0:T(8,128)S(1)}, u32[]{:S(2)}, u32[]{:S(2)}) collective-permute-start(f32[6,2048]{1,0:T(8,128)S(1)} %add.251), channel_id=1, source_target_pairs={{0,4},{4,0},{8,12},{12,8},{16,20},{20,16},{24,28},{28,24},{1,5},{5... | collective-permute-start | bytes 147464 | tf_op jit(solution)/shard_map/ppermute | solution.py:26
  973.6 229.3 %collective-permute-start.28 = (bf16[768,512]{1,0:T(8,128)(2,1)S(1)}, bf16[768,512]{1,0:T(8,128)(2,1)S(1)}, u32[]{:S(2)}, u32[]{:S(2)}) collective-permute-start(bf16[768,512]{1,0:T(8,128)(2,1)S(1)} %get-tuple-element.153), channel_id=1, source_target_pairs={{0,16},{4,20},{8,24},{12,28},{16,0},{20,4},{24,8},{28,12},{1,17},{... | collective-permute-start | bytes 2359304 | tf_op jit(solution)/shard_map/ppermute | solution.py:26
  1200.3 48.2 %collective-permute-start.56 = (bf16[1024,512]{1,0:T(8,128)(2,1)S(1)}, bf16[1024,512]{1,0:T(8,128)(2,1)S(1)}, u32[]{:S(2)}, u32[]{:S(2)}) collective-permute-start(bf16[1024,512]{1,0:T(8,128)(2,1)S(1)} %fusion.62), channel_id=1, source_target_pairs={{0,2},{1,3},{2,0},{3,1},{4,6},{5,7},{6,4},{7,5},{8,10},{9,11},{10,... | collective-permute-start | bytes 3145736 | tf_op jit(solution)/shard_map/ppermute | solution.py:26
  1231.9 59.1 %collective-permute-start.62 = (f32[6,2048]{1,0:T(8,128)S(1)}, f32[6,2048]{1,0:T(8,128)S(1)}, u32[]{:S(2)}, u32[]{:S(2)}) collective-permute-start(f32[6,2048]{1,0:T(8,128)S(1)} %add.253), channel_id=1, source_target_pairs={{0,16},{4,20},{8,24},{12,28},{16,0},{20,4},{24,8},{28,12},{1,17},{... | collective-permute-start | bytes 147464 | tf_op jit(solution)/shard_map/ppermute | solution.py:26
  1252.7 53.4 %collective-permute-start.31 = (bf16[1024,1024]{1,0:T(8,128)(2,1)}, bf16[1024,1024]{1,0:T(8,128)(2,1)}, u32[]{:S(2)}, u32[]{:S(2)}) collective-permute-start(bf16[1024,1024]{1,0:T(8,128)(2,1)} %pad_maximum_fusion.7), channel_id=1, source_target_pairs={{0,1},{1,0},{2,3},{3,2},{4,5},{5,4},{6,7},{7,6},{8,9},{9,8},{10,11... | collective-permute-start | bytes 6291464 | tf_op jit(solution)/shard_map/ppermute | solution.py:26
  (104 other events, 2229.2 us)
Sparse Core Ops, SparseCore 0:
  11.7 108.9 all-gather.3
  122.9 61.3 all-gather.5
  298.6 96.6 all-gather.7
  654.0 179.0 reduce-scatter.3
  885.8 67.8 reduce-scatter.7
  957.7 172.8 reduce-scatter.5

commit v3 on v2

--- a/solution.py
+++ b/solution.py
@@ -53,7 +53,7 @@
     return value
 
 
-def tensor_reduce(part):
+def tensor_reduce(part, filler=None):
     count = lax.axis_size("tensor")
     place = lax.axis_index("tensor")
     size = part.shape[1] // count
@@ -64,6 +64,8 @@
         given = [jnp.where(upper, a, b) for a, b in zip(blocks[::2], blocks[1::2])]
         sent = jnp.concatenate([v.astype(low) for v in given], 1)
         came = swap(sent, "tensor", 1 << bit)
+        if filler is not None and bit == levels_of(count) - 1:
+            came = after(came, *filler(sent))
         blocks = [
             v.astype(full) + came[:, i * size : (i + 1) * size].astype(full)
             for i, v in enumerate(kept)
@@ -71,7 +73,7 @@
     return blocks[0]
 
 
-def tensor_gather(own):
+def tensor_gather(own, filler=None):
     count = lax.axis_size("tensor")
     place = lax.axis_index("tensor")
     size = own.shape[1]
@@ -79,6 +81,8 @@
     order = list(range(levels_of(count)))[::-1]
     for bit in order:
         came = swap(held, "tensor", 1 << bit)
+        if filler is not None and bit == order[0]:
+            came = after(came, *filler(held))
         upper = side_of(place, bit)
         number = held.shape[1] // size
         mine = [held[:, i * size : (i + 1) * size] for i in range(number)]
@@ -215,16 +219,136 @@
     )(query, keys, values, logs, grad, cosine, sine)
 
 
-def expert_kernel(count, carried, *refs):
+def place_rows(pieces, held, sems, upper, first):
+    copies = []
+    for ref, start, number, mine, there, column in pieces:
+        half = held.shape[0] // 2
+        columns = ref.shape[1]
+        side = upper if mine else 1 - upper
+        copies.append(
+            pltpu.make_async_copy(
+                ref.at[pl.ds(start, number), :],
+                held.at[
+                    pl.ds(pl.multiple_of(side * half + there, 64), number),
+                    pl.ds(column * columns, columns),
+                ],
+                sems.at[len(copies)],
+            )
+        )
+
+    @pl.when(first)
+    def _():
+        for copy in copies:
+            copy.start()
+        for copy in copies:
+            copy.wait()
+
+
+def down_pieces(own, came):
+    half = own.shape[0]
+    return [(own, 0, half, True, 0, 0), (came, 0, half, False, 0, 0)]
+
+
+def pair_pieces(own_gate, own_up, came, rest):
+    half, less = own_gate.shape[0], rest.shape[0]
+    more = half - less
+    return [
+        (own_gate, 0, half, True, 0, 0),
+        (own_up, 0, half, True, 0, 1),
+        (came, 0, half, False, 0, 0),
+        (came, half, more, False, 0, 1),
+        (rest, 0, less, False, more, 1),
+    ]
+
+
+def column_block(where, i, size):
+    return pl.ds(pl.multiple_of((i ^ where[0]) * size, size), size)
+
+
+def down_kernel(split, where, mine, rest, own, came, rows_out, raw, held, sems):
+    step = pl.program_id(0)
+    place_rows(down_pieces(own, came), held, sems, where[1], step == 0)
+
+    @pl.when(step < split)
+    def _():
+        rows_out[...] = mine[...]
+
+    @pl.when(step >= split)
+    def _():
+        rows_out[...] = rest[...]
+
+    raw[...] = jnp.dot(rows_out[...], held[...], preferred_element_type=full).astype(low)
+
+
+def down_pass(where, mine, rest, own, came):
+    total = mine.shape[0] + rest.shape[0]
+    width, hidden = 2 * own.shape[0], own.shape[1]
+    tile = 256
+    split = mine.shape[0] // tile
+    spec = lambda columns: pl.BlockSpec((tile, columns), lambda i, where: (i, 0))
+    return pl.pallas_call(
+        functools.partial(down_kernel, split),
+        grid_spec=pltpu.PrefetchScalarGridSpec(
+            num_scalar_prefetch=1,
+            grid=(total // tile,),
+            in_specs=[
+                pl.BlockSpec((tile, width), lambda i, where: (jnp.minimum(i, split - 1), 0)),
+                pl.BlockSpec((tile, width), lambda i, where: (jnp.maximum(i - split, 0), 0)),
+            ]
+            + [pl.BlockSpec(memory_space=pl.ANY)] * 2,
+            out_specs=[spec(width), spec(hidden)],
+            scratch_shapes=[pltpu.VMEM((width, hidden), low), pltpu.SemaphoreType.DMA((2,))],
+        ),
+        out_shape=[
+            jax.ShapeDtypeStruct((total, width), low),
+            jax.ShapeDtypeStruct((total, hidden), low),
+        ],
+        compiler_params=limits(48),
+        cost_estimate=cost(
+            2 * total * width * hidden, (total * (2 * width + hidden) + width * hidden) * 2
+        ),
+        name="down",
+    )(where, mine, rest, own, came)
+
+
+def up_kernel(where, act, own, came, out, held, sems):
+    place_rows(down_pieces(own, came), held, sems, where[1], pl.program_id(0) == 0)
+    out[...] = dot_cols(act[...], held[...]).astype(low)
+
+
+def up_pass(where, act, own, came):
+    total, hidden = act.shape
+    width = 2 * own.shape[0]
+    tile = 256
+    spec = lambda columns: pl.BlockSpec((tile, columns), lambda i, where: (i, 0))
+    return pl.pallas_call(
+        up_kernel,
+        grid_spec=pltpu.PrefetchScalarGridSpec(
+            num_scalar_prefetch=1,
+            grid=(total // tile,),
+            in_specs=[spec(hidden)] + [pl.BlockSpec(memory_space=pl.ANY)] * 2,
+            out_specs=spec(width),
+            scratch_shapes=[pltpu.VMEM((width, hidden), low), pltpu.SemaphoreType.DMA((2,))],
+        ),
+        out_shape=jax.ShapeDtypeStruct((total, width), low),
+        compiler_params=limits(48),
+        cost_estimate=cost(
+            2 * total * width * hidden, (total * (width + hidden) + width * hidden) * 2
+        ),
+        name="up",
+    )(where, act, own, came)
+
+
+def expert_kernel(count, carried, where, *refs):
     blocks, refs = refs[:count], refs[count:]
-    pair, raw, gate = refs[:3]
-    rows_out, act_out, grad_out, even, odd, gate_grad, held = refs[3 + carried :]
+    weights, raw, gate = refs[:4], refs[4], refs[5]
+    rows_out, act_out, grad_out, even, odd, gate_grad, pair, part, sems = refs[6 + carried :]
     size = blocks[0].shape[1]
     hidden = raw.shape[1]
+    place_rows(pair_pieces(*weights), pair, sems, where[1], pl.program_id(0) == 0)
     for i, ref in enumerate(blocks):
-        held[:, i * size : (i + 1) * size] = ref[...]
-    rows_out[...] = held[...]
-    both = jnp.dot(held[...], pair[...], preferred_element_type=full)
+        rows_out[:, column_block(where, i, size)] = ref[...]
+    both = jnp.dot(rows_out[...], pair[...], preferred_element_type=full)
     pre_gate = both[:, :hidden]
     pre_up = both[:, hidden:]
     sigma = 1.0 / (1.0 + jnp.exp(-pre_gate))
@@ -236,45 +360,50 @@
     back = back * gate[...]
     grad_out[:, :hidden] = (back * pre_up * sigma * (1.0 + pre_gate * (1.0 - sigma))).astype(low)
     grad_out[:, hidden:] = (back * silu).astype(low)
-    part = dot_cols(grad_out[...], pair[...]).astype(low)
+    part[...] = dot_cols(grad_out[...], pair[...]).astype(low)
     for i in range(count):
         (odd if i % 2 else even)[:, i // 2 * size : (i // 2 + 1) * size] = part[
-            :, i * size : (i + 1) * size
+            :, column_block(where, i, size)
         ]
 
 
-def expert_pass(step, blocks, pair, raw, gate, carried):
+def expert_pass(step, where, blocks, weights, raw, gate, carried):
     count = len(blocks)
     size = blocks[0].shape[1]
-    width, both = pair.shape
-    hidden = both // 2
+    width, hidden = 2 * weights[0].shape[0], weights[0].shape[1]
+    both = 2 * hidden
     total = raw.shape[0]
     tile = 256
     steps = MOST // tile
-    here = lambda i: (step * steps + i, 0)
-    near = lambda i: (i, 0)
+    here = lambda i, where: (step * steps + i, 0)
+    near = lambda i, where: (i, 0)
     near_spec = lambda columns: pl.BlockSpec((tile, columns), near)
     here_spec = lambda columns: pl.BlockSpec((tile, columns), here)
+    anywhere = pl.BlockSpec(memory_space=pl.ANY)
     shape = lambda r, c, t=low: jax.ShapeDtypeStruct((r, c), t)
-    inputs = [*blocks, pair, raw, gate, *carried]
     return pl.pallas_call(
         functools.partial(expert_kernel, count, len(carried)),
-        grid=(steps,),
-        in_specs=[near_spec(size)] * count
-        + [
-            pl.BlockSpec((width, both), lambda i: (0, 0), pipeline_mode=pl.Buffered(1)),
-            here_spec(hidden),
-            near_spec(1),
-        ]
-        + [pl.BlockSpec(memory_space=pl.ANY)] * len(carried),
-        out_specs=[
-            here_spec(width),
-            here_spec(hidden),
-            here_spec(both),
-            near_spec(width // 2),
-            near_spec(width // 2),
-            near_spec(1),
-        ],
+        grid_spec=pltpu.PrefetchScalarGridSpec(
+            num_scalar_prefetch=1,
+            grid=(steps,),
+            in_specs=[near_spec(size)] * count
+            + [anywhere] * 4
+            + [here_spec(hidden), near_spec(1)]
+            + [anywhere] * len(carried),
+            out_specs=[
+                here_spec(width),
+                here_spec(hidden),
+                here_spec(both),
+                near_spec(width // 2),
+                near_spec(width // 2),
+                near_spec(1),
+            ],
+            scratch_shapes=[
+                pltpu.VMEM((width, both), low),
+                pltpu.VMEM((tile, width), low),
+                pltpu.SemaphoreType.DMA((5,)),
+            ],
+        ),
         out_shape=[
             shape(total, width),
             shape(total, hidden),
@@ -283,61 +412,57 @@
             shape(MOST, width // 2),
             shape(MOST, 1, full),
         ],
-        scratch_shapes=[pltpu.VMEM((tile, width), low)],
-        input_output_aliases={count + 3 + i: i for i in range(len(carried))},
+        input_output_aliases={count + 7 + i: i for i in range(len(carried))},
         compiler_params=limits(60),
         cost_estimate=cost(
             4 * MOST * width * both, width * both * 2 + MOST * (width * 8 + hidden * 8), MOST * hidden
         ),
         name="expert",
-    )(*inputs)
-
-
-def expert_grad_kernel(hidden, turn, pair_a, pair_b, down_a, down_b, out):
-    which = pl.program_id(0)
-
-    @pl.when(which < 2)
-    def _():
-        out[0] = (pair_a[...].astype(full) + pair_b[...].astype(full))[:, :hidden]
-
-    @pl.when(which == 2)
-    def _():
-        out[0] = (down_a[...].astype(full) + down_b[...].astype(full))[:, :hidden]
-
-
-def expert_grad_sum(turn, pair_a, pair_b, down_a, down_b, hidden, inner):
-    rows = pair_a.shape[0]
-    padded = pair_a.shape[1] // 2
+    )(where, *blocks, *weights, raw, gate, *carried)
+
+
+def expert_grad_kernel(hidden, *refs):
+    out = refs[-1]
+    for k in range(3):
+
+        @pl.when(pl.program_id(0) == k)
+        def _():
+            out[0] = (refs[2 * k][...].astype(full) + refs[2 * k + 1][...].astype(full))[:, :hidden]
+
+
+def expert_grad_sum(terms, hidden):
+    rows, padded = terms[0].shape
     tile = 256
-    per = rows // inner // tile
-    pair_spec = pl.BlockSpec(
-        (tile, padded), lambda w, i, turn: (i ^ (turn[0] * per), jnp.minimum(w, 1))
-    )
-    down_spec = pl.BlockSpec((tile, padded), lambda w, i, turn: (jnp.where(w == 2, i, 0), 0))
+    last = rows // tile - 1
+
+    def spec(k):
+        return pl.BlockSpec(
+            (tile, padded), lambda w, i: (jnp.where(w == k, i, jnp.where(w < k, 0, last)), 0)
+        )
+
     return pl.pallas_call(
         functools.partial(expert_grad_kernel, hidden),
-        grid_spec=pltpu.PrefetchScalarGridSpec(
-            num_scalar_prefetch=1,
-            grid=(3, rows // tile),
-            in_specs=[pair_spec, pair_spec, down_spec, down_spec],
-            out_specs=pl.BlockSpec((1, tile, hidden), lambda w, i, turn: (w, i, 0)),
-        ),
+        grid=(3, rows // tile),
+        in_specs=[spec(k // 2) for k in range(6)],
+        out_specs=pl.BlockSpec((1, tile, hidden), lambda w, i: (w, i, 0)),
         out_shape=jax.ShapeDtypeStruct((3, rows, hidden), full),
         compiler_params=limits(32),
         cost_estimate=cost(rows * padded * 3, rows * padded * 24),
         name="expert_grad_sum",
-    )(turn, pair_a, pair_b, down_a, down_b)
-
-
-def near_blocks(own):
+    )(*terms)
+
+
+def near_blocks(own, *others):
     held = [own]
     for bit in range(levels_of(lax.axis_size("tensor")))[::-1]:
         theirs = [swap(v, "tensor", 1 << bit) for v in held]
+        if bit and others:
+            theirs = [after(v, *others) for v in theirs]
         held = [v for pair in zip(held, theirs) for v in pair]
     return held
 
 
-def near_reduce(even, odd):
+def near_reduce(even, odd, meet, *others):
     count = lax.axis_size("tensor")
     number = count // 2
     size = even.shape[1] // number
@@ -348,40 +473,35 @@
             + came[:, i * size : (i + 1) * size].astype(full)
             for i in range(number)
         ]
-        sent = [v.astype(low) for v in blocks[1::2]]
+        sent = jnp.concatenate([v.astype(low) for v in blocks[1::2]], 1)
+        if bit == levels_of(count) - 1:
+            sent = after(sent, *others)
+            meet.append(sent)
         even = jnp.concatenate(blocks[::2], 1)
-        came = swap(jnp.concatenate(sent, 1), "tensor", 1 << bit)
+        came = swap(sent, "tensor", 1 << bit)
         number //= 2
     return (even.astype(full) + came.astype(full)).astype(low)
 
-def turn_blocks(value, index, number):
-    size = value.shape[0] // number
-    blocks = [value[i * size : (i + 1) * size] for i in range(number)]
-    for bit in range(levels_of(number)):
-        upper = side_of(index, bit)
-        blocks = [jnp.where(upper, blocks[i ^ (1 << bit)], blocks[i]) for i in range(number)]
-    return jnp.concatenate(blocks, 0) if number > 1 else value
-
-
-def group_gather(local, position, group_count):
+
+def half_gather(local, group_count):
     held = local
-    for bit in range(levels_of(group_count)):
-        partner = swap(held, "dp", 1 << bit)
-        upper = side_of(position, bit)
-        held = jnp.concatenate(
-            [jnp.where(upper, partner, held), jnp.where(upper, held, partner)], axis=0
-        )
+    place = lax.axis_index("dp") % group_count
+    for bit in range(levels_of(group_count) - 1):
+        came = swap(held, "dp", 1 << bit)
+        upper = side_of(place, bit)
+        held = jnp.concatenate([jnp.where(upper, came, held), jnp.where(upper, held, came)], 0)
     return held
 
 
-def group_sum(term, width, position, group_count):
-    top = levels_of(group_count) - 1
-    half = width // 2
-    upper = (position >> top) & 1
-    given = term((1 - upper) * half, half)
-    came = swap(given, "dp", 1 << top)
-    kept = functools.partial(term, upper * half, half)
-    return given, came, kept
+def dp_scatter(value):
+    index = lax.axis_index("dp")
+    for bit in range(levels_of(lax.axis_size("dp")))[::-1]:
+        middle = value.shape[0] // 2
+        upper = (index >> bit) & 1
+        kept = lax.dynamic_slice_in_dim(value, upper * middle, middle, 0)
+        given = lax.dynamic_slice_in_dim(value, (1 - upper) * middle, middle, 0)
+        value = kept.astype(full) + swap(given.astype(low), "dp", 1 << bit).astype(full)
+    return value
 
 
 def group_finish(kept, came, position, group_count):
@@ -419,9 +539,8 @@
     index = lax.axis_index("dp")
     expert = index // group_count
     member = index % group_count
-    inner = tensor_count // group_count
-    position = member ^ (place // inner)
-    turn = place % inner
+    top_half = member >> (levels_of(group_count) - 1)
+    where = jnp.stack([place, top_half]).astype(jnp.int32)
 
     def own_columns(value):
         return lax.dynamic_slice_in_dim(value, place * size, size, 1)
@@ -429,17 +548,20 @@
     extras = jnp.concatenate([router_weight, attn_gain[:, None], moe_gain[:, None]], 1)
     extras = jnp.pad(extras, ((0, 0), (0, 128 - extras.shape[1])))
     first = lax.all_gather(
-        jnp.concatenate([qkv_weight.reshape(-1, 3 * size), extras], 1), "dp", axis=0, tiled=True
+        jnp.concatenate([qkv_weight.reshape(-1, 3 * size), out_weight, extras], 1),
+        "dp",
+        axis=0,
+        tiled=True,
     )
     qkv_flat = first[:, : 3 * size]
-    small = first[:, 3 * size :].T
+    out_full = first[:, 3 * size : 4 * size]
+    small = first[:, 4 * size :].T
     router_full = small[:EXPERTS]
     gain_first = small[EXPERTS : EXPERTS + 1].astype(full)
     gain_second = small[EXPERTS + 1 : EXPERTS + 2].astype(full)
     gain_first_own = own_columns(gain_first)
     gain_second_own = own_columns(gain_second)
     router_own = own_columns(router_full)
-    out_full = lax.all_gather(out_weight, "dp", axis=0, tiled=True)
 
     near = jnp.arange(EXPERTS, dtype=jnp.int32) ^ expert
     names = jnp.arange(EXPERTS, dtype=jnp.int32)
@@ -464,30 +586,39 @@
     def widened(value):
         return jnp.pad(value, ((0, 0), (0, padded - hidden_size)))
 
-    down_local = widened(expert_weight[2])
-    pair_local = turn_blocks(
-        jnp.concatenate([widened(expert_weight[0]), widened(expert_weight[1])], 1), turn, inner
-    )
-    down_weight = lax.optimization_barrier(
-        group_gather(after(down_local, first), member, group_count)
-    )
-    pair_weight = group_gather(after(pair_local, down_weight), position, group_count)
+    gate_mine, up_mine, down_mine = [
+        half_gather(widened(expert_weight[k]), group_count) for k in range(3)
+    ]
+    half = width // 2
+    mine_at, given_at = top_half * half, (1 - top_half) * half
+    reach = group_count // 2
+
+    def group_send(given, *others):
+        return swap(after(given, *others), "dp", reach)
+
+    cut = half // 2
+    down = (down_mine, group_send(down_mine))
+    pair_came = group_send(jnp.concatenate([gate_mine, up_mine[:cut]], 0), down[1])
+    pair_rest = group_send(up_mine[cut:], pair_came)
+    pair = (gate_mine, up_mine, pair_came, pair_rest)
 
     grad_own = own_columns(cotangent)
-    grad_packed = [after(v, first) for v in packed(grad_own)]
-    grad_rows = lax.all_gather(
-        jnp.concatenate(exchange(grad_packed), 0), "tensor", axis=1, tiled=True
+    grad_mine = jnp.dot(chosen[0], cotangent, preferred_element_type=full).astype(low)
+    grad_came = exchange([after(v, down[1]) for v in packed(grad_own)])[1:]
+    grad_rest = lax.all_gather(
+        after(jnp.concatenate(grad_came, 0), pair_came), "tensor", axis=1, tiled=True
     )
 
     inputs = tokens.astype(full)
     scale_one = lax.rsqrt(jnp.mean(inputs * inputs, axis=1, keepdims=True) + epsilon)
     normed_in = (inputs * scale_one * gain_first).astype(low)
     inputs_own = own_columns(tokens).astype(full)
+    qkv_flat = after(qkv_flat, *grad_came)
     qkv = jnp.dot(normed_in, qkv_flat, preferred_element_type=full)
     cosine, sine = rotary_tables()
     context, query, keys, values, logs = attention(qkv, cosine, sine, scale)
     attn_part = contract(context, out_full, 1, 1).astype(low)
-    hidden = after(inputs_own + tensor_reduce(attn_part), down_weight)
+    hidden = after(inputs_own + tensor_reduce(attn_part), pair_rest)
 
     scaled_hidden = (hidden * gain_second_own).astype(low)
     sums = tensor_sum(
@@ -511,9 +642,12 @@
         return jnp.stack([a, b, (value - a.astype(full) - b.astype(full)).astype(low)])
 
     moe_packed = packed(moe_in)
-    arrived = [near_blocks(v) for v in exchange(moe_packed)]
-
-    gates_near = jnp.take(gates, near, axis=0)
+    crossed = [moe_packed[0]] + [
+        swap(moe_packed[s], "dp", s * group_count) for s in range(1, EXPERTS - 1)
+    ]
+    arrived = [near_blocks(moe_packed[0])]
+
+    gates_near = after(jnp.take(gates, near, axis=0), crossed[1])
     gate_rows = exchange(
         [
             jnp.sum(contract(three_parts(gates_near[s]), chosen[s], 1, 1), 0)
@@ -521,44 +655,62 @@
         ]
     )
 
-    grad_rows = after(grad_rows, *moe_packed)
-    raw = jnp.dot(grad_rows, down_weight, preferred_element_type=full).astype(low)
+    grad_rows, raw = down_pass(where, after(grad_mine, *moe_packed), grad_rest, *down)
     carried = ()
+    sums_sent = []
     returned = []
     gate_grads = []
     for step in range(EXPERTS):
+        gate = gate_rows[step][:, None]
+        if step == 2:
+            gate = after(gate, sums_sent[0])
+        if step == 3:
+            gate = after(gate, sums_sent[1], returned[0])
         moe_rows, activation, pre_grad, even, odd, gate_grad = expert_pass(
-            step, arrived[step], pair_weight, raw, gate_rows[step][:, None], carried
+            step, where, arrived[step], pair, raw, gate, carried
         )
         carried = (moe_rows, activation, pre_grad)
-        returned.append(near_reduce(even, odd))
+        if step == 0:
+            arrived.append(near_blocks(crossed[1], even))
+            crossed[2] = after(crossed[2], even)
+            crossed.append(swap(after(moe_packed[3], crossed[2]), "dp", 3 * group_count))
+        if step == 1:
+            arrived.append(near_blocks(crossed[2], even))
+            crossed[3] = after(crossed[3], even)
+        if step == 2:
+            arrived.append(near_blocks(crossed[3], even))
+        returned.append(near_reduce(even, odd, sums_sent, *returned[2:]))
         gate_grads.append(gate_grad)
-    back = unpacked(exchange(returned))
+    own_returned = returned
+    returned = exchange(returned)
     gate_grad_rows = tensor_sum(jnp.concatenate(gate_grads, 1).T)
-    gate_grad_near = jnp.stack(exchange([gate_grad_rows[s] for s in range(EXPERTS)]))
-
-    def down_term(start, number):
-        part = lax.dynamic_slice_in_dim(grad_rows, start, number, 1)
-        return contract(part, activation, 0, 0).astype(low)
-
-    def pair_term(start, number):
-        part = lax.dynamic_slice_in_dim(moe_rows, start, number, 1)
-        return contract(part, pre_grad, 0, 0).astype(low)
-
-    down_given, down_came, down_kept = group_sum(down_term, width, member, group_count)
-    pair_given, pair_came, pair_kept = group_sum(pair_term, width, position, group_count)
-    expert_part = contract(
-        after(activation, down_given, pair_given), down_weight, 1, 1
-    ).astype(low)
+    gate_grad_near = exchange([gate_grad_rows[s] for s in range(EXPERTS)])
+
+    def term(left, right):
+        def part(start, number):
+            taken = lax.dynamic_slice_in_dim(left, start, number, 1)
+            return contract(taken, right, 0, 0).astype(low)
+
+        return part
+
+    down_term = term(grad_rows, after(activation, sums_sent[2], own_returned[1]))
+    down_given = down_term(given_at, half)
+    gate_term = term(moe_rows, after(pre_grad[:, :padded], down_given, sums_sent[3]))
+    gate_given = gate_term(given_at, half)
+    up_term = term(moe_rows, after(pre_grad[:, padded:], gate_given, own_returned[3]))
+    up_given = up_term(given_at, half)
+    down_came = group_send(down_given)
+    gate_came = group_send(gate_given, down_came)
+    up_came = group_send(up_given, gate_came)
+    expert_part = up_pass(
+        where, after(activation, up_given, returned[1], *gate_grad_near), *down
+    )
+    expert_part = after(expert_part, down_came, returned[2])
     expert_own = lax.psum_scatter(expert_part, "tensor", scatter_dimension=1, tiled=True)
     mixed = unpacked(exchange([expert_own[s * MOST : (s + 1) * MOST] for s in range(EXPERTS)]))
     layer_own = hidden + mixed
     layer_out = tensor_gather(layer_own.astype(low)).astype(full)
-    down_a, down_b = group_finish(down_kept(), down_came, member, group_count)
-    pair_a, pair_b = group_finish(pair_kept(), pair_came, position, group_count)
-    expert_grad = expert_grad_sum(
-        turn[None].astype(jnp.int32), pair_a, pair_b, down_a, down_b, hidden_size, inner
-    )
+    back = unpacked(returned)
 
     gate_grad = jnp.stack(
         [
@@ -577,22 +729,40 @@
     moe_gain_grad = jnp.sum(moe_grad * normed_two, axis=0)
     mean_two = tensor_sum(jnp.sum(scaled_grad * normed_two, axis=1)[None]) / width
     hidden_grad = grad_out + scale_two * (scaled_grad - normed_two * mean_two.reshape(rows, 1))
-    attn_grad = tensor_gather(hidden_grad.astype(low))
-    out_grad = contract(attn_grad, context, 0, 0)
-    out_shard = lax.psum_scatter(
-        out_grad.astype(low), "dp", scatter_dimension=0, tiled=True
-    ).astype(full)
+    kept = []
+
+    def first_kept(sent):
+        kept.append(term(grad_rows, after(activation, sent))(mine_at, half))
+        kept.append(term(moe_rows, after(pre_grad[:, :padded], sent))(mine_at, half))
+        return kept
+
+    def last_kept(sent):
+        kept.append(term(moe_rows, after(pre_grad[:, padded:], sent))(mine_at, half))
+        return kept[2:]
+
+    attn_grad = tensor_gather(hidden_grad.astype(low), first_kept)
     context_grad = jnp.dot(attn_grad, out_full, preferred_element_type=full).astype(low)
     qkv_grad_rows = attention_back(query, keys, values, logs, context_grad, cosine, sine, scale)
+    qkv_grad_rows = after(qkv_grad_rows, gate_came)
     qkv_grad = contract(normed_in, qkv_grad_rows, 0, 0).astype(low)
     qkv_shard = lax.psum_scatter(qkv_grad, "dp", scatter_dimension=0, tiled=True).astype(full)
-    normed_grad = tensor_reduce(contract(qkv_grad_rows, qkv_flat, 1, 1).astype(low))
+    normed_grad = tensor_reduce(
+        contract(after(qkv_grad_rows, qkv_grad), qkv_flat, 1, 1).astype(low), last_kept
+    )
+    out_shard = dp_scatter(contract(attn_grad, context, 0, 0).astype(low))
     normed_one = inputs_own * scale_one
     scaled_in = normed_grad * gain_first_own
     attn_gain_grad = jnp.sum(normed_grad * normed_one, axis=0)
     mean_one = tensor_sum(jnp.sum(scaled_in * normed_one, axis=1)[None]) / width
     input_own = hidden_grad + scale_one * (scaled_in - normed_one * mean_one.reshape(rows, 1))
+    input_own = after(input_own, up_came)
     input_grad = tensor_gather(input_own.astype(low)).astype(full)
+    terms = []
+    for mine_part, came in zip(
+        (kept[1], kept[2], kept[0]), (gate_came, up_came, down_came)
+    ):
+        terms += group_finish(mine_part, came, member, group_count)
+    expert_grad = expert_grad_sum(terms, hidden_size)
 
     mine = jnp.concatenate([router_grad, attn_gain_grad[None], moe_gain_grad[None]], 0)
     mine = lax.dynamic_update_slice_in_dim(

time: 1330 us -> 1150 us (0.86)
  waiting for transfers between devices: 700 us -> 498 us
  Pallas kernels: 143 us -> 201 us
  matrix products: 206 us -> 168 us
  other arithmetic: 102 us -> 71.6 us
  starting transfers between devices: 108 us -> 127 us
  local copies, waits for them, and re-layouts: 44.7 us -> 62.4 us
    all_gather x3 -> x2, waiting for transfers between devices: 131 us -> 0.02 us  [the longest x1 0.02 us: body(): lax.all_gather(jnp.concatenate([qkv_weight.reshape(-1, 3 * size), out_wei...]
    ppermute x65 -> x70, waiting for transfers between devices: 568 us -> 498 us  [swap(): lax.ppermute(value, axis, [(i, i ^ distance) for i in range(lax.axis_size...]
    pallas_call x1 -> x3, Pallas kernels: 12.7 us -> 63.4 us  [the longest x1 26.2 us: down_pass(): pl.pallas_call(functools.partial(down_kernel, split), grid_spec=pltpu.Pre...]
    dot_general x1, matrix products: 25.3 us -> 5.13 us  [body(): jnp.dot(chosen[0], cotangent, preferred_element_type=full).astype(low)]
    ppermute x65 -> x70, starting transfers between devices: 107 us -> 126 us  [swap(): lax.ppermute(value, axis, [(i, i ^ distance) for i in range(lax.axis_size...]
    select_n x4 -> x1, other arithmetic: 17.7 us -> 0.07 us  [body(): gates_near = after(jnp.take(gates, near, axis=0), crossed[1])]
    concatenate x5 -> x3, other arithmetic: 19.9 us -> 5.07 us  [the longest x1 2.38 us: body(): jnp.concatenate([gate_mine, up_mine[:cut]], 0)]
    dot_general x27 -> x28, matrix products: 151 us -> 136 us  [contract(): lax.dot_general(left, right, (((left_dim,), (right_dim,)), ((), ())), pre...]
  transfers between devices with their start and end apart: 71 -> 74, of which waited for: 28 -> 32; matrix products, arithmetic and copies ran while one was open for 19% -> 24% of each run, Pallas kernels for 9% -> 15%
where the time goes in v3:
time: 1150 us; the launch traced here: 1140 us
  waiting for transfers between devices  498 us (43%)
  Pallas kernels  201 us (17%)
  matrix products  168 us (15%)
  starting transfers between devices  127 us (11%)
  other arithmetic  71.6 us (6%)
  local copies, waits for them, and re-layouts  62.4 us (5%)
  between operations  15.9 us (1%)
    ppermute x70, waiting for transfers between devices, swap(): lax.ppermute(value, axis, [(i, i ^ distance) for i in range(lax.axis_size...  498 us
    dot_general x28, matrix products, contract(): lax.dot_general(left, right, (((left_dim,), (right_dim,)), ((), ())), pre...  136 us
    ppermute x70, starting transfers between devices, swap(): lax.ppermute(value, axis, [(i, i ^ distance) for i in range(lax.axis_size...  126 us
    pallas_call x4, Pallas kernels, expert_pass(): pl.pallas_call(functools.partial(expert_kernel, count, len(carried)), gri...  110 us
    pallas_call x1, Pallas kernels, down_pass(): pl.pallas_call(functools.partial(down_kernel, split), grid_spec=pltpu.Pre...  26.2 us
    pallas_call x1, Pallas kernels, up_pass(): pl.pallas_call(up_kernel, grid_spec=pltpu.PrefetchScalarGridSpec(num_scal...  25.1 us
  transfers between devices with their start and end apart: 74, of which 32 were waited for; matrix products, arithmetic and copies ran while one was open for 24% of the time, Pallas kernels for 15%

profile of v3, /device:TPU:0, one launch (start us, length us, event | category | flops | bytes accessed | tf_op | source)
XLA Modules:
  0.0 1143.8 jit_solution(8957156236266382447)
XLA Ops:
  26.2 81.6 %collective-permute-done.came = bf16[1024,1408]{1,0:T(8,128)(2,1)S(1)} collective-permute-done((bf16[1024,1408]{1,0:T(8,128)(2,1)S(1)}, bf16[1024,1408]{1,0:T(8,128)(2,1)S(1)}, u32[]{:S(2)}, u32[]{:S(2)}) %collective-permute-start) | collective-permute-done | bytes 2883616 | tf_op jit(solution)/shard_map/ppermute | solution.py:26
  123.3 42.9 %collective-permute-done.1 = bf16[768,512]{1,0:T(8,128)(2,1)S(1)} collective-permute-done((bf16[768,512]{1,0:T(8,128)(2,1)S(1)}, bf16[768,512]{1,0:T(8,128)(2,1)S(1)}, u32[]{:S(2)}, u32[]{:S(2)}) %collective-permute-start.1) | collective-permute-done | bytes 786464 | tf_op jit(solution)/shard_map/ppermute | solution.py:26
  166.2 32.0 %collective-permute-done.2 = bf16[768,512]{1,0:T(8,128)(2,1)S(1)} collective-permute-done((bf16[768,512]{1,0:T(8,128)(2,1)S(1)}, bf16[768,512]{1,0:T(8,128)(2,1)S(1)}, u32[]{:S(2)}, u32[]{:S(2)}) %collective-permute-start.2) | collective-permute-done | bytes 786464 | tf_op jit(solution)/shard_map/ppermute | solution.py:26
  199.8 35.9 %collective-permute-done.6.refs_6_ = bf16[1536,1408]{1,0:T(8,128)(2,1)} collective-permute-done((bf16[1536,1408]{1,0:T(8,128)(2,1)}, bf16[1536,1408]{1,0:T(8,128)(2,1)}, u32[]{:S(2)}, u32[]{:S(2)}) %collective-permute-start.6) | collective-permute-done | bytes 4325408 | tf_op jit(solution)/shard_map/ppermute | solution.py:26
  254.4 12.5 %attention.1 = (bf16[1024,512]{1,0:T(8,128)(2,1)S(1)}, bf16[1024,512]{1,0:T(8,128)(2,1)S(1)}, bf16[1024,512]{1,0:T(8,128)(2,1)S(1)}, bf16[1024,512]{1,0:T(8,128)(2,1)S(1)}, f32[4,1024,1]{2,1,0:T(8,128)}) custom-call(f32[1024,1536]{1,0:T(8,128)} %fusion.102.q_in.k_in.v_in, f32[1024,1536]{1,0:T(8,128)} %fusion.102.q_in.k_in.v_in, ...), custom_call_target="tpu_custom_call" | custom-call | flops 1342177280 | bytes 10485760 | tf_op jit(solution)/shard_map/attention/pallas_call | solution.py:155
  293.5 28.8 %collective-permute-done.5 = bf16[1024,512]{1,0:T(8,128)(2,1)S(1)} collective-permute-done((bf16[1024,512]{1,0:T(8,128)(2,1)S(1)}, bf16[1024,512]{1,0:T(8,128)(2,1)S(1)}, u32[]{:S(2)}, u32[]{:S(2)}) %collective-permute-start.5) | collective-permute-done | bytes 1048608 | tf_op jit(solution)/shard_map/ppermute | solution.py:26
  346.9 16.5 %collective-permute-done.14.refs_0_ = bf16[768,512]{1,0:T(8,128)(2,1)} collective-permute-done((bf16[768,512]{1,0:T(8,128)(2,1)}, bf16[768,512]{1,0:T(8,128)(2,1)}, u32[]{:S(2)}, u32[]{:S(2)}) %collective-permute-start.14) | collective-permute-done | bytes 786464 | tf_op jit(solution)/shard_map/ppermute | solution.py:26
  367.4 26.2 %down.1 = (bf16[3072,2048]{1,0:T(8,128)(2,1)}, bf16[3072,1408]{1,0:T(8,128)(2,1)}) custom-call(s32[2]{0:T(128)S(1)} %pad_add_fusion.where, bf16[768,2048]{1,0:T(8,128)(2,1)} %convolution_convert_fusion.3.mine, bf16[2304,2048]{1,0:T(8,128)(2,1)} %all-gather.5.cloned.1.call-done.rest, bf16[1024,1408]{1,0:T(8,128)(2,1)S(1)} %get-tuple-element.185.own, ...), custom_call_target="tpu_custom_call" | custom-call | flops 17716740096 | bytes 39583744 | tf_op jit(solution)/shard_map/down/pallas_call | solution.py:289
  393.6 27.4 %expert.4 = (bf16[3072,2048]{1,0:T(8,128)(2,1)}, bf16[3072,1408]{1,0:T(8,128)(2,1)}, bf16[3072,2816]{1,0:T(8,128)(2,1)}, bf16[768,1024]{1,0:T(8,128)(2,1)}, bf16[768,1024]{1,0:T(8,128)(2,1)}, /*index=5*/f32[768,1]{1,0:T(8,128)}) custom-call(s32[2]{0:T(128)} %copy-done.16, bf16[768,512]{1,0:T(8,128)(2,1)} %fusion.100.refs_0_, ...), custom_call_target="tpu_custom_call" | custom-call | flops 17716740096 | bytes 32768000 | tf_op jit(solution)/shard_map/expert/pallas_call | solution.py:384
  431.3 27.4 %expert.5 = (bf16[3072,2048]{1,0:T(8,128)(2,1)}, bf16[3072,1408]{1,0:T(8,128)(2,1)}, bf16[3072,2816]{1,0:T(8,128)(2,1)}, bf16[768,1024]{1,0:T(8,128)(2,1)}, bf16[768,1024]{1,0:T(8,128)(2,1)}, /*index=5*/f32[768,1]{1,0:T(8,128)}) custom-call(s32[2]{0:T(128)} %copy-done.16, ...), custom_call_target="tpu_custom_call", output_to_operand_aliasing={{0}: (11, {}), {1}: (12, {}), {2}: (13, {})} | custom-call | flops 17716740096 | bytes 32768000 | tf_op jit(solution)/shard_map/expert/pallas_call | solution.py:384
  471.0 27.2 %expert.6 = (bf16[3072,2048]{1,0:T(8,128)(2,1)}, bf16[3072,1408]{1,0:T(8,128)(2,1)}, bf16[3072,2816]{1,0:T(8,128)(2,1)}, bf16[768,1024]{1,0:T(8,128)(2,1)}, bf16[768,1024]{1,0:T(8,128)(2,1)}, /*index=5*/f32[768,1]{1,0:T(8,128)}) custom-call(s32[2]{0:T(128)} %copy-done.16, ...), custom_call_target="tpu_custom_call", output_to_operand_aliasing={{0}: (11, {}), {1}: (12, {}), {2}: (13, {})} | custom-call | flops 17716740096 | bytes 32768000 | tf_op jit(solution)/shard_map/expert/pallas_call | solution.py:384
  514.1 27.6 %expert.7 = (bf16[3072,2048]{1,0:T(8,128)(2,1)}, bf16[3072,1408]{1,0:T(8,128)(2,1)}, bf16[3072,2816]{1,0:T(8,128)(2,1)}, bf16[768,1024]{1,0:T(8,128)(2,1)}, bf16[768,1024]{1,0:T(8,128)(2,1)}, /*index=5*/f32[768,1]{1,0:T(8,128)}) custom-call(s32[2]{0:T(128)} %copy-done.16, ...), custom_call_target="tpu_custom_call", output_to_operand_aliasing={{0}: (11, {}), {1}: (12, {}), {2}: (13, {})} | custom-call | flops 17716740096 | bytes 32768000 | tf_op jit(solution)/shard_map/expert/pallas_call | solution.py:384
  552.5 11.1 collective-permute-done.38
  572.0 15.8 %fusion.27 = bf16[1024,1408]{1,0:T(8,128)(2,1)} fusion(bf16[3072,1408]{1,0:T(8,128)(2,1)} %get-tuple-element.129.act, bf16[3072,2048]{1,0:T(8,128)(2,1)} %get-tuple-element.111, s32[]{:T(128)S(6)} %select_n.232), kind=kOutput, calls=%fused_computation.30 | convolution fusion | flops 8859811840 | bytes 17825796 | tf_op jit(solution)/shard_map/dot_general | solution.py:30
  592.6 13.2 %fusion.15 = bf16[1024,1408]{1,0:T(8,128)(2,1)} fusion(bf16[3072,1408]{1,0:T(8,128)(2,1)S(1)} %get-tuple-element.130, bf16[3072,2048]{1,0:T(8,128)(2,1)} %get-tuple-element.109, s32[]{:T(128)S(6)} %select_n.232), kind=kOutput, calls=%fused_computation.26 | convolution fusion | flops 8859811840 | bytes 17825796 | tf_op jit(solution)/shard_map/dot_general | solution.py:30
  611.4 13.6 %fusion.18 = bf16[1024,1408]{1,0:T(8,128)(2,1)} fusion(bf16[3072,1408]{1,0:T(8,128)(2,1)S(1)} %get-tuple-element.135, bf16[3072,2048]{1,0:T(8,128)(2,1)} %get-tuple-element.109, s32[]{:T(128)S(6)} %select_n.232), kind=kOutput, calls=%fused_computation.27 | convolution fusion | flops 8859811840 | bytes 17825796 | tf_op jit(solution)/shard_map/dot_general | solution.py:30
  627.6 25.1 %up.1 = bf16[3072,2048]{1,0:T(8,128)(2,1)} custom-call(s32[2]{0:T(128)S(1)} %copy-done.17, bf16[3072,1408]{1,0:T(8,128)(2,1)} %get-tuple-element.129.act, bf16[1024,1408]{1,0:T(8,128)(2,1)S(1)} %get-tuple-element.185.own, bf16[1024,1408]{1,0:T(8,128)(2,1)S(1)} %copy-done.8), custom_call_target="tpu_custom_call" | custom-call | flops 17716740096 | bytes 27000832 | tf_op jit(solution)/shard_map/up/pallas_call | solution.py:324
  659.7 11.1 collective-permute-done.42.refs_5_
  706.9 15.3 %fusion.21.refs_0_ = bf16[1024,1408]{1,0:T(8,128)(2,1)S(1)} fusion(bf16[3072,1408]{1,0:T(8,128)(2,1)} %copy-done.39, bf16[3072,2048]{1,0:T(8,128)(2,1)} %get-tuple-element.109, s32[]{:T(128)S(6)} %select_n.239), kind=kOutput, calls=%fused_computation.28 | convolution fusion | flops 8859811840 | bytes 17825796 | tf_op jit(solution)/shard_map/dot_general | solution.py:30
  722.3 11.5 %fusion.30.refs_4_ = bf16[1024,1408]{1,0:T(8,128)(2,1)} fusion(bf16[3072,1408]{1,0:T(8,128)(2,1)S(1)} %bitcast.154, bf16[3072,2048]{1,0:T(8,128)(2,1)S(1)} %bitcast.156, s32[]{:T(128)S(6)} %select_n.239), kind=kOutput, calls=%fused_computation.31 | convolution fusion | flops 8859811840 | bytes 17825796 | tf_op jit(solution)/shard_map/dot_general | solution.py:30
  733.8 19.8 %collective-permute-done.52 = bf16[1024,512]{1,0:T(8,128)(2,1)S(1)} collective-permute-done((bf16[1024,512]{1,0:T(8,128)(2,1)S(1)}, bf16[1024,512]{1,0:T(8,128)(2,1)S(1)}, u32[]{:S(2)}, u32[]{:S(2)}) %collective-permute-start.52) | collective-permute-done | bytes 1048608 | tf_op jit(solution)/shard_map/ppermute | solution.py:26
  764.2 15.9 %attention_back.1 = bf16[1024,1536]{1,0:T(8,128)(2,1)} custom-call(bf16[1024,512]{1,0:T(8,128)(2,1)S(1)} %copy-done.11, bf16[1024,512]{1,0:T(8,128)(2,1)S(1)} %copy-done.13, bf16[1024,512]{1,0:T(8,128)(2,1)S(1)} %copy-done.15, f32[4,1024,1]{2,1,0:T(8,128)} %get-tuple-element.128.logs, bf16[1024,512]{1,0:T(8,128)(2,1)S(1)} %fusion.91.grad, ...), custom_call_target="tpu_custom_call" | custom-call | flops 3355443200 | bytes 8388608 | tf_op jit(solution)/shard_map/attention_back/pallas_call | solution.py:208
  780.1 39.1 %collective-permute-done.54.refs_1_ = bf16[1024,1408]{1,0:T(8,128)(2,1)S(1)} collective-permute-done((bf16[1024,1408]{1,0:T(8,128)(2,1)}, bf16[1024,1408]{1,0:T(8,128)(2,1)S(1)}, u32[]{:S(2)}, u32[]{:S(2)}) %collective-permute-start.54) | collective-permute-done | bytes 2883616 | tf_op jit(solution)/shard_map/ppermute | solution.py:26
  820.8 10.9 convolution_convert_fusion
  850.4 17.0 %collective-permute-start.67 = (bf16[1024,512]{1,0:T(8,128)(2,1)S(1)}, bf16[1024,512]{1,0:T(8,128)(2,1)S(1)}, u32[]{:S(2)}, u32[]{:S(2)}) collective-permute-start(bf16[1024,512]{1,0:T(8,128)(2,1)S(1)} %constant_dynamic-slice_fusion), channel_id=1, source_target_pairs={{0,16},{4,20},{8,24},{12,28},{16,0},{20,4},{24,8},{28,12},{1,17},{... | collective-permute-start | bytes 3145736 | tf_op jit(solution)/shard_map/ppermute | solution.py:26
  872.7 13.2 %fusion.24.refs_2_ = bf16[1024,1408]{1,0:T(8,128)(2,1)} fusion(bf16[3072,1408]{1,0:T(8,128)(2,1)S(1)} %bitcast.87, bf16[3072,2048]{1,0:T(8,128)(2,1)} %get-tuple-element.109, s32[]{:T(128)S(6)} %select_n.239), kind=kOutput, calls=%fused_computation.29 | convolution fusion | flops 8859811840 | bytes 17825796 | tf_op jit(solution)/shard_map/dot_general | solution.py:30
  900.6 51.3 %collective-permute-done.67 = bf16[1024,512]{1,0:T(8,128)(2,1)S(1)} collective-permute-done((bf16[1024,512]{1,0:T(8,128)(2,1)S(1)}, bf16[1024,512]{1,0:T(8,128)(2,1)S(1)}, u32[]{:S(2)}, u32[]{:S(2)}) %collective-permute-start.67) | collective-permute-done | bytes 1048608 | tf_op jit(solution)/shard_map/ppermute | solution.py:26
  967.5 37.2 %collective-permute-done.44 = bf16[768,512]{1,0:T(8,128)(2,1)S(1)} collective-permute-done((bf16[768,512]{1,0:T(8,128)(2,1)S(1)}, bf16[768,512]{1,0:T(8,128)(2,1)S(1)}, u32[]{:S(2)}, u32[]{:S(2)}) %collective-permute-start.44) | collective-permute-done | bytes 786464 | tf_op jit(solution)/shard_map/ppermute | solution.py:26
  1006.8 15.7 %collective-permute-done.46 = bf16[768,512]{1,0:T(8,128)(2,1)S(1)} collective-permute-done((bf16[768,512]{1,0:T(8,128)(2,1)S(1)}, bf16[768,512]{1,0:T(8,128)(2,1)S(1)}, u32[]{:S(2)}, u32[]{:S(2)}) %collective-permute-start.46) | collective-permute-done | bytes 786464 | tf_op jit(solution)/shard_map/ppermute | solution.py:26
  1026.1 29.8 %collective-permute-start.68 = (bf16[512,512]{1,0:T(8,128)(2,1)S(1)}, bf16[512,512]{1,0:T(8,128)(2,1)S(1)}, u32[]{:S(2)}, u32[]{:S(2)}) collective-permute-start(bf16[512,512]{1,0:T(8,128)(2,1)S(1)} %dynamic-slice_convert_fusion), channel_id=1, source_target_pairs={{0,8},{4,12},{8,0},{12,4},{16,24},{20,28},{24,16},{28,20},{1,9},{5... | collective-permute-start | bytes 1572872 | tf_op jit(solution)/shard_map/ppermute | solution.py:26
  1082.2 12.5 %collective-permute-start.65 = (f32[6,2048]{1,0:T(8,128)S(1)}, f32[6,2048]{1,0:T(8,128)S(1)}, u32[]{:S(2)}, u32[]{:S(2)}) collective-permute-start(f32[6,2048]{1,0:T(8,128)S(1)} %add.270), channel_id=1, source_target_pairs={{0,8},{4,12},{8,0},{12,4},{16,24},{20,28},{24,16},{28,20},{1,9},{5... | collective-permute-start | bytes 147464 | tf_op jit(solution)/shard_map/ppermute | solution.py:26
  1106.3 12.0 %expert_grad_sum.1 = f32[3,1024,1408]{2,1,0:T(8,128)} custom-call(bf16[1024,1408]{1,0:T(8,128)(2,1)S(1)} %fusion.21.refs_0_, bf16[1024,1408]{1,0:T(8,128)(2,1)S(1)} %copy-done.2, bf16[1024,1408]{1,0:T(8,128)(2,1)S(1)} %copy-done.3, bf16[1024,1408]{1,0:T(8,128)(2,1)} %collective-permute-done.59.refs_3_, bf16[1024,1408]{1,0:T(8,128)(2,1)S(1)} %copy-done, ...), custom_call_target="tpu_custom_call" | custom-call | flops 4325376 | bytes 34603008 | tf_op jit(solution)/shard_map/expert_grad_sum/pallas_call | solution.py:443
  (476 shorter events, 350.8 us)
Async XLA Ops:
  7.2 232.7 %all-gather.3.cloned.1.call-start = ((), (), s32[]{:S(2)}) async-start(), calls=%async_computation.2 | async-start | bytes 10027008 | tf_op jit(solution)/shard_map/all_gather | solution.py:550
  12.8 352.7 %all-gather.5.cloned.1.call-start = ((), (), s32[]{:S(2)}) async-start(), calls=%async_computation.3 | async-start | bytes 11796480 | tf_op jit(solution)/shard_map/all_gather | solution.py:608
  17.8 90.0 %collective-permute-start = (bf16[1024,1408]{1,0:T(8,128)(2,1)S(1)}, bf16[1024,1408]{1,0:T(8,128)(2,1)S(1)}, u32[]{:S(2)}, u32[]{:S(2)}) collective-permute-start(bf16[1024,1408]{1,0:T(8,128)(2,1)S(1)} %get-tuple-element.185.own), channel_id=1, source_target_pairs={{0,4},{4,0},{8,12},{12,8},{16,20},{20,16},{24,28},{28,24},{1,5},{5... | collective-permute-start | bytes 8650760 | tf_op jit(solution)/shard_map/ppermute | solution.py:26
  109.4 126.3 %collective-permute-start.6 = (bf16[1536,1408]{1,0:T(8,128)(2,1)}, bf16[1536,1408]{1,0:T(8,128)(2,1)}, u32[]{:S(2)}, u32[]{:S(2)}) collective-permute-start(bf16[1536,1408]{1,0:T(8,128)(2,1)} %pad_maximum_fusion), channel_id=1, source_target_pairs={{0,4},{4,0},{8,12},{12,8},{16,20},{20,16},{24,28},{28,24},{1,5},{5... | collective-permute-start | bytes 12976136 | tf_op jit(solution)/shard_map/ppermute | solution.py:26
  118.8 47.3 %collective-permute-start.1 = (bf16[768,512]{1,0:T(8,128)(2,1)S(1)}, bf16[768,512]{1,0:T(8,128)(2,1)S(1)}, u32[]{:S(2)}, u32[]{:S(2)}) collective-permute-start(bf16[768,512]{1,0:T(8,128)(2,1)S(1)} %fusion.94), channel_id=1, source_target_pairs={{0,8},{4,12},{8,0},{12,4},{16,24},{20,28},{24,16},{28,20},{1,9},{5... | collective-permute-start | bytes 2359304 | tf_op jit(solution)/shard_map/ppermute | solution.py:26
  120.3 77.9 %collective-permute-start.2 = (bf16[768,512]{1,0:T(8,128)(2,1)S(1)}, bf16[768,512]{1,0:T(8,128)(2,1)S(1)}, u32[]{:S(2)}, u32[]{:S(2)}) collective-permute-start(bf16[768,512]{1,0:T(8,128)(2,1)S(1)} %fusion.96), channel_id=1, source_target_pairs={{0,16},{4,20},{8,24},{12,28},{16,0},{20,4},{24,8},{28,12},{1,17},{... | collective-permute-start | bytes 2359304 | tf_op jit(solution)/shard_map/ppermute | solution.py:26
  123.1 75.1 %collective-permute-start.3 = (bf16[768,512]{1,0:T(8,128)(2,1)S(1)}, bf16[768,512]{1,0:T(8,128)(2,1)S(1)}, u32[]{:S(2)}, u32[]{:S(2)}) collective-permute-start(bf16[768,512]{1,0:T(8,128)(2,1)S(1)} %fusion.98), channel_id=1, source_target_pairs={{0,24},{4,28},{8,16},{12,20},{16,8},{20,12},{24,0},{28,4},{1,25},{... | collective-permute-start | bytes 2359304 | tf_op jit(solution)/shard_map/ppermute | solution.py:26
  235.7 719.4 %reduce-scatter.3.cloned.1.call-start = ((), (), s32[]{:S(2)}) async-start(), calls=%async_computation.4 | async-start | bytes 15728640 | tf_op jit(solution)/shard_map/reduce_scatter | solution.py:709
  343.7 49.9 %collective-permute-start.11 = (bf16[768,512]{1,0:T(8,128)(2,1)}, bf16[768,512]{1,0:T(8,128)(2,1)}, u32[]{:S(2)}, u32[]{:S(2)}) collective-permute-start(bf16[768,512]{1,0:T(8,128)(2,1)} %fusion.100.refs_0_), channel_id=1, source_target_pairs={{0,1},{1,0},{2,3},{3,2},{4,5},{5,4},{6,7},{7,6},{8,9},{9,8},{10,11... | collective-permute-start | bytes 2359304 | tf_op jit(solution)/shard_map/ppermute | solution.py:26
  343.7 82.6 %collective-permute-start.10 = (bf16[768,512]{1,0:T(8,128)(2,1)}, bf16[768,512]{1,0:T(8,128)(2,1)}, u32[]{:S(2)}, u32[]{:S(2)}) collective-permute-start(bf16[768,512]{1,0:T(8,128)(2,1)} %fusion.97), channel_id=1, source_target_pairs={{0,16},{4,20},{8,24},{12,28},{16,0},{20,4},{24,8},{28,12},{1,17},{... | collective-permute-start | bytes 2359304 | tf_op jit(solution)/shard_map/ppermute | solution.py:26
  365.0 56.0 %collective-permute-start.17 = (bf16[768,512]{1,0:T(8,128)(2,1)}, bf16[768,512]{1,0:T(8,128)(2,1)}, u32[]{:S(2)}, u32[]{:S(2)}) collective-permute-start(bf16[768,512]{1,0:T(8,128)(2,1)} %collective-permute-done.14.refs_0_), channel_id=1, source_target_pairs={{0,2},{1,3},{2,0},{3,1},{4,6},{5,7},{6,4},{7,5},{8,10},{9,11},{10,... | collective-permute-start | bytes 2359304 | tf_op jit(solution)/shard_map/ppermute | solution.py:26
  365.0 63.9 %collective-permute-start.16 = (bf16[768,512]{1,0:T(8,128)(2,1)}, bf16[768,512]{1,0:T(8,128)(2,1)}, u32[]{:S(2)}, u32[]{:S(2)}) collective-permute-start(bf16[768,512]{1,0:T(8,128)(2,1)} %collective-permute-done.14.refs_0_), channel_id=1, source_target_pairs={{0,1},{1,0},{2,3},{3,2},{4,5},{5,4},{6,7},{7,6},{8,9},{9,8},{10,11... | collective-permute-start | bytes 2359304 | tf_op jit(solution)/shard_map/ppermute | solution.py:26
  465.1 49.0 %collective-permute-start.20 = (bf16[768,512]{1,0:T(8,128)(2,1)}, bf16[768,512]{1,0:T(8,128)(2,1)}, u32[]{:S(2)}, u32[]{:S(2)}) collective-permute-start(bf16[768,512]{1,0:T(8,128)(2,1)} %collective-permute-done.15.refs_0_), channel_id=1, source_target_pairs={{0,1},{1,0},{2,3},{3,2},{4,5},{5,4},{6,7},{7,6},{8,9},{9,8},{10,11... | collective-permute-start | bytes 2359304 | tf_op jit(solution)/shard_map/ppermute | solution.py:26
  465.1 42.8 %collective-permute-start.29 = (bf16[768,1024]{1,0:T(8,128)(2,1)}, bf16[768,1024]{1,0:T(8,128)(2,1)}, u32[]{:S(2)}, u32[]{:S(2)}) collective-permute-start(bf16[768,1024]{1,0:T(8,128)(2,1)} %get-tuple-element.103), channel_id=1, source_target_pairs={{0,1},{1,0},{2,3},{3,2},{4,5},{5,4},{6,7},{7,6},{8,9},{9,8},{10,11... | collective-permute-start | bytes 4718600 | tf_op jit(solution)/shard_map/ppermute | solution.py:26
  543.6 46.8 %collective-permute-start.33 = (bf16[768,1024]{1,0:T(8,128)(2,1)}, bf16[768,1024]{1,0:T(8,128)(2,1)S(1)}, u32[]{:S(2)}, u32[]{:S(2)}) collective-permute-start(bf16[768,1024]{1,0:T(8,128)(2,1)} %get-tuple-element.115), channel_id=1, source_target_pairs={{0,1},{1,0},{2,3},{3,2},{4,5},{5,4},{6,7},{7,6},{8,9},{9,8},{10,11... | collective-permute-start | bytes 4718600 | tf_op jit(solution)/shard_map/ppermute | solution.py:26
  563.6 61.4 %collective-permute-start.39 = (f32[768]{0:T(1024)S(1)}, f32[768]{0:T(1024)S(1)}, u32[]{:S(2)}, u32[]{:S(2)}) collective-permute-start(f32[768]{0:T(1024)S(1)} %get-tuple-element.177), channel_id=1, source_target_pairs={{0,8},{4,12},{8,0},{12,4},{16,24},{20,28},{24,16},{28,20},{1,9},{5... | collective-permute-start | bytes 9224 | tf_op jit(solution)/shard_map/ppermute | solution.py:26
  563.7 63.9 %collective-permute-start.40 = (f32[768]{0:T(1024)S(1)}, f32[768]{0:T(1024)S(1)}, u32[]{:S(2)}, u32[]{:S(2)}) collective-permute-start(f32[768]{0:T(1024)S(1)} %get-tuple-element.176), channel_id=1, source_target_pairs={{0,16},{4,20},{8,24},{12,28},{16,0},{20,4},{24,8},{28,12},{1,17},{... | collective-permute-start | bytes 9224 | tf_op jit(solution)/shard_map/ppermute | solution.py:26
  566.6 61.0 %collective-permute-start.41 = (f32[768]{0:T(1024)S(1)}, f32[768]{0:T(1024)S(1)}, u32[]{:S(2)}, u32[]{:S(2)}) collective-permute-start(f32[768]{0:T(1024)S(1)} %get-tuple-element.175), channel_id=1, source_target_pairs={{0,24},{4,28},{8,16},{12,20},{16,8},{20,12},{24,0},{28,4},{1,25},{... | collective-permute-start | bytes 9224 | tf_op jit(solution)/shard_map/ppermute | solution.py:26
  608.7 62.1 %collective-permute-start.42 = (bf16[1024,1408]{1,0:T(8,128)(2,1)}, bf16[1024,1408]{1,0:T(8,128)(2,1)}, u32[]{:S(2)}, u32[]{:S(2)}) collective-permute-start(bf16[1024,1408]{1,0:T(8,128)(2,1)} %fusion.27), channel_id=1, source_target_pairs={{0,4},{4,0},{8,12},{12,8},{16,20},{20,16},{24,28},{28,24},{1,5},{5... | collective-permute-start | bytes 8650760 | tf_op jit(solution)/shard_map/ppermute | solution.py:26
  670.8 454.5 %reduce-scatter.5.cloned.1.call-start = ((), (), s32[]{:S(2)}) async-start(), calls=%async_computation.5 | async-start | bytes 7077888 | tf_op jit(solution)/shard_map/reduce_scatter | solution.py:748
  705.6 48.0 %collective-permute-start.52 = (bf16[1024,512]{1,0:T(8,128)(2,1)S(1)}, bf16[1024,512]{1,0:T(8,128)(2,1)S(1)}, u32[]{:S(2)}, u32[]{:S(2)}) collective-permute-start(bf16[1024,512]{1,0:T(8,128)(2,1)S(1)} %fusion.203), channel_id=1, source_target_pairs={{0,2},{1,3},{2,0},{3,1},{4,6},{5,7},{6,4},{7,5},{8,10},{9,11},{10,... | collective-permute-start | bytes 3145736 | tf_op jit(solution)/shard_map/ppermute | solution.py:26
  754.1 65.1 %collective-permute-start.54 = (bf16[1024,1408]{1,0:T(8,128)(2,1)}, bf16[1024,1408]{1,0:T(8,128)(2,1)S(1)}, u32[]{:S(2)}, u32[]{:S(2)}) collective-permute-start(bf16[1024,1408]{1,0:T(8,128)(2,1)} %fusion.15), channel_id=1, source_target_pairs={{0,4},{4,0},{8,12},{12,8},{16,20},{20,16},{24,28},{28,24},{1,5},{5... | collective-permute-start | bytes 8650760 | tf_op jit(solution)/shard_map/ppermute | solution.py:26
  850.4 101.5 %collective-permute-start.67 = (bf16[1024,512]{1,0:T(8,128)(2,1)S(1)}, bf16[1024,512]{1,0:T(8,128)(2,1)S(1)}, u32[]{:S(2)}, u32[]{:S(2)}) collective-permute-start(bf16[1024,512]{1,0:T(8,128)(2,1)S(1)} %constant_dynamic-slice_fusion), channel_id=1, source_target_pairs={{0,16},{4,20},{8,24},{12,28},{16,0},{20,4},{24,8},{28,12},{1,17},{... | collective-permute-start | bytes 3145736 | tf_op jit(solution)/shard_map/ppermute | solution.py:26
  867.4 94.9 %collective-permute-start.59 = (bf16[1024,1408]{1,0:T(8,128)(2,1)}, bf16[1024,1408]{1,0:T(8,128)(2,1)}, u32[]{:S(2)}, u32[]{:S(2)}) collective-permute-start(bf16[1024,1408]{1,0:T(8,128)(2,1)} %fusion.18), channel_id=1, source_target_pairs={{0,4},{4,0},{8,12},{12,8},{16,20},{20,16},{24,28},{28,24},{1,5},{5... | collective-permute-start | bytes 8650760 | tf_op jit(solution)/shard_map/ppermute | solution.py:26
  900.6 52.9 %collective-permute-start.57 = (f32[1,1024]{1,0:T(1,128)S(1)}, f32[1,1024]{1,0:T(1,128)S(1)}, u32[]{:S(2)}, u32[]{:S(2)}) collective-permute-start(f32[1,1024]{1,0:T(1,128)S(1)} %bitcast.122), channel_id=1, source_target_pairs={{0,1},{1,0},{2,3},{3,2},{4,5},{5,4},{6,7},{7,6},{8,9},{9,8},{10,11... | collective-permute-start | bytes 12296 | tf_op jit(solution)/shard_map/ppermute | solution.py:26
  957.1 47.6 %collective-permute-start.44 = (bf16[768,512]{1,0:T(8,128)(2,1)S(1)}, bf16[768,512]{1,0:T(8,128)(2,1)S(1)}, u32[]{:S(2)}, u32[]{:S(2)}) collective-permute-start(bf16[768,512]{1,0:T(8,128)(2,1)S(1)} %get-tuple-element.206), channel_id=1, source_target_pairs={{0,8},{4,12},{8,0},{12,4},{16,24},{20,28},{24,16},{28,20},{1,9},{5... | collective-permute-start | bytes 2359304 | tf_op jit(solution)/shard_map/ppermute | solution.py:26
  957.2 48.5 %collective-permute-start.45 = (bf16[768,512]{1,0:T(8,128)(2,1)S(1)}, bf16[768,512]{1,0:T(8,128)(2,1)S(1)}, u32[]{:S(2)}, u32[]{:S(2)}) collective-permute-start(bf16[768,512]{1,0:T(8,128)(2,1)S(1)} %get-tuple-element.205), channel_id=1, source_target_pairs={{0,16},{4,20},{8,24},{12,28},{16,0},{20,4},{24,8},{28,12},{1,17},{... | collective-permute-start | bytes 2359304 | tf_op jit(solution)/shard_map/ppermute | solution.py:26
  962.3 93.6 %collective-permute-start.60 = (bf16[1024,512]{1,0:T(8,128)(2,1)S(1)}, bf16[1024,512]{1,0:T(8,128)(2,1)S(1)}, u32[]{:S(2)}, u32[]{:S(2)}) collective-permute-start(bf16[1024,512]{1,0:T(8,128)(2,1)S(1)} %fusion.62), channel_id=1, source_target_pairs={{0,2},{1,3},{2,0},{3,1},{4,6},{5,7},{6,4},{7,5},{8,10},{9,11},{10,... | collective-permute-start | bytes 3145736 | tf_op jit(solution)/shard_map/ppermute | solution.py:26
  962.8 59.7 %collective-permute-start.46 = (bf16[768,512]{1,0:T(8,128)(2,1)S(1)}, bf16[768,512]{1,0:T(8,128)(2,1)S(1)}, u32[]{:S(2)}, u32[]{:S(2)}) collective-permute-start(bf16[768,512]{1,0:T(8,128)(2,1)S(1)} %get-tuple-element.204), channel_id=1, source_target_pairs={{0,24},{4,28},{8,16},{12,20},{16,8},{20,12},{24,0},{28,4},{1,25},{... | collective-permute-start | bytes 2359304 | tf_op jit(solution)/shard_map/ppermute | solution.py:26
  1023.7 42.9 %collective-permute-start.47 = (bf16[1024,512]{1,0:T(8,128)(2,1)S(1)}, bf16[1024,512]{1,0:T(8,128)(2,1)S(1)}, u32[]{:S(2)}, u32[]{:S(2)}) collective-permute-start(bf16[1024,512]{1,0:T(8,128)(2,1)S(1)} %add_convert_fusion), channel_id=1, source_target_pairs={{0,2},{1,3},{2,0},{3,1},{4,6},{5,7},{6,4},{7,5},{8,10},{9,11},{10,... | collective-permute-start | bytes 3145736 | tf_op jit(solution)/shard_map/ppermute | solution.py:26
  1057.7 61.8 %collective-permute-start.61 = (bf16[1024,1024]{1,0:T(8,128)(2,1)}, bf16[1024,1024]{1,0:T(8,128)(2,1)}, u32[]{:S(2)}, u32[]{:S(2)}) collective-permute-start(bf16[1024,1024]{1,0:T(8,128)(2,1)} %pad_maximum_fusion.7), channel_id=1, source_target_pairs={{0,1},{1,0},{2,3},{3,2},{4,5},{5,4},{6,7},{7,6},{8,9},{9,8},{10,11... | collective-permute-start | bytes 6291464 | tf_op jit(solution)/shard_map/ppermute | solution.py:26
  1069.5 61.6 %collective-permute-start.48 = (bf16[1024,1024]{1,0:T(8,128)(2,1)}, bf16[1024,1024]{1,0:T(8,128)(2,1)}, u32[]{:S(2)}, u32[]{:S(2)}) collective-permute-start(bf16[1024,1024]{1,0:T(8,128)(2,1)} %pad_maximum_fusion.4), channel_id=1, source_target_pairs={{0,1},{1,0},{2,3},{3,2},{4,5},{5,4},{6,7},{7,6},{8,9},{9,8},{10,11... | collective-permute-start | bytes 6291464 | tf_op jit(solution)/shard_map/ppermute | solution.py:26
  (128 other events, 2527.2 us)
Sparse Core Ops, SparseCore 0:
  12.9 207.8 all-gather.2
  235.9 78.4 all-gather.4
  670.9 121.4 reduce-scatter.2
  831.8 217.2 reduce-scatter.4

commit v4 on v3

--- a/solution.py
+++ b/solution.py
@@ -249,15 +249,14 @@
     return [(own, 0, half, True, 0, 0), (came, 0, half, False, 0, 0)]
 
 
-def pair_pieces(own_gate, own_up, came, rest):
-    half, less = own_gate.shape[0], rest.shape[0]
-    more = half - less
+def pair_pieces(own_gate, own_up, came, near, far):
+    half, more = own_gate.shape[0], near.shape[0]
     return [
         (own_gate, 0, half, True, 0, 0),
         (own_up, 0, half, True, 0, 1),
         (came, 0, half, False, 0, 0),
-        (came, half, more, False, 0, 1),
-        (rest, 0, less, False, more, 1),
+        (near, 0, more, False, 0, 1),
+        (far, 0, half - more, False, more, 1),
     ]
 
 
@@ -265,8 +264,11 @@
     return pl.ds(pl.multiple_of((i ^ where[0]) * size, size), size)
 
 
-def down_kernel(split, where, mine, rest, own, came, rows_out, raw, held, sems):
+def down_kernel(count, split, where, mine, *refs):
+    blocks = refs[:count]
+    own, came, rows_out, raw, held, sems = refs[count:]
     step = pl.program_id(0)
+    size = blocks[0].shape[1]
     place_rows(down_pieces(own, came), held, sems, where[1], step == 0)
 
     @pl.when(step < split)
@@ -275,27 +277,32 @@
 
     @pl.when(step >= split)
     def _():
-        rows_out[...] = rest[...]
+        for i, ref in enumerate(blocks):
+            rows_out[:, column_block(where, i, size)] = ref[...]
 
     raw[...] = jnp.dot(rows_out[...], held[...], preferred_element_type=full).astype(low)
 
 
-def down_pass(where, mine, rest, own, came):
-    total = mine.shape[0] + rest.shape[0]
+def down_pass(where, mine, blocks, own, came):
+    count = len(blocks)
+    size = blocks[0].shape[1]
     width, hidden = 2 * own.shape[0], own.shape[1]
+    total = mine.shape[0] + blocks[0].shape[0]
     tile = 256
     split = mine.shape[0] // tile
+    anywhere = pl.BlockSpec(memory_space=pl.ANY)
     spec = lambda columns: pl.BlockSpec((tile, columns), lambda i, where: (i, 0))
+    late = pl.BlockSpec((tile, size), lambda i, where: (jnp.maximum(i - split, 0), 0))
     return pl.pallas_call(
-        functools.partial(down_kernel, split),
+        functools.partial(down_kernel, count, split),
         grid_spec=pltpu.PrefetchScalarGridSpec(
             num_scalar_prefetch=1,
             grid=(total // tile,),
             in_specs=[
-                pl.BlockSpec((tile, width), lambda i, where: (jnp.minimum(i, split - 1), 0)),
-                pl.BlockSpec((tile, width), lambda i, where: (jnp.maximum(i - split, 0), 0)),
+                pl.BlockSpec((tile, width), lambda i, where: (jnp.minimum(i, split - 1), 0))
             ]
-            + [pl.BlockSpec(memory_space=pl.ANY)] * 2,
+            + [late] * count
+            + [anywhere] * 2,
             out_specs=[spec(width), spec(hidden)],
             scratch_shapes=[pltpu.VMEM((width, hidden), low), pltpu.SemaphoreType.DMA((2,))],
         ),
@@ -308,7 +315,7 @@
             2 * total * width * hidden, (total * (2 * width + hidden) + width * hidden) * 2
         ),
         name="down",
-    )(where, mine, rest, own, came)
+    )(where, mine, *blocks, own, came)
 
 
 def up_kernel(where, act, own, came, out, held, sems):
@@ -341,8 +348,8 @@
 
 def expert_kernel(count, carried, where, *refs):
     blocks, refs = refs[:count], refs[count:]
-    weights, raw, gate = refs[:4], refs[4], refs[5]
-    rows_out, act_out, grad_out, even, odd, gate_grad, pair, part, sems = refs[6 + carried :]
+    weights, raw, routed, router = refs[:5], refs[5], refs[6], refs[7]
+    rows_out, act_out, grad_out, even, odd, gate_grad, pair, part, sems = refs[8 + carried :]
     size = blocks[0].shape[1]
     hidden = raw.shape[1]
     place_rows(pair_pieces(*weights), pair, sems, where[1], pl.program_id(0) == 0)
@@ -355,9 +362,17 @@
     silu = pre_gate * sigma
     act = silu * pre_up
     back = raw[...].astype(full)
-    gate_grad[...] = jnp.sum(act * back, axis=1, keepdims=True)
-    act_out[...] = (act * gate[...]).astype(low)
-    back = back * gate[...]
+    tile = back.shape[0]
+    own = where[2].astype(full)
+    other = jnp.broadcast_to(routed[...], (128, tile)).T - own
+    logits = jnp.dot(rows_out[...], router[...], preferred_element_type=full)
+    lane = lax.broadcasted_iota(jnp.int32, (tile, 128), 1).astype(full)
+    ahead = jnp.where(lane == other, logits, 0.0) - jnp.where(lane == own, logits, 0.0)
+    gate = 1.0 / (1.0 + jnp.exp(jnp.sum(ahead, axis=1, keepdims=True)))
+    gate_sum = jnp.sum(act * back, axis=1, keepdims=True)
+    gate_grad[...] = jnp.broadcast_to(gate_sum, (tile, 128)).T[:1]
+    act_out[...] = (act * gate).astype(low)
+    back = back * gate
     grad_out[:, :hidden] = (back * pre_up * sigma * (1.0 + pre_gate * (1.0 - sigma))).astype(low)
     grad_out[:, hidden:] = (back * silu).astype(low)
     part[...] = dot_cols(grad_out[...], pair[...]).astype(low)
@@ -367,7 +382,7 @@
         ]
 
 
-def expert_pass(step, where, blocks, weights, raw, gate, carried):
+def expert_pass(step, where, blocks, weights, raw, routed, router, carried):
     count = len(blocks)
     size = blocks[0].shape[1]
     width, hidden = 2 * weights[0].shape[0], weights[0].shape[1]
@@ -379,6 +394,7 @@
     near = lambda i, where: (i, 0)
     near_spec = lambda columns: pl.BlockSpec((tile, columns), near)
     here_spec = lambda columns: pl.BlockSpec((tile, columns), here)
+    row_spec = pl.BlockSpec((1, tile), lambda i, where: (0, i))
     anywhere = pl.BlockSpec(memory_space=pl.ANY)
     shape = lambda r, c, t=low: jax.ShapeDtypeStruct((r, c), t)
     return pl.pallas_call(
@@ -387,8 +403,12 @@
             num_scalar_prefetch=1,
             grid=(steps,),
             in_specs=[near_spec(size)] * count
-            + [anywhere] * 4
-            + [here_spec(hidden), near_spec(1)]
+            + [anywhere] * 5
+            + [
+                here_spec(hidden),
+                row_spec,
+                pl.BlockSpec((width, 128), lambda i, where: (0, 0)),
+            ]
             + [anywhere] * len(carried),
             out_specs=[
                 here_spec(width),
@@ -396,7 +416,7 @@
                 here_spec(both),
                 near_spec(width // 2),
                 near_spec(width // 2),
-                near_spec(1),
+                row_spec,
             ],
             scratch_shapes=[
                 pltpu.VMEM((width, both), low),
@@ -410,46 +430,65 @@
             shape(total, both),
             shape(MOST, width // 2),
             shape(MOST, width // 2),
-            shape(MOST, 1, full),
+            shape(1, MOST, full),
         ],
-        input_output_aliases={count + 7 + i: i for i in range(len(carried))},
+        input_output_aliases={count + 9 + i: i for i in range(len(carried))},
         compiler_params=limits(60),
         cost_estimate=cost(
             4 * MOST * width * both, width * both * 2 + MOST * (width * 8 + hidden * 8), MOST * hidden
         ),
         name="expert",
-    )(where, *blocks, *weights, raw, gate, *carried)
-
-
-def expert_grad_kernel(hidden, *refs):
+    )(where, *blocks, *weights, raw, routed, router, *carried)
+
+
+def expert_grad_kernel(hidden, pieces, per, *refs):
     out = refs[-1]
-    for k in range(3):
-
-        @pl.when(pl.program_id(0) == k)
+    which, at = pl.program_id(0), pl.program_id(1)
+
+    def add(ref, other):
+        out[0] = (ref[...].astype(full) + other[...].astype(full))[:, :hidden]
+
+    for k in range(pieces):
+
+        @pl.when((which < 2) & (at // per == k))
         def _():
-            out[0] = (refs[2 * k][...].astype(full) + refs[2 * k + 1][...].astype(full))[:, :hidden]
-
-
-def expert_grad_sum(terms, hidden):
-    rows, padded = terms[0].shape
-    tile = 256
+            add(refs[0], refs[1 + k])
+
+    @pl.when(which == 2)
+    def _():
+        add(refs[1 + pieces], refs[2 + pieces])
+
+
+def expert_grad_sum(pair, down, hidden):
+    rows, padded = down[0].shape
+    tile = min(256, rows)
+    pieces = len(pair) - 1
+    per = rows // tile // pieces
     last = rows // tile - 1
 
-    def spec(k):
+    def piece_spec(k):
         return pl.BlockSpec(
-            (tile, padded), lambda w, i: (jnp.where(w == k, i, jnp.where(w < k, 0, last)), 0)
+            (tile, padded),
+            lambda w, i: (
+                jnp.where(w == 2, per - 1, jnp.clip(i - k * per, 0, per - 1)),
+                jnp.minimum(w, 1),
+            ),
         )
 
+    pair_spec = pl.BlockSpec(
+        (tile, padded), lambda w, i: (jnp.where(w == 2, last, i), jnp.minimum(w, 1))
+    )
+    down_spec = pl.BlockSpec((tile, padded), lambda w, i: (jnp.where(w == 2, i, 0), 0))
     return pl.pallas_call(
-        functools.partial(expert_grad_kernel, hidden),
+        functools.partial(expert_grad_kernel, hidden, pieces, per),
         grid=(3, rows // tile),
-        in_specs=[spec(k // 2) for k in range(6)],
+        in_specs=[pair_spec] + [piece_spec(k) for k in range(pieces)] + [down_spec] * 2,
         out_specs=pl.BlockSpec((1, tile, hidden), lambda w, i: (w, i, 0)),
         out_shape=jax.ShapeDtypeStruct((3, rows, hidden), full),
-        compiler_params=limits(32),
+        compiler_params=limits(40),
         cost_estimate=cost(rows * padded * 3, rows * padded * 24),
         name="expert_grad_sum",
-    )(*terms)
+    )(*pair, *down)
 
 
 def near_blocks(own, *others):
@@ -493,18 +532,9 @@
     return held
 
 
-def dp_scatter(value):
-    index = lax.axis_index("dp")
-    for bit in range(levels_of(lax.axis_size("dp")))[::-1]:
-        middle = value.shape[0] // 2
-        upper = (index >> bit) & 1
-        kept = lax.dynamic_slice_in_dim(value, upper * middle, middle, 0)
-        given = lax.dynamic_slice_in_dim(value, (1 - upper) * middle, middle, 0)
-        value = kept.astype(full) + swap(given.astype(low), "dp", 1 << bit).astype(full)
-    return value
-
-
 def group_finish(kept, came, position, group_count):
+    if group_count > 2:
+        came = jnp.concatenate(came, 0)
     for bit in range(levels_of(group_count) - 1)[::-1]:
         current = kept.astype(full) + came.astype(full)
         middle = current.shape[0] // 2
@@ -512,7 +542,7 @@
         kept = lax.dynamic_slice_in_dim(current, upper * middle, middle, 0)
         given = lax.dynamic_slice_in_dim(current, (1 - upper) * middle, middle, 0)
         came = swap(given.astype(low), "dp", 1 << bit)
-    return kept, came
+    return [kept, *came] if isinstance(came, list) else [kept, came]
 
 
 def body(
@@ -540,7 +570,7 @@
     expert = index // group_count
     member = index % group_count
     top_half = member >> (levels_of(group_count) - 1)
-    where = jnp.stack([place, top_half]).astype(jnp.int32)
+    where = jnp.stack([place, top_half, expert]).astype(jnp.int32)
 
     def own_columns(value):
         return lax.dynamic_slice_in_dim(value, place * size, size, 1)
@@ -598,27 +628,33 @@
 
     cut = half // 2
     down = (down_mine, group_send(down_mine))
-    pair_came = group_send(jnp.concatenate([gate_mine, up_mine[:cut]], 0), down[1])
-    pair_rest = group_send(up_mine[cut:], pair_came)
-    pair = (gate_mine, up_mine, pair_came, pair_rest)
+    gate_came = group_send(gate_mine)
+    up_near = group_send(up_mine[:cut], first)
+    pair = (gate_mine, up_mine, gate_came, up_near, group_send(up_mine[cut:], up_near))
 
     grad_own = own_columns(cotangent)
     grad_mine = jnp.dot(chosen[0], cotangent, preferred_element_type=full).astype(low)
-    grad_came = exchange([after(v, down[1]) for v in packed(grad_own)])[1:]
-    grad_rest = lax.all_gather(
-        after(jnp.concatenate(grad_came, 0), pair_came), "tensor", axis=1, tiled=True
-    )
+    grad_came = exchange(packed(grad_own))[1:]
+    grad_blocks = near_blocks(after(jnp.concatenate(grad_came, 0), down[1]))
+    route_sums = jnp.sum(routes, axis=1)[None].astype(low)
+    routed = exchange([contract(route_sums, c, 1, 1) for c in chosen])
 
     inputs = tokens.astype(full)
     scale_one = lax.rsqrt(jnp.mean(inputs * inputs, axis=1, keepdims=True) + epsilon)
     normed_in = (inputs * scale_one * gain_first).astype(low)
     inputs_own = own_columns(tokens).astype(full)
-    qkv_flat = after(qkv_flat, *grad_came)
+    qkv_flat = after(qkv_flat, down[1], gate_came, *grad_blocks, *routed)
     qkv = jnp.dot(normed_in, qkv_flat, preferred_element_type=full)
     cosine, sine = rotary_tables()
     context, query, keys, values, logs = attention(qkv, cosine, sine, scale)
     attn_part = contract(context, out_full, 1, 1).astype(low)
-    hidden = after(inputs_own + tensor_reduce(attn_part), pair_rest)
+    rows_raw = []
+
+    def down_filler(sent):
+        rows_raw.extend(down_pass(where, after(grad_mine, sent), grad_blocks, *down))
+        return rows_raw
+
+    hidden = after(inputs_own + tensor_reduce(attn_part, down_filler), up_near)
 
     scaled_hidden = (hidden * gain_second_own).astype(low)
     sums = tensor_sum(
@@ -647,27 +683,19 @@
     ]
     arrived = [near_blocks(moe_packed[0])]
 
-    gates_near = after(jnp.take(gates, near, axis=0), crossed[1])
-    gate_rows = exchange(
-        [
-            jnp.sum(contract(three_parts(gates_near[s]), chosen[s], 1, 1), 0)
-            for s in range(EXPERTS)
-        ]
-    )
-
-    grad_rows, raw = down_pass(where, after(grad_mine, *moe_packed), grad_rest, *down)
     carried = ()
     sums_sent = []
     returned = []
     gate_grads = []
+    router_block = first[:, 4 * size :]
     for step in range(EXPERTS):
-        gate = gate_rows[step][:, None]
+        named_sum = routed[step]
         if step == 2:
-            gate = after(gate, sums_sent[0])
+            named_sum = after(named_sum, sums_sent[0])
         if step == 3:
-            gate = after(gate, sums_sent[1], returned[0])
+            named_sum = after(named_sum, sums_sent[1], returned[0], gate_grads[1])
         moe_rows, activation, pre_grad, even, odd, gate_grad = expert_pass(
-            step, where, arrived[step], pair, raw, gate, carried
+            step, where, arrived[step], pair, rows_raw[1], named_sum, router_block, carried
         )
         carried = (moe_rows, activation, pre_grad)
         if step == 0:
@@ -680,11 +708,11 @@
         if step == 2:
             arrived.append(near_blocks(crossed[3], even))
         returned.append(near_reduce(even, odd, sums_sent, *returned[2:]))
-        gate_grads.append(gate_grad)
+        gate_grads.append(swap(gate_grad, "dp", step * group_count) if step else gate_grad)
     own_returned = returned
     returned = exchange(returned)
-    gate_grad_rows = tensor_sum(jnp.concatenate(gate_grads, 1).T)
-    gate_grad_near = exchange([gate_grad_rows[s] for s in range(EXPERTS)])
+    gate_grad_near = gate_grads
+    grad_rows = rows_raw[0]
 
     def term(left, right):
         def part(start, number):
@@ -693,76 +721,85 @@
 
         return part
 
-    down_term = term(grad_rows, after(activation, sums_sent[2], own_returned[1]))
-    down_given = down_term(given_at, half)
-    gate_term = term(moe_rows, after(pre_grad[:, :padded], down_given, sums_sent[3]))
-    gate_given = gate_term(given_at, half)
-    up_term = term(moe_rows, after(pre_grad[:, padded:], gate_given, own_returned[3]))
-    up_given = up_term(given_at, half)
-    down_came = group_send(down_given)
-    gate_came = group_send(gate_given, down_came)
-    up_came = group_send(up_given, gate_came)
-    expert_part = up_pass(
-        where, after(activation, up_given, returned[1], *gate_grad_near), *down
-    )
-    expert_part = after(expert_part, down_came, returned[2])
-    expert_own = lax.psum_scatter(expert_part, "tensor", scatter_dimension=1, tiled=True)
+    expert_part = up_pass(where, after(activation, sums_sent[2], own_returned[1], gate_grads[2]), *down)
+    expert_own = lax.psum_scatter(
+        after(expert_part, sums_sent[3], gate_grads[3]), "tensor", scatter_dimension=1, tiled=True
+    )
+    down_given = term(grad_rows, after(activation, expert_part, sums_sent[3], own_returned[2]))(
+        given_at, half
+    )
+    down_sum = group_send(down_given)
+    pair_term = term(moe_rows, after(pre_grad, down_given, own_returned[3]))
+    quarter = half // 2
+    pair_given = [pair_term(given_at + k * quarter, quarter) for k in range(2)]
+    pair_sum = [group_send(pair_given[0], down_sum)]
+    pair_sum.append(group_send(pair_given[1], pair_sum[0]))
     mixed = unpacked(exchange([expert_own[s * MOST : (s + 1) * MOST] for s in range(EXPERTS)]))
     layer_own = hidden + mixed
     layer_out = tensor_gather(layer_own.astype(low)).astype(full)
+    returned = [after(v, *pair_given) for v in returned]
+    returned[3] = after(returned[3], down_sum)
     back = unpacked(returned)
 
-    gate_grad = jnp.stack(
+    gate_grad = jnp.concatenate(
         [
-            jnp.sum(contract(three_parts(gate_grad_near[s]), chosen[s], 1, 0), 0)
+            jnp.sum(contract(three_parts(gate_grad_near[s][0]), chosen[s], 1, 0), 0, keepdims=True)
             for s in range(EXPERTS)
-        ]
-    )
-    gate_grad = jnp.take(gate_grad, near, axis=0)
+        ],
+        0,
+    )
+    scaled_back = back * gain_second_own
+    sums = tensor_sum(
+        jnp.concatenate([gate_grad, jnp.sum(scaled_back * normed_two, axis=1)[None]], 0)
+    )
+    gate_grad = jnp.take(sums[:EXPERTS], near, axis=0)
     weighted = jnp.sum(gates * gate_grad, axis=0, keepdims=True)
     logit_grad = (gates * (gate_grad - weighted)).astype(low)
+    mean_two = (
+        sums[EXPERTS:] + jnp.sum(logit_grad.astype(full) * logits, axis=0, keepdims=True)
+    ) / width
+    moe_grad = contract(logit_grad, router_own, 0, 0) + back
+
+    grad_out = grad_own.astype(full)
+    hidden_grad = grad_out + scale_two * (
+        moe_grad * gain_second_own - normed_two * mean_two.reshape(rows, 1)
+    )
     router_grad = jnp.dot(logit_grad, moe_in, preferred_element_type=full)
-    moe_grad = contract(logit_grad, router_own, 0, 0) + back
-
-    grad_out = grad_own.astype(full)
-    scaled_grad = moe_grad * gain_second_own
     moe_gain_grad = jnp.sum(moe_grad * normed_two, axis=0)
-    mean_two = tensor_sum(jnp.sum(scaled_grad * normed_two, axis=1)[None]) / width
-    hidden_grad = grad_out + scale_two * (scaled_grad - normed_two * mean_two.reshape(rows, 1))
     kept = []
 
-    def first_kept(sent):
+    def keep(sent):
         kept.append(term(grad_rows, after(activation, sent))(mine_at, half))
-        kept.append(term(moe_rows, after(pre_grad[:, :padded], sent))(mine_at, half))
-        return kept
-
-    def last_kept(sent):
-        kept.append(term(moe_rows, after(pre_grad[:, padded:], sent))(mine_at, half))
-        return kept[2:]
-
-    attn_grad = tensor_gather(hidden_grad.astype(low), first_kept)
+        return kept[:1]
+
+    def keep_pair(sent):
+        kept.append(term(moe_rows, after(pre_grad, sent))(mine_at, half))
+        return kept[1:]
+
+    attn_grad = tensor_gather(hidden_grad.astype(low), keep)
     context_grad = jnp.dot(attn_grad, out_full, preferred_element_type=full).astype(low)
+    out_shard = lax.psum_scatter(
+        contract(after(attn_grad, context_grad), context, 0, 0).astype(low), "dp", scatter_dimension=0, tiled=True
+    ).astype(full)
     qkv_grad_rows = attention_back(query, keys, values, logs, context_grad, cosine, sine, scale)
-    qkv_grad_rows = after(qkv_grad_rows, gate_came)
+    qkv_grad_rows = after(qkv_grad_rows, pair_sum[0])
     qkv_grad = contract(normed_in, qkv_grad_rows, 0, 0).astype(low)
     qkv_shard = lax.psum_scatter(qkv_grad, "dp", scatter_dimension=0, tiled=True).astype(full)
     normed_grad = tensor_reduce(
-        contract(after(qkv_grad_rows, qkv_grad), qkv_flat, 1, 1).astype(low), last_kept
-    )
-    out_shard = dp_scatter(contract(attn_grad, context, 0, 0).astype(low))
+        contract(after(qkv_grad_rows, qkv_grad), qkv_flat, 1, 1).astype(low), keep_pair
+    )
     normed_one = inputs_own * scale_one
     scaled_in = normed_grad * gain_first_own
     attn_gain_grad = jnp.sum(normed_grad * normed_one, axis=0)
     mean_one = tensor_sum(jnp.sum(scaled_in * normed_one, axis=1)[None]) / width
     input_own = hidden_grad + scale_one * (scaled_in - normed_one * mean_one.reshape(rows, 1))
-    input_own = after(input_own, up_came)
+    input_own = after(input_own, pair_sum[1])
     input_grad = tensor_gather(input_own.astype(low)).astype(full)
-    terms = []
-    for mine_part, came in zip(
-        (kept[1], kept[2], kept[0]), (gate_came, up_came, down_came)
-    ):
-        terms += group_finish(mine_part, came, member, group_count)
-    expert_grad = expert_grad_sum(terms, hidden_size)
+    expert_grad = expert_grad_sum(
+        group_finish(kept[1], pair_sum, member, group_count),
+        group_finish(kept[0], [down_sum], member, group_count),
+        hidden_size,
+    )
 
     mine = jnp.concatenate([router_grad, attn_gain_grad[None], moe_gain_grad[None]], 0)
     mine = lax.dynamic_update_slice_in_dim(

time: 1150 us -> 1020 us (0.89)
  waiting for transfers between devices: 498 us -> 355 us
  starting transfers between devices: 127 us -> 152 us
  local copies, waits for them, and re-layouts: 62.4 us -> 42.8 us
  Pallas kernels: 201 us -> 216 us
    ppermute x70 -> x69, waiting for transfers between devices: 498 us -> 335 us  [swap(): lax.ppermute(value, axis, [(i, i ^ distance) for i in range(lax.axis_size...]
    ppermute x70 -> x69, starting transfers between devices: 126 us -> 152 us  [swap(): lax.ppermute(value, axis, [(i, i ^ distance) for i in range(lax.axis_size...]
    all_gather x1, waiting for transfers between devices: 0.02 us -> 20.4 us  [body(): lax.all_gather(jnp.concatenate([qkv_weight.reshape(-1, 3 * size), out_wei...]
    dot_general x28 -> x27, matrix products: 136 us -> 140 us  [contract(): lax.dot_general(left, right, (((left_dim,), (right_dim,)), ((), ())), pre...]
  transfers between devices with their start and end apart: 74 -> 73, of which waited for: 32 -> 26; matrix products, arithmetic and copies ran while one was open for 24% -> 23% of each run, Pallas kernels for 15% -> 20%
where the time goes in v4:
time: 1020 us; the launch traced here: 1010 us
  waiting for transfers between devices  355 us (35%)
  Pallas kernels  216 us (21%)
  matrix products  168 us (16%)
  starting transfers between devices  152 us (15%)
  other arithmetic  64 us (6%)
  local copies, waits for them, and re-layouts  42.8 us (4%)
  between operations  15.7 us (2%)
    ppermute x69, waiting for transfers between devices, swap(): lax.ppermute(value, axis, [(i, i ^ distance) for i in range(lax.axis_size...  335 us
    ppermute x69, starting transfers between devices, swap(): lax.ppermute(value, axis, [(i, i ^ distance) for i in range(lax.axis_size...  152 us
    dot_general x27, matrix products, contract(): lax.dot_general(left, right, (((left_dim,), (right_dim,)), ((), ())), pre...  140 us
    pallas_call x4, Pallas kernels, expert_pass(): pl.pallas_call(functools.partial(expert_kernel, count, len(carried)), gri...  119 us
    pallas_call x1, Pallas kernels, down_pass(): pl.pallas_call(functools.partial(down_kernel, count, split), grid_spec=pl...  29.1 us
    pallas_call x1, Pallas kernels, up_pass(): pl.pallas_call(up_kernel, grid_spec=pltpu.PrefetchScalarGridSpec(num_scal...  26.8 us
  transfers between devices with their start and end apart: 73, of which 26 were waited for; matrix products, arithmetic and copies ran while one was open for 23% of the time, Pallas kernels for 20%

profile of v4, /device:TPU:0, one launch (start us, length us, event | category | flops | bytes accessed | tf_op | source)
XLA Modules:
  0.0 1014.4 jit_solution(13338215248423247349)
XLA Ops:
  30.8 62.9 %collective-permute-done.2 = bf16[768,512]{1,0:T(8,128)(2,1)S(1)} collective-permute-done((bf16[768,512]{1,0:T(8,128)(2,1)S(1)}, bf16[768,512]{1,0:T(8,128)(2,1)S(1)}, u32[]{:S(2)}, u32[]{:S(2)}) %collective-permute-start.2) | collective-permute-done | bytes 786464 | tf_op jit(solution)/shard_map/ppermute | solution.py:26
  96.6 16.9 %collective-permute-done.4 = bf16[768,512]{1,0:T(8,128)(2,1)S(1)} collective-permute-done((bf16[768,512]{1,0:T(8,128)(2,1)S(1)}, bf16[768,512]{1,0:T(8,128)(2,1)S(1)}, u32[]{:S(2)}, u32[]{:S(2)}) %collective-permute-start.4) | collective-permute-done | bytes 786464 | tf_op jit(solution)/shard_map/ppermute | solution.py:26
  118.0 50.2 %collective-permute-done.6.refs_2_ = bf16[2304,512]{1,0:T(8,128)(2,1)} collective-permute-done((bf16[2304,512]{1,0:T(8,128)(2,1)}, bf16[2304,512]{1,0:T(8,128)(2,1)}, u32[]{:S(2)}, u32[]{:S(2)}) %collective-permute-start.6) | collective-permute-done | bytes 2359328 | tf_op jit(solution)/shard_map/ppermute | solution.py:26
  169.7 43.3 %collective-permute-start.8 = (f32[1,768]{1,0:T(1,128)S(1)}, f32[1,768]{1,0:T(1,128)S(1)}, u32[]{:S(2)}, u32[]{:S(2)}) collective-permute-start(f32[1,768]{1,0:T(1,128)S(1)} %fusion.41), channel_id=1, source_target_pairs={{0,8},{4,12},{8,0},{12,4},{16,24},{20,28},{24,16},{28,20},{1,9},{5... | collective-permute-start | bytes 9224 | tf_op jit(solution)/shard_map/ppermute | solution.py:26
  219.5 20.4 %all-gather.2.cloned.1.call-done = bf16[2048,2176]{1,0:T(8,128)(2,1)} async-done(((bf16[256,2176]{1,0:T(8,128)(2,1)}), bf16[2048,2176]{1,0:T(8,128)(2,1)}) %all-gather.2.cloned.1.call-update) | async-done | bytes 8912912 | tf_op jit(solution)/shard_map/all_gather | solution.py:580
  246.5 9.0 fusion.90.q_in.k_in.v_in
  255.5 12.5 %attention.1 = (bf16[1024,512]{1,0:T(8,128)(2,1)S(1)}, bf16[1024,512]{1,0:T(8,128)(2,1)S(1)}, bf16[1024,512]{1,0:T(8,128)(2,1)S(1)}, bf16[1024,512]{1,0:T(8,128)(2,1)S(1)}, f32[4,1024,1]{2,1,0:T(8,128)}) custom-call(f32[1024,1536]{1,0:T(8,128)} %fusion.90.q_in.k_in.v_in, f32[1024,1536]{1,0:T(8,128)} %fusion.90.q_in.k_in.v_in, ...), custom_call_target="tpu_custom_call" | custom-call | flops 1342177280 | bytes 10485760 | tf_op jit(solution)/shard_map/attention/pallas_call | solution.py:155
  268.1 5.5 convolution_convert_fusion.4
  291.3 29.1 %down.1 = (bf16[3072,2048]{1,0:T(8,128)(2,1)}, bf16[3072,1408]{1,0:T(8,128)(2,1)}) custom-call(s32[3]{0:T(128)S(1)} %pad_add_fusion.where, bf16[768,2048]{1,0:T(8,128)(2,1)} %convolution_convert_fusion.5.mine, bf16[2304,512]{1,0:T(8,128)(2,1)} %pad_maximum_fusion.1.refs_0_, bf16[2304,512]{1,0:T(8,128)(2,1)S(1)} %collective-permute-done.5.refs_1_, ...), custom_call_target="tpu_custom_call" | custom-call | flops 17716740096 | bytes 39583744 | tf_op jit(solution)/shard_map/down/pallas_call | solution.py:296
  336.6 12.6 %collective-permute-done.18.refs_2_ = bf16[768,512]{1,0:T(8,128)(2,1)S(1)} collective-permute-done((bf16[768,512]{1,0:T(8,128)(2,1)S(1)}, bf16[768,512]{1,0:T(8,128)(2,1)S(1)}, u32[]{:S(2)}, u32[]{:S(2)}) %collective-permute-start.18) | collective-permute-done | bytes 786464 | tf_op jit(solution)/shard_map/ppermute | solution.py:26
  356.5 6.8 collective-permute-done.20.refs_8_
  365.2 29.7 %expert.4 = (bf16[3072,2048]{1,0:T(8,128)(2,1)}, bf16[3072,1408]{1,0:T(8,128)(2,1)}, bf16[3072,2816]{1,0:T(8,128)(2,1)}, bf16[768,1024]{1,0:T(8,128)(2,1)}, bf16[768,1024]{1,0:T(8,128)(2,1)}, /*index=5*/f32[1,768]{1,0:T(1,128)}) custom-call(s32[3]{0:T(128)} %copy-done.7, bf16[768,512]{1,0:T(8,128)(2,1)} %copy-done.59, bf16[768,512]{1,0:T(8,128)(2,1)} %copy-done.61, ...), custom_call_target="tpu_custom_call" | custom-call | flops 17716740096 | bytes 32768000 | tf_op jit(solution)/shard_map/expert/pallas_call | solution.py:400
  403.2 29.8 %expert.5 = (bf16[3072,2048]{1,0:T(8,128)(2,1)}, bf16[3072,1408]{1,0:T(8,128)(2,1)}, bf16[3072,2816]{1,0:T(8,128)(2,1)}, bf16[768,1024]{1,0:T(8,128)(2,1)}, bf16[768,1024]{1,0:T(8,128)(2,1)}, /*index=5*/f32[1,768]{1,0:T(1,128)}) custom-call(s32[3]{0:T(128)} %copy-done.7, ...), custom_call_target="tpu_custom_call", output_to_operand_aliasing={{0}: (13, {}), {1}: (14, {}), {2}: (15, {})} | custom-call | flops 17716740096 | bytes 32768000 | tf_op jit(solution)/shard_map/expert/pallas_call | solution.py:400
  438.0 29.8 %expert.6 = (bf16[3072,2048]{1,0:T(8,128)(2,1)}, bf16[3072,1408]{1,0:T(8,128)(2,1)}, bf16[3072,2816]{1,0:T(8,128)(2,1)}, bf16[768,1024]{1,0:T(8,128)(2,1)}, bf16[768,1024]{1,0:T(8,128)(2,1)}, /*index=5*/f32[1,768]{1,0:T(1,128)}) custom-call(s32[3]{0:T(128)} %copy-done.7, ...), custom_call_target="tpu_custom_call", output_to_operand_aliasing={{0}: (13, {}), {1}: (14, {}), {2}: (15, {})} | custom-call | flops 17716740096 | bytes 32768000 | tf_op jit(solution)/shard_map/expert/pallas_call | solution.py:400
  480.6 30.1 %expert.7 = (bf16[3072,2048]{1,0:T(8,128)(2,1)}, bf16[3072,1408]{1,0:T(8,128)(2,1)}, bf16[3072,2816]{1,0:T(8,128)(2,1)}, bf16[768,1024]{1,0:T(8,128)(2,1)}, bf16[768,1024]{1,0:T(8,128)(2,1)}, /*index=5*/f32[1,768]{1,0:T(1,128)}) custom-call(s32[3]{0:T(128)} %copy-done.7, ...), custom_call_target="tpu_custom_call", output_to_operand_aliasing={{0}: (13, {}), {1}: (14, {}), {2}: (15, {})} | custom-call | flops 17716740096 | bytes 32768000 | tf_op jit(solution)/shard_map/expert/pallas_call | solution.py:400
  518.3 26.8 %up.1 = bf16[3072,2048]{1,0:T(8,128)(2,1)} custom-call(s32[3]{0:T(128)S(1)} %copy-done.8, bf16[3072,1408]{1,0:T(8,128)(2,1)} %get-tuple-element.130.act, bf16[1024,1408]{1,0:T(8,128)(2,1)S(1)} %copy-done.1, bf16[1024,1408]{1,0:T(8,128)(2,1)} %collective-permute-done.refs_5_.came), custom_call_target="tpu_custom_call" | custom-call | flops 17716740096 | bytes 27000832 | tf_op jit(solution)/shard_map/up/pallas_call | solution.py:331
  558.0 16.6 %fusion.12 = bf16[1024,1408]{1,0:T(8,128)(2,1)S(1)} fusion(bf16[3072,1408]{1,0:T(8,128)(2,1)} %get-tuple-element.130.act, bf16[3072,2048]{1,0:T(8,128)(2,1)} %get-tuple-element.78, s32[]{:T(128)S(6)} %select_n.221), kind=kOutput, calls=%fused_computation.21 | convolution fusion | flops 8859811840 | bytes 17825796 | tf_op jit(solution)/shard_map/dot_general | solution.py:30
  579.5 14.9 %convolution_convert_fusion.2 = bf16[512,2816]{1,0:T(8,128)(2,1)} fusion(bf16[3072,2816]{1,0:T(8,128)(2,1)} %get-tuple-element.135, bf16[3072,2048]{1,0:T(8,128)(2,1)S(1)} %bitcast.144, s32[]{:T(128)S(6)} %select_n.221), kind=kOutput, calls=%fused_computation.16 | convolution fusion | flops 8859811840 | bytes 23330820 | tf_op jit(solution)/shard_map/dot_general | solution.py:30
  594.4 15.6 %convolution_convert_fusion.1 = bf16[512,2816]{1,0:T(8,128)(2,1)} fusion(bf16[3072,2816]{1,0:T(8,128)(2,1)} %get-tuple-element.135, bf16[3072,2048]{1,0:T(8,128)(2,1)S(1)} %bitcast.144, s32[]{:T(128)S(6)} %select_n.222), kind=kOutput, calls=%fused_computation.15 | convolution fusion | flops 8859811840 | bytes 23330820 | tf_op jit(solution)/shard_map/dot_general | solution.py:30
  613.2 24.8 %collective-permute-done.51.refs_4_ = bf16[1024,1408]{1,0:T(8,128)(2,1)S(1)} collective-permute-done((bf16[1024,1408]{1,0:T(8,128)(2,1)S(1)}, bf16[1024,1408]{1,0:T(8,128)(2,1)S(1)}, u32[]{:S(2)}, u32[]{:S(2)}) %collective-permute-start.51) | collective-permute-done | bytes 2883616 | tf_op jit(solution)/shard_map/ppermute | solution.py:26
  654.1 15.9 %fusion.15.refs_3_ = bf16[1024,1408]{1,0:T(8,128)(2,1)} fusion(bf16[3072,1408]{1,0:T(8,128)(2,1)} %get-tuple-element.130.act, bf16[3072,2048]{1,0:T(8,128)(2,1)} %get-tuple-element.78, s32[]{:T(128)S(6)} %select_n.224), kind=kOutput, calls=%fused_computation.22 | convolution fusion | flops 8859811840 | bytes 17825796 | tf_op jit(solution)/shard_map/dot_general | solution.py:30
  670.0 7.3 collective-permute-done.54
  698.1 15.6 %attention_back.1 = bf16[1024,1536]{1,0:T(8,128)(2,1)} custom-call(bf16[1024,512]{1,0:T(8,128)(2,1)S(1)} %copy-done.10, bf16[1024,512]{1,0:T(8,128)(2,1)S(1)} %copy-done.12, bf16[1024,512]{1,0:T(8,128)(2,1)S(1)} %copy-done.14, f32[4,1024,1]{2,1,0:T(8,128)} %get-tuple-element.129.logs, bf16[1024,512]{1,0:T(8,128)(2,1)S(1)} %copy-done.17, ...), custom_call_target="tpu_custom_call" | custom-call | flops 3355443200 | bytes 8388608 | tf_op jit(solution)/shard_map/attention_back/pallas_call | solution.py:208
  713.8 40.9 %collective-permute-done.56.refs_1_ = bf16[512,2816]{1,0:T(8,128)(2,1)} collective-permute-done((bf16[512,2816]{1,0:T(8,128)(2,1)}, bf16[512,2816]{1,0:T(8,128)(2,1)}, u32[]{:S(2)}, u32[]{:S(2)}) %collective-permute-start.56) | collective-permute-done | bytes 2883616 | tf_op jit(solution)/shard_map/ppermute | solution.py:26
  754.7 10.9 %convolution_convert_fusion = bf16[2048,1536]{1,0:T(8,128)(2,1)} fusion(bf16[1024,1536]{1,0:T(8,128)(2,1)} %attention_back.1, bf16[1024,2048]{1,0:T(8,128)(2,1)S(1)} %copy-done.25, f32[2048]{0:T(1024)S(1)} %copy-done.51, f32[1024]{0:T(1024)S(1)} %copy-done.48), kind=kOutput, calls=%fused_computation.7 | convolution fusion | flops 6453985280 | bytes 13643776 | tf_op jit(solution)/shard_map/dot_general | solution.py:30
  765.7 9.9 convolution_convert_fusion.3
  782.4 24.3 %fusion.9.refs_0_ = bf16[1024,2816]{1,0:T(8,128)(2,1)} fusion(bf16[3072,2816]{1,0:T(8,128)(2,1)} %get-tuple-element.135, bf16[3072,2048]{1,0:T(8,128)(2,1)S(1)} %bitcast.146, s32[]{:T(128)S(6)} %select_n.224), kind=kOutput, calls=%fused_computation.14 | convolution fusion | flops 17719623680 | bytes 29360132 | tf_op jit(solution)/shard_map/dot_general | solution.py:30
  819.4 45.0 %collective-permute-done.61.refs_2_ = bf16[512,2816]{1,0:T(8,128)(2,1)} collective-permute-done((bf16[512,2816]{1,0:T(8,128)(2,1)}, bf16[512,2816]{1,0:T(8,128)(2,1)}, u32[]{:S(2)}, u32[]{:S(2)}) %collective-permute-start.61) | collective-permute-done | bytes 2883616 | tf_op jit(solution)/shard_map/ppermute | solution.py:26
  870.5 15.5 %collective-permute-done.44 = bf16[768,512]{1,0:T(8,128)(2,1)S(1)} collective-permute-done((bf16[768,512]{1,0:T(8,128)(2,1)S(1)}, bf16[768,512]{1,0:T(8,128)(2,1)S(1)}, u32[]{:S(2)}, u32[]{:S(2)}) %collective-permute-start.44) | collective-permute-done | bytes 786464 | tf_op jit(solution)/shard_map/ppermute | solution.py:26
  891.8 19.7 %collective-permute-done.45 = bf16[1024,512]{1,0:T(8,128)(2,1)S(1)} collective-permute-done((bf16[1024,512]{1,0:T(8,128)(2,1)S(1)}, bf16[1024,512]{1,0:T(8,128)(2,1)S(1)}, u32[]{:S(2)}, u32[]{:S(2)}) %collective-permute-start.45) | collective-permute-done | bytes 1048608 | tf_op jit(solution)/shard_map/ppermute | solution.py:26
  926.2 41.9 %collective-permute-start.67 = (f32[6,2048]{1,0:T(8,128)S(1)}, f32[6,2048]{1,0:T(8,128)S(1)}, u32[]{:S(2)}, u32[]{:S(2)}) collective-permute-start(f32[6,2048]{1,0:T(8,128)S(1)} %add.248), channel_id=1, source_target_pairs={{0,8},{4,12},{8,0},{12,4},{16,24},{20,28},{24,16},{28,20},{1,9},{5... | collective-permute-start | bytes 147464 | tf_op jit(solution)/shard_map/ppermute | solution.py:26
  973.6 12.8 %expert_grad_sum.1 = f32[3,1024,1408]{2,1,0:T(8,128)} custom-call(bf16[1024,2816]{1,0:T(8,128)(2,1)} %fusion.9.refs_0_, bf16[512,2816]{1,0:T(8,128)(2,1)} %collective-permute-done.56.refs_1_, bf16[512,2816]{1,0:T(8,128)(2,1)} %collective-permute-done.61.refs_2_, bf16[1024,1408]{1,0:T(8,128)(2,1)S(1)} %copy-done.2, ...), custom_call_target="tpu_custom_call" | custom-call | flops 4325376 | bytes 34603008 | tf_op jit(solution)/shard_map/expert_grad_sum/pallas_call | solution.py:482
  (423 shorter events, 251.5 us)
Async XLA Ops:
  7.2 232.6 %all-gather.2.cloned.1.call-start = ((), (), s32[]{:S(2)}) async-start(), calls=%async_computation.3 | async-start | bytes 10027008 | tf_op jit(solution)/shard_map/all_gather | solution.py:580
  10.3 802.4 %reduce-scatter.4.cloned.1.call-start = ((), (), s32[]{:S(2)}) async-start(), calls=%async_computation.4 | async-start | bytes 15728640 | tf_op jit(solution)/shard_map/reduce_scatter | solution.py:725
  15.8 99.4 %collective-permute-start = (bf16[1024,1408]{1,0:T(8,128)(2,1)S(1)}, bf16[1024,1408]{1,0:T(8,128)(2,1)}, u32[]{:S(2)}, u32[]{:S(2)}) collective-permute-start(bf16[1024,1408]{1,0:T(8,128)(2,1)S(1)} %get-tuple-element.187.refs_4_.own), channel_id=1, source_target_pairs={{0,4},{4,0},{8,12},{12,8},{16,20},{20,16},{24,28},{28,24},{1,5},{5... | collective-permute-start | bytes 8650760 | tf_op jit(solution)/shard_map/ppermute | solution.py:26
  24.2 69.5 %collective-permute-start.2 = (bf16[768,512]{1,0:T(8,128)(2,1)S(1)}, bf16[768,512]{1,0:T(8,128)(2,1)S(1)}, u32[]{:S(2)}, u32[]{:S(2)}) collective-permute-start(bf16[768,512]{1,0:T(8,128)(2,1)S(1)} %fusion.82), channel_id=1, source_target_pairs={{0,8},{4,12},{8,0},{12,4},{16,24},{20,28},{24,16},{28,20},{1,9},{5... | collective-permute-start | bytes 2359304 | tf_op jit(solution)/shard_map/ppermute | solution.py:26
  26.9 69.8 %collective-permute-start.3 = (bf16[768,512]{1,0:T(8,128)(2,1)S(1)}, bf16[768,512]{1,0:T(8,128)(2,1)S(1)}, u32[]{:S(2)}, u32[]{:S(2)}) collective-permute-start(bf16[768,512]{1,0:T(8,128)(2,1)S(1)} %fusion.84), channel_id=1, source_target_pairs={{0,16},{4,20},{8,24},{12,28},{16,0},{20,4},{24,8},{28,12},{1,17},{... | collective-permute-start | bytes 2359304 | tf_op jit(solution)/shard_map/ppermute | solution.py:26
  30.5 83.0 %collective-permute-start.4 = (bf16[768,512]{1,0:T(8,128)(2,1)S(1)}, bf16[768,512]{1,0:T(8,128)(2,1)S(1)}, u32[]{:S(2)}, u32[]{:S(2)}) collective-permute-start(bf16[768,512]{1,0:T(8,128)(2,1)S(1)} %fusion.86), channel_id=1, source_target_pairs={{0,24},{4,28},{8,16},{12,20},{16,8},{20,12},{24,0},{28,4},{1,25},{... | collective-permute-start | bytes 2359304 | tf_op jit(solution)/shard_map/ppermute | solution.py:26
  115.2 53.0 %collective-permute-start.6 = (bf16[2304,512]{1,0:T(8,128)(2,1)}, bf16[2304,512]{1,0:T(8,128)(2,1)}, u32[]{:S(2)}, u32[]{:S(2)}) collective-permute-start(bf16[2304,512]{1,0:T(8,128)(2,1)} %pad_maximum_fusion.1.refs_0_), channel_id=1, source_target_pairs={{0,2},{1,3},{2,0},{3,1},{4,6},{5,7},{6,4},{7,5},{8,10},{9,11},{10,... | collective-permute-start | bytes 7077896 | tf_op jit(solution)/shard_map/ppermute | solution.py:26
  116.6 126.6 %collective-permute-start.1 = (bf16[1024,1408]{1,0:T(8,128)(2,1)}, bf16[1024,1408]{1,0:T(8,128)(2,1)}, u32[]{:S(2)}, u32[]{:S(2)}) collective-permute-start(bf16[1024,1408]{1,0:T(8,128)(2,1)} %get-tuple-element.186.refs_4_), channel_id=1, source_target_pairs={{0,4},{4,0},{8,12},{12,8},{16,20},{20,16},{24,28},{28,24},{1,5},{5... | collective-permute-start | bytes 8650760 | tf_op jit(solution)/shard_map/ppermute | solution.py:26
  118.0 125.3 %collective-permute-start.5 = (bf16[2304,512]{1,0:T(8,128)(2,1)}, bf16[2304,512]{1,0:T(8,128)(2,1)S(1)}, u32[]{:S(2)}, u32[]{:S(2)}) collective-permute-start(bf16[2304,512]{1,0:T(8,128)(2,1)} %pad_maximum_fusion.1.refs_0_), channel_id=1, source_target_pairs={{0,1},{1,0},{2,3},{3,2},{4,5},{5,4},{6,7},{7,6},{8,9},{9,8},{10,11... | collective-permute-start | bytes 7077896 | tf_op jit(solution)/shard_map/ppermute | solution.py:26
  168.2 75.1 %collective-permute-start.7 = (bf16[2304,512]{1,0:T(8,128)(2,1)}, bf16[2304,512]{1,0:T(8,128)(2,1)}, u32[]{:S(2)}, u32[]{:S(2)}) collective-permute-start(bf16[2304,512]{1,0:T(8,128)(2,1)} %collective-permute-done.6.refs_2_), channel_id=1, source_target_pairs={{0,1},{1,0},{2,3},{3,2},{4,5},{5,4},{6,7},{7,6},{8,9},{9,8},{10,11... | collective-permute-start | bytes 7077896 | tf_op jit(solution)/shard_map/ppermute | solution.py:26
  168.8 48.8 %collective-permute-start.10 = (f32[1,768]{1,0:T(1,128)S(1)}, f32[1,768]{1,0:T(1,128)S(1)}, u32[]{:S(2)}, u32[]{:S(2)}) collective-permute-start(f32[1,768]{1,0:T(1,128)S(1)} %fusion.29), channel_id=1, source_target_pairs={{0,24},{4,28},{8,16},{12,20},{16,8},{20,12},{24,0},{28,4},{1,25},{... | collective-permute-start | bytes 9224 | tf_op jit(solution)/shard_map/ppermute | solution.py:26
  169.7 73.5 %collective-permute-start.8 = (f32[1,768]{1,0:T(1,128)S(1)}, f32[1,768]{1,0:T(1,128)S(1)}, u32[]{:S(2)}, u32[]{:S(2)}) collective-permute-start(f32[1,768]{1,0:T(1,128)S(1)} %fusion.41), channel_id=1, source_target_pairs={{0,8},{4,12},{8,0},{12,4},{16,24},{20,28},{24,16},{28,20},{1,9},{5... | collective-permute-start | bytes 9224 | tf_op jit(solution)/shard_map/ppermute | solution.py:26
  351.1 45.3 %collective-permute-start.16 = (bf16[768,512]{1,0:T(8,128)(2,1)}, bf16[768,512]{1,0:T(8,128)(2,1)}, u32[]{:S(2)}, u32[]{:S(2)}) collective-permute-start(bf16[768,512]{1,0:T(8,128)(2,1)} %fusion.85), channel_id=1, source_target_pairs={{0,16},{4,20},{8,24},{12,28},{16,0},{20,4},{24,8},{28,12},{1,17},{... | collective-permute-start | bytes 2359304 | tf_op jit(solution)/shard_map/ppermute | solution.py:26
  356.1 38.8 %collective-permute-start.24 = (bf16[768,512]{1,0:T(8,128)(2,1)}, bf16[768,512]{1,0:T(8,128)(2,1)}, u32[]{:S(2)}, u32[]{:S(2)}) collective-permute-start(bf16[768,512]{1,0:T(8,128)(2,1)} %collective-permute-done.22.refs_0_), channel_id=1, source_target_pairs={{0,2},{1,3},{2,0},{3,1},{4,6},{5,7},{6,4},{7,5},{8,10},{9,11},{10,... | collective-permute-start | bytes 2359304 | tf_op jit(solution)/shard_map/ppermute | solution.py:26
  398.2 38.2 %collective-permute-start.28 = (bf16[768,512]{1,0:T(8,128)(2,1)}, bf16[768,512]{1,0:T(8,128)(2,1)}, u32[]{:S(2)}, u32[]{:S(2)}) collective-permute-start(bf16[768,512]{1,0:T(8,128)(2,1)} %collective-permute-done.16.refs_0_), channel_id=1, source_target_pairs={{0,1},{1,0},{2,3},{3,2},{4,5},{5,4},{6,7},{7,6},{8,9},{9,8},{10,11... | collective-permute-start | bytes 2359304 | tf_op jit(solution)/shard_map/ppermute | solution.py:26
  433.6 47.1 %collective-permute-start.26 = (bf16[768,512]{1,0:T(8,128)(2,1)}, bf16[768,512]{1,0:T(8,128)(2,1)}, u32[]{:S(2)}, u32[]{:S(2)}) collective-permute-start(bf16[768,512]{1,0:T(8,128)(2,1)} %collective-permute-done.21.refs_0_), channel_id=1, source_target_pairs={{0,1},{1,0},{2,3},{3,2},{4,5},{5,4},{6,7},{7,6},{8,9},{9,8},{10,11... | collective-permute-start | bytes 2359304 | tf_op jit(solution)/shard_map/ppermute | solution.py:26
  433.7 41.5 %collective-permute-start.33 = (bf16[768,1024]{1,0:T(8,128)(2,1)}, bf16[768,1024]{1,0:T(8,128)(2,1)}, u32[]{:S(2)}, u32[]{:S(2)}) collective-permute-start(bf16[768,1024]{1,0:T(8,128)(2,1)} %get-tuple-element.101), channel_id=1, source_target_pairs={{0,1},{1,0},{2,3},{3,2},{4,5},{5,4},{6,7},{7,6},{8,9},{9,8},{10,11... | collective-permute-start | bytes 4718600 | tf_op jit(solution)/shard_map/ppermute | solution.py:26
  472.5 38.8 %collective-permute-start.36 = (bf16[768,1024]{1,0:T(8,128)(2,1)}, bf16[768,1024]{1,0:T(8,128)(2,1)}, u32[]{:S(2)}, u32[]{:S(2)}) collective-permute-start(bf16[768,1024]{1,0:T(8,128)(2,1)} %get-tuple-element.108), channel_id=1, source_target_pairs={{0,1},{1,0},{2,3},{3,2},{4,5},{5,4},{6,7},{7,6},{8,9},{9,8},{10,11... | collective-permute-start | bytes 4718600 | tf_op jit(solution)/shard_map/ppermute | solution.py:26
  475.2 43.1 %collective-permute-start.38 = (f32[1,768]{1,0:T(1,128)S(1)}, f32[1,768]{1,0:T(1,128)S(1)}, u32[]{:S(2)}, u32[]{:S(2)}) collective-permute-start(f32[1,768]{1,0:T(1,128)S(1)} %copy-done.67), channel_id=1, source_target_pairs={{0,16},{4,20},{8,24},{12,28},{16,0},{20,4},{24,8},{28,12},{1,17},{... | collective-permute-start | bytes 9224 | tf_op jit(solution)/shard_map/ppermute | solution.py:26
  510.9 39.5 %collective-permute-start.41 = (f32[1,768]{1,0:T(1,128)}, f32[1,768]{1,0:T(1,128)S(1)}, u32[]{:S(2)}, u32[]{:S(2)}) collective-permute-start(f32[1,768]{1,0:T(1,128)} %get-tuple-element.114), channel_id=1, source_target_pairs={{0,24},{4,28},{8,16},{12,20},{16,8},{20,12},{24,0},{28,4},{1,25},{... | collective-permute-start | bytes 9224 | tf_op jit(solution)/shard_map/ppermute | solution.py:26
  550.3 437.3 %reduce-scatter.8.cloned.1.call-start = ((), (), s32[]{:S(2)}) async-start(), calls=%async_computation.6 | async-start | bytes 2359296 | tf_op jit(solution)/shard_map/reduce_scatter | solution.py:781
  553.7 56.3 %collective-permute-start.48 = (bf16[768,512]{1,0:T(8,128)(2,1)}, bf16[768,512]{1,0:T(8,128)(2,1)S(1)}, u32[]{:S(2)}, u32[]{:S(2)}) collective-permute-start(bf16[768,512]{1,0:T(8,128)(2,1)} %add_convert_fusion.4), channel_id=1, source_target_pairs={{0,8},{4,12},{8,0},{12,4},{16,24},{20,28},{24,16},{28,20},{1,9},{5... | collective-permute-start | bytes 2359304 | tf_op jit(solution)/shard_map/ppermute | solution.py:26
  554.5 55.5 %collective-permute-start.49 = (bf16[768,512]{1,0:T(8,128)(2,1)}, bf16[768,512]{1,0:T(8,128)(2,1)S(1)}, u32[]{:S(2)}, u32[]{:S(2)}) collective-permute-start(bf16[768,512]{1,0:T(8,128)(2,1)} %add_convert_fusion.2), channel_id=1, source_target_pairs={{0,16},{4,20},{8,24},{12,28},{16,0},{20,4},{24,8},{28,12},{1,17},{... | collective-permute-start | bytes 2359304 | tf_op jit(solution)/shard_map/ppermute | solution.py:26
  574.5 63.4 %collective-permute-start.51 = (bf16[1024,1408]{1,0:T(8,128)(2,1)S(1)}, bf16[1024,1408]{1,0:T(8,128)(2,1)S(1)}, u32[]{:S(2)}, u32[]{:S(2)}) collective-permute-start(bf16[1024,1408]{1,0:T(8,128)(2,1)S(1)} %fusion.12), channel_id=1, source_target_pairs={{0,4},{4,0},{8,12},{12,8},{16,20},{20,16},{24,28},{28,24},{1,5},{5... | collective-permute-start | bytes 8650760 | tf_op jit(solution)/shard_map/ppermute | solution.py:26
  677.8 76.9 %collective-permute-start.56 = (bf16[512,2816]{1,0:T(8,128)(2,1)}, bf16[512,2816]{1,0:T(8,128)(2,1)}, u32[]{:S(2)}, u32[]{:S(2)}) collective-permute-start(bf16[512,2816]{1,0:T(8,128)(2,1)} %convolution_convert_fusion.2), channel_id=1, source_target_pairs={{0,4},{4,0},{8,12},{12,8},{16,20},{20,16},{24,28},{28,24},{1,5},{5... | collective-permute-start | bytes 8650760 | tf_op jit(solution)/shard_map/ppermute | solution.py:26
  692.0 303.8 %reduce-scatter.6.cloned.1.call-start = ((), (), s32[]{:S(2)}) async-start(), calls=%async_computation.5 | async-start | bytes 7077888 | tf_op jit(solution)/shard_map/reduce_scatter | solution.py:787
  777.8 86.6 %collective-permute-start.61 = (bf16[512,2816]{1,0:T(8,128)(2,1)}, bf16[512,2816]{1,0:T(8,128)(2,1)}, u32[]{:S(2)}, u32[]{:S(2)}) collective-permute-start(bf16[512,2816]{1,0:T(8,128)(2,1)} %convolution_convert_fusion.1), channel_id=1, source_target_pairs={{0,4},{4,0},{8,12},{12,8},{16,20},{20,16},{24,28},{28,24},{1,5},{5... | collective-permute-start | bytes 8650760 | tf_op jit(solution)/shard_map/ppermute | solution.py:26
  814.7 53.7 %collective-permute-start.42 = (bf16[768,512]{1,0:T(8,128)(2,1)S(1)}, bf16[768,512]{1,0:T(8,128)(2,1)S(1)}, u32[]{:S(2)}, u32[]{:S(2)}) collective-permute-start(bf16[768,512]{1,0:T(8,128)(2,1)S(1)} %get-tuple-element.208), channel_id=1, source_target_pairs={{0,8},{4,12},{8,0},{12,4},{16,24},{20,28},{24,16},{28,20},{1,9},{5... | collective-permute-start | bytes 2359304 | tf_op jit(solution)/shard_map/ppermute | solution.py:26
  815.4 54.0 %collective-permute-start.43 = (bf16[768,512]{1,0:T(8,128)(2,1)S(1)}, bf16[768,512]{1,0:T(8,128)(2,1)S(1)}, u32[]{:S(2)}, u32[]{:S(2)}) collective-permute-start(bf16[768,512]{1,0:T(8,128)(2,1)S(1)} %get-tuple-element.207), channel_id=1, source_target_pairs={{0,16},{4,20},{8,24},{12,28},{16,0},{20,4},{24,8},{28,12},{1,17},{... | collective-permute-start | bytes 2359304 | tf_op jit(solution)/shard_map/ppermute | solution.py:26
  891.7 97.7 %collective-permute-start.63 = (bf16[1024,1024]{1,0:T(8,128)(2,1)}, bf16[1024,1024]{1,0:T(8,128)(2,1)}, u32[]{:S(2)}, u32[]{:S(2)}) collective-permute-start(bf16[1024,1024]{1,0:T(8,128)(2,1)} %pad_maximum_fusion.6), channel_id=1, source_target_pairs={{0,1},{1,0},{2,3},{3,2},{4,5},{5,4},{6,7},{7,6},{8,9},{9,8},{10,11... | collective-permute-start | bytes 6291464 | tf_op jit(solution)/shard_map/ppermute | solution.py:26
  913.3 88.3 %collective-permute-start.46 = (bf16[1024,1024]{1,0:T(8,128)(2,1)}, bf16[1024,1024]{1,0:T(8,128)(2,1)}, u32[]{:S(2)}, u32[]{:S(2)}) collective-permute-start(bf16[1024,1024]{1,0:T(8,128)(2,1)} %pad_maximum_fusion.3), channel_id=1, source_target_pairs={{0,1},{1,0},{2,3},{3,2},{4,5},{5,4},{6,7},{7,6},{8,9},{9,8},{10,11... | collective-permute-start | bytes 6291464 | tf_op jit(solution)/shard_map/ppermute | solution.py:26
  926.2 44.2 %collective-permute-start.67 = (f32[6,2048]{1,0:T(8,128)S(1)}, f32[6,2048]{1,0:T(8,128)S(1)}, u32[]{:S(2)}, u32[]{:S(2)}) collective-permute-start(f32[6,2048]{1,0:T(8,128)S(1)} %add.248), channel_id=1, source_target_pairs={{0,8},{4,12},{8,0},{12,4},{16,24},{20,28},{24,16},{28,20},{1,9},{5... | collective-permute-start | bytes 147464 | tf_op jit(solution)/shard_map/ppermute | solution.py:26
  (118 other events, 1809.5 us)
Sparse Core Ops, SparseCore 0:
  10.8 228.9 all-gather.1
  550.5 99.6 reduce-scatter.3
  692.2 74.0 reduce-scatter.7
  769.7 159.4 reduce-scatter.5

commit v5 on v4

--- a/solution.py
+++ b/solution.py
@@ -53,7 +53,7 @@
     return value
 
 
-def tensor_reduce(part, filler=None):
+def tensor_reduce(part, filler=None, others=()):
     count = lax.axis_size("tensor")
     place = lax.axis_index("tensor")
     size = part.shape[1] // count
@@ -63,6 +63,8 @@
         kept = [jnp.where(upper, b, a) for a, b in zip(blocks[::2], blocks[1::2])]
         given = [jnp.where(upper, a, b) for a, b in zip(blocks[::2], blocks[1::2])]
         sent = jnp.concatenate([v.astype(low) for v in given], 1)
+        if others and bit == levels_of(count) - 1:
+            sent = after(sent, *others)
         came = swap(sent, "tensor", 1 << bit)
         if filler is not None and bit == levels_of(count) - 1:
             came = after(came, *filler(sent))
@@ -249,15 +251,26 @@
     return [(own, 0, half, True, 0, 0), (came, 0, half, False, 0, 0)]
 
 
-def pair_pieces(own_gate, own_up, came, near, far):
-    half, more = own_gate.shape[0], near.shape[0]
-    return [
-        (own_gate, 0, half, True, 0, 0),
-        (own_up, 0, half, True, 0, 1),
-        (came, 0, half, False, 0, 0),
-        (near, 0, more, False, 0, 1),
-        (far, 0, half - more, False, more, 1),
-    ]
+cuts = (
+    ((0, 0, 48),),
+    ((0, 48, 64),),
+    ((0, 64, 88),),
+    ((0, 88, 100),),
+    ((0, 100, 128), (1, 0, 28)),
+    ((1, 28, 128),),
+)
+
+
+def pair_pieces(own_gate, own_up, *came):
+    half = own_gate.shape[0]
+    pieces = [(own_gate, 0, half, True, 0, 0), (own_up, 0, half, True, 0, 1)]
+    for cut, ref in zip(cuts, came):
+        at = 0
+        for which, start, stop in cut:
+            number = (stop - start) * half // 128
+            pieces.append((ref, at, number, False, start * half // 128, which))
+            at += number
+    return pieces
 
 
 def column_block(where, i, size):
@@ -348,8 +361,11 @@
 
 def expert_kernel(count, carried, where, *refs):
     blocks, refs = refs[:count], refs[count:]
-    weights, raw, routed, router = refs[:5], refs[5], refs[6], refs[7]
-    rows_out, act_out, grad_out, even, odd, gate_grad, pair, part, sems = refs[8 + carried :]
+    number = 2 + len(cuts)
+    weights, (raw, routed, router) = refs[:number], refs[number : number + 3]
+    rows_out, act_out, grad_out, even, odd, gate_grad, pair, part, sems = refs[
+        number + 3 + carried :
+    ]
     size = blocks[0].shape[1]
     hidden = raw.shape[1]
     place_rows(pair_pieces(*weights), pair, sems, where[1], pl.program_id(0) == 0)
@@ -403,7 +419,7 @@
             num_scalar_prefetch=1,
             grid=(steps,),
             in_specs=[near_spec(size)] * count
-            + [anywhere] * 5
+            + [anywhere] * len(weights)
             + [
                 here_spec(hidden),
                 row_spec,
@@ -421,7 +437,7 @@
             scratch_shapes=[
                 pltpu.VMEM((width, both), low),
                 pltpu.VMEM((tile, width), low),
-                pltpu.SemaphoreType.DMA((5,)),
+                pltpu.SemaphoreType.DMA((2 + sum(len(cut) for cut in cuts),)),
             ],
         ),
         out_shape=[
@@ -432,7 +448,9 @@
             shape(MOST, width // 2),
             shape(1, MOST, full),
         ],
-        input_output_aliases={count + 9 + i: i for i in range(len(carried))},
+        input_output_aliases={
+            count + len(weights) + 4 + i: i for i in range(len(carried))
+        },
         compiler_params=limits(60),
         cost_estimate=cost(
             4 * MOST * width * both, width * both * 2 + MOST * (width * 8 + hidden * 8), MOST * hidden
@@ -626,11 +644,18 @@
     def group_send(given, *others):
         return swap(after(given, *others), "dp", reach)
 
-    cut = half // 2
     down = (down_mine, group_send(down_mine))
-    gate_came = group_send(gate_mine)
-    up_near = group_send(up_mine[:cut], first)
-    pair = (gate_mine, up_mine, gate_came, up_near, group_send(up_mine[cut:], up_near))
+    crossing = []
+
+    def cross(*others):
+        pieces = [
+            (gate_mine, up_mine)[which][start * half // 128 : stop * half // 128]
+            for which, start, stop in cuts[len(crossing)]
+        ]
+        crossing.append(group_send(jnp.concatenate(pieces, 0), *crossing[-1:], *others))
+
+    cross(down[1])
+    cross(first)
 
     grad_own = own_columns(cotangent)
     grad_mine = jnp.dot(chosen[0], cotangent, preferred_element_type=full).astype(low)
@@ -643,18 +668,23 @@
     scale_one = lax.rsqrt(jnp.mean(inputs * inputs, axis=1, keepdims=True) + epsilon)
     normed_in = (inputs * scale_one * gain_first).astype(low)
     inputs_own = own_columns(tokens).astype(full)
-    qkv_flat = after(qkv_flat, down[1], gate_came, *grad_blocks, *routed)
+    normed_in = after(normed_in, crossing[0], grad_mine, *grad_blocks, *routed)
     qkv = jnp.dot(normed_in, qkv_flat, preferred_element_type=full)
+    cross(qkv)
     cosine, sine = rotary_tables()
     context, query, keys, values, logs = attention(qkv, cosine, sine, scale)
+    context = after(context, crossing[2])
+    cross(context)
     attn_part = contract(context, out_full, 1, 1).astype(low)
     rows_raw = []
 
     def down_filler(sent):
+        cross(sent)
         rows_raw.extend(down_pass(where, after(grad_mine, sent), grad_blocks, *down))
-        return rows_raw
-
-    hidden = after(inputs_own + tensor_reduce(attn_part, down_filler), up_near)
+        return (*rows_raw, crossing[4])
+
+    hidden = inputs_own + tensor_reduce(attn_part, down_filler, (crossing[3],))
+    cross(rows_raw[1])
 
     scaled_hidden = (hidden * gain_second_own).astype(low)
     sums = tensor_sum(
@@ -678,6 +708,7 @@
         return jnp.stack([a, b, (value - a.astype(full) - b.astype(full)).astype(low)])
 
     moe_packed = packed(moe_in)
+    pair = (gate_mine, up_mine, *crossing)
     crossed = [moe_packed[0]] + [
         swap(moe_packed[s], "dp", s * group_count) for s in range(1, EXPERTS - 1)
     ]
@@ -693,7 +724,7 @@
         if step == 2:
             named_sum = after(named_sum, sums_sent[0])
         if step == 3:
-            named_sum = after(named_sum, sums_sent[1], returned[0], gate_grads[1])
+            named_sum = after(named_sum, sums_sent[1], returned[0])
         moe_rows, activation, pre_grad, even, odd, gate_grad = expert_pass(
             step, where, arrived[step], pair, rows_raw[1], named_sum, router_block, carried
         )
@@ -708,10 +739,10 @@
         if step == 2:
             arrived.append(near_blocks(crossed[3], even))
         returned.append(near_reduce(even, odd, sums_sent, *returned[2:]))
-        gate_grads.append(swap(gate_grad, "dp", step * group_count) if step else gate_grad)
+        gate_grads.append(gate_grad)
     own_returned = returned
     returned = exchange(returned)
-    gate_grad_near = gate_grads
+    gate_grad_near = exchange([gate_grads[0]] + [after(v, even) for v in gate_grads[1:]])
     grad_rows = rows_raw[0]
 
     def term(left, right):
@@ -721,22 +752,17 @@
 
         return part
 
-    expert_part = up_pass(where, after(activation, sums_sent[2], own_returned[1], gate_grads[2]), *down)
-    expert_own = lax.psum_scatter(
-        after(expert_part, sums_sent[3], gate_grads[3]), "tensor", scatter_dimension=1, tiled=True
-    )
-    down_given = term(grad_rows, after(activation, expert_part, sums_sent[3], own_returned[2]))(
-        given_at, half
-    )
+    down_given = term(grad_rows, after(activation, sums_sent[2], own_returned[1]))(given_at, half)
     down_sum = group_send(down_given)
-    pair_term = term(moe_rows, after(pre_grad, down_given, own_returned[3]))
+    expert_part = up_pass(
+        where, after(activation, down_given, sums_sent[3], own_returned[2], *gate_grad_near), *down
+    )
+    expert_own = lax.psum_scatter(expert_part, "tensor", scatter_dimension=1, tiled=True)
+    pair_term = term(moe_rows, after(pre_grad, expert_part, own_returned[3]))
     quarter = half // 2
     pair_given = [pair_term(given_at + k * quarter, quarter) for k in range(2)]
     pair_sum = [group_send(pair_given[0], down_sum)]
     pair_sum.append(group_send(pair_given[1], pair_sum[0]))
-    mixed = unpacked(exchange([expert_own[s * MOST : (s + 1) * MOST] for s in range(EXPERTS)]))
-    layer_own = hidden + mixed
-    layer_out = tensor_gather(layer_own.astype(low)).astype(full)
     returned = [after(v, *pair_given) for v in returned]
     returned[3] = after(returned[3], down_sum)
     back = unpacked(returned)
@@ -766,27 +792,35 @@
     )
     router_grad = jnp.dot(logit_grad, moe_in, preferred_element_type=full)
     moe_gain_grad = jnp.sum(moe_grad * normed_two, axis=0)
-    kept = []
-
-    def keep(sent):
-        kept.append(term(grad_rows, after(activation, sent))(mine_at, half))
-        return kept[:1]
+    kept = {}
+    outputs = {0: expert_own[:MOST]}
 
     def keep_pair(sent):
-        kept.append(term(moe_rows, after(pre_grad, sent))(mine_at, half))
-        return kept[1:]
-
-    attn_grad = tensor_gather(hidden_grad.astype(low), keep)
+        kept["pair"] = term(moe_rows, after(pre_grad, sent, expert_own))(mine_at, half)
+        outputs[2] = swap(expert_own[2 * MOST : 3 * MOST], "dp", 2 * group_count)
+        return (kept["pair"],)
+
+    def keep_down(sent):
+        kept["down"] = term(grad_rows, after(activation, sent))(mine_at, half)
+        return (kept["down"],)
+
+    attn_grad = tensor_gather(hidden_grad.astype(low), keep_pair)
+    attn_grad = after(attn_grad, outputs[2])
+    for s in (3, 1):
+        part = after(expert_own[s * MOST : (s + 1) * MOST], outputs[2])
+        outputs[s] = swap(part, "dp", s * group_count)
     context_grad = jnp.dot(attn_grad, out_full, preferred_element_type=full).astype(low)
     out_shard = lax.psum_scatter(
         contract(after(attn_grad, context_grad), context, 0, 0).astype(low), "dp", scatter_dimension=0, tiled=True
     ).astype(full)
     qkv_grad_rows = attention_back(query, keys, values, logs, context_grad, cosine, sine, scale)
-    qkv_grad_rows = after(qkv_grad_rows, pair_sum[0])
     qkv_grad = contract(normed_in, qkv_grad_rows, 0, 0).astype(low)
     qkv_shard = lax.psum_scatter(qkv_grad, "dp", scatter_dimension=0, tiled=True).astype(full)
     normed_grad = tensor_reduce(
-        contract(after(qkv_grad_rows, qkv_grad), qkv_flat, 1, 1).astype(low), keep_pair
+        contract(
+            after(qkv_grad_rows, qkv_grad, pair_sum[0], outputs[1], outputs[3]), qkv_flat, 1, 1
+        ).astype(low),
+        keep_down,
     )
     normed_one = inputs_own * scale_one
     scaled_in = normed_grad * gain_first_own
@@ -795,9 +829,11 @@
     input_own = hidden_grad + scale_one * (scaled_in - normed_one * mean_one.reshape(rows, 1))
     input_own = after(input_own, pair_sum[1])
     input_grad = tensor_gather(input_own.astype(low)).astype(full)
+    layer_own = hidden + unpacked([outputs[s] for s in range(EXPERTS)])
+    layer_out = tensor_gather(layer_own.astype(low)).astype(full)
     expert_grad = expert_grad_sum(
-        group_finish(kept[1], pair_sum, member, group_count),
-        group_finish(kept[0], [down_sum], member, group_count),
+        group_finish(kept["pair"], pair_sum, member, group_count),
+        group_finish(kept["down"], [down_sum], member, group_count),
         hidden_size,
     )
 

time: 1020 us -> 1060 us (1.039)
  starting transfers between devices: 152 us -> 196 us
  waiting for transfers between devices: 355 us -> 329 us
    ppermute x69 -> x72, starting transfers between devices: 152 us -> 196 us  [swap(): lax.ppermute(value, axis, [(i, i ^ distance) for i in range(lax.axis_size...]
    ppermute x69 -> x72, waiting for transfers between devices: 335 us -> 299 us  [swap(): lax.ppermute(value, axis, [(i, i ^ distance) for i in range(lax.axis_size...]
    reduce_scatter x1, waiting for transfers between devices: 0.01 us -> 24.8 us  [body(): lax.psum_scatter(expert_part, 'tensor', scatter_dimension=1, tiled=True)]
    all_gather x1, waiting for transfers between devices: 20.4 us -> 4.57 us  [body(): lax.all_gather(jnp.concatenate([qkv_weight.reshape(-1, 3 * size), out_wei...]
    unnamed x157 -> x179, local copies, waits for them, and re-layouts: 19.7 us -> 21.3 us
  transfers between devices with their start and end apart: 73 -> 76, of which waited for: 26 -> 29; matrix products, arithmetic and copies ran while one was open for 23% -> 23% of each run, Pallas kernels for 20% -> 19%
where the time goes in v5:
time: 1060 us; the launch traced here: 1050 us
  waiting for transfers between devices  329 us (31%)
  Pallas kernels  226 us (21%)
  starting transfers between devices  196 us (18%)
  matrix products  174 us (16%)
  other arithmetic  66.6 us (6%)
  local copies, waits for them, and re-layouts  45.7 us (4%)
  between operations  15.7 us (1%)
    ppermute x72, waiting for transfers between devices, swap(): lax.ppermute(value, axis, [(i, i ^ distance) for i in range(lax.axis_size...  299 us
    ppermute x72, starting transfers between devices, swap(): lax.ppermute(value, axis, [(i, i ^ distance) for i in range(lax.axis_size...  196 us
    dot_general x27, matrix products, contract(): lax.dot_general(left, right, (((left_dim,), (right_dim,)), ((), ())), pre...  143 us
    pallas_call x4, Pallas kernels, expert_pass(): pl.pallas_call(functools.partial(expert_kernel, count, len(carried)), gri...  120 us
    pallas_call x1, Pallas kernels, down_pass(): pl.pallas_call(functools.partial(down_kernel, count, split), grid_spec=pl...  38.7 us
    pallas_call x1, Pallas kernels, up_pass(): pl.pallas_call(up_kernel, grid_spec=pltpu.PrefetchScalarGridSpec(num_scal...  26.8 us
    reduce_scatter x1, waiting for transfers between devices, body(): lax.psum_scatter(expert_part, 'tensor', scatter_dimension=1, tiled=True)  24.8 us
    unnamed x179, local copies, waits for them, and re-layouts  21.3 us
  transfers between devices with their start and end apart: 76, of which 29 were waited for; matrix products, arithmetic and copies ran while one was open for 23% of the time, Pallas kernels for 19%

profile of v5, /device:TPU:0, one launch (start us, length us, event | category | flops | bytes accessed | tf_op | source)
XLA Modules:
  0.0 1053.5 jit_solution(12572777225758325551)
XLA Ops:
  33.3 61.4 %collective-permute-done.2 = bf16[768,512]{1,0:T(8,128)(2,1)} collective-permute-done((bf16[768,512]{1,0:T(8,128)(2,1)}, bf16[768,512]{1,0:T(8,128)(2,1)}, u32[]{:S(2)}, u32[]{:S(2)}) %collective-permute-start.2) | collective-permute-done | bytes 786464 | tf_op jit(solution)/shard_map/ppermute | solution.py:26
  95.4 27.2 %collective-permute-done.4 = bf16[768,512]{1,0:T(8,128)(2,1)} collective-permute-done((bf16[768,512]{1,0:T(8,128)(2,1)}, bf16[768,512]{1,0:T(8,128)(2,1)}, u32[]{:S(2)}, u32[]{:S(2)}) %collective-permute-start.4) | collective-permute-done | bytes 786464 | tf_op jit(solution)/shard_map/ppermute | solution.py:26
  128.9 53.7 %collective-permute-start.8 = (f32[1,768]{1,0:T(1,128)S(1)}, f32[1,768]{1,0:T(1,128)S(1)}, u32[]{:S(2)}, u32[]{:S(2)}) collective-permute-start(f32[1,768]{1,0:T(1,128)S(1)} %fusion.43), channel_id=1, source_target_pairs={{0,8},{4,12},{8,0},{12,4},{16,24},{20,28},{24,16},{28,20},{1,9},{5... | collective-permute-start | bytes 9224 | tf_op jit(solution)/shard_map/ppermute | solution.py:26
  204.5 35.1 %collective-permute-start.9 = (f32[1,768]{1,0:T(1,128)S(1)}, f32[1,768]{1,0:T(1,128)S(1)}, u32[]{:S(2)}, u32[]{:S(2)}) collective-permute-start(f32[1,768]{1,0:T(1,128)S(1)} %fusion.37), channel_id=1, source_target_pairs={{0,16},{4,20},{8,24},{12,28},{16,0},{20,4},{24,8},{28,12},{1,17},{... | collective-permute-start | bytes 9224 | tf_op jit(solution)/shard_map/ppermute | solution.py:26
  243.5 8.8 fusion.14.q_in.k_in.v_in
  256.4 12.9 %attention.1 = (bf16[1024,512]{1,0:T(8,128)(2,1)S(1)}, bf16[1024,512]{1,0:T(8,128)(2,1)S(1)}, bf16[1024,512]{1,0:T(8,128)(2,1)S(1)}, bf16[1024,512]{1,0:T(8,128)(2,1)S(1)}, f32[4,1024,1]{2,1,0:T(8,128)}) custom-call(f32[1024,1536]{1,0:T(8,128)} %fusion.14.q_in.k_in.v_in, f32[1024,1536]{1,0:T(8,128)} %fusion.14.q_in.k_in.v_in, ...), custom_call_target="tpu_custom_call" | custom-call | flops 1342177280 | bytes 10485760 | tf_op jit(solution)/shard_map/attention/pallas_call | solution.py:157
  294.3 38.7 %down.1 = (bf16[3072,2048]{1,0:T(8,128)(2,1)}, bf16[3072,1408]{1,0:T(8,128)(2,1)}) custom-call(s32[3]{0:T(128)S(1)} %pad_add_fusion.where, bf16[768,2048]{1,0:T(8,128)(2,1)} %convolution_convert_fusion.4.mine, bf16[2304,512]{1,0:T(8,128)(2,1)} %pad_maximum_fusion.1.refs_0_, bf16[2304,512]{1,0:T(8,128)(2,1)S(1)} %collective-permute-done.5.refs_1_, ...), custom_call_target="tpu_custom_call" | custom-call | flops 17716740096 | bytes 39583744 | tf_op jit(solution)/shard_map/down/pallas_call | solution.py:309
  345.4 21.9 %collective-permute-start.25 = (bf16[768,512]{1,0:T(8,128)(2,1)S(1)}, bf16[768,512]{1,0:T(8,128)(2,1)}, u32[]{:S(2)}, u32[]{:S(2)}) collective-permute-start(bf16[768,512]{1,0:T(8,128)(2,1)S(1)} %fusion.91), channel_id=1, source_target_pairs={{0,8},{4,12},{8,0},{12,4},{16,24},{20,28},{24,16},{28,20},{1,9},{5... | collective-permute-start | bytes 2359304 | tf_op jit(solution)/shard_map/ppermute | solution.py:26
  369.8 13.9 %collective-permute-start.19 = (bf16[768,512]{1,0:T(8,128)(2,1)}, bf16[768,512]{1,0:T(8,128)(2,1)S(1)}, u32[]{:S(2)}, u32[]{:S(2)}) collective-permute-start(bf16[768,512]{1,0:T(8,128)(2,1)} %fusion.93), channel_id=1, source_target_pairs={{0,16},{4,20},{8,24},{12,28},{16,0},{20,4},{24,8},{28,12},{1,17},{... | collective-permute-start | bytes 2359304 | tf_op jit(solution)/shard_map/ppermute | solution.py:26
  393.0 29.7 %expert.4 = (bf16[3072,2048]{1,0:T(8,128)(2,1)}, bf16[3072,1408]{1,0:T(8,128)(2,1)}, bf16[3072,2816]{1,0:T(8,128)(2,1)}, bf16[768,1024]{1,0:T(8,128)(2,1)}, bf16[768,1024]{1,0:T(8,128)(2,1)}, /*index=5*/f32[1,768]{1,0:T(1,128)}) custom-call(s32[3]{0:T(128)} %copy-done.9, bf16[768,512]{1,0:T(8,128)(2,1)} %copy-done.68, bf16[768,512]{1,0:T(8,128)(2,1)} %copy-done.70, ...), custom_call_target="tpu_custom_call" | custom-call | flops 17716740096 | bytes 32768000 | tf_op jit(solution)/shard_map/expert/pallas_call | solution.py:416
  431.1 30.1 %expert.5 = (bf16[3072,2048]{1,0:T(8,128)(2,1)}, bf16[3072,1408]{1,0:T(8,128)(2,1)}, bf16[3072,2816]{1,0:T(8,128)(2,1)}, bf16[768,1024]{1,0:T(8,128)(2,1)}, bf16[768,1024]{1,0:T(8,128)(2,1)}, /*index=5*/f32[1,768]{1,0:T(1,128)}) custom-call(s32[3]{0:T(128)} %copy-done.9, ...), custom_call_target="tpu_custom_call", output_to_operand_aliasing={{0}: (16, {}), {1}: (17, {}), {2}: (18, {})} | custom-call | flops 17716740096 | bytes 32768000 | tf_op jit(solution)/shard_map/expert/pallas_call | solution.py:416
  467.2 30.3 %expert.6 = (bf16[3072,2048]{1,0:T(8,128)(2,1)}, bf16[3072,1408]{1,0:T(8,128)(2,1)}, bf16[3072,2816]{1,0:T(8,128)(2,1)}, bf16[768,1024]{1,0:T(8,128)(2,1)}, bf16[768,1024]{1,0:T(8,128)(2,1)}, /*index=5*/f32[1,768]{1,0:T(1,128)}) custom-call(s32[3]{0:T(128)} %copy-done.9, ...), custom_call_target="tpu_custom_call", output_to_operand_aliasing={{0}: (16, {}), {1}: (17, {}), {2}: (18, {})} | custom-call | flops 17716740096 | bytes 32768000 | tf_op jit(solution)/shard_map/expert/pallas_call | solution.py:416
  504.7 29.8 %expert.7 = (bf16[3072,2048]{1,0:T(8,128)(2,1)}, bf16[3072,1408]{1,0:T(8,128)(2,1)}, bf16[3072,2816]{1,0:T(8,128)(2,1)}, bf16[768,1024]{1,0:T(8,128)(2,1)}, bf16[768,1024]{1,0:T(8,128)(2,1)}, /*index=5*/f32[1,768]{1,0:T(1,128)}) custom-call(s32[3]{0:T(128)} %copy-done.9, ...), custom_call_target="tpu_custom_call", output_to_operand_aliasing={{0}: (16, {}), {1}: (17, {}), {2}: (18, {})} | custom-call | flops 17716740096 | bytes 32768000 | tf_op jit(solution)/shard_map/expert/pallas_call | solution.py:416
  534.8 18.8 %collective-permute-start.43 = (f32[1,768]{1,0:T(1,128)S(1)}, f32[1,768]{1,0:T(1,128)S(1)}, u32[]{:S(2)}, u32[]{:S(2)}) collective-permute-start(f32[1,768]{1,0:T(1,128)S(1)} %copy-done.80), channel_id=1, source_target_pairs={{0,16},{4,20},{8,24},{12,28},{16,0},{20,4},{24,8},{28,12},{1,17},{... | collective-permute-start | bytes 9224 | tf_op jit(solution)/shard_map/ppermute | solution.py:26
  558.6 15.9 %fusion.19 = bf16[1024,1408]{1,0:T(8,128)(2,1)} fusion(bf16[3072,1408]{1,0:T(8,128)(2,1)} %get-tuple-element.153.act, bf16[3072,2048]{1,0:T(8,128)(2,1)} %get-tuple-element.93, s32[]{:T(128)S(6)} %select_n.213), kind=kOutput, calls=%fused_computation.25 | convolution fusion | flops 8859811840 | bytes 17825796 | tf_op jit(solution)/shard_map/dot_general | solution.py:30
  579.3 26.8 %up.1 = bf16[3072,2048]{1,0:T(8,128)(2,1)} custom-call(s32[3]{0:T(128)S(1)} %copy-done.10, bf16[3072,1408]{1,0:T(8,128)(2,1)} %get-tuple-element.153.act, bf16[1024,1408]{1,0:T(8,128)(2,1)S(1)} %copy-done.1, bf16[1024,1408]{1,0:T(8,128)(2,1)} %collective-permute-done.refs_5_.came), custom_call_target="tpu_custom_call" | custom-call | flops 17716740096 | bytes 27000832 | tf_op jit(solution)/shard_map/up/pallas_call | solution.py:344
  614.4 11.7 %collective-permute-done.50 = bf16[768,512]{1,0:T(8,128)(2,1)S(1)} collective-permute-done((bf16[768,512]{1,0:T(8,128)(2,1)}, bf16[768,512]{1,0:T(8,128)(2,1)S(1)}, u32[]{:S(2)}, u32[]{:S(2)}) %collective-permute-start.50) | collective-permute-done | bytes 786464 | tf_op jit(solution)/shard_map/ppermute | solution.py:26
  630.4 17.1 %convolution_convert_fusion.2 = bf16[512,2816]{1,0:T(8,128)(2,1)} fusion(bf16[3072,2816]{1,0:T(8,128)(2,1)} %get-tuple-element.148, bf16[3072,2048]{1,0:T(8,128)(2,1)} %get-tuple-element.136, s32[]{:T(128)S(6)} %select_n.213), kind=kOutput, calls=%fused_computation.20 | convolution fusion | flops 8859811840 | bytes 23330820 | tf_op jit(solution)/shard_map/dot_general | solution.py:30
  647.6 12.4 %convolution_convert_fusion.1 = bf16[512,2816]{1,0:T(8,128)(2,1)} fusion(bf16[3072,2816]{1,0:T(8,128)(2,1)S(1)} %bitcast.155, bf16[3072,2048]{1,0:T(8,128)(2,1)} %get-tuple-element.136, s32[]{:T(128)S(6)} %select_n.222), kind=kOutput, calls=%fused_computation.19 | convolution fusion | flops 8859811840 | bytes 23330820 | tf_op jit(solution)/shard_map/dot_general | solution.py:30
  659.9 8.3 collective-permute-done.52
  691.1 24.8 %reduce-scatter.4.cloned.1.call-done = bf16[3072,512]{1,0:T(8,128)(2,1)} async-done(((bf16[3072,2048]{1,0:T(8,128)(2,1)}), bf16[3072,512]{1,0:T(8,128)(2,1)}) %reduce-scatter.4.cloned.1.call-update) | async-done | bytes 3145744 | tf_op jit(solution)/shard_map/reduce_scatter | solution.py:760
  716.0 26.1 %fusion.9.refs_0_ = bf16[1024,2816]{1,0:T(8,128)(2,1)} fusion(bf16[3072,2816]{1,0:T(8,128)(2,1)} %get-tuple-element.148, bf16[3072,2048]{1,0:T(8,128)(2,1)} %get-tuple-element.136, s32[]{:T(128)S(6)} %select_n.224), kind=kOutput, calls=%fused_computation.14 | convolution fusion | flops 17719623680 | bytes 29360132 | tf_op jit(solution)/shard_map/dot_general | solution.py:30
  749.2 34.4 %collective-permute-done.45 = bf16[768,512]{1,0:T(8,128)(2,1)S(1)} collective-permute-done((bf16[768,512]{1,0:T(8,128)(2,1)S(1)}, bf16[768,512]{1,0:T(8,128)(2,1)S(1)}, u32[]{:S(2)}, u32[]{:S(2)}) %collective-permute-start.45) | collective-permute-done | bytes 786464 | tf_op jit(solution)/shard_map/ppermute | solution.py:26
  801.9 15.6 %attention_back.1 = bf16[1024,1536]{1,0:T(8,128)(2,1)} custom-call(bf16[1024,512]{1,0:T(8,128)(2,1)S(1)} %copy-done.12, bf16[1024,512]{1,0:T(8,128)(2,1)S(1)} %copy-done.14, bf16[1024,512]{1,0:T(8,128)(2,1)S(1)} %copy-done.16, f32[4,1024,1]{2,1,0:T(8,128)} %get-tuple-element.147.logs, bf16[1024,512]{1,0:T(8,128)(2,1)S(1)} %copy-done.19, ...), custom_call_target="tpu_custom_call" | custom-call | flops 3355443200 | bytes 8388608 | tf_op jit(solution)/shard_map/attention_back/pallas_call | solution.py:210
  817.5 10.5 convolution_convert_fusion
  828.0 39.5 %collective-permute-done.59.refs_1_ = bf16[512,2816]{1,0:T(8,128)(2,1)} collective-permute-done((bf16[512,2816]{1,0:T(8,128)(2,1)}, bf16[512,2816]{1,0:T(8,128)(2,1)}, u32[]{:S(2)}, u32[]{:S(2)}) %collective-permute-start.59) | collective-permute-done | bytes 2883616 | tf_op jit(solution)/shard_map/ppermute | solution.py:26
  867.5 10.2 fusion.16
  892.5 16.1 %fusion.22.refs_3_ = bf16[1024,1408]{1,0:T(8,128)(2,1)} fusion(bf16[3072,1408]{1,0:T(8,128)(2,1)} %get-tuple-element.153.act, bf16[3072,2048]{1,0:T(8,128)(2,1)} %get-tuple-element.93, s32[]{:T(128)S(6)} %select_n.224), kind=kOutput, calls=%fused_computation.26 | convolution fusion | flops 8859811840 | bytes 17825796 | tf_op jit(solution)/shard_map/dot_general | solution.py:30
  908.6 28.3 %collective-permute-done.61 = bf16[1024,512]{1,0:T(8,128)(2,1)S(1)} collective-permute-done((bf16[1024,512]{1,0:T(8,128)(2,1)S(1)}, bf16[1024,512]{1,0:T(8,128)(2,1)S(1)}, u32[]{:S(2)}, u32[]{:S(2)}) %collective-permute-start.61) | collective-permute-done | bytes 1048608 | tf_op jit(solution)/shard_map/ppermute | solution.py:26
  946.4 25.5 %collective-permute-done.64.refs_2_ = bf16[512,2816]{1,0:T(8,128)(2,1)S(1)} collective-permute-done((bf16[512,2816]{1,0:T(8,128)(2,1)S(1)}, bf16[512,2816]{1,0:T(8,128)(2,1)S(1)}, u32[]{:S(2)}, u32[]{:S(2)}) %collective-permute-start.64) | collective-permute-done | bytes 2883616 | tf_op jit(solution)/shard_map/ppermute | solution.py:26
  974.0 21.4 %collective-permute-done.65 = bf16[1024,512]{1,0:T(8,128)(2,1)S(1)} collective-permute-done((bf16[1024,512]{1,0:T(8,128)(2,1)S(1)}, bf16[1024,512]{1,0:T(8,128)(2,1)S(1)}, u32[]{:S(2)}, u32[]{:S(2)}) %collective-permute-start.65) | collective-permute-done | bytes 1048608 | tf_op jit(solution)/shard_map/ppermute | solution.py:26
  1012.7 12.3 %expert_grad_sum.1 = f32[3,1024,1408]{2,1,0:T(8,128)} custom-call(bf16[1024,2816]{1,0:T(8,128)(2,1)} %fusion.9.refs_0_, bf16[512,2816]{1,0:T(8,128)(2,1)} %collective-permute-done.59.refs_1_, bf16[512,2816]{1,0:T(8,128)(2,1)S(1)} %copy-done.3, bf16[1024,1408]{1,0:T(8,128)(2,1)S(1)} %copy-done.4, bf16[1024,1408]{1,0:T(8,128)(2,1)S(1)} %collective-permute-done.54.refs_4_), custom_call_target="tpu_custom_call" | custom-call | flops 4325376 | bytes 34603008 | tf_op jit(solution)/shard_map/expert_grad_sum/pallas_call | solution.py:500
  (455 shorter events, 268.4 us)
Async XLA Ops:
  7.2 194.8 %all-gather.2.cloned.1.call-start = ((), (), s32[]{:S(2)}) async-start(), calls=%async_computation.3 | async-start | bytes 10027008 | tf_op jit(solution)/shard_map/all_gather | solution.py:598
  10.3 705.6 %reduce-scatter.4.cloned.1.call-start = ((), (), s32[]{:S(2)}) async-start(), calls=%async_computation.4 | async-start | bytes 15728640 | tf_op jit(solution)/shard_map/reduce_scatter | solution.py:760
  15.8 110.0 %collective-permute-start = (bf16[1024,1408]{1,0:T(8,128)(2,1)S(1)}, bf16[1024,1408]{1,0:T(8,128)(2,1)}, u32[]{:S(2)}, u32[]{:S(2)}) collective-permute-start(bf16[1024,1408]{1,0:T(8,128)(2,1)S(1)} %get-tuple-element.205.refs_4_.own), channel_id=1, source_target_pairs={{0,4},{4,0},{8,12},{12,8},{16,20},{20,16},{24,28},{28,24},{1,5},{5... | collective-permute-start | bytes 8650760 | tf_op jit(solution)/shard_map/ppermute | solution.py:26
  25.1 69.6 %collective-permute-start.2 = (bf16[768,512]{1,0:T(8,128)(2,1)}, bf16[768,512]{1,0:T(8,128)(2,1)}, u32[]{:S(2)}, u32[]{:S(2)}) collective-permute-start(bf16[768,512]{1,0:T(8,128)(2,1)} %fusion.90), channel_id=1, source_target_pairs={{0,8},{4,12},{8,0},{12,4},{16,24},{20,28},{24,16},{28,20},{1,9},{5... | collective-permute-start | bytes 2359304 | tf_op jit(solution)/shard_map/ppermute | solution.py:26
  28.6 66.7 %collective-permute-start.3 = (bf16[768,512]{1,0:T(8,128)(2,1)}, bf16[768,512]{1,0:T(8,128)(2,1)}, u32[]{:S(2)}, u32[]{:S(2)}) collective-permute-start(bf16[768,512]{1,0:T(8,128)(2,1)} %fusion.92), channel_id=1, source_target_pairs={{0,16},{4,20},{8,24},{12,28},{16,0},{20,4},{24,8},{28,12},{1,17},{... | collective-permute-start | bytes 2359304 | tf_op jit(solution)/shard_map/ppermute | solution.py:26
  33.1 89.6 %collective-permute-start.4 = (bf16[768,512]{1,0:T(8,128)(2,1)}, bf16[768,512]{1,0:T(8,128)(2,1)}, u32[]{:S(2)}, u32[]{:S(2)}) collective-permute-start(bf16[768,512]{1,0:T(8,128)(2,1)} %fusion.94), channel_id=1, source_target_pairs={{0,24},{4,28},{8,16},{12,20},{16,8},{20,12},{24,0},{28,4},{1,25},{... | collective-permute-start | bytes 2359304 | tf_op jit(solution)/shard_map/ppermute | solution.py:26
  125.8 63.6 %collective-permute-start.6 = (bf16[2304,512]{1,0:T(8,128)(2,1)}, bf16[2304,512]{1,0:T(8,128)(2,1)}, u32[]{:S(2)}, u32[]{:S(2)}) collective-permute-start(bf16[2304,512]{1,0:T(8,128)(2,1)} %pad_maximum_fusion.1.refs_0_), channel_id=1, source_target_pairs={{0,2},{1,3},{2,0},{3,1},{4,6},{5,7},{6,4},{7,5},{8,10},{9,11},{10,... | collective-permute-start | bytes 7077896 | tf_op jit(solution)/shard_map/ppermute | solution.py:26
  127.9 76.6 %collective-permute-start.10 = (f32[1,768]{1,0:T(1,128)S(1)}, f32[1,768]{1,0:T(1,128)S(1)}, u32[]{:S(2)}, u32[]{:S(2)}) collective-permute-start(f32[1,768]{1,0:T(1,128)S(1)} %fusion.31), channel_id=1, source_target_pairs={{0,24},{4,28},{8,16},{12,20},{16,8},{20,12},{24,0},{28,4},{1,25},{... | collective-permute-start | bytes 9224 | tf_op jit(solution)/shard_map/ppermute | solution.py:26
  128.9 114.0 %collective-permute-start.8 = (f32[1,768]{1,0:T(1,128)S(1)}, f32[1,768]{1,0:T(1,128)S(1)}, u32[]{:S(2)}, u32[]{:S(2)}) collective-permute-start(f32[1,768]{1,0:T(1,128)S(1)} %fusion.43), channel_id=1, source_target_pairs={{0,8},{4,12},{8,0},{12,4},{16,24},{20,28},{24,16},{28,20},{1,9},{5... | collective-permute-start | bytes 9224 | tf_op jit(solution)/shard_map/ppermute | solution.py:26
  189.4 53.5 %collective-permute-start.5 = (bf16[2304,512]{1,0:T(8,128)(2,1)}, bf16[2304,512]{1,0:T(8,128)(2,1)S(1)}, u32[]{:S(2)}, u32[]{:S(2)}) collective-permute-start(bf16[2304,512]{1,0:T(8,128)(2,1)} %pad_maximum_fusion.1.refs_0_), channel_id=1, source_target_pairs={{0,1},{1,0},{2,3},{3,2},{4,5},{5,4},{6,7},{7,6},{8,9},{9,8},{10,11... | collective-permute-start | bytes 7077896 | tf_op jit(solution)/shard_map/ppermute | solution.py:26
  189.5 53.5 %collective-permute-start.7 = (bf16[2304,512]{1,0:T(8,128)(2,1)}, bf16[2304,512]{1,0:T(8,128)(2,1)}, u32[]{:S(2)}, u32[]{:S(2)}) collective-permute-start(bf16[2304,512]{1,0:T(8,128)(2,1)} %collective-permute-done.6.refs_2_), channel_id=1, source_target_pairs={{0,1},{1,0},{2,3},{3,2},{4,5},{5,4},{6,7},{7,6},{8,9},{9,8},{10,11... | collective-permute-start | bytes 7077896 | tf_op jit(solution)/shard_map/ppermute | solution.py:26
  196.0 47.0 %collective-permute-start.1 = (bf16[384,1408]{1,0:T(8,128)(2,1)}, bf16[384,1408]{1,0:T(8,128)(2,1)}, u32[]{:S(2)}, u32[]{:S(2)}) collective-permute-start(bf16[384,1408]{1,0:T(8,128)(2,1)} %slice_bitcast_fusion.4), channel_id=1, source_target_pairs={{0,4},{4,0},{8,12},{12,8},{16,20},{20,16},{24,28},{28,24},{1,5},{5... | collective-permute-start | bytes 3244040 | tf_op jit(solution)/shard_map/ppermute | solution.py:26
  340.8 50.8 %collective-permute-start.23 = (bf16[800,1408]{1,0:T(8,128)(2,1)S(1)}, bf16[800,1408]{1,0:T(8,128)(2,1)S(1)}, u32[]{:S(2)}, u32[]{:S(2)}) collective-permute-start(bf16[800,1408]{1,0:T(8,128)(2,1)S(1)} %slice_bitcast_fusion.3), channel_id=1, source_target_pairs={{0,4},{4,0},{8,12},{12,8},{16,20},{20,16},{24,28},{28,24},{1,5},{5... | collective-permute-start | bytes 6758408 | tf_op jit(solution)/shard_map/ppermute | solution.py:26
  369.8 55.0 %collective-permute-start.19 = (bf16[768,512]{1,0:T(8,128)(2,1)}, bf16[768,512]{1,0:T(8,128)(2,1)S(1)}, u32[]{:S(2)}, u32[]{:S(2)}) collective-permute-start(bf16[768,512]{1,0:T(8,128)(2,1)} %fusion.93), channel_id=1, source_target_pairs={{0,16},{4,20},{8,24},{12,28},{16,0},{20,4},{24,8},{28,12},{1,17},{... | collective-permute-start | bytes 2359304 | tf_op jit(solution)/shard_map/ppermute | solution.py:26
  497.6 56.1 %collective-permute-start.38 = (bf16[768,1024]{1,0:T(8,128)(2,1)}, bf16[768,1024]{1,0:T(8,128)(2,1)}, u32[]{:S(2)}, u32[]{:S(2)}) collective-permute-start(bf16[768,1024]{1,0:T(8,128)(2,1)} %get-tuple-element.121), channel_id=1, source_target_pairs={{0,1},{1,0},{2,3},{3,2},{4,5},{5,4},{6,7},{7,6},{8,9},{9,8},{10,11... | collective-permute-start | bytes 4718600 | tf_op jit(solution)/shard_map/ppermute | solution.py:26
  500.4 55.4 %collective-permute-start.39 = (bf16[768,512]{1,0:T(8,128)(2,1)}, bf16[768,512]{1,0:T(8,128)(2,1)S(1)}, u32[]{:S(2)}, u32[]{:S(2)}) collective-permute-start(bf16[768,512]{1,0:T(8,128)(2,1)} %add_convert_fusion.7), channel_id=1, source_target_pairs={{0,2},{1,3},{2,0},{3,1},{4,6},{5,7},{6,4},{7,5},{8,10},{9,11},{10,... | collective-permute-start | bytes 2359304 | tf_op jit(solution)/shard_map/ppermute | solution.py:26
  534.6 44.7 %collective-permute-start.44 = (f32[1,768]{1,0:T(1,128)}, f32[1,768]{1,0:T(1,128)S(1)}, u32[]{:S(2)}, u32[]{:S(2)}) collective-permute-start(f32[1,768]{1,0:T(1,128)} %get-tuple-element.132), channel_id=1, source_target_pairs={{0,24},{4,28},{8,16},{12,20},{16,8},{20,12},{24,0},{28,4},{1,25},{... | collective-permute-start | bytes 9224 | tf_op jit(solution)/shard_map/ppermute | solution.py:26
  534.8 44.5 %collective-permute-start.43 = (f32[1,768]{1,0:T(1,128)S(1)}, f32[1,768]{1,0:T(1,128)S(1)}, u32[]{:S(2)}, u32[]{:S(2)}) collective-permute-start(f32[1,768]{1,0:T(1,128)S(1)} %copy-done.80), channel_id=1, source_target_pairs={{0,16},{4,20},{8,24},{12,28},{16,0},{20,4},{24,8},{28,12},{1,17},{... | collective-permute-start | bytes 9224 | tf_op jit(solution)/shard_map/ppermute | solution.py:26
  606.2 429.8 %reduce-scatter.8.cloned.1.call-start = ((), (), s32[]{:S(2)}) async-start(), calls=%async_computation.6 | async-start | bytes 2359296 | tf_op jit(solution)/shard_map/reduce_scatter | solution.py:813
  610.5 49.4 %collective-permute-start.51 = (bf16[768,512]{1,0:T(8,128)(2,1)}, bf16[768,512]{1,0:T(8,128)(2,1)S(1)}, u32[]{:S(2)}, u32[]{:S(2)}) collective-permute-start(bf16[768,512]{1,0:T(8,128)(2,1)} %add_convert_fusion.4), channel_id=1, source_target_pairs={{0,8},{4,12},{8,0},{12,4},{16,24},{20,28},{24,16},{28,20},{1,9},{5... | collective-permute-start | bytes 2359304 | tf_op jit(solution)/shard_map/ppermute | solution.py:26
  612.1 63.5 %collective-permute-start.54 = (bf16[1024,1408]{1,0:T(8,128)(2,1)}, bf16[1024,1408]{1,0:T(8,128)(2,1)S(1)}, u32[]{:S(2)}, u32[]{:S(2)}) collective-permute-start(bf16[1024,1408]{1,0:T(8,128)(2,1)} %fusion.19), channel_id=1, source_target_pairs={{0,4},{4,0},{8,12},{12,8},{16,20},{20,16},{24,28},{28,24},{1,5},{5... | collective-permute-start | bytes 8650760 | tf_op jit(solution)/shard_map/ppermute | solution.py:26
  613.0 55.3 %collective-permute-start.52 = (bf16[768,512]{1,0:T(8,128)(2,1)}, bf16[768,512]{1,0:T(8,128)(2,1)S(1)}, u32[]{:S(2)}, u32[]{:S(2)}) collective-permute-start(bf16[768,512]{1,0:T(8,128)(2,1)} %add_convert_fusion.2), channel_id=1, source_target_pairs={{0,16},{4,20},{8,24},{12,28},{16,0},{20,4},{24,8},{28,12},{1,17},{... | collective-permute-start | bytes 2359304 | tf_op jit(solution)/shard_map/ppermute | solution.py:26
  628.0 43.4 %collective-permute-start.53 = (bf16[768,512]{1,0:T(8,128)(2,1)S(1)}, bf16[768,512]{1,0:T(8,128)(2,1)S(1)}, u32[]{:S(2)}, u32[]{:S(2)}) collective-permute-start(bf16[768,512]{1,0:T(8,128)(2,1)S(1)} %add_convert_fusion.1), channel_id=1, source_target_pairs={{0,24},{4,28},{8,16},{12,20},{16,8},{20,12},{24,0},{28,4},{1,25},{... | collective-permute-start | bytes 2359304 | tf_op jit(solution)/shard_map/ppermute | solution.py:26
  690.8 51.3 %collective-permute-start.57 = (bf16[1024,512]{1,0:T(8,128)(2,1)}, bf16[1024,512]{1,0:T(8,128)(2,1)}, u32[]{:S(2)}, u32[]{:S(2)}) collective-permute-start(bf16[1024,512]{1,0:T(8,128)(2,1)} %get-tuple-element.209), channel_id=1, source_target_pairs={{0,2},{1,3},{2,0},{3,1},{4,6},{5,7},{6,4},{7,5},{8,10},{9,11},{10,... | collective-permute-start | bytes 3145736 | tf_op jit(solution)/shard_map/ppermute | solution.py:26
  792.5 251.0 %reduce-scatter.6.cloned.1.call-start = ((), (), s32[]{:S(2)}) async-start(), calls=%async_computation.5 | async-start | bytes 7077888 | tf_op jit(solution)/shard_map/reduce_scatter | solution.py:818
  792.6 74.9 %collective-permute-start.59 = (bf16[512,2816]{1,0:T(8,128)(2,1)}, bf16[512,2816]{1,0:T(8,128)(2,1)}, u32[]{:S(2)}, u32[]{:S(2)}) collective-permute-start(bf16[512,2816]{1,0:T(8,128)(2,1)} %convolution_convert_fusion.2), channel_id=1, source_target_pairs={{0,4},{4,0},{8,12},{12,8},{16,20},{20,16},{24,28},{28,24},{1,5},{5... | collective-permute-start | bytes 8650760 | tf_op jit(solution)/shard_map/ppermute | solution.py:26
  794.7 72.8 %collective-permute-start.47 = (bf16[768,512]{1,0:T(8,128)(2,1)}, bf16[768,512]{1,0:T(8,128)(2,1)}, u32[]{:S(2)}, u32[]{:S(2)}) collective-permute-start(bf16[768,512]{1,0:T(8,128)(2,1)} %get-tuple-element.135), channel_id=1, source_target_pairs={{0,24},{4,28},{8,16},{12,20},{16,8},{20,12},{24,0},{28,4},{1,25},{... | collective-permute-start | bytes 2359304 | tf_op jit(solution)/shard_map/ppermute | solution.py:26
  795.9 71.6 %collective-permute-start.46 = (bf16[768,512]{1,0:T(8,128)(2,1)}, bf16[768,512]{1,0:T(8,128)(2,1)}, u32[]{:S(2)}, u32[]{:S(2)}) collective-permute-start(bf16[768,512]{1,0:T(8,128)(2,1)} %get-tuple-element.134), channel_id=1, source_target_pairs={{0,8},{4,12},{8,0},{12,4},{16,24},{20,28},{24,16},{28,20},{1,9},{5... | collective-permute-start | bytes 2359304 | tf_op jit(solution)/shard_map/ppermute | solution.py:26
  879.9 92.0 %collective-permute-start.64 = (bf16[512,2816]{1,0:T(8,128)(2,1)S(1)}, bf16[512,2816]{1,0:T(8,128)(2,1)S(1)}, u32[]{:S(2)}, u32[]{:S(2)}) collective-permute-start(bf16[512,2816]{1,0:T(8,128)(2,1)S(1)} %copy-done.62), channel_id=1, source_target_pairs={{0,4},{4,0},{8,12},{12,8},{16,20},{20,16},{24,28},{28,24},{1,5},{5... | collective-permute-start | bytes 8650760 | tf_op jit(solution)/shard_map/ppermute | solution.py:26
  889.4 51.8 %collective-permute-start.48 = (bf16[1024,512]{1,0:T(8,128)(2,1)S(1)}, bf16[1024,512]{1,0:T(8,128)(2,1)S(1)}, u32[]{:S(2)}, u32[]{:S(2)}) collective-permute-start(bf16[1024,512]{1,0:T(8,128)(2,1)S(1)} %add_convert_fusion), channel_id=1, source_target_pairs={{0,2},{1,3},{2,0},{3,1},{4,6},{5,7},{6,4},{7,5},{8,10},{9,11},{10,... | collective-permute-start | bytes 3145736 | tf_op jit(solution)/shard_map/ppermute | solution.py:26
  891.2 45.7 %collective-permute-start.61 = (bf16[1024,512]{1,0:T(8,128)(2,1)S(1)}, bf16[1024,512]{1,0:T(8,128)(2,1)S(1)}, u32[]{:S(2)}, u32[]{:S(2)}) collective-permute-start(bf16[1024,512]{1,0:T(8,128)(2,1)S(1)} %select_convert_fusion), channel_id=1, source_target_pairs={{0,2},{1,3},{2,0},{3,1},{4,6},{5,7},{6,4},{7,5},{8,10},{9,11},{10,... | collective-permute-start | bytes 3145736 | tf_op jit(solution)/shard_map/ppermute | solution.py:26
  974.0 51.2 %collective-permute-start.49 = (bf16[1024,1024]{1,0:T(8,128)(2,1)}, bf16[1024,1024]{1,0:T(8,128)(2,1)}, u32[]{:S(2)}, u32[]{:S(2)}) collective-permute-start(bf16[1024,1024]{1,0:T(8,128)(2,1)} %pad_maximum_fusion.3), channel_id=1, source_target_pairs={{0,1},{1,0},{2,3},{3,2},{4,5},{5,4},{6,7},{7,6},{8,9},{9,8},{10,11... | collective-permute-start | bytes 6291464 | tf_op jit(solution)/shard_map/ppermute | solution.py:26
  (132 other events, 2265.7 us)
Sparse Core Ops, SparseCore 0:
  10.8 191.1 all-gather.1
  606.3 109.6 reduce-scatter.3
  792.6 91.0 reduce-scatter.7
  887.2 130.2 reduce-scatter.5

commit v6 on v5

--- a/solution.py
+++ b/solution.py
@@ -252,12 +252,11 @@
 
 
 cuts = (
-    ((0, 0, 48),),
-    ((0, 48, 64),),
-    ((0, 64, 88),),
-    ((0, 88, 100),),
-    ((0, 100, 128), (1, 0, 28)),
-    ((1, 28, 128),),
+    ((0, 0, 16),),
+    ((0, 16, 40),),
+    ((0, 40, 56),),
+    ((0, 56, 108),),
+    ((0, 108, 128), (1, 0, 128)),
 )
 
 
@@ -277,58 +276,41 @@
     return pl.ds(pl.multiple_of((i ^ where[0]) * size, size), size)
 
 
-def down_kernel(count, split, where, mine, *refs):
-    blocks = refs[:count]
-    own, came, rows_out, raw, held, sems = refs[count:]
-    step = pl.program_id(0)
-    size = blocks[0].shape[1]
-    place_rows(down_pieces(own, came), held, sems, where[1], step == 0)
-
-    @pl.when(step < split)
-    def _():
-        rows_out[...] = mine[...]
-
-    @pl.when(step >= split)
-    def _():
-        for i, ref in enumerate(blocks):
-            rows_out[:, column_block(where, i, size)] = ref[...]
-
-    raw[...] = jnp.dot(rows_out[...], held[...], preferred_element_type=full).astype(low)
-
-
-def down_pass(where, mine, blocks, own, came):
-    count = len(blocks)
-    size = blocks[0].shape[1]
-    width, hidden = 2 * own.shape[0], own.shape[1]
-    total = mine.shape[0] + blocks[0].shape[0]
+def down_kernel(carried, where, rows, own, came, *refs):
+    rows_out, raw, held, sems = refs[carried:]
+    place_rows(down_pieces(own, came), held, sems, where[1], pl.program_id(0) == 0)
+    rows_out[...] = rows[...]
+    raw[...] = jnp.dot(rows[...], held[...], preferred_element_type=full).astype(low)
+
+
+def down_pass(where, rows, own, came, start, total, carried):
+    number, width = rows.shape
+    hidden = own.shape[1]
     tile = 256
-    split = mine.shape[0] // tile
+    first = start // tile
     anywhere = pl.BlockSpec(memory_space=pl.ANY)
-    spec = lambda columns: pl.BlockSpec((tile, columns), lambda i, where: (i, 0))
-    late = pl.BlockSpec((tile, size), lambda i, where: (jnp.maximum(i - split, 0), 0))
+    here = lambda columns: pl.BlockSpec((tile, columns), lambda i, where: (first + i, 0))
     return pl.pallas_call(
-        functools.partial(down_kernel, count, split),
+        functools.partial(down_kernel, len(carried)),
         grid_spec=pltpu.PrefetchScalarGridSpec(
             num_scalar_prefetch=1,
-            grid=(total // tile,),
-            in_specs=[
-                pl.BlockSpec((tile, width), lambda i, where: (jnp.minimum(i, split - 1), 0))
-            ]
-            + [late] * count
-            + [anywhere] * 2,
-            out_specs=[spec(width), spec(hidden)],
+            grid=(number // tile,),
+            in_specs=[pl.BlockSpec((tile, width), lambda i, where: (i, 0))]
+            + [anywhere] * (2 + len(carried)),
+            out_specs=[here(width), here(hidden)],
             scratch_shapes=[pltpu.VMEM((width, hidden), low), pltpu.SemaphoreType.DMA((2,))],
         ),
         out_shape=[
             jax.ShapeDtypeStruct((total, width), low),
             jax.ShapeDtypeStruct((total, hidden), low),
         ],
+        input_output_aliases={4 + i: i for i in range(len(carried))},
         compiler_params=limits(48),
         cost_estimate=cost(
-            2 * total * width * hidden, (total * (2 * width + hidden) + width * hidden) * 2
+            2 * number * width * hidden, (number * (2 * width + hidden) + width * hidden) * 2
         ),
         name="down",
-    )(where, mine, *blocks, own, came)
+    )(where, rows, own, came, *carried)
 
 
 def up_kernel(where, act, own, came, out, held, sems):
@@ -654,13 +636,17 @@
         ]
         crossing.append(group_send(jnp.concatenate(pieces, 0), *crossing[-1:], *others))
 
-    cross(down[1])
     cross(first)
 
     grad_own = own_columns(cotangent)
     grad_mine = jnp.dot(chosen[0], cotangent, preferred_element_type=full).astype(low)
-    grad_came = exchange(packed(grad_own))[1:]
-    grad_blocks = near_blocks(after(jnp.concatenate(grad_came, 0), down[1]))
+    planes = [
+        [m + g * group_count for g in range(EXPERTS)] for m in range(group_count)
+    ]
+    grad_planes = lax.all_gather(
+        after(grad_own, first), "dp", axis=0, tiled=True, axis_index_groups=planes
+    )
+    slots_came = exchange([slot_near[s][None].astype(full) for s in range(EXPERTS)])
     route_sums = jnp.sum(routes, axis=1)[None].astype(low)
     routed = exchange([contract(route_sums, c, 1, 1) for c in chosen])
 
@@ -668,23 +654,32 @@
     scale_one = lax.rsqrt(jnp.mean(inputs * inputs, axis=1, keepdims=True) + epsilon)
     normed_in = (inputs * scale_one * gain_first).astype(low)
     inputs_own = own_columns(tokens).astype(full)
-    normed_in = after(normed_in, crossing[0], grad_mine, *grad_blocks, *routed)
+    normed_in = after(normed_in, down[1], grad_mine, *slots_came, *routed)
     qkv = jnp.dot(normed_in, qkv_flat, preferred_element_type=full)
     cross(qkv)
     cosine, sine = rotary_tables()
     context, query, keys, values, logs = attention(qkv, cosine, sine, scale)
-    context = after(context, crossing[2])
+    context = after(context, crossing[1])
     cross(context)
     attn_part = contract(context, out_full, 1, 1).astype(low)
     rows_raw = []
 
+    total = EXPERTS * MOST
+
     def down_filler(sent):
         cross(sent)
-        rows_raw.extend(down_pass(where, after(grad_mine, sent), grad_blocks, *down))
-        return (*rows_raw, crossing[4])
-
-    hidden = inputs_own + tensor_reduce(attn_part, down_filler, (crossing[3],))
+        rows_raw.extend(down_pass(where, after(grad_mine, sent), *down, 0, total, ()))
+        return (rows_raw[1], crossing[3])
+
+    hidden = inputs_own + tensor_reduce(attn_part, down_filler, (crossing[2],))
     cross(rows_raw[1])
+    grad_planes = after(grad_planes, hidden)
+    grad_packed = []
+    for s in range(1, EXPERTS):
+        source = lax.dynamic_slice_in_dim(grad_planes, (expert ^ s) * rows, rows, 0)
+        taken = (places.astype(full) == slots_came[s]).astype(low)
+        grad_packed.append(jnp.dot(taken, source, preferred_element_type=full).astype(low))
+    grad_rest = lax.all_gather(jnp.concatenate(grad_packed, 0), "tensor", axis=1, tiled=True)
 
     scaled_hidden = (hidden * gain_second_own).astype(low)
     sums = tensor_sum(
@@ -721,6 +716,8 @@
     router_block = first[:, 4 * size :]
     for step in range(EXPERTS):
         named_sum = routed[step]
+        if step == 1:
+            rows_raw = down_pass(where, after(grad_rest, even), *down, MOST, total, rows_raw)
         if step == 2:
             named_sum = after(named_sum, sums_sent[0])
         if step == 3:
@@ -752,19 +749,22 @@
 
         return part
 
+    unit = half // 128
     down_given = term(grad_rows, after(activation, sums_sent[2], own_returned[1]))(given_at, half)
-    down_sum = group_send(down_given)
+    down_sums = [group_send(down_given[: 52 * unit])]
     expert_part = up_pass(
         where, after(activation, down_given, sums_sent[3], own_returned[2], *gate_grad_near), *down
     )
+    expert_part = after(expert_part, down_sums[0])
     expert_own = lax.psum_scatter(expert_part, "tensor", scatter_dimension=1, tiled=True)
     pair_term = term(moe_rows, after(pre_grad, expert_part, own_returned[3]))
+    down_sums.append(group_send(down_given[52 * unit : 108 * unit], down_sums[0], expert_part))
     quarter = half // 2
     pair_given = [pair_term(given_at + k * quarter, quarter) for k in range(2)]
-    pair_sum = [group_send(pair_given[0], down_sum)]
-    pair_sum.append(group_send(pair_given[1], pair_sum[0]))
     returned = [after(v, *pair_given) for v in returned]
-    returned[3] = after(returned[3], down_sum)
+    returned[3] = after(returned[3], down_sums[1])
+    down_sums.append(group_send(down_given[108 * unit :], down_sums[1]))
+    pair_sums = [group_send(pair_given[0][: 26 * unit], down_sums[1])]
     back = unpacked(returned)
 
     gate_grad = jnp.concatenate(
@@ -796,44 +796,52 @@
     outputs = {0: expert_own[:MOST]}
 
     def keep_pair(sent):
-        kept["pair"] = term(moe_rows, after(pre_grad, sent, expert_own))(mine_at, half)
-        outputs[2] = swap(expert_own[2 * MOST : 3 * MOST], "dp", 2 * group_count)
-        return (kept["pair"],)
+        kept["pair"] = term(moe_rows, after(pre_grad, sent))(mine_at, half)
+        return (kept["pair"], down_sums[2], pair_sums[0])
 
     def keep_down(sent):
         kept["down"] = term(grad_rows, after(activation, sent))(mine_at, half)
-        return (kept["down"],)
+        return (kept["down"], outputs[1])
 
     attn_grad = tensor_gather(hidden_grad.astype(low), keep_pair)
-    attn_grad = after(attn_grad, outputs[2])
-    for s in (3, 1):
-        part = after(expert_own[s * MOST : (s + 1) * MOST], outputs[2])
+    attn_grad = after(attn_grad, expert_own)
+    pair_sums.append(
+        group_send(pair_given[0][26 * unit : 42 * unit], pair_sums[0], down_sums[2], kept["pair"])
+    )
+    context_grad = jnp.dot(attn_grad, out_full, preferred_element_type=full).astype(low)
+    for s in (2, 3, 1):
+        part = after(expert_own[s * MOST : (s + 1) * MOST], context_grad, *list(outputs.values())[1:])
         outputs[s] = swap(part, "dp", s * group_count)
-    context_grad = jnp.dot(attn_grad, out_full, preferred_element_type=full).astype(low)
     out_shard = lax.psum_scatter(
         contract(after(attn_grad, context_grad), context, 0, 0).astype(low), "dp", scatter_dimension=0, tiled=True
     ).astype(full)
     qkv_grad_rows = attention_back(query, keys, values, logs, context_grad, cosine, sine, scale)
+    qkv_grad_rows = after(qkv_grad_rows, pair_sums[1])
     qkv_grad = contract(normed_in, qkv_grad_rows, 0, 0).astype(low)
+    pair_sums.append(group_send(pair_given[0][42 * unit :], pair_sums[1], qkv_grad))
+    pair_last = group_send(pair_given[1], pair_sums[1], qkv_grad)
     qkv_shard = lax.psum_scatter(qkv_grad, "dp", scatter_dimension=0, tiled=True).astype(full)
     normed_grad = tensor_reduce(
         contract(
-            after(qkv_grad_rows, qkv_grad, pair_sum[0], outputs[1], outputs[3]), qkv_flat, 1, 1
+            after(qkv_grad_rows, qkv_grad, outputs[2]), qkv_flat, 1, 1
         ).astype(low),
         keep_down,
+        (outputs[3],),
     )
     normed_one = inputs_own * scale_one
     scaled_in = normed_grad * gain_first_own
     attn_gain_grad = jnp.sum(normed_grad * normed_one, axis=0)
     mean_one = tensor_sum(jnp.sum(scaled_in * normed_one, axis=1)[None]) / width
     input_own = hidden_grad + scale_one * (scaled_in - normed_one * mean_one.reshape(rows, 1))
-    input_own = after(input_own, pair_sum[1])
+    input_own = after(input_own, pair_last, pair_sums[2])
     input_grad = tensor_gather(input_own.astype(low)).astype(full)
     layer_own = hidden + unpacked([outputs[s] for s in range(EXPERTS)])
     layer_out = tensor_gather(layer_own.astype(low)).astype(full)
     expert_grad = expert_grad_sum(
-        group_finish(kept["pair"], pair_sum, member, group_count),
-        group_finish(kept["down"], [down_sum], member, group_count),
+        group_finish(
+            kept["pair"], [jnp.concatenate(pair_sums, 0), pair_last], member, group_count
+        ),
+        group_finish(kept["down"], [jnp.concatenate(down_sums, 0)], member, group_count),
         hidden_size,
     )
 

time: 1060 us -> 1000 us (0.943)
  starting transfers between devices: 196 us -> 88.2 us
  waiting for transfers between devices: 329 us -> 371 us
    all_gather x1, waiting for transfers between devices: 4.57 us -> 127 us  [body(): lax.all_gather(jnp.concatenate([qkv_weight.reshape(-1, 3 * size), out_wei...]
    ppermute x72, starting transfers between devices: 196 us -> 87.7 us  [swap(): lax.ppermute(value, axis, [(i, i ^ distance) for i in range(lax.axis_size...]
    ppermute x72, waiting for transfers between devices: 299 us -> 243 us  [swap(): lax.ppermute(value, axis, [(i, i ^ distance) for i in range(lax.axis_size...]
    reduce_scatter x1, waiting for transfers between devices: 24.8 us -> 0.01 us  [body(): lax.psum_scatter(expert_part, 'tensor', scatter_dimension=1, tiled=True)]
    unnamed x179 -> x181, local copies, waits for them, and re-layouts: 21.3 us -> 14.8 us
    pallas_call x1 -> x2, Pallas kernels: 38.7 us -> 32.9 us  [down_pass(): pl.pallas_call(functools.partial(down_kernel, len(carried)), grid_spec=pl...]
  transfers between devices with their start and end apart: 76 -> 78, of which waited for: 29 -> 28; matrix products, arithmetic and copies ran while one was open for 23% -> 27% of each run, Pallas kernels for 19% -> 22%
where the time goes in v6:
time: 1000 us; the launch traced here: 994 us
  waiting for transfers between devices  371 us (37%)
  Pallas kernels  219 us (22%)
  matrix products  175 us (18%)
  starting transfers between devices  88.2 us (9%)
  other arithmetic  77.1 us (8%)
  local copies, waits for them, and re-layouts  47.9 us (5%)
  between operations  16.1 us (2%)
    ppermute x72, waiting for transfers between devices, swap(): lax.ppermute(value, axis, [(i, i ^ distance) for i in range(lax.axis_size...  243 us
    dot_general x27, matrix products, contract(): lax.dot_general(left, right, (((left_dim,), (right_dim,)), ((), ())), pre...  139 us
    all_gather x1, waiting for transfers between devices, body(): lax.all_gather(jnp.concatenate([qkv_weight.reshape(-1, 3 * size), out_wei...  127 us
    pallas_call x4, Pallas kernels, expert_pass(): pl.pallas_call(functools.partial(expert_kernel, count, len(carried)), gri...  120 us
    ppermute x72, starting transfers between devices, swap(): lax.ppermute(value, axis, [(i, i ^ distance) for i in range(lax.axis_size...  87.7 us
    pallas_call x2, Pallas kernels, down_pass(): pl.pallas_call(functools.partial(down_kernel, len(carried)), grid_spec=pl...  32.9 us
    pallas_call x1, Pallas kernels, up_pass(): pl.pallas_call(up_kernel, grid_spec=pltpu.PrefetchScalarGridSpec(num_scal...  26.9 us
  transfers between devices with their start and end apart: 78, of which 28 were waited for; matrix products, arithmetic and copies ran while one was open for 27% of the time, Pallas kernels for 22%

profile of v6, /device:TPU:0, one launch (start us, length us, event | category | flops | bytes accessed | tf_op | source)
XLA Modules:
  0.0 994.2 jit_solution(5518808607967254607)
XLA Ops:
  47.1 127.3 %all-gather.4.cloned.1.call-done = bf16[2048,2176]{1,0:T(8,128)(2,1)} async-done(((bf16[256,2176]{1,0:T(8,128)(2,1)}), bf16[2048,2176]{1,0:T(8,128)(2,1)}) %all-gather.4.cloned.1.call-update) | async-done | bytes 8912912 | tf_op jit(solution)/shard_map/all_gather | solution.py:580
  184.9 11.7 %fusion.14.q_in.k_in.v_in = f32[1024,1536]{1,0:T(8,128)} fusion(bf16[1024,2048]{1,0:T(8,128)(2,1)} %fusion.2, bf16[2048,2176]{1,0:T(8,128)(2,1)} %all-gather.4.cloned.1.call-done), kind=kOutput, calls=%fused_computation.17 | convolution fusion | flops 6442450944 | bytes 16777216 | tf_op jit(solution)/shard_map/dot_general | solution.py:658
  200.8 12.7 %attention.1 = (bf16[1024,512]{1,0:T(8,128)(2,1)S(1)}, bf16[1024,512]{1,0:T(8,128)(2,1)S(1)}, bf16[1024,512]{1,0:T(8,128)(2,1)S(1)}, bf16[1024,512]{1,0:T(8,128)(2,1)S(1)}, f32[4,1024,1]{2,1,0:T(8,128)}) custom-call(f32[1024,1536]{1,0:T(8,128)} %fusion.14.q_in.k_in.v_in, f32[1024,1536]{1,0:T(8,128)} %fusion.14.q_in.k_in.v_in, ...), custom_call_target="tpu_custom_call" | custom-call | flops 1342177280 | bytes 10485760 | tf_op jit(solution)/shard_map/attention/pallas_call | solution.py:157
  238.4 11.3 %down.2 = (bf16[3072,2048]{1,0:T(8,128)(2,1)}, bf16[3072,1408]{1,0:T(8,128)(2,1)}) custom-call(s32[3]{0:T(128)S(1)} %pad_add_fusion.where, bf16[768,2048]{1,0:T(8,128)(2,1)} %convolution_convert_fusion.4.rows, bf16[1024,1408]{1,0:T(8,128)(2,1)S(1)} %get-tuple-element.227.own, bf16[1024,1408]{1,0:T(8,128)(2,1)} %collective-permute-done.came), custom_call_target="tpu_custom_call" | custom-call | flops 4429185024 | bytes 14221312 | tf_op jit(solution)/shard_map/down/pallas_call | solution.py:293
  249.8 11.7 %collective-permute-done.11 = bf16[1024,512]{1,0:T(8,128)(2,1)} collective-permute-done((bf16[1024,512]{1,0:T(8,128)(2,1)}, bf16[1024,512]{1,0:T(8,128)(2,1)}, u32[]{:S(2)}, u32[]{:S(2)}) %collective-permute-start.11) | collective-permute-done | bytes 1048608 | tf_op jit(solution)/shard_map/ppermute | solution.py:26
  291.8 32.5 %collective-permute-done.17.refs_2_ = bf16[768,512]{1,0:T(8,128)(2,1)S(1)} collective-permute-done((bf16[768,512]{1,0:T(8,128)(2,1)S(1)}, bf16[768,512]{1,0:T(8,128)(2,1)S(1)}, u32[]{:S(2)}, u32[]{:S(2)}) %collective-permute-start.17) | collective-permute-done | bytes 786464 | tf_op jit(solution)/shard_map/ppermute | solution.py:26
  331.2 19.7 %collective-permute-done.19.refs_10_ = bf16[1184,1408]{1,0:T(8,128)(2,1)S(1)} collective-permute-done((bf16[1184,1408]{1,0:T(8,128)(2,1)S(1)}, bf16[1184,1408]{1,0:T(8,128)(2,1)S(1)}, u32[]{:S(2)}, u32[]{:S(2)}) %collective-permute-start.19) | collective-permute-done | bytes 3334176 | tf_op jit(solution)/shard_map/ppermute | solution.py:26
  352.7 30.0 %expert.4 = (bf16[3072,2048]{1,0:T(8,128)(2,1)}, bf16[3072,1408]{1,0:T(8,128)(2,1)}, bf16[3072,2816]{1,0:T(8,128)(2,1)}, bf16[768,1024]{1,0:T(8,128)(2,1)}, bf16[768,1024]{1,0:T(8,128)(2,1)}, /*index=5*/f32[1,768]{1,0:T(1,128)}) custom-call(s32[3]{0:T(128)} %copy-done.5, bf16[768,512]{1,0:T(8,128)(2,1)} %copy-done.74, bf16[768,512]{1,0:T(8,128)(2,1)} %copy-done.78, ...), custom_call_target="tpu_custom_call" | custom-call | flops 17716740096 | bytes 32768000 | tf_op jit(solution)/shard_map/expert/pallas_call | solution.py:398
  384.8 21.6 %down.3 = (bf16[3072,2048]{1,0:T(8,128)(2,1)}, bf16[3072,1408]{1,0:T(8,128)(2,1)}) custom-call(s32[3]{0:T(128)S(1)} %copy-done.6, bf16[2304,2048]{1,0:T(8,128)(2,1)} %all-gather.8.cloned.1.call-done.rows, bf16[1024,1408]{1,0:T(8,128)(2,1)S(1)} %get-tuple-element.227.own, ...), custom_call_target="tpu_custom_call", output_to_operand_aliasing={{0}: (4, {}), {1}: (5, {})} | custom-call | flops 13287555072 | bytes 31129600 | tf_op jit(solution)/shard_map/down/pallas_call | solution.py:293
  409.8 30.0 %expert.5 = (bf16[3072,2048]{1,0:T(8,128)(2,1)}, bf16[3072,1408]{1,0:T(8,128)(2,1)}, bf16[3072,2816]{1,0:T(8,128)(2,1)}, bf16[768,1024]{1,0:T(8,128)(2,1)}, bf16[768,1024]{1,0:T(8,128)(2,1)}, /*index=5*/f32[1,768]{1,0:T(1,128)}) custom-call(s32[3]{0:T(128)} %copy-done.5, ...), custom_call_target="tpu_custom_call", output_to_operand_aliasing={{0}: (15, {}), {1}: (16, {}), {2}: (17, {})} | custom-call | flops 17716740096 | bytes 32768000 | tf_op jit(solution)/shard_map/expert/pallas_call | solution.py:398
  446.1 30.2 %expert.6 = (bf16[3072,2048]{1,0:T(8,128)(2,1)}, bf16[3072,1408]{1,0:T(8,128)(2,1)}, bf16[3072,2816]{1,0:T(8,128)(2,1)}, bf16[768,1024]{1,0:T(8,128)(2,1)}, bf16[768,1024]{1,0:T(8,128)(2,1)}, /*index=5*/f32[1,768]{1,0:T(1,128)}) custom-call(s32[3]{0:T(128)} %copy-done.5, ...), custom_call_target="tpu_custom_call", output_to_operand_aliasing={{0}: (15, {}), {1}: (16, {}), {2}: (17, {})} | custom-call | flops 17716740096 | bytes 32768000 | tf_op jit(solution)/shard_map/expert/pallas_call | solution.py:398
  485.8 29.8 %expert.7 = (bf16[3072,2048]{1,0:T(8,128)(2,1)}, bf16[3072,1408]{1,0:T(8,128)(2,1)}, bf16[3072,2816]{1,0:T(8,128)(2,1)}, bf16[768,1024]{1,0:T(8,128)(2,1)}, bf16[768,1024]{1,0:T(8,128)(2,1)}, /*index=5*/f32[1,768]{1,0:T(1,128)}) custom-call(s32[3]{0:T(128)} %copy-done.5, ...), custom_call_target="tpu_custom_call", output_to_operand_aliasing={{0}: (15, {}), {1}: (16, {}), {2}: (17, {})} | custom-call | flops 17716740096 | bytes 32768000 | tf_op jit(solution)/shard_map/expert/pallas_call | solution.py:398
  525.7 14.3 %fusion.19 = bf16[1024,1408]{1,0:T(8,128)(2,1)S(1)} fusion(bf16[3072,1408]{1,0:T(8,128)(2,1)} %get-tuple-element.174.act, bf16[3072,2048]{1,0:T(8,128)(2,1)} %get-tuple-element.134, s32[]{:T(128)S(6)} %select_n.225), kind=kOutput, calls=%fused_computation.25 | convolution fusion | flops 8859811840 | bytes 17825796 | tf_op jit(solution)/shard_map/dot_general | solution.py:30
  545.8 26.9 %up.1 = bf16[3072,2048]{1,0:T(8,128)(2,1)} custom-call(s32[3]{0:T(128)S(1)} %copy-done.7, bf16[3072,1408]{1,0:T(8,128)(2,1)} %get-tuple-element.174.act, bf16[1024,1408]{1,0:T(8,128)(2,1)S(1)} %get-tuple-element.227.own, bf16[1024,1408]{1,0:T(8,128)(2,1)} %collective-permute-done.came), custom_call_target="tpu_custom_call" | custom-call | flops 17716740096 | bytes 27000832 | tf_op jit(solution)/shard_map/up/pallas_call | solution.py:326
  581.2 11.8 %collective-permute-done.42 = bf16[768,512]{1,0:T(8,128)(2,1)S(1)} collective-permute-done((bf16[768,512]{1,0:T(8,128)(2,1)S(1)}, bf16[768,512]{1,0:T(8,128)(2,1)S(1)}, u32[]{:S(2)}, u32[]{:S(2)}) %collective-permute-start.42) | collective-permute-done | bytes 786464 | tf_op jit(solution)/shard_map/ppermute | solution.py:26
  594.1 15.8 %convolution_convert_fusion.2 = bf16[512,2816]{1,0:T(8,128)(2,1)} fusion(bf16[3072,2816]{1,0:T(8,128)(2,1)} %get-tuple-element.158, bf16[3072,2048]{1,0:T(8,128)(2,1)} %get-tuple-element.149, s32[]{:T(128)S(6)} %select_n.225), kind=kOutput, calls=%fused_computation.20 | convolution fusion | flops 8859811840 | bytes 23330820 | tf_op jit(solution)/shard_map/dot_general | solution.py:30
  609.9 16.4 %convolution_convert_fusion.1 = bf16[512,2816]{1,0:T(8,128)(2,1)} fusion(bf16[3072,2816]{1,0:T(8,128)(2,1)} %get-tuple-element.158, bf16[3072,2048]{1,0:T(8,128)(2,1)} %get-tuple-element.149, s32[]{:T(128)S(6)} %select_n.228), kind=kOutput, calls=%fused_computation.19 | convolution fusion | flops 8859811840 | bytes 23330820 | tf_op jit(solution)/shard_map/dot_general | solution.py:30
  626.3 8.1 collective-permute-done.44
  655.3 26.1 %fusion.9.refs_0_ = bf16[1024,2816]{1,0:T(8,128)(2,1)} fusion(bf16[3072,2816]{1,0:T(8,128)(2,1)} %get-tuple-element.158, bf16[3072,2048]{1,0:T(8,128)(2,1)} %get-tuple-element.149, s32[]{:T(128)S(6)} %select_n.230), kind=kOutput, calls=%fused_computation.14 | convolution fusion | flops 17719623680 | bytes 29360132 | tf_op jit(solution)/shard_map/dot_general | solution.py:30
  681.5 9.7 collective-permute-done.49
  713.9 15.6 %attention_back.1 = bf16[1024,1536]{1,0:T(8,128)(2,1)} custom-call(bf16[1024,512]{1,0:T(8,128)(2,1)S(1)} %copy-done.9, bf16[1024,512]{1,0:T(8,128)(2,1)S(1)} %copy-done.11, bf16[1024,512]{1,0:T(8,128)(2,1)S(1)} %copy-done.13, f32[4,1024,1]{2,1,0:T(8,128)} %get-tuple-element.169.logs, bf16[1024,512]{1,0:T(8,128)(2,1)S(1)} %copy-done.16, ...), custom_call_target="tpu_custom_call" | custom-call | flops 3355443200 | bytes 8388608 | tf_op jit(solution)/shard_map/attention_back/pallas_call | solution.py:210
  739.8 10.7 %convolution_convert_fusion = bf16[2048,1536]{1,0:T(8,128)(2,1)} fusion(bf16[1024,2048]{1,0:T(8,128)(2,1)S(1)} %copy-done.29, bf16[1024,1536]{1,0:T(8,128)(2,1)} %attention_back.1), kind=kOutput, calls=%fused_computation.7 | convolution fusion | flops 6445596672 | bytes 13631488 | tf_op jit(solution)/shard_map/dot_general | solution.py:30
  750.5 26.0 %collective-permute-done.53 = bf16[768,512]{1,0:T(8,128)(2,1)S(1)} collective-permute-done((bf16[768,512]{1,0:T(8,128)(2,1)S(1)}, bf16[768,512]{1,0:T(8,128)(2,1)S(1)}, u32[]{:S(2)}, u32[]{:S(2)}) %collective-permute-start.53) | collective-permute-done | bytes 786464 | tf_op jit(solution)/shard_map/ppermute | solution.py:26
  777.4 10.0 %fusion.16 = bf16[1024,2048]{1,0:T(8,128)(2,1)S(1)} fusion(bf16[1024,1536]{1,0:T(8,128)(2,1)} %attention_back.1, bf16[2048,2176]{1,0:T(8,128)(2,1)} %all-gather.4.cloned.1.call-done), kind=kOutput, calls=%fused_computation.24 | convolution fusion | flops 6444548096 | bytes 13631488 | tf_op jit(solution)/shard_map/dot_general | solution.py:30
  798.0 14.7 %collective-permute-done.54 = bf16[768,512]{1,0:T(8,128)(2,1)S(1)} collective-permute-done((bf16[768,512]{1,0:T(8,128)(2,1)}, bf16[768,512]{1,0:T(8,128)(2,1)S(1)}, u32[]{:S(2)}, u32[]{:S(2)}) %collective-permute-start.54) | collective-permute-done | bytes 786464 | tf_op jit(solution)/shard_map/ppermute | solution.py:26
  812.7 16.7 %collective-permute-start.55 = (bf16[768,512]{1,0:T(8,128)(2,1)S(1)}, bf16[768,512]{1,0:T(8,128)(2,1)S(1)}, u32[]{:S(2)}, u32[]{:S(2)}) collective-permute-start(bf16[768,512]{1,0:T(8,128)(2,1)S(1)} %copy-done.45), channel_id=1, source_target_pairs={{0,8},{4,12},{8,0},{12,4},{16,24},{20,28},{24,16},{28,20},{1,9},{5... | collective-permute-start | bytes 2359304 | tf_op jit(solution)/shard_map/ppermute | solution.py:26
  831.8 15.7 %fusion.22.refs_3_ = bf16[1024,1408]{1,0:T(8,128)(2,1)} fusion(bf16[3072,1408]{1,0:T(8,128)(2,1)} %get-tuple-element.174.act, bf16[3072,2048]{1,0:T(8,128)(2,1)} %get-tuple-element.134, s32[]{:T(128)S(6)} %select_n.230), kind=kOutput, calls=%fused_computation.26 | convolution fusion | flops 8859811840 | bytes 17825796 | tf_op jit(solution)/shard_map/dot_general | solution.py:30
  847.5 33.2 %collective-permute-done.55 = bf16[768,512]{1,0:T(8,128)(2,1)S(1)} collective-permute-done((bf16[768,512]{1,0:T(8,128)(2,1)S(1)}, bf16[768,512]{1,0:T(8,128)(2,1)S(1)}, u32[]{:S(2)}, u32[]{:S(2)}) %collective-permute-start.55) | collective-permute-done | bytes 786464 | tf_op jit(solution)/shard_map/ppermute | solution.py:26
  890.4 8.3 collective-permute-done.63.refs_2_
  898.7 13.3 %collective-permute-done.56 = bf16[1024,512]{1,0:T(8,128)(2,1)S(1)} collective-permute-done((bf16[1024,512]{1,0:T(8,128)(2,1)S(1)}, bf16[1024,512]{1,0:T(8,128)(2,1)S(1)}, u32[]{:S(2)}, u32[]{:S(2)}) %collective-permute-start.56) | collective-permute-done | bytes 1048608 | tf_op jit(solution)/shard_map/ppermute | solution.py:26
  913.9 19.7 %collective-permute-done.65 = bf16[1024,512]{1,0:T(8,128)(2,1)S(1)} collective-permute-done((bf16[1024,512]{1,0:T(8,128)(2,1)S(1)}, bf16[1024,512]{1,0:T(8,128)(2,1)S(1)}, u32[]{:S(2)}, u32[]{:S(2)}) %collective-permute-start.65) | collective-permute-done | bytes 1048608 | tf_op jit(solution)/shard_map/ppermute | solution.py:26
  958.0 11.2 %expert_grad_sum.1 = f32[3,1024,1408]{2,1,0:T(8,128)} custom-call(bf16[1024,2816]{1,0:T(8,128)(2,1)} %fusion.9.refs_0_, bf16[512,2816]{1,0:T(8,128)(2,1)S(1)} %pad_maximum_fusion.2.refs_1_, bf16[512,2816]{1,0:T(8,128)(2,1)S(1)} %collective-permute-done.63.refs_2_, bf16[1024,1408]{1,0:T(8,128)(2,1)S(1)} %copy-done, ...), custom_call_target="tpu_custom_call" | custom-call | flops 4325376 | bytes 34603008 | tf_op jit(solution)/shard_map/expert_grad_sum/pallas_call | solution.py:482
  (471 shorter events, 285.3 us)
Async XLA Ops:
  7.2 167.2 %all-gather.4.cloned.1.call-start = ((), (), s32[]{:S(2)}) async-start(), calls=%async_computation.3 | async-start | bytes 10027008 | tf_op jit(solution)/shard_map/all_gather | solution.py:580
  10.3 258.4 %all-gather.6.cloned.1.call-start = ((), (), s32[]{:S(2)}) async-start(), calls=%async_computation.4 | async-start | bytes 5242880 | tf_op jit(solution)/shard_map/all_gather | solution.py:646
  14.0 162.8 %collective-permute-start.4 = (f32[1,768]{1,0:T(1,128)S(1)}, f32[1,768]{1,0:T(1,128)S(1)}, u32[]{:S(2)}, u32[]{:S(2)}) collective-permute-start(f32[1,768]{1,0:T(1,128)S(1)} %fusion.41), channel_id=1, source_target_pairs={{0,8},{4,12},{8,0},{12,4},{16,24},{20,28},{24,16},{28,20},{1,9},{5... | collective-permute-start | bytes 9224 | tf_op jit(solution)/shard_map/ppermute | solution.py:26
  17.7 160.7 %collective-permute-start.5 = (f32[1,768]{1,0:T(1,128)S(1)}, f32[1,768]{1,0:T(1,128)S(1)}, u32[]{:S(2)}, u32[]{:S(2)}) collective-permute-start(f32[1,768]{1,0:T(1,128)S(1)} %fusion.36), channel_id=1, source_target_pairs={{0,16},{4,20},{8,24},{12,28},{16,0},{20,4},{24,8},{28,12},{1,17},{... | collective-permute-start | bytes 9224 | tf_op jit(solution)/shard_map/ppermute | solution.py:26
  20.9 163.3 %collective-permute-start.6 = (f32[1,768]{1,0:T(1,128)S(1)}, f32[1,768]{1,0:T(1,128)S(1)}, u32[]{:S(2)}, u32[]{:S(2)}) collective-permute-start(f32[1,768]{1,0:T(1,128)S(1)} %fusion.31), channel_id=1, source_target_pairs={{0,24},{4,28},{8,16},{12,20},{16,8},{20,12},{24,0},{28,4},{1,25},{... | collective-permute-start | bytes 9224 | tf_op jit(solution)/shard_map/ppermute | solution.py:26
  20.9 163.3 %collective-permute-start.1 = (f32[1,1024]{1,0:T(1,128)S(1)}, f32[1,1024]{1,0:T(1,128)S(1)}, u32[]{:S(2)}, u32[]{:S(2)}) collective-permute-start(f32[1,1024]{1,0:T(1,128)S(1)} %get-tuple-element.266), channel_id=1, source_target_pairs={{0,8},{4,12},{8,0},{12,4},{16,24},{20,28},{24,16},{28,20},{1,9},{5... | collective-permute-start | bytes 12296 | tf_op jit(solution)/shard_map/ppermute | solution.py:26
  27.7 156.5 %collective-permute-start = (bf16[1024,1408]{1,0:T(8,128)(2,1)S(1)}, bf16[1024,1408]{1,0:T(8,128)(2,1)}, u32[]{:S(2)}, u32[]{:S(2)}) collective-permute-start(bf16[1024,1408]{1,0:T(8,128)(2,1)S(1)} %get-tuple-element.227.own), channel_id=1, source_target_pairs={{0,4},{4,0},{8,12},{12,8},{16,20},{20,16},{24,28},{28,24},{1,5},{5... | collective-permute-start | bytes 8650760 | tf_op jit(solution)/shard_map/ppermute | solution.py:26
  184.7 200.2 %all-gather.8.cloned.1.call-start = ((), (), s32[]{:S(2)}) async-start(), calls=%async_computation.5 | async-start | bytes 11796480 | tf_op jit(solution)/shard_map/all_gather | solution.py:682
  274.8 423.6 %reduce-scatter.4.cloned.1.call-start = ((), (), s32[]{:S(2)}) async-start(), calls=%async_computation.6 | async-start | bytes 15728640 | tf_op jit(solution)/shard_map/reduce_scatter | solution.py:759
  278.0 73.0 %collective-permute-start.19 = (bf16[1184,1408]{1,0:T(8,128)(2,1)S(1)}, bf16[1184,1408]{1,0:T(8,128)(2,1)S(1)}, u32[]{:S(2)}, u32[]{:S(2)}) collective-permute-start(bf16[1184,1408]{1,0:T(8,128)(2,1)S(1)} %pad_maximum_fusion.1), channel_id=1, source_target_pairs={{0,4},{4,0},{8,12},{12,8},{16,20},{20,16},{24,28},{28,24},{1,5},{5... | collective-permute-start | bytes 10002440 | tf_op jit(solution)/shard_map/ppermute | solution.py:26
  291.8 39.4 %collective-permute-start.16 = (bf16[768,512]{1,0:T(8,128)(2,1)S(1)}, bf16[768,512]{1,0:T(8,128)(2,1)S(1)}, u32[]{:S(2)}, u32[]{:S(2)}) collective-permute-start(bf16[768,512]{1,0:T(8,128)(2,1)S(1)} %fusion.104.refs_0_), channel_id=1, source_target_pairs={{0,1},{1,0},{2,3},{3,2},{4,5},{5,4},{6,7},{7,6},{8,9},{9,8},{10,11... | collective-permute-start | bytes 2359304 | tf_op jit(solution)/shard_map/ppermute | solution.py:26
  326.2 56.5 %collective-permute-start.15 = (bf16[768,512]{1,0:T(8,128)(2,1)}, bf16[768,512]{1,0:T(8,128)(2,1)}, u32[]{:S(2)}, u32[]{:S(2)}) collective-permute-start(bf16[768,512]{1,0:T(8,128)(2,1)} %fusion.106), channel_id=1, source_target_pairs={{0,16},{4,20},{8,24},{12,28},{16,0},{20,4},{24,8},{28,12},{1,17},{... | collective-permute-start | bytes 2359304 | tf_op jit(solution)/shard_map/ppermute | solution.py:26
  329.6 54.8 %collective-permute-start.23 = (bf16[768,512]{1,0:T(8,128)(2,1)}, bf16[768,512]{1,0:T(8,128)(2,1)}, u32[]{:S(2)}, u32[]{:S(2)}) collective-permute-start(bf16[768,512]{1,0:T(8,128)(2,1)} %collective-permute-done.21.refs_0_), channel_id=1, source_target_pairs={{0,2},{1,3},{2,0},{3,1},{4,6},{5,7},{6,4},{7,5},{8,10},{9,11},{10,... | collective-permute-start | bytes 2359304 | tf_op jit(solution)/shard_map/ppermute | solution.py:26
  331.2 75.2 %collective-permute-start.22 = (bf16[768,512]{1,0:T(8,128)(2,1)}, bf16[768,512]{1,0:T(8,128)(2,1)}, u32[]{:S(2)}, u32[]{:S(2)}) collective-permute-start(bf16[768,512]{1,0:T(8,128)(2,1)} %collective-permute-done.21.refs_0_), channel_id=1, source_target_pairs={{0,1},{1,0},{2,3},{3,2},{4,5},{5,4},{6,7},{7,6},{8,9},{9,8},{10,11... | collective-permute-start | bytes 2359304 | tf_op jit(solution)/shard_map/ppermute | solution.py:26
  382.7 57.1 %collective-permute-start.28 = (bf16[768,512]{1,0:T(8,128)(2,1)}, bf16[768,512]{1,0:T(8,128)(2,1)}, u32[]{:S(2)}, u32[]{:S(2)}) collective-permute-start(bf16[768,512]{1,0:T(8,128)(2,1)} %collective-permute-done.15.refs_0_), channel_id=1, source_target_pairs={{0,2},{1,3},{2,0},{3,1},{4,6},{5,7},{6,4},{7,5},{8,10},{9,11},{10,... | collective-permute-start | bytes 2359304 | tf_op jit(solution)/shard_map/ppermute | solution.py:26
  384.3 60.3 %collective-permute-start.27 = (bf16[768,512]{1,0:T(8,128)(2,1)}, bf16[768,512]{1,0:T(8,128)(2,1)}, u32[]{:S(2)}, u32[]{:S(2)}) collective-permute-start(bf16[768,512]{1,0:T(8,128)(2,1)} %collective-permute-done.15.refs_0_), channel_id=1, source_target_pairs={{0,1},{1,0},{2,3},{3,2},{4,5},{5,4},{6,7},{7,6},{8,9},{9,8},{10,11... | collective-permute-start | bytes 2359304 | tf_op jit(solution)/shard_map/ppermute | solution.py:26
  384.8 55.3 %collective-permute-start.30 = (bf16[768,1024]{1,0:T(8,128)(2,1)}, bf16[768,1024]{1,0:T(8,128)(2,1)}, u32[]{:S(2)}, u32[]{:S(2)}) collective-permute-start(bf16[768,1024]{1,0:T(8,128)(2,1)} %get-tuple-element.121), channel_id=1, source_target_pairs={{0,1},{1,0},{2,3},{3,2},{4,5},{5,4},{6,7},{7,6},{8,9},{9,8},{10,11... | collective-permute-start | bytes 4718600 | tf_op jit(solution)/shard_map/ppermute | solution.py:26
  444.6 41.2 %collective-permute-start.25 = (bf16[768,512]{1,0:T(8,128)(2,1)}, bf16[768,512]{1,0:T(8,128)(2,1)}, u32[]{:S(2)}, u32[]{:S(2)}) collective-permute-start(bf16[768,512]{1,0:T(8,128)(2,1)} %collective-permute-done.20.refs_0_), channel_id=1, source_target_pairs={{0,1},{1,0},{2,3},{3,2},{4,5},{5,4},{6,7},{7,6},{8,9},{9,8},{10,11... | collective-permute-start | bytes 2359304 | tf_op jit(solution)/shard_map/ppermute | solution.py:26
  572.8 397.7 %reduce-scatter.8.cloned.1.call-start = ((), (), s32[]{:S(2)}) async-start(), calls=%async_computation.8 | async-start | bytes 2359296 | tf_op jit(solution)/shard_map/reduce_scatter | solution.py:815
  578.6 47.7 %collective-permute-start.43 = (bf16[768,512]{1,0:T(8,128)(2,1)S(1)}, bf16[768,512]{1,0:T(8,128)(2,1)S(1)}, u32[]{:S(2)}, u32[]{:S(2)}) collective-permute-start(bf16[768,512]{1,0:T(8,128)(2,1)S(1)} %copy-done.47), channel_id=1, source_target_pairs={{0,8},{4,12},{8,0},{12,4},{16,24},{20,28},{24,16},{28,20},{1,9},{5... | collective-permute-start | bytes 2359304 | tf_op jit(solution)/shard_map/ppermute | solution.py:26
  579.3 55.1 %collective-permute-start.44 = (bf16[768,512]{1,0:T(8,128)(2,1)S(1)}, bf16[768,512]{1,0:T(8,128)(2,1)S(1)}, u32[]{:S(2)}, u32[]{:S(2)}) collective-permute-start(bf16[768,512]{1,0:T(8,128)(2,1)S(1)} %copy-done.48), channel_id=1, source_target_pairs={{0,16},{4,20},{8,24},{12,28},{16,0},{20,4},{24,8},{28,12},{1,17},{... | collective-permute-start | bytes 2359304 | tf_op jit(solution)/shard_map/ppermute | solution.py:26
  579.7 57.9 %collective-permute-start.46 = (bf16[448,1408]{1,0:T(8,128)(2,1)S(1)}, bf16[448,1408]{1,0:T(8,128)(2,1)S(1)}, u32[]{:S(2)}, u32[]{:S(2)}) collective-permute-start(bf16[448,1408]{1,0:T(8,128)(2,1)S(1)} %slice.348), channel_id=1, source_target_pairs={{0,4},{4,0},{8,12},{12,8},{16,20},{20,16},{24,28},{28,24},{1,5},{5... | collective-permute-start | bytes 3784712 | tf_op jit(solution)/shard_map/ppermute | solution.py:26
  593.5 44.1 %collective-permute-start.45 = (bf16[768,512]{1,0:T(8,128)(2,1)S(1)}, bf16[768,512]{1,0:T(8,128)(2,1)S(1)}, u32[]{:S(2)}, u32[]{:S(2)}) collective-permute-start(bf16[768,512]{1,0:T(8,128)(2,1)S(1)} %add_convert_fusion.1), channel_id=1, source_target_pairs={{0,24},{4,28},{8,16},{12,20},{16,8},{20,12},{24,0},{28,4},{1,25},{... | collective-permute-start | bytes 2359304 | tf_op jit(solution)/shard_map/ppermute | solution.py:26
  647.8 43.3 %collective-permute-start.51 = (bf16[208,2816]{1,0:T(8,128)(2,1)}, bf16[208,2816]{1,0:T(8,128)(2,1)}, u32[]{:S(2)}, u32[]{:S(2)}) collective-permute-start(bf16[208,2816]{1,0:T(8,128)(2,1)} %slice.352), channel_id=1, source_target_pairs={{0,4},{4,0},{8,12},{12,8},{16,20},{20,16},{24,28},{28,24},{1,5},{5... | collective-permute-start | bytes 3514376 | tf_op jit(solution)/shard_map/ppermute | solution.py:26
  708.5 275.4 %reduce-scatter.6.cloned.1.call-start = ((), (), s32[]{:S(2)}) async-start(), calls=%async_computation.7 | async-start | bytes 7077888 | tf_op jit(solution)/shard_map/reduce_scatter | solution.py:823
  732.4 44.1 %collective-permute-start.53 = (bf16[768,512]{1,0:T(8,128)(2,1)S(1)}, bf16[768,512]{1,0:T(8,128)(2,1)S(1)}, u32[]{:S(2)}, u32[]{:S(2)}) collective-permute-start(bf16[768,512]{1,0:T(8,128)(2,1)S(1)} %get-tuple-element.163), channel_id=1, source_target_pairs={{0,16},{4,20},{8,24},{12,28},{16,0},{20,4},{24,8},{28,12},{1,17},{... | collective-permute-start | bytes 2359304 | tf_op jit(solution)/shard_map/ppermute | solution.py:26
  787.9 41.4 %collective-permute-start.59 = (bf16[1024,1024]{1,0:T(8,128)(2,1)S(1)}, bf16[1024,1024]{1,0:T(8,128)(2,1)S(1)}, u32[]{:S(2)}, u32[]{:S(2)}) collective-permute-start(bf16[1024,1024]{1,0:T(8,128)(2,1)S(1)} %pad_maximum_fusion.8), channel_id=1, source_target_pairs={{0,1},{1,0},{2,3},{3,2},{4,5},{5,4},{6,7},{7,6},{8,9},{9,8},{10,11... | collective-permute-start | bytes 6291464 | tf_op jit(solution)/shard_map/ppermute | solution.py:26
  792.7 97.7 %collective-permute-start.64 = (bf16[176,2816]{1,0:T(8,128)(2,1)S(1)}, bf16[176,2816]{1,0:T(8,128)(2,1)S(1)}, u32[]{:S(2)}, u32[]{:S(2)}) collective-permute-start(bf16[176,2816]{1,0:T(8,128)(2,1)S(1)} %slice.366), channel_id=1, source_target_pairs={{0,4},{4,0},{8,12},{12,8},{16,20},{20,16},{24,28},{28,24},{1,5},{5... | collective-permute-start | bytes 2973704 | tf_op jit(solution)/shard_map/ppermute | solution.py:26
  793.4 105.3 %collective-permute-start.63 = (bf16[512,2816]{1,0:T(8,128)(2,1)S(1)}, bf16[512,2816]{1,0:T(8,128)(2,1)S(1)}, u32[]{:S(2)}, u32[]{:S(2)}) collective-permute-start(bf16[512,2816]{1,0:T(8,128)(2,1)S(1)} %copy-done.73), channel_id=1, source_target_pairs={{0,4},{4,0},{8,12},{12,8},{16,20},{20,16},{24,28},{28,24},{1,5},{5... | collective-permute-start | bytes 8650760 | tf_op jit(solution)/shard_map/ppermute | solution.py:26
  812.7 68.0 %collective-permute-start.55 = (bf16[768,512]{1,0:T(8,128)(2,1)S(1)}, bf16[768,512]{1,0:T(8,128)(2,1)S(1)}, u32[]{:S(2)}, u32[]{:S(2)}) collective-permute-start(bf16[768,512]{1,0:T(8,128)(2,1)S(1)} %copy-done.45), channel_id=1, source_target_pairs={{0,8},{4,12},{8,0},{12,4},{16,24},{20,28},{24,16},{28,20},{1,9},{5... | collective-permute-start | bytes 2359304 | tf_op jit(solution)/shard_map/ppermute | solution.py:26
  830.2 50.4 %collective-permute-start.60 = (bf16[1024,512]{1,0:T(8,128)(2,1)S(1)}, bf16[1024,512]{1,0:T(8,128)(2,1)S(1)}, u32[]{:S(2)}, u32[]{:S(2)}) collective-permute-start(bf16[1024,512]{1,0:T(8,128)(2,1)S(1)} %select_convert_fusion), channel_id=1, source_target_pairs={{0,2},{1,3},{2,0},{3,1},{4,6},{5,7},{6,4},{7,5},{8,10},{9,11},{10,... | collective-permute-start | bytes 3145736 | tf_op jit(solution)/shard_map/ppermute | solution.py:26
  913.9 58.3 %collective-permute-start.57 = (bf16[1024,1024]{1,0:T(8,128)(2,1)}, bf16[1024,1024]{1,0:T(8,128)(2,1)}, u32[]{:S(2)}, u32[]{:S(2)}) collective-permute-start(bf16[1024,1024]{1,0:T(8,128)(2,1)} %pad_maximum_fusion.7), channel_id=1, source_target_pairs={{0,1},{1,0},{2,3},{3,2},{4,5},{5,4},{6,7},{7,6},{8,9},{9,8},{10,11... | collective-permute-start | bytes 6291464 | tf_op jit(solution)/shard_map/ppermute | solution.py:26
  (135 other events, 1980.2 us)
Sparse Core Ops, SparseCore 0:
  10.8 163.5 all-gather.3
  184.8 81.8 all-gather.5
  275.0 97.9 all-gather.7
  572.9 109.9 reduce-scatter.3
  708.6 106.8 reduce-scatter.7
  819.0 136.0 reduce-scatter.5

commit v7 on v6

--- a/solution.py
+++ b/solution.py
@@ -51,28 +51,6 @@
         for bit in range(levels_of(lax.axis_size(axis))):
             value = value + swap(value, axis, 1 << bit)
     return value
-
-
-def tensor_reduce(part, filler=None, others=()):
-    count = lax.axis_size("tensor")
-    place = lax.axis_index("tensor")
-    size = part.shape[1] // count
-    blocks = [part[:, i * size : (i + 1) * size] for i in range(count)]
-    for bit in range(levels_of(count)):
-        upper = side_of(place, bit)
-        kept = [jnp.where(upper, b, a) for a, b in zip(blocks[::2], blocks[1::2])]
-        given = [jnp.where(upper, a, b) for a, b in zip(blocks[::2], blocks[1::2])]
-        sent = jnp.concatenate([v.astype(low) for v in given], 1)
-        if others and bit == levels_of(count) - 1:
-            sent = after(sent, *others)
-        came = swap(sent, "tensor", 1 << bit)
-        if filler is not None and bit == levels_of(count) - 1:
-            came = after(came, *filler(sent))
-        blocks = [
-            v.astype(full) + came[:, i * size : (i + 1) * size].astype(full)
-            for i, v in enumerate(kept)
-        ]
-    return blocks[0]
 
 
 def tensor_gather(own, filler=None):
@@ -252,11 +230,13 @@
 
 
 cuts = (
-    ((0, 0, 16),),
-    ((0, 16, 40),),
+    ((0, 0, 40),),
     ((0, 40, 56),),
-    ((0, 56, 108),),
-    ((0, 108, 128), (1, 0, 128)),
+    ((0, 56, 80),),
+    ((0, 80, 96),),
+    ((0, 96, 128), (1, 0, 20)),
+    ((1, 20, 46),),
+    ((1, 46, 128),),
 )
 
 
@@ -311,6 +291,40 @@
         ),
         name="down",
     )(where, rows, own, came, *carried)
+
+
+def spread_kernel(count, where, left, right, even, odd, part):
+    size = part.shape[1] // count
+    part[...] = dot_cols(left[...], right[...]).astype(low)
+    for i in range(count):
+        (odd if i % 2 else even)[:, i // 2 * size : (i // 2 + 1) * size] = part[
+            :, column_block(where, i, size)
+        ]
+
+
+def spread_dot(where, left, right, column, count):
+    rows, depth = left.shape
+    width = right.shape[0]
+    tile = 256
+    spec = lambda columns: pl.BlockSpec((tile, columns), lambda i, where: (i, 0))
+    half = jax.ShapeDtypeStruct((rows, width // 2), low)
+    return pl.pallas_call(
+        functools.partial(spread_kernel, count),
+        grid_spec=pltpu.PrefetchScalarGridSpec(
+            num_scalar_prefetch=1,
+            grid=(rows // tile,),
+            in_specs=[
+                spec(depth),
+                pl.BlockSpec((width, depth), lambda i, where: (0, column)),
+            ],
+            out_specs=[spec(width // 2)] * 2,
+            scratch_shapes=[pltpu.VMEM((tile, width), low)],
+        ),
+        out_shape=[half, half],
+        compiler_params=limits(48),
+        cost_estimate=cost(2 * rows * width * depth, (rows * (width + depth) + width * depth) * 2),
+        name="spread",
+    )(where, left, right)
 
 
 def up_kernel(where, act, own, came, out, held, sems):
@@ -501,7 +515,7 @@
     return held
 
 
-def near_reduce(even, odd, meet, *others):
+def near_reduce(even, odd, meet, *others, filler=None):
     count = lax.axis_size("tensor")
     number = count // 2
     size = even.shape[1] // number
@@ -518,8 +532,10 @@
             meet.append(sent)
         even = jnp.concatenate(blocks[::2], 1)
         came = swap(sent, "tensor", 1 << bit)
+        if filler is not None and bit == levels_of(count) - 1:
+            came = after(came, *filler(sent))
         number //= 2
-    return (even.astype(full) + came.astype(full)).astype(low)
+    return even.astype(full) + came.astype(full)
 
 
 def half_gather(local, group_count):
@@ -636,6 +652,7 @@
         ]
         crossing.append(group_send(jnp.concatenate(pieces, 0), *crossing[-1:], *others))
 
+    cross(down[1])
     cross(first)
 
     grad_own = own_columns(cotangent)
@@ -654,14 +671,14 @@
     scale_one = lax.rsqrt(jnp.mean(inputs * inputs, axis=1, keepdims=True) + epsilon)
     normed_in = (inputs * scale_one * gain_first).astype(low)
     inputs_own = own_columns(tokens).astype(full)
-    normed_in = after(normed_in, down[1], grad_mine, *slots_came, *routed)
+    normed_in = after(normed_in, crossing[0], grad_mine, *slots_came, *routed)
     qkv = jnp.dot(normed_in, qkv_flat, preferred_element_type=full)
     cross(qkv)
     cosine, sine = rotary_tables()
     context, query, keys, values, logs = attention(qkv, cosine, sine, scale)
-    context = after(context, crossing[1])
+    context = after(context, crossing[2])
     cross(context)
-    attn_part = contract(context, out_full, 1, 1).astype(low)
+    attn_parts = spread_dot(where, context, first, 3, tensor_count)
     rows_raw = []
 
     total = EXPERTS * MOST
@@ -669,9 +686,9 @@
     def down_filler(sent):
         cross(sent)
         rows_raw.extend(down_pass(where, after(grad_mine, sent), *down, 0, total, ()))
-        return (rows_raw[1], crossing[3])
-
-    hidden = inputs_own + tensor_reduce(attn_part, down_filler, (crossing[2],))
+        return (rows_raw[1], crossing[4])
+
+    hidden = inputs_own + near_reduce(*attn_parts, [], crossing[3], filler=down_filler)
     cross(rows_raw[1])
     grad_planes = after(grad_planes, hidden)
     grad_packed = []
@@ -702,7 +719,8 @@
         b = (value - a.astype(full)).astype(low)
         return jnp.stack([a, b, (value - a.astype(full) - b.astype(full)).astype(low)])
 
-    moe_packed = packed(moe_in)
+    moe_packed = packed(after(moe_in, crossing[5]))
+    cross(moe_packed[0])
     pair = (gate_mine, up_mine, *crossing)
     crossed = [moe_packed[0]] + [
         swap(moe_packed[s], "dp", s * group_count) for s in range(1, EXPERTS - 1)
@@ -735,7 +753,7 @@
             crossed[3] = after(crossed[3], even)
         if step == 2:
             arrived.append(near_blocks(crossed[3], even))
-        returned.append(near_reduce(even, odd, sums_sent, *returned[2:]))
+        returned.append(near_reduce(even, odd, sums_sent, *returned[2:]).astype(low))
         gate_grads.append(gate_grad)
     own_returned = returned
     returned = exchange(returned)
@@ -750,21 +768,24 @@
         return part
 
     unit = half // 128
-    down_given = term(grad_rows, after(activation, sums_sent[2], own_returned[1]))(given_at, half)
-    down_sums = [group_send(down_given[: 52 * unit])]
-    expert_part = up_pass(
-        where, after(activation, down_given, sums_sent[3], own_returned[2], *gate_grad_near), *down
-    )
-    expert_part = after(expert_part, down_sums[0])
+    expert_part = up_pass(where, after(activation, sums_sent[2], own_returned[1]), *down)
+    expert_part = after(expert_part, sums_sent[3], own_returned[2])
     expert_own = lax.psum_scatter(expert_part, "tensor", scatter_dimension=1, tiled=True)
-    pair_term = term(moe_rows, after(pre_grad, expert_part, own_returned[3]))
-    down_sums.append(group_send(down_given[52 * unit : 108 * unit], down_sums[0], expert_part))
+    act_late = after(activation, expert_part)
+    down_given = term(grad_rows, act_late)(given_at, half)
+    down_sums = [group_send(down_given[: 40 * unit])]
+    pair_term = term(
+        moe_rows, after(pre_grad, down_given, own_returned[3], returned[1], *gate_grad_near)
+    )
     quarter = half // 2
-    pair_given = [pair_term(given_at + k * quarter, quarter) for k in range(2)]
+    pair_given = [pair_term(given_at, quarter)]
+    down_sums.append(group_send(down_given[40 * unit : 80 * unit], down_sums[0], pair_given[0]))
+    pair_term = term(moe_rows, after(pre_grad, pair_given[0], down_sums[0], returned[2]))
+    pair_given.append(pair_term(given_at + quarter, quarter))
     returned = [after(v, *pair_given) for v in returned]
     returned[3] = after(returned[3], down_sums[1])
-    down_sums.append(group_send(down_given[108 * unit :], down_sums[1]))
-    pair_sums = [group_send(pair_given[0][: 26 * unit], down_sums[1])]
+    down_sums.append(group_send(down_given[80 * unit :], down_sums[1]))
+    pair_sums = [group_send(pair_given[0][: 16 * unit], down_sums[1])]
     back = unpacked(returned)
 
     gate_grad = jnp.concatenate(
@@ -796,20 +817,20 @@
     outputs = {0: expert_own[:MOST]}
 
     def keep_pair(sent):
-        kept["pair"] = term(moe_rows, after(pre_grad, sent))(mine_at, half)
-        return (kept["pair"], down_sums[2], pair_sums[0])
+        kept["pair"] = term(moe_rows, after(pre_grad, sent, expert_own))(mine_at, half)
+        outputs[2] = swap(expert_own[2 * MOST : 3 * MOST], "dp", 2 * group_count)
+        return (kept["pair"], down_sums[2], pair_sums[0], outputs[2])
 
     def keep_down(sent):
         kept["down"] = term(grad_rows, after(activation, sent))(mine_at, half)
         return (kept["down"], outputs[1])
 
     attn_grad = tensor_gather(hidden_grad.astype(low), keep_pair)
-    attn_grad = after(attn_grad, expert_own)
     pair_sums.append(
-        group_send(pair_given[0][26 * unit : 42 * unit], pair_sums[0], down_sums[2], kept["pair"])
+        group_send(pair_given[0][16 * unit : 34 * unit], pair_sums[0], down_sums[2], kept["pair"])
     )
     context_grad = jnp.dot(attn_grad, out_full, preferred_element_type=full).astype(low)
-    for s in (2, 3, 1):
+    for s in (3, 1):
         part = after(expert_own[s * MOST : (s + 1) * MOST], context_grad, *list(outputs.values())[1:])
         outputs[s] = swap(part, "dp", s * group_count)
     out_shard = lax.psum_scatter(
@@ -818,25 +839,22 @@
     qkv_grad_rows = attention_back(query, keys, values, logs, context_grad, cosine, sine, scale)
     qkv_grad_rows = after(qkv_grad_rows, pair_sums[1])
     qkv_grad = contract(normed_in, qkv_grad_rows, 0, 0).astype(low)
-    pair_sums.append(group_send(pair_given[0][42 * unit :], pair_sums[1], qkv_grad))
+    pair_sums.append(group_send(pair_given[0][34 * unit :], pair_sums[1], qkv_grad))
     pair_last = group_send(pair_given[1], pair_sums[1], qkv_grad)
     qkv_shard = lax.psum_scatter(qkv_grad, "dp", scatter_dimension=0, tiled=True).astype(full)
-    normed_grad = tensor_reduce(
-        contract(
-            after(qkv_grad_rows, qkv_grad, outputs[2]), qkv_flat, 1, 1
-        ).astype(low),
-        keep_down,
-        (outputs[3],),
-    )
+    parts = spread_dot(where, after(qkv_grad_rows, qkv_grad, outputs[3]), first, 0, tensor_count)
+    normed_grad = near_reduce(*parts, [], filler=keep_down)
     normed_one = inputs_own * scale_one
     scaled_in = normed_grad * gain_first_own
     attn_gain_grad = jnp.sum(normed_grad * normed_one, axis=0)
     mean_one = tensor_sum(jnp.sum(scaled_in * normed_one, axis=1)[None]) / width
     input_own = hidden_grad + scale_one * (scaled_in - normed_one * mean_one.reshape(rows, 1))
+    mine = jnp.concatenate([router_grad, attn_gain_grad[None], moe_gain_grad[None]], 0)
+    mine = lax.dynamic_update_slice_in_dim(
+        jnp.zeros((mine.shape[0], width), full), mine, place * size, 1
+    )
+    mine = all_sum(mine)
     input_own = after(input_own, pair_last, pair_sums[2])
-    input_grad = tensor_gather(input_own.astype(low)).astype(full)
-    layer_own = hidden + unpacked([outputs[s] for s in range(EXPERTS)])
-    layer_out = tensor_gather(layer_own.astype(low)).astype(full)
     expert_grad = expert_grad_sum(
         group_finish(
             kept["pair"], [jnp.concatenate(pair_sums, 0), pair_last], member, group_count
@@ -844,13 +862,12 @@
         group_finish(kept["down"], [jnp.concatenate(down_sums, 0)], member, group_count),
         hidden_size,
     )
-
-    mine = jnp.concatenate([router_grad, attn_gain_grad[None], moe_gain_grad[None]], 0)
-    mine = lax.dynamic_update_slice_in_dim(
-        jnp.zeros((mine.shape[0], width), full), mine, place * size, 1
-    )
+    input_grad = tensor_gather(input_own.astype(low), lambda sent: (expert_grad, mine))
+    input_grad = input_grad.astype(full)
+    layer_own = hidden + unpacked([outputs[s] for s in range(EXPERTS)])
+    layer_out = tensor_gather(layer_own.astype(low)).astype(full)
     share = width // dp_count
-    mine = lax.dynamic_slice_in_dim(all_sum(mine), index * share, share, 1)
+    mine = lax.dynamic_slice_in_dim(mine, index * share, share, 1)
     return (
         layer_out,
         input_grad,

time: 1000 us -> 1020 us (1.020)
  waiting for transfers between devices: 371 us -> 393 us
  matrix products: 175 us -> 154 us
  Pallas kernels: 219 us -> 236 us
    ppermute x72 -> x74, waiting for transfers between devices: 243 us -> 331 us  [swap(): lax.ppermute(value, axis, [(i, i ^ distance) for i in range(lax.axis_size...]
    all_gather x1, waiting for transfers between devices: 127 us -> 62.3 us  [body(): lax.all_gather(jnp.concatenate([qkv_weight.reshape(-1, 3 * size), out_wei...]
    dot_general x27 -> x25, matrix products: 139 us -> 122 us  [contract(): lax.dot_general(left, right, (((left_dim,), (right_dim,)), ((), ())), pre...]
    pallas_call x0 -> x2, Pallas kernels: none -> 17 us  [spread_dot(): pl.pallas_call(functools.partial(spread_kernel, count), grid_spec=pltpu.P...]
    ppermute x72 -> x74, starting transfers between devices: 87.7 us -> 79.5 us  [swap(): lax.ppermute(value, axis, [(i, i ^ distance) for i in range(lax.axis_size...]
  transfers between devices with their start and end apart: 78 -> 80, of which waited for: 28 -> 30; matrix products, arithmetic and copies ran while one was open for 27% -> 24% of each run, Pallas kernels for 22% -> 23%
where the time goes in v7:
time: 1020 us; the launch traced here: 1010 us
  waiting for transfers between devices  393 us (39%)
  Pallas kernels  236 us (23%)
  matrix products  154 us (15%)
  starting transfers between devices  80.2 us (8%)
  other arithmetic  74.5 us (7%)
  local copies, waits for them, and re-layouts  55.3 us (5%)
  between operations  15.8 us (2%)
    ppermute x74, waiting for transfers between devices, swap(): lax.ppermute(value, axis, [(i, i ^ distance) for i in range(lax.axis_size...  331 us
    dot_general x25, matrix products, contract(): lax.dot_general(left, right, (((left_dim,), (right_dim,)), ((), ())), pre...  122 us
    pallas_call x4, Pallas kernels, expert_pass(): pl.pallas_call(functools.partial(expert_kernel, count, len(carried)), gri...  120 us
    ppermute x74, starting transfers between devices, swap(): lax.ppermute(value, axis, [(i, i ^ distance) for i in range(lax.axis_size...  79.5 us
    all_gather x1, waiting for transfers between devices, body(): lax.all_gather(jnp.concatenate([qkv_weight.reshape(-1, 3 * size), out_wei...  62.3 us
    pallas_call x2, Pallas kernels, down_pass(): pl.pallas_call(functools.partial(down_kernel, len(carried)), grid_spec=pl...  32.6 us
    pallas_call x1, Pallas kernels, up_pass(): pl.pallas_call(up_kernel, grid_spec=pltpu.PrefetchScalarGridSpec(num_scal...  26.8 us
  transfers between devices with their start and end apart: 80, of which 30 were waited for; matrix products, arithmetic and copies ran while one was open for 24% of the time, Pallas kernels for 23%

profile of v7, /device:TPU:0, one launch (start us, length us, event | category | flops | bytes accessed | tf_op | source)
XLA Modules:
  0.0 1009.0 jit_solution(5558415964252222218)
XLA Ops:
  47.1 80.7 %collective-permute-done.came = bf16[1024,1408]{1,0:T(8,128)(2,1)} collective-permute-done((bf16[1024,1408]{1,0:T(8,128)(2,1)S(1)}, bf16[1024,1408]{1,0:T(8,128)(2,1)}, u32[]{:S(2)}, u32[]{:S(2)}) %collective-permute-start) | collective-permute-done | bytes 2883616 | tf_op jit(solution)/shard_map/ppermute | solution.py:26
  128.1 62.3 %all-gather.4.cloned.1.call-done.right = bf16[2048,2176]{1,0:T(8,128)(2,1)} async-done(((bf16[256,2176]{1,0:T(8,128)(2,1)}), bf16[2048,2176]{1,0:T(8,128)(2,1)}) %all-gather.4.cloned.1.call-update) | async-done | bytes 8912912 | tf_op jit(solution)/shard_map/all_gather | solution.py:596
  201.0 11.7 %fusion.3.q_in.k_in.v_in = f32[1024,1536]{1,0:T(8,128)} fusion(bf16[1024,2048]{1,0:T(8,128)(2,1)} %fusion.2, bf16[2048,2176]{1,0:T(8,128)(2,1)} %all-gather.4.cloned.1.call-done.right), kind=kOutput, calls=%fused_computation.8 | convolution fusion | flops 6442450944 | bytes 16777216 | tf_op jit(solution)/shard_map/dot_general | solution.py:675
  216.9 12.9 %attention.1 = (bf16[1024,512]{1,0:T(8,128)(2,1)S(1)}, bf16[1024,512]{1,0:T(8,128)(2,1)S(1)}, bf16[1024,512]{1,0:T(8,128)(2,1)S(1)}, bf16[1024,512]{1,0:T(8,128)(2,1)S(1)}, f32[4,1024,1]{2,1,0:T(8,128)}) custom-call(f32[1024,1536]{1,0:T(8,128)} %fusion.3.q_in.k_in.v_in, f32[1024,1536]{1,0:T(8,128)} %fusion.3.q_in.k_in.v_in, ...), custom_call_target="tpu_custom_call" | custom-call | flops 1342177280 | bytes 10485760 | tf_op jit(solution)/shard_map/attention/pallas_call | solution.py:135
  244.3 7.3 collective-permute-done.11.refs_9_
  253.9 11.0 %down.2 = (bf16[3072,2048]{1,0:T(8,128)(2,1)}, bf16[3072,1408]{1,0:T(8,128)(2,1)}) custom-call(s32[3]{0:T(128)S(1)} %pad_add_fusion.where, bf16[768,2048]{1,0:T(8,128)(2,1)} %convolution_convert_fusion.3.rows, bf16[1024,1408]{1,0:T(8,128)(2,1)S(1)} %get-tuple-element.238.own, bf16[1024,1408]{1,0:T(8,128)(2,1)} %collective-permute-done.came), custom_call_target="tpu_custom_call" | custom-call | flops 4429185024 | bytes 14221312 | tf_op jit(solution)/shard_map/down/pallas_call | solution.py:273
  264.9 12.3 %collective-permute-done.12 = bf16[1024,512]{1,0:T(8,128)(2,1)} collective-permute-done((bf16[1024,512]{1,0:T(8,128)(2,1)}, bf16[1024,512]{1,0:T(8,128)(2,1)}, u32[]{:S(2)}, u32[]{:S(2)}) %collective-permute-start.12) | collective-permute-done | bytes 1048608 | tf_op jit(solution)/shard_map/ppermute | solution.py:26
  298.3 9.8 collective-permute-done.16.refs_11_
  313.8 33.7 %collective-permute-done.19.refs_2_ = bf16[768,512]{1,0:T(8,128)(2,1)S(1)} collective-permute-done((bf16[768,512]{1,0:T(8,128)(2,1)S(1)}, bf16[768,512]{1,0:T(8,128)(2,1)S(1)}, u32[]{:S(2)}, u32[]{:S(2)}) %collective-permute-start.19) | collective-permute-done | bytes 786464 | tf_op jit(solution)/shard_map/ppermute | solution.py:26
  355.5 30.1 %expert.4 = (bf16[3072,2048]{1,0:T(8,128)(2,1)}, bf16[3072,1408]{1,0:T(8,128)(2,1)}, bf16[3072,2816]{1,0:T(8,128)(2,1)}, bf16[768,1024]{1,0:T(8,128)(2,1)}, bf16[768,1024]{1,0:T(8,128)(2,1)}, /*index=5*/f32[1,768]{1,0:T(1,128)}) custom-call(s32[3]{0:T(128)} %copy-done.8, bf16[768,512]{1,0:T(8,128)(2,1)} %copy-done.68, bf16[768,512]{1,0:T(8,128)(2,1)} %copy-done.70, ...), custom_call_target="tpu_custom_call" | custom-call | flops 17716740096 | bytes 32768000 | tf_op jit(solution)/shard_map/expert/pallas_call | solution.py:412
  389.4 21.6 %down.3 = (bf16[3072,2048]{1,0:T(8,128)(2,1)}, bf16[3072,1408]{1,0:T(8,128)(2,1)}) custom-call(s32[3]{0:T(128)S(1)} %copy-done.9, bf16[2304,2048]{1,0:T(8,128)(2,1)} %all-gather.8.cloned.1.call-done.rows, bf16[1024,1408]{1,0:T(8,128)(2,1)S(1)} %get-tuple-element.238.own, ...), custom_call_target="tpu_custom_call", output_to_operand_aliasing={{0}: (4, {}), {1}: (5, {})} | custom-call | flops 13287555072 | bytes 31129600 | tf_op jit(solution)/shard_map/down/pallas_call | solution.py:273
  412.9 30.2 %expert.5 = (bf16[3072,2048]{1,0:T(8,128)(2,1)}, bf16[3072,1408]{1,0:T(8,128)(2,1)}, bf16[3072,2816]{1,0:T(8,128)(2,1)}, bf16[768,1024]{1,0:T(8,128)(2,1)}, bf16[768,1024]{1,0:T(8,128)(2,1)}, /*index=5*/f32[1,768]{1,0:T(1,128)}) custom-call(s32[3]{0:T(128)} %copy-done.8, ...), custom_call_target="tpu_custom_call", output_to_operand_aliasing={{0}: (17, {}), {1}: (18, {}), {2}: (19, {})} | custom-call | flops 17716740096 | bytes 32768000 | tf_op jit(solution)/shard_map/expert/pallas_call | solution.py:412
  448.4 29.9 %expert.6 = (bf16[3072,2048]{1,0:T(8,128)(2,1)}, bf16[3072,1408]{1,0:T(8,128)(2,1)}, bf16[3072,2816]{1,0:T(8,128)(2,1)}, bf16[768,1024]{1,0:T(8,128)(2,1)}, bf16[768,1024]{1,0:T(8,128)(2,1)}, /*index=5*/f32[1,768]{1,0:T(1,128)}) custom-call(s32[3]{0:T(128)} %copy-done.8, ...), custom_call_target="tpu_custom_call", output_to_operand_aliasing={{0}: (17, {}), {1}: (18, {}), {2}: (19, {})} | custom-call | flops 17716740096 | bytes 32768000 | tf_op jit(solution)/shard_map/expert/pallas_call | solution.py:412
  489.1 29.8 %expert.7 = (bf16[3072,2048]{1,0:T(8,128)(2,1)}, bf16[3072,1408]{1,0:T(8,128)(2,1)}, bf16[3072,2816]{1,0:T(8,128)(2,1)}, bf16[768,1024]{1,0:T(8,128)(2,1)}, bf16[768,1024]{1,0:T(8,128)(2,1)}, /*index=5*/f32[1,768]{1,0:T(1,128)}) custom-call(s32[3]{0:T(128)} %copy-done.8, ...), custom_call_target="tpu_custom_call", output_to_operand_aliasing={{0}: (17, {}), {1}: (18, {}), {2}: (19, {})} | custom-call | flops 17716740096 | bytes 32768000 | tf_op jit(solution)/shard_map/expert/pallas_call | solution.py:412
  525.8 26.8 %up.1 = bf16[3072,2048]{1,0:T(8,128)(2,1)} custom-call(s32[3]{0:T(128)S(1)} %copy-done.10, bf16[3072,1408]{1,0:T(8,128)(2,1)} %get-tuple-element.185.act, bf16[1024,1408]{1,0:T(8,128)(2,1)S(1)} %get-tuple-element.238.own, bf16[1024,1408]{1,0:T(8,128)(2,1)} %collective-permute-done.came), custom_call_target="tpu_custom_call" | custom-call | flops 17716740096 | bytes 27000832 | tf_op jit(solution)/shard_map/up/pallas_call | solution.py:340
  570.1 15.9 %fusion.14 = bf16[1024,1408]{1,0:T(8,128)(2,1)S(1)} fusion(bf16[3072,1408]{1,0:T(8,128)(2,1)} %get-tuple-element.185.act, bf16[3072,2048]{1,0:T(8,128)(2,1)} %get-tuple-element.160, s32[]{:T(128)S(6)} %select_n.171), kind=kOutput, calls=%fused_computation.22 | convolution fusion | flops 8859811840 | bytes 17825796 | tf_op jit(solution)/shard_map/dot_general | solution.py:30
  591.2 11.3 %collective-permute-done.44 = bf16[768,512]{1,0:T(8,128)(2,1)S(1)} collective-permute-done((bf16[768,512]{1,0:T(8,128)(2,1)}, bf16[768,512]{1,0:T(8,128)(2,1)S(1)}, u32[]{:S(2)}, u32[]{:S(2)}) %collective-permute-start.44) | collective-permute-done | bytes 786464 | tf_op jit(solution)/shard_map/ppermute | solution.py:26
  602.6 16.3 %convolution_convert_fusion.2 = bf16[512,2816]{1,0:T(8,128)(2,1)} fusion(bf16[3072,2816]{1,0:T(8,128)(2,1)} %get-tuple-element.170, bf16[3072,2048]{1,0:T(8,128)(2,1)} %get-tuple-element.158, s32[]{:T(128)S(6)} %select_n.171), kind=kOutput, calls=%fused_computation.18 | convolution fusion | flops 8859811840 | bytes 23330820 | tf_op jit(solution)/shard_map/dot_general | solution.py:30
  621.5 12.5 %convolution_convert_fusion.1 = bf16[512,2816]{1,0:T(8,128)(2,1)} fusion(bf16[3072,2816]{1,0:T(8,128)(2,1)S(1)} %bitcast.157, bf16[3072,2048]{1,0:T(8,128)(2,1)} %get-tuple-element.158, s32[]{:T(128)S(6)} %select_n.172), kind=kOutput, calls=%fused_computation.17 | convolution fusion | flops 8859811840 | bytes 23330820 | tf_op jit(solution)/shard_map/dot_general | solution.py:30
  660.7 26.2 %fusion.11.refs_0_ = bf16[1024,2816]{1,0:T(8,128)(2,1)} fusion(bf16[3072,2816]{1,0:T(8,128)(2,1)} %get-tuple-element.170, bf16[3072,2048]{1,0:T(8,128)(2,1)} %get-tuple-element.158, s32[]{:T(128)S(6)} %select_n.174), kind=kOutput, calls=%fused_computation.16 | convolution fusion | flops 17719623680 | bytes 29360132 | tf_op jit(solution)/shard_map/dot_general | solution.py:30
  721.4 15.6 %attention_back.1.left = bf16[1024,1536]{1,0:T(8,128)(2,1)} custom-call(bf16[1024,512]{1,0:T(8,128)(2,1)S(1)} %copy-done.12, bf16[1024,512]{1,0:T(8,128)(2,1)S(1)} %copy-done.14, bf16[1024,512]{1,0:T(8,128)(2,1)S(1)} %copy-done.16, f32[4,1024,1]{2,1,0:T(8,128)} %get-tuple-element.179.logs, bf16[1024,512]{1,0:T(8,128)(2,1)S(1)} %copy-done.17, ...), custom_call_target="tpu_custom_call" | custom-call | flops 3355443200 | bytes 8388608 | tf_op jit(solution)/shard_map/attention_back/pallas_call | solution.py:188
  746.0 10.6 %convolution_convert_fusion = bf16[2048,1536]{1,0:T(8,128)(2,1)} fusion(bf16[1024,2048]{1,0:T(8,128)(2,1)S(1)} %copy-done.26, bf16[1024,1536]{1,0:T(8,128)(2,1)} %attention_back.1.left), kind=kOutput, calls=%fused_computation.7 | convolution fusion | flops 6445596672 | bytes 13631488 | tf_op jit(solution)/shard_map/dot_general | solution.py:30
  756.6 9.3 collective-permute-done.56
  765.9 11.4 %spread.3 = (bf16[1024,1024]{1,0:T(8,128)(2,1)S(1)}, bf16[1024,1024]{1,0:T(8,128)(2,1)S(1)}) custom-call(s32[3]{0:T(128)S(1)} %copy-done.10, bf16[1024,1536]{1,0:T(8,128)(2,1)} %attention_back.1.left, bf16[2048,2176]{1,0:T(8,128)(2,1)} %all-gather.4.cloned.1.call-done.right), custom_call_target="tpu_custom_call" | custom-call | flops 6442450944 | bytes 13631488 | tf_op jit(solution)/shard_map/spread/pallas_call | solution.py:311
  781.0 15.6 %collective-permute-start.57 = (bf16[768,512]{1,0:T(8,128)(2,1)S(1)}, bf16[768,512]{1,0:T(8,128)(2,1)S(1)}, u32[]{:S(2)}, u32[]{:S(2)}) collective-permute-start(bf16[768,512]{1,0:T(8,128)(2,1)S(1)} %get-tuple-element.175), channel_id=1, source_target_pairs={{0,8},{4,12},{8,0},{12,4},{16,24},{20,28},{24,16},{28,20},{1,9},{5... | collective-permute-start | bytes 2359304 | tf_op jit(solution)/shard_map/ppermute | solution.py:26
  802.2 17.0 %collective-permute-done.57 = bf16[768,512]{1,0:T(8,128)(2,1)S(1)} collective-permute-done((bf16[768,512]{1,0:T(8,128)(2,1)S(1)}, bf16[768,512]{1,0:T(8,128)(2,1)S(1)}, u32[]{:S(2)}, u32[]{:S(2)}) %collective-permute-start.57) | collective-permute-done | bytes 786464 | tf_op jit(solution)/shard_map/ppermute | solution.py:26
  821.9 14.3 %fusion.17.refs_3_ = bf16[1024,1408]{1,0:T(8,128)(2,1)S(1)} fusion(bf16[3072,1408]{1,0:T(8,128)(2,1)} %get-tuple-element.185.act, bf16[3072,2048]{1,0:T(8,128)(2,1)} %get-tuple-element.160, s32[]{:T(128)S(6)} %select_n.174), kind=kOutput, calls=%fused_computation.23 | convolution fusion | flops 8859811840 | bytes 17825796 | tf_op jit(solution)/shard_map/dot_general | solution.py:30
  836.3 9.3 collective-permute-done.62
  850.1 23.4 %collective-permute-done.64 = f32[1,1024]{1,0:T(1,128)S(1)} collective-permute-done((f32[1,1024]{1,0:T(1,128)S(1)}, f32[1,1024]{1,0:T(1,128)S(1)}, u32[]{:S(2)}, u32[]{:S(2)}) %collective-permute-start.64) | collective-permute-done | bytes 4128 | tf_op jit(solution)/shard_map/ppermute | solution.py:26
  876.4 59.0 %collective-permute-done.65.refs_2_ = bf16[512,2816]{1,0:T(8,128)(2,1)S(1)} collective-permute-done((bf16[512,2816]{1,0:T(8,128)(2,1)}, bf16[512,2816]{1,0:T(8,128)(2,1)S(1)}, u32[]{:S(2)}, u32[]{:S(2)}) %collective-permute-start.65) | collective-permute-done | bytes 2883616 | tf_op jit(solution)/shard_map/ppermute | solution.py:26
  939.0 20.7 %collective-permute-done.69 = f32[6,2048]{1,0:T(8,128)S(1)} collective-permute-done((f32[6,2048]{1,0:T(8,128)S(1)}, f32[6,2048]{1,0:T(8,128)S(1)}, u32[]{:S(2)}, u32[]{:S(2)}) %collective-permute-start.69) | collective-permute-done | bytes 49184 | tf_op jit(solution)/shard_map/ppermute | solution.py:26
  970.3 11.2 %expert_grad_sum.1 = f32[3,1024,1408]{2,1,0:T(8,128)} custom-call(bf16[1024,2816]{1,0:T(8,128)(2,1)} %fusion.11.refs_0_, bf16[512,2816]{1,0:T(8,128)(2,1)S(1)} %pad_maximum_fusion.1.refs_1_, bf16[512,2816]{1,0:T(8,128)(2,1)S(1)} %collective-permute-done.65.refs_2_, bf16[1024,1408]{1,0:T(8,128)(2,1)S(1)} %fusion.17.refs_3_, ...), custom_call_target="tpu_custom_call" | custom-call | flops 4325376 | bytes 34603008 | tf_op jit(solution)/shard_map/expert_grad_sum/pallas_call | solution.py:496
  (472 shorter events, 283.5 us)
Async XLA Ops:
  7.2 183.3 %all-gather.4.cloned.1.call-start = ((), (), s32[]{:S(2)}) async-start(), calls=%async_computation.3 | async-start | bytes 10027008 | tf_op jit(solution)/shard_map/all_gather | solution.py:596
  10.3 272.4 %all-gather.6.cloned.1.call-start = ((), (), s32[]{:S(2)}) async-start(), calls=%async_computation.4 | async-start | bytes 5242880 | tf_op jit(solution)/shard_map/all_gather | solution.py:663
  14.5 178.4 %collective-permute-start.5 = (f32[1,768]{1,0:T(1,128)S(1)}, f32[1,768]{1,0:T(1,128)S(1)}, u32[]{:S(2)}, u32[]{:S(2)}) collective-permute-start(f32[1,768]{1,0:T(1,128)S(1)} %fusion.36), channel_id=1, source_target_pairs={{0,8},{4,12},{8,0},{12,4},{16,24},{20,28},{24,16},{28,20},{1,9},{5... | collective-permute-start | bytes 9224 | tf_op jit(solution)/shard_map/ppermute | solution.py:26
  18.1 176.3 %collective-permute-start.6 = (f32[1,768]{1,0:T(1,128)S(1)}, f32[1,768]{1,0:T(1,128)S(1)}, u32[]{:S(2)}, u32[]{:S(2)}) collective-permute-start(f32[1,768]{1,0:T(1,128)S(1)} %fusion.31), channel_id=1, source_target_pairs={{0,16},{4,20},{8,24},{12,28},{16,0},{20,4},{24,8},{28,12},{1,17},{... | collective-permute-start | bytes 9224 | tf_op jit(solution)/shard_map/ppermute | solution.py:26
  21.3 178.7 %collective-permute-start.7 = (f32[1,768]{1,0:T(1,128)S(1)}, f32[1,768]{1,0:T(1,128)S(1)}, u32[]{:S(2)}, u32[]{:S(2)}) collective-permute-start(f32[1,768]{1,0:T(1,128)S(1)} %fusion.26), channel_id=1, source_target_pairs={{0,24},{4,28},{8,16},{12,20},{16,8},{20,12},{24,0},{28,4},{1,25},{... | collective-permute-start | bytes 9224 | tf_op jit(solution)/shard_map/ppermute | solution.py:26
  21.3 178.7 %collective-permute-start.2 = (f32[1,1024]{1,0:T(1,128)S(1)}, f32[1,1024]{1,0:T(1,128)S(1)}, u32[]{:S(2)}, u32[]{:S(2)}) collective-permute-start(f32[1,1024]{1,0:T(1,128)S(1)} %get-tuple-element.277), channel_id=1, source_target_pairs={{0,8},{4,12},{8,0},{12,4},{16,24},{20,28},{24,16},{28,20},{1,9},{5... | collective-permute-start | bytes 12296 | tf_op jit(solution)/shard_map/ppermute | solution.py:26
  28.0 99.9 %collective-permute-start = (bf16[1024,1408]{1,0:T(8,128)(2,1)S(1)}, bf16[1024,1408]{1,0:T(8,128)(2,1)}, u32[]{:S(2)}, u32[]{:S(2)}) collective-permute-start(bf16[1024,1408]{1,0:T(8,128)(2,1)S(1)} %get-tuple-element.238.own), channel_id=1, source_target_pairs={{0,4},{4,0},{8,12},{12,8},{16,20},{20,16},{24,28},{28,24},{1,5},{5... | collective-permute-start | bytes 8650760 | tf_op jit(solution)/shard_map/ppermute | solution.py:26
  127.8 72.2 %collective-permute-start.1 = (bf16[320,1408]{1,0:T(8,128)(2,1)}, bf16[320,1408]{1,0:T(8,128)(2,1)}, u32[]{:S(2)}, u32[]{:S(2)}) collective-permute-start(bf16[320,1408]{1,0:T(8,128)(2,1)} %slice_bitcast_fusion.4), channel_id=1, source_target_pairs={{0,4},{4,0},{8,12},{12,8},{16,20},{20,16},{24,28},{28,24},{1,5},{5... | collective-permute-start | bytes 2703368 | tf_op jit(solution)/shard_map/ppermute | solution.py:26
  200.5 188.9 %all-gather.8.cloned.1.call-start = ((), (), s32[]{:S(2)}) async-start(), calls=%async_computation.5 | async-start | bytes 11796480 | tf_op jit(solution)/shard_map/all_gather | solution.py:699
  288.8 367.7 %reduce-scatter.4.cloned.1.call-start = ((), (), s32[]{:S(2)}) async-start(), calls=%async_computation.6 | async-start | bytes 15728640 | tf_op jit(solution)/shard_map/reduce_scatter | solution.py:773
  309.2 44.5 %collective-permute-start.21 = (bf16[656,1408]{1,0:T(8,128)(2,1)S(1)}, bf16[656,1408]{1,0:T(8,128)(2,1)S(1)}, u32[]{:S(2)}, u32[]{:S(2)}) collective-permute-start(bf16[656,1408]{1,0:T(8,128)(2,1)S(1)} %slice_bitcast_fusion.3), channel_id=1, source_target_pairs={{0,4},{4,0},{8,12},{12,8},{16,20},{20,16},{24,28},{28,24},{1,5},{5... | collective-permute-start | bytes 5541896 | tf_op jit(solution)/shard_map/ppermute | solution.py:26
  313.2 39.0 %collective-permute-start.23 = (bf16[768,512]{1,0:T(8,128)(2,1)S(1)}, bf16[768,512]{1,0:T(8,128)(2,1)}, u32[]{:S(2)}, u32[]{:S(2)}) collective-permute-start(bf16[768,512]{1,0:T(8,128)(2,1)S(1)} %fusion.99), channel_id=1, source_target_pairs={{0,8},{4,12},{8,0},{12,4},{16,24},{20,28},{24,16},{28,20},{1,9},{5... | collective-permute-start | bytes 2359304 | tf_op jit(solution)/shard_map/ppermute | solution.py:26
  313.8 39.9 %collective-permute-start.18 = (bf16[768,512]{1,0:T(8,128)(2,1)S(1)}, bf16[768,512]{1,0:T(8,128)(2,1)S(1)}, u32[]{:S(2)}, u32[]{:S(2)}) collective-permute-start(bf16[768,512]{1,0:T(8,128)(2,1)S(1)} %fusion.98.refs_0_), channel_id=1, source_target_pairs={{0,1},{1,0},{2,3},{3,2},{4,5},{5,4},{6,7},{7,6},{8,9},{9,8},{10,11... | collective-permute-start | bytes 2359304 | tf_op jit(solution)/shard_map/ppermute | solution.py:26
  353.7 57.2 %collective-permute-start.24 = (bf16[768,512]{1,0:T(8,128)(2,1)}, bf16[768,512]{1,0:T(8,128)(2,1)}, u32[]{:S(2)}, u32[]{:S(2)}) collective-permute-start(bf16[768,512]{1,0:T(8,128)(2,1)} %collective-permute-done.23.refs_0_), channel_id=1, source_target_pairs={{0,1},{1,0},{2,3},{3,2},{4,5},{5,4},{6,7},{7,6},{8,9},{9,8},{10,11... | collective-permute-start | bytes 2359304 | tf_op jit(solution)/shard_map/ppermute | solution.py:26
  387.3 55.7 %collective-permute-start.30 = (bf16[768,512]{1,0:T(8,128)(2,1)}, bf16[768,512]{1,0:T(8,128)(2,1)}, u32[]{:S(2)}, u32[]{:S(2)}) collective-permute-start(bf16[768,512]{1,0:T(8,128)(2,1)} %collective-permute-done.17.refs_0_), channel_id=1, source_target_pairs={{0,2},{1,3},{2,0},{3,1},{4,6},{5,7},{6,4},{7,5},{8,10},{9,11},{10,... | collective-permute-start | bytes 2359304 | tf_op jit(solution)/shard_map/ppermute | solution.py:26
  388.8 59.1 %collective-permute-start.29 = (bf16[768,512]{1,0:T(8,128)(2,1)}, bf16[768,512]{1,0:T(8,128)(2,1)}, u32[]{:S(2)}, u32[]{:S(2)}) collective-permute-start(bf16[768,512]{1,0:T(8,128)(2,1)} %collective-permute-done.17.refs_0_), channel_id=1, source_target_pairs={{0,1},{1,0},{2,3},{3,2},{4,5},{5,4},{6,7},{7,6},{8,9},{9,8},{10,11... | collective-permute-start | bytes 2359304 | tf_op jit(solution)/shard_map/ppermute | solution.py:26
  388.8 54.5 %collective-permute-start.32 = (bf16[768,1024]{1,0:T(8,128)(2,1)}, bf16[768,1024]{1,0:T(8,128)(2,1)}, u32[]{:S(2)}, u32[]{:S(2)}) collective-permute-start(bf16[768,1024]{1,0:T(8,128)(2,1)} %get-tuple-element.132), channel_id=1, source_target_pairs={{0,1},{1,0},{2,3},{3,2},{4,5},{5,4},{6,7},{7,6},{8,9},{9,8},{10,11... | collective-permute-start | bytes 4718600 | tf_op jit(solution)/shard_map/ppermute | solution.py:26
  447.9 41.2 %collective-permute-start.27 = (bf16[768,512]{1,0:T(8,128)(2,1)}, bf16[768,512]{1,0:T(8,128)(2,1)}, u32[]{:S(2)}, u32[]{:S(2)}) collective-permute-start(bf16[768,512]{1,0:T(8,128)(2,1)} %collective-permute-done.22.refs_0_), channel_id=1, source_target_pairs={{0,1},{1,0},{2,3},{3,2},{4,5},{5,4},{6,7},{7,6},{8,9},{9,8},{10,11... | collective-permute-start | bytes 2359304 | tf_op jit(solution)/shard_map/ppermute | solution.py:26
  447.9 38.3 %collective-permute-start.34 = (bf16[768,1024]{1,0:T(8,128)(2,1)}, bf16[768,1024]{1,0:T(8,128)(2,1)}, u32[]{:S(2)}, u32[]{:S(2)}) collective-permute-start(bf16[768,1024]{1,0:T(8,128)(2,1)} %get-tuple-element.139), channel_id=1, source_target_pairs={{0,1},{1,0},{2,3},{3,2},{4,5},{5,4},{6,7},{7,6},{8,9},{9,8},{10,11... | collective-permute-start | bytes 4718600 | tf_op jit(solution)/shard_map/ppermute | solution.py:26
  557.9 427.7 %reduce-scatter.8.cloned.1.call-start = ((), (), s32[]{:S(2)}) async-start(), calls=%async_computation.8 | async-start | bytes 2359296 | tf_op jit(solution)/shard_map/reduce_scatter | solution.py:836
  568.6 52.9 %collective-permute-start.46 = (bf16[768,512]{1,0:T(8,128)(2,1)}, bf16[768,512]{1,0:T(8,128)(2,1)S(1)}, u32[]{:S(2)}, u32[]{:S(2)}) collective-permute-start(bf16[768,512]{1,0:T(8,128)(2,1)} %add_convert_fusion.4), channel_id=1, source_target_pairs={{0,16},{4,20},{8,24},{12,28},{16,0},{20,4},{24,8},{28,12},{1,17},{... | collective-permute-start | bytes 2359304 | tf_op jit(solution)/shard_map/ppermute | solution.py:26
  589.1 48.2 %collective-permute-start.47 = (bf16[768,512]{1,0:T(8,128)(2,1)S(1)}, bf16[768,512]{1,0:T(8,128)(2,1)S(1)}, u32[]{:S(2)}, u32[]{:S(2)}) collective-permute-start(bf16[768,512]{1,0:T(8,128)(2,1)S(1)} %add_convert_fusion.3), channel_id=1, source_target_pairs={{0,24},{4,28},{8,16},{12,20},{16,8},{20,12},{24,0},{28,4},{1,25},{... | collective-permute-start | bytes 2359304 | tf_op jit(solution)/shard_map/ppermute | solution.py:26
  648.9 38.0 %collective-permute-start.53 = (bf16[128,2816]{1,0:T(8,128)(2,1)}, bf16[128,2816]{1,0:T(8,128)(2,1)}, u32[]{:S(2)}, u32[]{:S(2)}) collective-permute-start(bf16[128,2816]{1,0:T(8,128)(2,1)} %slice.358), channel_id=1, source_target_pairs={{0,4},{4,0},{8,12},{12,8},{16,20},{20,16},{24,28},{28,24},{1,5},{5... | collective-permute-start | bytes 2162696 | tf_op jit(solution)/shard_map/ppermute | solution.py:26
  650.1 40.3 %collective-permute-start.52 = (bf16[384,1408]{1,0:T(8,128)(2,1)}, bf16[384,1408]{1,0:T(8,128)(2,1)}, u32[]{:S(2)}, u32[]{:S(2)}) collective-permute-start(bf16[384,1408]{1,0:T(8,128)(2,1)} %slice.357), channel_id=1, source_target_pairs={{0,4},{4,0},{8,12},{12,8},{16,20},{20,16},{24,28},{28,24},{1,5},{5... | collective-permute-start | bytes 3244040 | tf_op jit(solution)/shard_map/ppermute | solution.py:26
  715.1 283.8 %reduce-scatter.6.cloned.1.call-start = ((), (), s32[]{:S(2)}) async-start(), calls=%async_computation.7 | async-start | bytes 7077888 | tf_op jit(solution)/shard_map/reduce_scatter | solution.py:844
  777.3 42.9 %collective-permute-start.61 = (bf16[1024,1024]{1,0:T(8,128)(2,1)S(1)}, bf16[1024,1024]{1,0:T(8,128)(2,1)S(1)}, u32[]{:S(2)}, u32[]{:S(2)}) collective-permute-start(bf16[1024,1024]{1,0:T(8,128)(2,1)S(1)} %get-tuple-element.184), channel_id=1, source_target_pairs={{0,1},{1,0},{2,3},{3,2},{4,5},{5,4},{6,7},{7,6},{8,9},{9,8},{10,11... | collective-permute-start | bytes 6291464 | tf_op jit(solution)/shard_map/ppermute | solution.py:26
  781.0 38.1 %collective-permute-start.57 = (bf16[768,512]{1,0:T(8,128)(2,1)S(1)}, bf16[768,512]{1,0:T(8,128)(2,1)S(1)}, u32[]{:S(2)}, u32[]{:S(2)}) collective-permute-start(bf16[768,512]{1,0:T(8,128)(2,1)S(1)} %get-tuple-element.175), channel_id=1, source_target_pairs={{0,8},{4,12},{8,0},{12,4},{16,24},{20,28},{24,16},{28,20},{1,9},{5... | collective-permute-start | bytes 2359304 | tf_op jit(solution)/shard_map/ppermute | solution.py:26
  800.1 76.3 %collective-permute-start.66 = (bf16[240,2816]{1,0:T(8,128)(2,1)}, bf16[240,2816]{1,0:T(8,128)(2,1)}, u32[]{:S(2)}, u32[]{:S(2)}) collective-permute-start(bf16[240,2816]{1,0:T(8,128)(2,1)} %slice.369), channel_id=1, source_target_pairs={{0,4},{4,0},{8,12},{12,8},{16,20},{20,16},{24,28},{28,24},{1,5},{5... | collective-permute-start | bytes 4055048 | tf_op jit(solution)/shard_map/ppermute | solution.py:26
  801.4 134.0 %collective-permute-start.65 = (bf16[512,2816]{1,0:T(8,128)(2,1)}, bf16[512,2816]{1,0:T(8,128)(2,1)S(1)}, u32[]{:S(2)}, u32[]{:S(2)}) collective-permute-start(bf16[512,2816]{1,0:T(8,128)(2,1)} %convolution_convert_fusion.1), channel_id=1, source_target_pairs={{0,4},{4,0},{8,12},{12,8},{16,20},{20,16},{24,28},{28,24},{1,5},{5... | collective-permute-start | bytes 8650760 | tf_op jit(solution)/shard_map/ppermute | solution.py:26
  847.8 114.1 %collective-permute-start.58 = (bf16[1024,512]{1,0:T(8,128)(2,1)S(1)}, bf16[1024,512]{1,0:T(8,128)(2,1)S(1)}, u32[]{:S(2)}, u32[]{:S(2)}) collective-permute-start(bf16[1024,512]{1,0:T(8,128)(2,1)S(1)} %add_convert_fusion.1), channel_id=1, source_target_pairs={{0,2},{1,3},{2,0},{3,1},{4,6},{5,7},{6,4},{7,5},{8,10},{9,11},{10,... | collective-permute-start | bytes 3145736 | tf_op jit(solution)/shard_map/ppermute | solution.py:26
  850.0 86.3 %collective-permute-start.68 = (f32[6,2048]{1,0:T(8,128)S(1)}, f32[6,2048]{1,0:T(8,128)S(1)}, u32[]{:S(2)}, u32[]{:S(2)}) collective-permute-start(f32[6,2048]{1,0:T(8,128)S(1)} %fusion.120), channel_id=1, source_target_pairs={{0,1},{1,0},{2,3},{3,2},{4,5},{5,4},{6,7},{7,6},{8,9},{9,8},{10,11... | collective-permute-start | bytes 147464 | tf_op jit(solution)/shard_map/ppermute | solution.py:26
  935.4 46.2 %collective-permute-start.67 = (bf16[1024,512]{1,0:T(8,128)(2,1)S(1)}, bf16[1024,512]{1,0:T(8,128)(2,1)S(1)}, u32[]{:S(2)}, u32[]{:S(2)}) collective-permute-start(bf16[1024,512]{1,0:T(8,128)(2,1)S(1)} %fusion.55), channel_id=1, source_target_pairs={{0,2},{1,3},{2,0},{3,1},{4,6},{5,7},{6,4},{7,5},{8,10},{9,11},{10,... | collective-permute-start | bytes 3145736 | tf_op jit(solution)/shard_map/ppermute | solution.py:26
  (136 other events, 2066.8 us)
Sparse Core Ops, SparseCore 0:
  10.8 179.6 all-gather.3
  200.6 82.0 all-gather.5
  288.9 93.8 all-gather.7
  558.0 97.5 reduce-scatter.3
  715.2 87.5 reduce-scatter.7
  806.3 143.4 reduce-scatter.5

commit v8 on v7

--- a/solution.py
+++ b/solution.py
@@ -230,14 +230,13 @@
 
 
 cuts = (
-    ((0, 0, 40),),
+    ((0, 0, 16),),
+    ((0, 16, 40),),
     ((0, 40, 56),),
-    ((0, 56, 80),),
-    ((0, 80, 96),),
-    ((0, 96, 128), (1, 0, 20)),
-    ((1, 20, 46),),
-    ((1, 46, 128),),
+    ((0, 56, 108),),
+    ((0, 108, 128), (1, 0, 128)),
 )
+order = (0, 2, 3, 1)
 
 
 def pair_pieces(own_gate, own_up, *came):
@@ -652,7 +651,6 @@
         ]
         crossing.append(group_send(jnp.concatenate(pieces, 0), *crossing[-1:], *others))
 
-    cross(down[1])
     cross(first)
 
     grad_own = own_columns(cotangent)
@@ -671,12 +669,12 @@
     scale_one = lax.rsqrt(jnp.mean(inputs * inputs, axis=1, keepdims=True) + epsilon)
     normed_in = (inputs * scale_one * gain_first).astype(low)
     inputs_own = own_columns(tokens).astype(full)
-    normed_in = after(normed_in, crossing[0], grad_mine, *slots_came, *routed)
+    normed_in = after(normed_in, down[1], grad_mine, *slots_came, *routed)
     qkv = jnp.dot(normed_in, qkv_flat, preferred_element_type=full)
     cross(qkv)
     cosine, sine = rotary_tables()
     context, query, keys, values, logs = attention(qkv, cosine, sine, scale)
-    context = after(context, crossing[2])
+    context = after(context, crossing[1])
     cross(context)
     attn_parts = spread_dot(where, context, first, 3, tensor_count)
     rows_raw = []
@@ -686,13 +684,13 @@
     def down_filler(sent):
         cross(sent)
         rows_raw.extend(down_pass(where, after(grad_mine, sent), *down, 0, total, ()))
-        return (rows_raw[1], crossing[4])
-
-    hidden = inputs_own + near_reduce(*attn_parts, [], crossing[3], filler=down_filler)
+        return (rows_raw[1], crossing[3])
+
+    hidden = inputs_own + near_reduce(*attn_parts, [], crossing[2], filler=down_filler)
     cross(rows_raw[1])
     grad_planes = after(grad_planes, hidden)
     grad_packed = []
-    for s in range(1, EXPERTS):
+    for s in order[1:]:
         source = lax.dynamic_slice_in_dim(grad_planes, (expert ^ s) * rows, rows, 0)
         taken = (places.astype(full) == slots_came[s]).astype(low)
         grad_packed.append(jnp.dot(taken, source, preferred_element_type=full).astype(low))
@@ -719,45 +717,57 @@
         b = (value - a.astype(full)).astype(low)
         return jnp.stack([a, b, (value - a.astype(full) - b.astype(full)).astype(low)])
 
-    moe_packed = packed(after(moe_in, crossing[5]))
-    cross(moe_packed[0])
+    moe_packed = packed(moe_in)
     pair = (gate_mine, up_mine, *crossing)
-    crossed = [moe_packed[0]] + [
-        swap(moe_packed[s], "dp", s * group_count) for s in range(1, EXPERTS - 1)
-    ]
+    crossed = {2: swap(moe_packed[2], "dp", 2 * group_count)}
+    crossed[3] = swap(after(moe_packed[3], crossed[2]), "dp", 3 * group_count)
     arrived = [near_blocks(moe_packed[0])]
 
     carried = ()
     sums_sent = []
+    came_home = {}
     returned = []
     gate_grads = []
     router_block = first[:, 4 * size :]
     for step in range(EXPERTS):
-        named_sum = routed[step]
+        named_sum = routed[order[step]]
         if step == 1:
             rows_raw = down_pass(where, after(grad_rest, even), *down, MOST, total, rows_raw)
+            named_sum = after(named_sum, crossed[3])
         if step == 2:
-            named_sum = after(named_sum, sums_sent[0])
+            named_sum = after(named_sum, crossed[1], *sums_sent)
         if step == 3:
-            named_sum = after(named_sum, sums_sent[1], returned[0])
+            named_sum = after(named_sum, sums_sent[2])
         moe_rows, activation, pre_grad, even, odd, gate_grad = expert_pass(
             step, where, arrived[step], pair, rows_raw[1], named_sum, router_block, carried
         )
         carried = (moe_rows, activation, pre_grad)
         if step == 0:
-            arrived.append(near_blocks(crossed[1], even))
-            crossed[2] = after(crossed[2], even)
-            crossed.append(swap(after(moe_packed[3], crossed[2]), "dp", 3 * group_count))
-        if step == 1:
             arrived.append(near_blocks(crossed[2], even))
             crossed[3] = after(crossed[3], even)
+            crossed[1] = swap(after(moe_packed[1], crossed[3]), "dp", group_count)
+        if step == 1:
+            arrived.append(near_blocks(crossed[3], even))
+            odd = after(odd, crossed[1], arrived[2][tensor_count // 2])
         if step == 2:
-            arrived.append(near_blocks(crossed[3], even))
-        returned.append(near_reduce(even, odd, sums_sent, *returned[2:]).astype(low))
+            arrived.append(near_blocks(crossed[1], even))
+        if step == 2:
+            odd = after(odd, *returned, arrived[3][tensor_count // 2])
+        if step == 3:
+            came_home[2] = swap(returned[1], "dp", 2 * group_count)
+            odd = after(odd, returned[2], came_home[2])
+        returned.append(near_reduce(even, odd, sums_sent).astype(low))
         gate_grads.append(gate_grad)
-    own_returned = returned
-    returned = exchange(returned)
-    gate_grad_near = exchange([gate_grads[0]] + [after(v, even) for v in gate_grads[1:]])
+
+    def home(parts):
+        return {
+            s: swap(v, "dp", s * group_count) if s else v for s, v in zip(order, parts)
+        }
+
+    came_home[0] = returned[0]
+    came_home[3] = swap(returned[2], "dp", 3 * group_count)
+    came_home[1] = swap(returned[3], "dp", group_count)
+    gate_grad_near = home([gate_grads[0]] + [after(v, even) for v in gate_grads[1:]])
     grad_rows = rows_raw[0]
 
     def term(left, right):
@@ -768,25 +778,18 @@
         return part
 
     unit = half // 128
-    expert_part = up_pass(where, after(activation, sums_sent[2], own_returned[1]), *down)
-    expert_part = after(expert_part, sums_sent[3], own_returned[2])
-    expert_own = lax.psum_scatter(expert_part, "tensor", scatter_dimension=1, tiled=True)
-    act_late = after(activation, expert_part)
+    quarter = half // 2
+    act_late = after(activation, sums_sent[3], returned[2])
     down_given = term(grad_rows, act_late)(given_at, half)
     down_sums = [group_send(down_given[: 40 * unit])]
-    pair_term = term(
-        moe_rows, after(pre_grad, down_given, own_returned[3], returned[1], *gate_grad_near)
-    )
-    quarter = half // 2
-    pair_given = [pair_term(given_at, quarter)]
-    down_sums.append(group_send(down_given[40 * unit : 80 * unit], down_sums[0], pair_given[0]))
-    pair_term = term(moe_rows, after(pre_grad, pair_given[0], down_sums[0], returned[2]))
-    pair_given.append(pair_term(given_at + quarter, quarter))
-    returned = [after(v, *pair_given) for v in returned]
-    returned[3] = after(returned[3], down_sums[1])
-    down_sums.append(group_send(down_given[80 * unit :], down_sums[1]))
-    pair_sums = [group_send(pair_given[0][: 16 * unit], down_sums[1])]
-    back = unpacked(returned)
+    expert_part = up_pass(
+        where, after(activation, down_given, returned[3], *gate_grad_near.values()), *down
+    )
+    expert_part = after(expert_part, down_sums[0], came_home[3], came_home[1])
+    expert_own = lax.psum_scatter(expert_part, "tensor", scatter_dimension=1, tiled=True)
+    down_sums.append(group_send(down_given[40 * unit : 80 * unit], down_sums[0]))
+    came_home = {s: after(v, expert_part) for s, v in came_home.items()}
+    back = unpacked([came_home[s] for s in range(EXPERTS)])
 
     gate_grad = jnp.concatenate(
         [
@@ -813,37 +816,43 @@
     )
     router_grad = jnp.dot(logit_grad, moe_in, preferred_element_type=full)
     moe_gain_grad = jnp.sum(moe_grad * normed_two, axis=0)
-    kept = {}
-    outputs = {0: expert_own[:MOST]}
-
-    def keep_pair(sent):
-        kept["pair"] = term(moe_rows, after(pre_grad, sent, expert_own))(mine_at, half)
-        outputs[2] = swap(expert_own[2 * MOST : 3 * MOST], "dp", 2 * group_count)
-        return (kept["pair"], down_sums[2], pair_sums[0], outputs[2])
-
-    def keep_down(sent):
-        kept["down"] = term(grad_rows, after(activation, sent))(mine_at, half)
-        return (kept["down"], outputs[1])
-
-    attn_grad = tensor_gather(hidden_grad.astype(low), keep_pair)
-    pair_sums.append(
-        group_send(pair_given[0][16 * unit : 34 * unit], pair_sums[0], down_sums[2], kept["pair"])
-    )
+    pair_given = []
+    kept = []
+
+    def give_pair(sent):
+        down_sums.append(group_send(down_given[80 * unit :], down_sums[1], sent))
+        pair_term = term(moe_rows, after(pre_grad, sent, down_sums[1]))
+        pair_given.extend(pair_term(given_at + k * quarter, quarter) for k in range(2))
+        return (*pair_given, down_sums[2])
+
+    attn_grad = tensor_gather(hidden_grad.astype(low), give_pair)
+    pair_sums = [group_send(pair_given[0][: 16 * unit], down_sums[2])]
     context_grad = jnp.dot(attn_grad, out_full, preferred_element_type=full).astype(low)
-    for s in (3, 1):
-        part = after(expert_own[s * MOST : (s + 1) * MOST], context_grad, *list(outputs.values())[1:])
-        outputs[s] = swap(part, "dp", s * group_count)
-    out_shard = lax.psum_scatter(
-        contract(after(attn_grad, context_grad), context, 0, 0).astype(low), "dp", scatter_dimension=0, tiled=True
-    ).astype(full)
+    out_grad = contract(after(attn_grad, context_grad), context, 0, 0).astype(low)
     qkv_grad_rows = attention_back(query, keys, values, logs, context_grad, cosine, sine, scale)
-    qkv_grad_rows = after(qkv_grad_rows, pair_sums[1])
+    qkv_grad_rows = after(qkv_grad_rows, pair_sums[0], out_grad)
     qkv_grad = contract(normed_in, qkv_grad_rows, 0, 0).astype(low)
-    pair_sums.append(group_send(pair_given[0][34 * unit :], pair_sums[1], qkv_grad))
-    pair_last = group_send(pair_given[1], pair_sums[1], qkv_grad)
-    qkv_shard = lax.psum_scatter(qkv_grad, "dp", scatter_dimension=0, tiled=True).astype(full)
-    parts = spread_dot(where, after(qkv_grad_rows, qkv_grad, outputs[3]), first, 0, tensor_count)
-    normed_grad = near_reduce(*parts, [], filler=keep_down)
+    grads_both = jnp.concatenate([qkv_grad, out_grad], 1)
+    shards = lax.psum_scatter(grads_both, "dp", scatter_dimension=0, tiled=True)
+    pair_sums.append(group_send(pair_given[0][16 * unit : 32 * unit], pair_sums[0], grads_both))
+    pair_sums.append(group_send(pair_given[0][32 * unit :], pair_sums[1]))
+    pair_last = group_send(pair_given[1], pair_sums[2])
+    outputs = {}
+
+    def keep(sent):
+        part = after(expert_own[MOST : 2 * MOST], sent)
+        outputs[2] = swap(part, "dp", 2 * group_count)
+        late = after(pre_grad, sent, expert_own)
+        kept.append(term(moe_rows, late)(mine_at, half))
+        kept.append(term(grad_rows, after(activation, kept[0]))(mine_at, half))
+        return (*kept, outputs[2], pair_sums[1])
+
+    parts = spread_dot(where, after(qkv_grad_rows, grads_both), first, 0, tensor_count)
+    normed_grad = near_reduce(*parts, [], filler=keep)
+    outputs[0] = expert_own[:MOST]
+    for k in (2, 3):
+        part = after(expert_own[k * MOST : (k + 1) * MOST], outputs[2])
+        outputs[order[k]] = swap(part, "dp", order[k] * group_count)
     normed_one = inputs_own * scale_one
     scaled_in = normed_grad * gain_first_own
     attn_gain_grad = jnp.sum(normed_grad * normed_one, axis=0)
@@ -854,20 +863,20 @@
         jnp.zeros((mine.shape[0], width), full), mine, place * size, 1
     )
     mine = all_sum(mine)
-    input_own = after(input_own, pair_last, pair_sums[2])
+    input_own = after(input_own, outputs[3], outputs[1], pair_sums[2])
     expert_grad = expert_grad_sum(
-        group_finish(
-            kept["pair"], [jnp.concatenate(pair_sums, 0), pair_last], member, group_count
-        ),
-        group_finish(kept["down"], [jnp.concatenate(down_sums, 0)], member, group_count),
+        group_finish(kept[0], [jnp.concatenate(pair_sums, 0), pair_last], member, group_count),
+        group_finish(kept[1], [jnp.concatenate(down_sums, 0)], member, group_count),
         hidden_size,
     )
-    input_grad = tensor_gather(input_own.astype(low), lambda sent: (expert_grad, mine))
+    input_grad = tensor_gather(input_own.astype(low), lambda sent: (mine,))
     input_grad = input_grad.astype(full)
     layer_own = hidden + unpacked([outputs[s] for s in range(EXPERTS)])
     layer_out = tensor_gather(layer_own.astype(low)).astype(full)
     share = width // dp_count
     mine = lax.dynamic_slice_in_dim(mine, index * share, share, 1)
+    shards = after(shards, layer_out, input_grad, expert_grad).astype(full)
+    qkv_shard, out_shard = shards[:, : 3 * size], shards[:, 3 * size :]
     return (
         layer_out,
         input_grad,

time: 1020 us -> 1040 us (1.020)
  waiting for transfers between devices: 393 us -> 431 us
  starting transfers between devices: 80.2 us -> 61.1 us
    all_gather x1, waiting for transfers between devices: 62.3 us -> 127 us  [body(): lax.all_gather(jnp.concatenate([qkv_weight.reshape(-1, 3 * size), out_wei...]
    ppermute x74 -> x72, waiting for transfers between devices: 331 us -> 303 us  [swap(): lax.ppermute(value, axis, [(i, i ^ distance) for i in range(lax.axis_size...]
    ppermute x74 -> x72, starting transfers between devices: 79.5 us -> 60.2 us  [swap(): lax.ppermute(value, axis, [(i, i ^ distance) for i in range(lax.axis_size...]
  transfers between devices with their start and end apart: 80 -> 77, of which waited for: 30 -> 28; matrix products, arithmetic and copies ran while one was open for 24% -> 25% of each run, Pallas kernels for 23% -> 23%
where the time goes in v8:
time: 1040 us; the launch traced here: 1030 us
  waiting for transfers between devices  431 us (41%)
  Pallas kernels  237 us (23%)
  matrix products  156 us (15%)
  other arithmetic  81.5 us (8%)
  starting transfers between devices  61.1 us (6%)
  local copies, waits for them, and re-layouts  45.5 us (4%)
  between operations  15.7 us (2%)
    ppermute x72, waiting for transfers between devices, swap(): lax.ppermute(value, axis, [(i, i ^ distance) for i in range(lax.axis_size...  303 us
    all_gather x1, waiting for transfers between devices, body(): lax.all_gather(jnp.concatenate([qkv_weight.reshape(-1, 3 * size), out_wei...  127 us
    dot_general x25, matrix products, contract(): lax.dot_general(left, right, (((left_dim,), (right_dim,)), ((), ())), pre...  123 us
    pallas_call x4, Pallas kernels, expert_pass(): pl.pallas_call(functools.partial(expert_kernel, count, len(carried)), gri...  120 us
    ppermute x72, starting transfers between devices, swap(): lax.ppermute(value, axis, [(i, i ^ distance) for i in range(lax.axis_size...  60.2 us
    pallas_call x2, Pallas kernels, down_pass(): pl.pallas_call(functools.partial(down_kernel, len(carried)), grid_spec=pl...  32.6 us
    pallas_call x1, Pallas kernels, up_pass(): pl.pallas_call(up_kernel, grid_spec=pltpu.PrefetchScalarGridSpec(num_scal...  26.8 us
  transfers between devices with their start and end apart: 77, of which 28 were waited for; matrix products, arithmetic and copies ran while one was open for 25% of the time, Pallas kernels for 23%

profile of v8, /device:TPU:0, one launch (start us, length us, event | category | flops | bytes accessed | tf_op | source)
XLA Modules:
  0.0 1028.0 jit_solution(18172757711812184345)
XLA Ops:
  40.3 6.9 convolution_convert_fusion.3.rows
  47.2 127.3 %all-gather.4.cloned.1.call-done.right = bf16[2048,2176]{1,0:T(8,128)(2,1)} async-done(((bf16[256,2176]{1,0:T(8,128)(2,1)}), bf16[2048,2176]{1,0:T(8,128)(2,1)}) %all-gather.4.cloned.1.call-update) | async-done | bytes 8912912 | tf_op jit(solution)/shard_map/all_gather | solution.py:595
  185.1 11.7 %fusion.3.q_in.k_in.v_in = f32[1024,1536]{1,0:T(8,128)} fusion(bf16[1024,2048]{1,0:T(8,128)(2,1)} %fusion.2, bf16[2048,2176]{1,0:T(8,128)(2,1)} %all-gather.4.cloned.1.call-done.right), kind=kOutput, calls=%fused_computation.9 | convolution fusion | flops 6442450944 | bytes 16777216 | tf_op jit(solution)/shard_map/dot_general | solution.py:673
  201.0 12.9 %attention.1 = (bf16[1024,512]{1,0:T(8,128)(2,1)S(1)}, bf16[1024,512]{1,0:T(8,128)(2,1)S(1)}, bf16[1024,512]{1,0:T(8,128)(2,1)S(1)}, bf16[1024,512]{1,0:T(8,128)(2,1)S(1)}, f32[4,1024,1]{2,1,0:T(8,128)}) custom-call(f32[1024,1536]{1,0:T(8,128)} %fusion.3.q_in.k_in.v_in, f32[1024,1536]{1,0:T(8,128)} %fusion.3.q_in.k_in.v_in, ...), custom_call_target="tpu_custom_call" | custom-call | flops 1342177280 | bytes 10485760 | tf_op jit(solution)/shard_map/attention/pallas_call | solution.py:135
  237.0 11.0 %down.2 = (bf16[3072,2048]{1,0:T(8,128)(2,1)}, bf16[3072,1408]{1,0:T(8,128)(2,1)}) custom-call(s32[3]{0:T(128)S(1)} %pad_add_fusion.where, bf16[768,2048]{1,0:T(8,128)(2,1)} %convolution_convert_fusion.3.rows, bf16[1024,1408]{1,0:T(8,128)(2,1)S(1)} %get-tuple-element.238.own, bf16[1024,1408]{1,0:T(8,128)(2,1)} %collective-permute-done.came), custom_call_target="tpu_custom_call" | custom-call | flops 4429185024 | bytes 14221312 | tf_op jit(solution)/shard_map/down/pallas_call | solution.py:272
  248.0 12.1 %collective-permute-done.11 = bf16[1024,512]{1,0:T(8,128)(2,1)} collective-permute-done((bf16[1024,512]{1,0:T(8,128)(2,1)}, bf16[1024,512]{1,0:T(8,128)(2,1)}, u32[]{:S(2)}, u32[]{:S(2)}) %collective-permute-start.11) | collective-permute-done | bytes 1048608 | tf_op jit(solution)/shard_map/ppermute | solution.py:26
  289.5 33.7 %collective-permute-done.18.refs_2_ = bf16[768,512]{1,0:T(8,128)(2,1)S(1)} collective-permute-done((bf16[768,512]{1,0:T(8,128)(2,1)S(1)}, bf16[768,512]{1,0:T(8,128)(2,1)S(1)}, u32[]{:S(2)}, u32[]{:S(2)}) %collective-permute-start.18) | collective-permute-done | bytes 786464 | tf_op jit(solution)/shard_map/ppermute | solution.py:26
  330.0 20.0 %collective-permute-done.20.refs_10_ = bf16[1184,1408]{1,0:T(8,128)(2,1)S(1)} collective-permute-done((bf16[1184,1408]{1,0:T(8,128)(2,1)S(1)}, bf16[1184,1408]{1,0:T(8,128)(2,1)S(1)}, u32[]{:S(2)}, u32[]{:S(2)}) %collective-permute-start.20) | collective-permute-done | bytes 3334176 | tf_op jit(solution)/shard_map/ppermute | solution.py:26
  351.7 30.1 %expert.4 = (bf16[3072,2048]{1,0:T(8,128)(2,1)}, bf16[3072,1408]{1,0:T(8,128)(2,1)}, bf16[3072,2816]{1,0:T(8,128)(2,1)}, bf16[768,1024]{1,0:T(8,128)(2,1)}, bf16[768,1024]{1,0:T(8,128)(2,1)}, /*index=5*/f32[1,768]{1,0:T(1,128)}) custom-call(s32[3]{0:T(128)} %copy-done.9, bf16[768,512]{1,0:T(8,128)(2,1)} %copy-done.68, bf16[768,512]{1,0:T(8,128)(2,1)} %copy-done.70, ...), custom_call_target="tpu_custom_call" | custom-call | flops 17716740096 | bytes 32768000 | tf_op jit(solution)/shard_map/expert/pallas_call | solution.py:411
  383.6 21.6 %down.3 = (bf16[3072,2048]{1,0:T(8,128)(2,1)}, bf16[3072,1408]{1,0:T(8,128)(2,1)}) custom-call(s32[3]{0:T(128)S(1)} %copy-done.10, bf16[2304,2048]{1,0:T(8,128)(2,1)} %all-gather.8.cloned.1.call-done.rows, bf16[1024,1408]{1,0:T(8,128)(2,1)S(1)} %get-tuple-element.238.own, ...), custom_call_target="tpu_custom_call", output_to_operand_aliasing={{0}: (4, {}), {1}: (5, {})} | custom-call | flops 13287555072 | bytes 31129600 | tf_op jit(solution)/shard_map/down/pallas_call | solution.py:272
  405.2 30.0 %expert.5 = (bf16[3072,2048]{1,0:T(8,128)(2,1)}, bf16[3072,1408]{1,0:T(8,128)(2,1)}, bf16[3072,2816]{1,0:T(8,128)(2,1)}, bf16[768,1024]{1,0:T(8,128)(2,1)}, bf16[768,1024]{1,0:T(8,128)(2,1)}, /*index=5*/f32[1,768]{1,0:T(1,128)}) custom-call(s32[3]{0:T(128)} %copy-done.9, ...), custom_call_target="tpu_custom_call", output_to_operand_aliasing={{0}: (15, {}), {1}: (16, {}), {2}: (17, {})} | custom-call | flops 17716740096 | bytes 32768000 | tf_op jit(solution)/shard_map/expert/pallas_call | solution.py:411
  440.3 17.9 %collective-permute-done.33 = bf16[768,512]{1,0:T(8,128)(2,1)S(1)} collective-permute-done((bf16[768,512]{1,0:T(8,128)(2,1)S(1)}, bf16[768,512]{1,0:T(8,128)(2,1)S(1)}, u32[]{:S(2)}, u32[]{:S(2)}) %collective-permute-start.33) | collective-permute-done | bytes 786464 | tf_op jit(solution)/shard_map/ppermute | solution.py:26
  462.6 30.2 %expert.6 = (bf16[3072,2048]{1,0:T(8,128)(2,1)}, bf16[3072,1408]{1,0:T(8,128)(2,1)}, bf16[3072,2816]{1,0:T(8,128)(2,1)}, bf16[768,1024]{1,0:T(8,128)(2,1)}, bf16[768,1024]{1,0:T(8,128)(2,1)}, /*index=5*/f32[1,768]{1,0:T(1,128)}) custom-call(s32[3]{0:T(128)} %copy-done.9, ...), custom_call_target="tpu_custom_call", output_to_operand_aliasing={{0}: (15, {}), {1}: (16, {}), {2}: (17, {})} | custom-call | flops 17716740096 | bytes 32768000 | tf_op jit(solution)/shard_map/expert/pallas_call | solution.py:411
  504.4 29.9 %expert.7 = (bf16[3072,2048]{1,0:T(8,128)(2,1)}, bf16[3072,1408]{1,0:T(8,128)(2,1)}, bf16[3072,2816]{1,0:T(8,128)(2,1)}, bf16[768,1024]{1,0:T(8,128)(2,1)}, bf16[768,1024]{1,0:T(8,128)(2,1)}, /*index=5*/f32[1,768]{1,0:T(1,128)}) custom-call(s32[3]{0:T(128)} %copy-done.9, ...), custom_call_target="tpu_custom_call", output_to_operand_aliasing={{0}: (15, {}), {1}: (16, {}), {2}: (17, {})} | custom-call | flops 17716740096 | bytes 32768000 | tf_op jit(solution)/shard_map/expert/pallas_call | solution.py:411
  545.3 14.1 %fusion.14 = bf16[1024,1408]{1,0:T(8,128)(2,1)S(1)} fusion(bf16[3072,1408]{1,0:T(8,128)(2,1)} %get-tuple-element.184.act, bf16[3072,2048]{1,0:T(8,128)(2,1)} %get-tuple-element.146, s32[]{:T(128)S(6)} %select_n.169), kind=kOutput, calls=%fused_computation.23 | convolution fusion | flops 8859811840 | bytes 17825796 | tf_op jit(solution)/shard_map/dot_general | solution.py:30
  568.2 26.8 %up.1 = bf16[3072,2048]{1,0:T(8,128)(2,1)} custom-call(s32[3]{0:T(128)S(1)} %copy-done.11, bf16[3072,1408]{1,0:T(8,128)(2,1)} %get-tuple-element.184.act, bf16[1024,1408]{1,0:T(8,128)(2,1)S(1)} %get-tuple-element.238.own, bf16[1024,1408]{1,0:T(8,128)(2,1)} %collective-permute-done.came), custom_call_target="tpu_custom_call" | custom-call | flops 17716740096 | bytes 27000832 | tf_op jit(solution)/shard_map/up/pallas_call | solution.py:339
  621.2 14.1 %collective-permute-done.49 = bf16[320,1408]{1,0:T(8,128)(2,1)} collective-permute-done((bf16[320,1408]{1,0:T(8,128)(2,1)}, bf16[320,1408]{1,0:T(8,128)(2,1)}, u32[]{:S(2)}, u32[]{:S(2)}) %collective-permute-start.49) | collective-permute-done | bytes 901152 | tf_op jit(solution)/shard_map/ppermute | solution.py:26
  636.3 16.3 %convolution_convert_fusion.2 = bf16[512,2816]{1,0:T(8,128)(2,1)} fusion(bf16[3072,2816]{1,0:T(8,128)(2,1)} %get-tuple-element.183, bf16[3072,2048]{1,0:T(8,128)(2,1)} %get-tuple-element.168, s32[]{:T(128)S(6)} %select_n.169), kind=kOutput, calls=%fused_computation.19 | convolution fusion | flops 8859811840 | bytes 23330820 | tf_op jit(solution)/shard_map/dot_general | solution.py:30
  652.6 12.0 %convolution_convert_fusion.1 = bf16[512,2816]{1,0:T(8,128)(2,1)} fusion(bf16[3072,2816]{1,0:T(8,128)(2,1)S(1)} %bitcast.151, bf16[3072,2048]{1,0:T(8,128)(2,1)} %get-tuple-element.168, s32[]{:T(128)S(6)} %select_n.173), kind=kOutput, calls=%fused_computation.18 | convolution fusion | flops 8859811840 | bytes 23330820 | tf_op jit(solution)/shard_map/dot_general | solution.py:30
  679.3 15.8 %attention_back.1.left = bf16[1024,1536]{1,0:T(8,128)(2,1)} custom-call(bf16[1024,512]{1,0:T(8,128)(2,1)S(1)} %copy-done.13, bf16[1024,512]{1,0:T(8,128)(2,1)S(1)} %copy-done.15, bf16[1024,512]{1,0:T(8,128)(2,1)S(1)} %copy-done.17, f32[4,1024,1]{2,1,0:T(8,128)} %get-tuple-element.163.logs, bf16[1024,512]{1,0:T(8,128)(2,1)S(1)} %fusion.86.grad, ...), custom_call_target="tpu_custom_call" | custom-call | flops 3355443200 | bytes 8388608 | tf_op jit(solution)/shard_map/attention_back/pallas_call | solution.py:188
  698.8 8.7 convolution_convert_fusion
  707.5 7.6 pad_maximum_fusion
  715.2 12.1 %spread.3 = (bf16[1024,1024]{1,0:T(8,128)(2,1)S(1)}, bf16[1024,1024]{1,0:T(8,128)(2,1)}) custom-call(s32[3]{0:T(128)S(1)} %copy-done.11, bf16[1024,1536]{1,0:T(8,128)(2,1)} %attention_back.1.left, bf16[2048,2176]{1,0:T(8,128)(2,1)} %all-gather.4.cloned.1.call-done.right), custom_call_target="tpu_custom_call" | custom-call | flops 6442450944 | bytes 13631488 | tf_op jit(solution)/shard_map/spread/pallas_call | solution.py:310
  731.8 20.6 %collective-permute-done.60 = bf16[128,2816]{1,0:T(8,128)(2,1)S(1)} collective-permute-done((bf16[128,2816]{1,0:T(8,128)(2,1)}, bf16[128,2816]{1,0:T(8,128)(2,1)S(1)}, u32[]{:S(2)}, u32[]{:S(2)}) %collective-permute-start.60) | collective-permute-done | bytes 720928 | tf_op jit(solution)/shard_map/ppermute | solution.py:26
  757.0 26.7 %fusion.11.refs_0_ = bf16[1024,2816]{1,0:T(8,128)(2,1)} fusion(bf16[3072,2816]{1,0:T(8,128)(2,1)} %get-tuple-element.183, bf16[3072,2048]{1,0:T(8,128)(2,1)} %get-tuple-element.168, s32[]{:T(128)S(6)} %select_n.186), kind=kOutput, calls=%fused_computation.17 | convolution fusion | flops 17719623680 | bytes 29360132 | tf_op jit(solution)/shard_map/dot_general | solution.py:30
  786.2 15.9 %fusion.17.refs_3_ = bf16[1024,1408]{1,0:T(8,128)(2,1)} fusion(bf16[3072,1408]{1,0:T(8,128)(2,1)} %get-tuple-element.184.act, bf16[3072,2048]{1,0:T(8,128)(2,1)} %get-tuple-element.146, s32[]{:T(128)S(6)} %select_n.186), kind=kOutput, calls=%fused_computation.24 | convolution fusion | flops 8859811840 | bytes 17825796 | tf_op jit(solution)/shard_map/dot_general | solution.py:30
  802.2 29.0 %collective-permute-done.54 = bf16[768,512]{1,0:T(8,128)(2,1)S(1)} collective-permute-done((bf16[768,512]{1,0:T(8,128)(2,1)S(1)}, bf16[768,512]{1,0:T(8,128)(2,1)S(1)}, u32[]{:S(2)}, u32[]{:S(2)}) %collective-permute-start.54) | collective-permute-done | bytes 786464 | tf_op jit(solution)/shard_map/ppermute | solution.py:26
  841.8 22.4 %collective-permute-done.56 = bf16[768,512]{1,0:T(8,128)(2,1)S(1)} collective-permute-done((bf16[768,512]{1,0:T(8,128)(2,1)S(1)}, bf16[768,512]{1,0:T(8,128)(2,1)S(1)}, u32[]{:S(2)}, u32[]{:S(2)}) %collective-permute-start.56) | collective-permute-done | bytes 786464 | tf_op jit(solution)/shard_map/ppermute | solution.py:26
  864.2 39.7 %collective-permute-done.55 = bf16[768,512]{1,0:T(8,128)(2,1)S(1)} collective-permute-done((bf16[768,512]{1,0:T(8,128)(2,1)S(1)}, bf16[768,512]{1,0:T(8,128)(2,1)S(1)}, u32[]{:S(2)}, u32[]{:S(2)}) %collective-permute-start.55) | collective-permute-done | bytes 786464 | tf_op jit(solution)/shard_map/ppermute | solution.py:26
  911.8 40.0 %collective-permute-done.66 = f32[6,2048]{1,0:T(8,128)S(1)} collective-permute-done((f32[6,2048]{1,0:T(8,128)S(1)}, f32[6,2048]{1,0:T(8,128)S(1)}, u32[]{:S(2)}, u32[]{:S(2)}) %collective-permute-start.66) | collective-permute-done | bytes 49184 | tf_op jit(solution)/shard_map/ppermute | solution.py:26
  951.9 21.0 %collective-permute-done.67 = f32[6,2048]{1,0:T(8,128)S(1)} collective-permute-done((f32[6,2048]{1,0:T(8,128)S(1)}, f32[6,2048]{1,0:T(8,128)S(1)}, u32[]{:S(2)}, u32[]{:S(2)}) %collective-permute-start.67) | collective-permute-done | bytes 49184 | tf_op jit(solution)/shard_map/ppermute | solution.py:26
  992.5 11.3 %expert_grad_sum.1 = f32[3,1024,1408]{2,1,0:T(8,128)} custom-call(bf16[1024,2816]{1,0:T(8,128)(2,1)} %fusion.11.refs_0_, bf16[512,2816]{1,0:T(8,128)(2,1)S(1)} %pad_maximum_fusion.3.refs_1_, bf16[512,2816]{1,0:T(8,128)(2,1)S(1)} %collective-permute-done.71.refs_2_, bf16[1024,1408]{1,0:T(8,128)(2,1)S(1)} %copy-done, ...), custom_call_target="tpu_custom_call" | custom-call | flops 4325376 | bytes 34603008 | tf_op jit(solution)/shard_map/expert_grad_sum/pallas_call | solution.py:495
  (463 shorter events, 262.9 us)
Async XLA Ops:
  7.2 167.2 %all-gather.4.cloned.1.call-start = ((), (), s32[]{:S(2)}) async-start(), calls=%async_computation.2 | async-start | bytes 10027008 | tf_op jit(solution)/shard_map/all_gather | solution.py:595
  10.3 256.4 %all-gather.6.cloned.1.call-start = ((), (), s32[]{:S(2)}) async-start(), calls=%async_computation.3 | async-start | bytes 5242880 | tf_op jit(solution)/shard_map/all_gather | solution.py:661
  14.0 162.8 %collective-permute-start.4 = (f32[1,768]{1,0:T(1,128)S(1)}, f32[1,768]{1,0:T(1,128)S(1)}, u32[]{:S(2)}, u32[]{:S(2)}) collective-permute-start(f32[1,768]{1,0:T(1,128)S(1)} %fusion.36), channel_id=1, source_target_pairs={{0,8},{4,12},{8,0},{12,4},{16,24},{20,28},{24,16},{28,20},{1,9},{5... | collective-permute-start | bytes 9224 | tf_op jit(solution)/shard_map/ppermute | solution.py:26
  17.7 160.7 %collective-permute-start.5 = (f32[1,768]{1,0:T(1,128)S(1)}, f32[1,768]{1,0:T(1,128)S(1)}, u32[]{:S(2)}, u32[]{:S(2)}) collective-permute-start(f32[1,768]{1,0:T(1,128)S(1)} %fusion.31), channel_id=1, source_target_pairs={{0,16},{4,20},{8,24},{12,28},{16,0},{20,4},{24,8},{28,12},{1,17},{... | collective-permute-start | bytes 9224 | tf_op jit(solution)/shard_map/ppermute | solution.py:26
  20.9 163.3 %collective-permute-start.6 = (f32[1,768]{1,0:T(1,128)S(1)}, f32[1,768]{1,0:T(1,128)S(1)}, u32[]{:S(2)}, u32[]{:S(2)}) collective-permute-start(f32[1,768]{1,0:T(1,128)S(1)} %fusion.26), channel_id=1, source_target_pairs={{0,24},{4,28},{8,16},{12,20},{16,8},{20,12},{24,0},{28,4},{1,25},{... | collective-permute-start | bytes 9224 | tf_op jit(solution)/shard_map/ppermute | solution.py:26
  20.9 163.3 %collective-permute-start.1 = (f32[1,1024]{1,0:T(1,128)S(1)}, f32[1,1024]{1,0:T(1,128)S(1)}, u32[]{:S(2)}, u32[]{:S(2)}) collective-permute-start(f32[1,1024]{1,0:T(1,128)S(1)} %get-tuple-element.279), channel_id=1, source_target_pairs={{0,8},{4,12},{8,0},{12,4},{16,24},{20,28},{24,16},{28,20},{1,9},{5... | collective-permute-start | bytes 12296 | tf_op jit(solution)/shard_map/ppermute | solution.py:26
  27.7 156.5 %collective-permute-start = (bf16[1024,1408]{1,0:T(8,128)(2,1)S(1)}, bf16[1024,1408]{1,0:T(8,128)(2,1)}, u32[]{:S(2)}, u32[]{:S(2)}) collective-permute-start(bf16[1024,1408]{1,0:T(8,128)(2,1)S(1)} %get-tuple-element.238.own), channel_id=1, source_target_pairs={{0,4},{4,0},{8,12},{12,8},{16,20},{20,16},{24,28},{28,24},{1,5},{5... | collective-permute-start | bytes 8650760 | tf_op jit(solution)/shard_map/ppermute | solution.py:26
  184.6 199.0 %all-gather.8.cloned.1.call-start = ((), (), s32[]{:S(2)}) async-start(), calls=%async_computation.4 | async-start | bytes 11796480 | tf_op jit(solution)/shard_map/all_gather | solution.py:697
  272.8 484.2 %reduce-scatter.3.cloned.1.call-start = ((), (), s32[]{:S(2)}) async-start(), calls=%async_computation.5 | async-start | bytes 15728640 | tf_op jit(solution)/shard_map/reduce_scatter | solution.py:789
  276.0 74.0 %collective-permute-start.20 = (bf16[1184,1408]{1,0:T(8,128)(2,1)S(1)}, bf16[1184,1408]{1,0:T(8,128)(2,1)S(1)}, u32[]{:S(2)}, u32[]{:S(2)}) collective-permute-start(bf16[1184,1408]{1,0:T(8,128)(2,1)S(1)} %pad_maximum_fusion.2), channel_id=1, source_target_pairs={{0,4},{4,0},{8,12},{12,8},{16,20},{20,16},{24,28},{28,24},{1,5},{5... | collective-permute-start | bytes 10002440 | tf_op jit(solution)/shard_map/ppermute | solution.py:26
  286.5 36.7 %collective-permute-start.18 = (bf16[768,512]{1,0:T(8,128)(2,1)S(1)}, bf16[768,512]{1,0:T(8,128)(2,1)S(1)}, u32[]{:S(2)}, u32[]{:S(2)}) collective-permute-start(bf16[768,512]{1,0:T(8,128)(2,1)S(1)} %fusion.98.refs_0_), channel_id=1, source_target_pairs={{0,2},{1,3},{2,0},{3,1},{4,6},{5,7},{6,4},{7,5},{8,10},{9,11},{10,... | collective-permute-start | bytes 2359304 | tf_op jit(solution)/shard_map/ppermute | solution.py:26
  289.0 38.1 %collective-permute-start.15 = (bf16[768,512]{1,0:T(8,128)(2,1)S(1)}, bf16[768,512]{1,0:T(8,128)(2,1)}, u32[]{:S(2)}, u32[]{:S(2)}) collective-permute-start(bf16[768,512]{1,0:T(8,128)(2,1)S(1)} %fusion.100), channel_id=1, source_target_pairs={{0,16},{4,20},{8,24},{12,28},{16,0},{20,4},{24,8},{28,12},{1,17},{... | collective-permute-start | bytes 2359304 | tf_op jit(solution)/shard_map/ppermute | solution.py:26
  289.5 40.4 %collective-permute-start.17 = (bf16[768,512]{1,0:T(8,128)(2,1)S(1)}, bf16[768,512]{1,0:T(8,128)(2,1)S(1)}, u32[]{:S(2)}, u32[]{:S(2)}) collective-permute-start(bf16[768,512]{1,0:T(8,128)(2,1)S(1)} %fusion.98.refs_0_), channel_id=1, source_target_pairs={{0,1},{1,0},{2,3},{3,2},{4,5},{5,4},{6,7},{7,6},{8,9},{9,8},{10,11... | collective-permute-start | bytes 2359304 | tf_op jit(solution)/shard_map/ppermute | solution.py:26
  327.0 54.8 %collective-permute-start.16 = (bf16[768,512]{1,0:T(8,128)(2,1)}, bf16[768,512]{1,0:T(8,128)(2,1)}, u32[]{:S(2)}, u32[]{:S(2)}) collective-permute-start(bf16[768,512]{1,0:T(8,128)(2,1)} %fusion.101), channel_id=1, source_target_pairs={{0,24},{4,28},{8,16},{12,20},{16,8},{20,12},{24,0},{28,4},{1,25},{... | collective-permute-start | bytes 2359304 | tf_op jit(solution)/shard_map/ppermute | solution.py:26
  328.5 53.3 %collective-permute-start.27 = (bf16[768,512]{1,0:T(8,128)(2,1)}, bf16[768,512]{1,0:T(8,128)(2,1)}, u32[]{:S(2)}, u32[]{:S(2)}) collective-permute-start(bf16[768,512]{1,0:T(8,128)(2,1)} %collective-permute-done.15.refs_0_), channel_id=1, source_target_pairs={{0,2},{1,3},{2,0},{3,1},{4,6},{5,7},{6,4},{7,5},{8,10},{9,11},{10,... | collective-permute-start | bytes 2359304 | tf_op jit(solution)/shard_map/ppermute | solution.py:26
  329.9 75.2 %collective-permute-start.26 = (bf16[768,512]{1,0:T(8,128)(2,1)}, bf16[768,512]{1,0:T(8,128)(2,1)}, u32[]{:S(2)}, u32[]{:S(2)}) collective-permute-start(bf16[768,512]{1,0:T(8,128)(2,1)} %collective-permute-done.15.refs_0_), channel_id=1, source_target_pairs={{0,1},{1,0},{2,3},{3,2},{4,5},{5,4},{6,7},{7,6},{8,9},{9,8},{10,11... | collective-permute-start | bytes 2359304 | tf_op jit(solution)/shard_map/ppermute | solution.py:26
  381.9 53.4 %collective-permute-start.25 = (bf16[768,512]{1,0:T(8,128)(2,1)}, bf16[768,512]{1,0:T(8,128)(2,1)}, u32[]{:S(2)}, u32[]{:S(2)}) collective-permute-start(bf16[768,512]{1,0:T(8,128)(2,1)} %collective-permute-done.16.refs_0_), channel_id=1, source_target_pairs={{0,2},{1,3},{2,0},{3,1},{4,6},{5,7},{6,4},{7,5},{8,10},{9,11},{10,... | collective-permute-start | bytes 2359304 | tf_op jit(solution)/shard_map/ppermute | solution.py:26
  383.4 51.8 %collective-permute-start.21 = (bf16[768,512]{1,0:T(8,128)(2,1)}, bf16[768,512]{1,0:T(8,128)(2,1)}, u32[]{:S(2)}, u32[]{:S(2)}) collective-permute-start(bf16[768,512]{1,0:T(8,128)(2,1)} %fusion.99), channel_id=1, source_target_pairs={{0,8},{4,12},{8,0},{12,4},{16,24},{20,28},{24,16},{28,20},{1,9},{5... | collective-permute-start | bytes 2359304 | tf_op jit(solution)/shard_map/ppermute | solution.py:26
  383.5 52.3 %collective-permute-start.30 = (bf16[768,1024]{1,0:T(8,128)(2,1)}, bf16[768,1024]{1,0:T(8,128)(2,1)}, u32[]{:S(2)}, u32[]{:S(2)}) collective-permute-start(bf16[768,1024]{1,0:T(8,128)(2,1)} %get-tuple-element.130), channel_id=1, source_target_pairs={{0,1},{1,0},{2,3},{3,2},{4,5},{5,4},{6,7},{7,6},{8,9},{9,8},{10,11... | collective-permute-start | bytes 4718600 | tf_op jit(solution)/shard_map/ppermute | solution.py:26
  438.8 54.0 %collective-permute-start.23 = (bf16[768,512]{1,0:T(8,128)(2,1)}, bf16[768,512]{1,0:T(8,128)(2,1)}, u32[]{:S(2)}, u32[]{:S(2)}) collective-permute-start(bf16[768,512]{1,0:T(8,128)(2,1)} %collective-permute-done.21.refs_0_), channel_id=1, source_target_pairs={{0,2},{1,3},{2,0},{3,1},{4,6},{5,7},{6,4},{7,5},{8,10},{9,11},{10,... | collective-permute-start | bytes 2359304 | tf_op jit(solution)/shard_map/ppermute | solution.py:26
  496.3 40.9 %collective-permute-start.37 = (bf16[768,512]{1,0:T(8,128)(2,1)}, bf16[768,512]{1,0:T(8,128)(2,1)}, u32[]{:S(2)}, u32[]{:S(2)}) collective-permute-start(bf16[768,512]{1,0:T(8,128)(2,1)} %add_convert_fusion.7), channel_id=1, source_target_pairs={{0,16},{4,20},{8,24},{12,28},{16,0},{20,4},{24,8},{28,12},{1,17},{... | collective-permute-start | bytes 2359304 | tf_op jit(solution)/shard_map/ppermute | solution.py:26
  541.2 53.8 %collective-permute-start.44 = (bf16[768,512]{1,0:T(8,128)(2,1)}, bf16[768,512]{1,0:T(8,128)(2,1)}, u32[]{:S(2)}, u32[]{:S(2)}) collective-permute-start(bf16[768,512]{1,0:T(8,128)(2,1)} %add_convert_fusion.5), channel_id=1, source_target_pairs={{0,24},{4,28},{8,16},{12,20},{16,8},{20,12},{24,0},{28,4},{1,25},{... | collective-permute-start | bytes 2359304 | tf_op jit(solution)/shard_map/ppermute | solution.py:26
  595.1 421.9 %reduce-scatter.5.cloned.1.call-start = ((), (), s32[]{:S(2)}) async-start(), calls=%async_computation.6 | async-start | bytes 9437184 | tf_op jit(solution)/shard_map/reduce_scatter | solution.py:836
  619.6 46.7 %collective-permute-start.48 = (bf16[1024,512]{1,0:T(8,128)(2,1)S(1)}, bf16[1024,512]{1,0:T(8,128)(2,1)S(1)}, u32[]{:S(2)}, u32[]{:S(2)}) collective-permute-start(bf16[1024,512]{1,0:T(8,128)(2,1)S(1)} %get-tuple-element.242), channel_id=1, source_target_pairs={{0,2},{1,3},{2,0},{3,1},{4,6},{5,7},{6,4},{7,5},{8,10},{9,11},{10,... | collective-permute-start | bytes 3145736 | tf_op jit(solution)/shard_map/ppermute | solution.py:26
  752.4 89.4 %collective-permute-start.63 = (bf16[256,2816]{1,0:T(8,128)(2,1)}, bf16[256,2816]{1,0:T(8,128)(2,1)}, u32[]{:S(2)}, u32[]{:S(2)}) collective-permute-start(bf16[256,2816]{1,0:T(8,128)(2,1)} %slice.350), channel_id=1, source_target_pairs={{0,4},{4,0},{8,12},{12,8},{16,20},{20,16},{24,28},{28,24},{1,5},{5... | collective-permute-start | bytes 4325384 | tf_op jit(solution)/shard_map/ppermute | solution.py:26
  755.3 46.9 %collective-permute-start.59 = (bf16[1024,512]{1,0:T(8,128)(2,1)}, bf16[1024,512]{1,0:T(8,128)(2,1)}, u32[]{:S(2)}, u32[]{:S(2)}) collective-permute-start(bf16[1024,512]{1,0:T(8,128)(2,1)} %add_convert_fusion.1), channel_id=1, source_target_pairs={{0,2},{1,3},{2,0},{3,1},{4,6},{5,7},{6,4},{7,5},{8,10},{9,11},{10,... | collective-permute-start | bytes 3145736 | tf_op jit(solution)/shard_map/ppermute | solution.py:26
  784.0 47.2 %collective-permute-start.54 = (bf16[768,512]{1,0:T(8,128)(2,1)S(1)}, bf16[768,512]{1,0:T(8,128)(2,1)S(1)}, u32[]{:S(2)}, u32[]{:S(2)}) collective-permute-start(bf16[768,512]{1,0:T(8,128)(2,1)S(1)} %get-tuple-element.180), channel_id=1, source_target_pairs={{0,16},{4,20},{8,24},{12,28},{16,0},{20,4},{24,8},{28,12},{1,17},{... | collective-permute-start | bytes 2359304 | tf_op jit(solution)/shard_map/ppermute | solution.py:26
  834.9 69.0 %collective-permute-start.55 = (bf16[768,512]{1,0:T(8,128)(2,1)S(1)}, bf16[768,512]{1,0:T(8,128)(2,1)S(1)}, u32[]{:S(2)}, u32[]{:S(2)}) collective-permute-start(bf16[768,512]{1,0:T(8,128)(2,1)S(1)} %get-tuple-element.181), channel_id=1, source_target_pairs={{0,8},{4,12},{8,0},{12,4},{16,24},{20,28},{24,16},{28,20},{1,9},{5... | collective-permute-start | bytes 2359304 | tf_op jit(solution)/shard_map/ppermute | solution.py:26
  903.8 79.0 %collective-permute-start.64 = (bf16[1024,512]{1,0:T(8,128)(2,1)S(1)}, bf16[1024,512]{1,0:T(8,128)(2,1)S(1)}, u32[]{:S(2)}, u32[]{:S(2)}) collective-permute-start(bf16[1024,512]{1,0:T(8,128)(2,1)S(1)} %fusion.55), channel_id=1, source_target_pairs={{0,2},{1,3},{2,0},{3,1},{4,6},{5,7},{6,4},{7,5},{8,10},{9,11},{10,... | collective-permute-start | bytes 3145736 | tf_op jit(solution)/shard_map/ppermute | solution.py:26
  906.5 78.3 %collective-permute-start.57 = (bf16[1024,512]{1,0:T(8,128)(2,1)S(1)}, bf16[1024,512]{1,0:T(8,128)(2,1)S(1)}, u32[]{:S(2)}, u32[]{:S(2)}) collective-permute-start(bf16[1024,512]{1,0:T(8,128)(2,1)S(1)} %add_convert_fusion), channel_id=1, source_target_pairs={{0,2},{1,3},{2,0},{3,1},{4,6},{5,7},{6,4},{7,5},{8,10},{9,11},{10,... | collective-permute-start | bytes 3145736 | tf_op jit(solution)/shard_map/ppermute | solution.py:26
  908.4 83.6 %collective-permute-start.71 = (bf16[512,2816]{1,0:T(8,128)(2,1)}, bf16[512,2816]{1,0:T(8,128)(2,1)S(1)}, u32[]{:S(2)}, u32[]{:S(2)}) collective-permute-start(bf16[512,2816]{1,0:T(8,128)(2,1)} %convolution_convert_fusion.1), channel_id=1, source_target_pairs={{0,4},{4,0},{8,12},{12,8},{16,20},{20,16},{24,28},{28,24},{1,5},{5... | collective-permute-start | bytes 8650760 | tf_op jit(solution)/shard_map/ppermute | solution.py:26
  909.8 41.9 %collective-permute-start.66 = (f32[6,2048]{1,0:T(8,128)S(1)}, f32[6,2048]{1,0:T(8,128)S(1)}, u32[]{:S(2)}, u32[]{:S(2)}) collective-permute-start(f32[6,2048]{1,0:T(8,128)S(1)} %add_dynamic-update-slice_fusion), channel_id=1, source_target_pairs={{0,2},{1,3},{2,0},{3,1},{4,6},{5,7},{6,4},{7,5},{8,10},{9,11},{10,... | collective-permute-start | bytes 147464 | tf_op jit(solution)/shard_map/ppermute | solution.py:26
  (133 other events, 1805.1 us)
Sparse Core Ops, SparseCore 0:
  10.8 163.5 all-gather.3
  184.7 81.9 all-gather.5
  273.0 97.7 all-gather.7
  595.2 118.0 reduce-scatter.2
  716.8 189.8 reduce-scatter.4

commit v9 on v8

--- a/solution.py
+++ b/solution.py
@@ -735,9 +735,9 @@
             rows_raw = down_pass(where, after(grad_rest, even), *down, MOST, total, rows_raw)
             named_sum = after(named_sum, crossed[3])
         if step == 2:
-            named_sum = after(named_sum, crossed[1], *sums_sent)
+            named_sum = after(named_sum, crossed[1], sums_sent[0])
         if step == 3:
-            named_sum = after(named_sum, sums_sent[2])
+            named_sum = after(named_sum, sums_sent[1])
         moe_rows, activation, pre_grad, even, odd, gate_grad = expert_pass(
             step, where, arrived[step], pair, rows_raw[1], named_sum, router_block, carried
         )
@@ -754,9 +754,12 @@
         if step == 2:
             odd = after(odd, *returned, arrived[3][tensor_count // 2])
         if step == 3:
-            came_home[2] = swap(returned[1], "dp", 2 * group_count)
-            odd = after(odd, returned[2], came_home[2])
-        returned.append(near_reduce(even, odd, sums_sent).astype(low))
+            came_home[2] = swap(returned[0], "dp", 2 * group_count)
+            odd = after(odd, returned[1], came_home[2])
+        if step == 0:
+            own_parts = (even, odd)
+        else:
+            returned.append(near_reduce(even, odd, sums_sent).astype(low))
         gate_grads.append(gate_grad)
 
     def home(parts):
@@ -764,9 +767,10 @@
             s: swap(v, "dp", s * group_count) if s else v for s, v in zip(order, parts)
         }
 
-    came_home[0] = returned[0]
-    came_home[3] = swap(returned[2], "dp", 3 * group_count)
-    came_home[1] = swap(returned[3], "dp", group_count)
+    came_home[3] = swap(returned[1], "dp", 3 * group_count)
+    came_home[1] = swap(returned[2], "dp", group_count)
+    own_even, own_odd = own_parts
+    came_home[0] = near_reduce(own_even, after(own_odd, sums_sent[2]), []).astype(low)
     gate_grad_near = home([gate_grads[0]] + [after(v, even) for v in gate_grads[1:]])
     grad_rows = rows_raw[0]
 
@@ -779,16 +783,12 @@
 
     unit = half // 128
     quarter = half // 2
-    act_late = after(activation, sums_sent[3], returned[2])
+    expert_part = up_pass(where, after(activation, sums_sent[2], returned[1]), *down)
+    expert_part = after(expert_part, returned[2], came_home[3])
+    expert_own = lax.psum_scatter(expert_part, "tensor", scatter_dimension=1, tiled=True)
+    act_late = after(activation, expert_part, *gate_grad_near.values())
     down_given = term(grad_rows, act_late)(given_at, half)
-    down_sums = [group_send(down_given[: 40 * unit])]
-    expert_part = up_pass(
-        where, after(activation, down_given, returned[3], *gate_grad_near.values()), *down
-    )
-    expert_part = after(expert_part, down_sums[0], came_home[3], came_home[1])
-    expert_own = lax.psum_scatter(expert_part, "tensor", scatter_dimension=1, tiled=True)
-    down_sums.append(group_send(down_given[40 * unit : 80 * unit], down_sums[0]))
-    came_home = {s: after(v, expert_part) for s, v in came_home.items()}
+    came_home = {s: after(v, down_given) for s, v in came_home.items()}
     back = unpacked([came_home[s] for s in range(EXPERTS)])
 
     gate_grad = jnp.concatenate(
@@ -817,42 +817,43 @@
     router_grad = jnp.dot(logit_grad, moe_in, preferred_element_type=full)
     moe_gain_grad = jnp.sum(moe_grad * normed_two, axis=0)
     pair_given = []
+    down_sums = []
     kept = []
 
     def give_pair(sent):
-        down_sums.append(group_send(down_given[80 * unit :], down_sums[1], sent))
-        pair_term = term(moe_rows, after(pre_grad, sent, down_sums[1]))
+        down_sums.append(group_send(down_given[: 56 * unit], sent))
+        pair_term = term(moe_rows, after(pre_grad, sent))
         pair_given.extend(pair_term(given_at + k * quarter, quarter) for k in range(2))
-        return (*pair_given, down_sums[2])
+        return (*pair_given, down_sums[0])
 
     attn_grad = tensor_gather(hidden_grad.astype(low), give_pair)
-    pair_sums = [group_send(pair_given[0][: 16 * unit], down_sums[2])]
+    down_sums.append(group_send(down_given[56 * unit : 96 * unit], down_sums[0], *pair_given))
     context_grad = jnp.dot(attn_grad, out_full, preferred_element_type=full).astype(low)
     out_grad = contract(after(attn_grad, context_grad), context, 0, 0).astype(low)
+    out_shard = lax.psum_scatter(out_grad, "dp", scatter_dimension=0, tiled=True).astype(full)
+    outputs = {0: expert_own[:MOST]}
+    part = after(expert_own[MOST : 2 * MOST], context_grad)
+    outputs[2] = swap(part, "dp", 2 * group_count)
+    context_grad = after(context_grad, out_grad)
     qkv_grad_rows = attention_back(query, keys, values, logs, context_grad, cosine, sine, scale)
-    qkv_grad_rows = after(qkv_grad_rows, pair_sums[0], out_grad)
+    qkv_grad_rows = after(qkv_grad_rows, down_sums[1])
     qkv_grad = contract(normed_in, qkv_grad_rows, 0, 0).astype(low)
-    grads_both = jnp.concatenate([qkv_grad, out_grad], 1)
-    shards = lax.psum_scatter(grads_both, "dp", scatter_dimension=0, tiled=True)
-    pair_sums.append(group_send(pair_given[0][16 * unit : 32 * unit], pair_sums[0], grads_both))
-    pair_sums.append(group_send(pair_given[0][32 * unit :], pair_sums[1]))
-    pair_last = group_send(pair_given[1], pair_sums[2])
-    outputs = {}
-
-    def keep(sent):
-        part = after(expert_own[MOST : 2 * MOST], sent)
-        outputs[2] = swap(part, "dp", 2 * group_count)
-        late = after(pre_grad, sent, expert_own)
-        kept.append(term(moe_rows, late)(mine_at, half))
-        kept.append(term(grad_rows, after(activation, kept[0]))(mine_at, half))
-        return (*kept, outputs[2], pair_sums[1])
-
-    parts = spread_dot(where, after(qkv_grad_rows, grads_both), first, 0, tensor_count)
-    normed_grad = near_reduce(*parts, [], filler=keep)
-    outputs[0] = expert_own[:MOST]
+    qkv_shard = lax.psum_scatter(qkv_grad, "dp", scatter_dimension=0, tiled=True).astype(full)
+    down_sums.append(group_send(down_given[96 * unit :], down_sums[1], qkv_grad))
+    pair_sums = [group_send(v, down_sums[2]) for v in pair_given]
     for k in (2, 3):
         part = after(expert_own[k * MOST : (k + 1) * MOST], outputs[2])
         outputs[order[k]] = swap(part, "dp", order[k] * group_count)
+
+    def keep(sent):
+        kept.append(term(moe_rows, after(pre_grad, sent))(mine_at, half))
+        kept.append(term(grad_rows, after(activation, kept[0]))(mine_at, half))
+        return (*kept, outputs[3], outputs[1])
+
+    parts = spread_dot(
+        where, after(qkv_grad_rows, qkv_grad, outputs[2]), first, 0, tensor_count
+    )
+    normed_grad = near_reduce(*parts, [], filler=keep)
     normed_one = inputs_own * scale_one
     scaled_in = normed_grad * gain_first_own
     attn_gain_grad = jnp.sum(normed_grad * normed_one, axis=0)
@@ -863,9 +864,8 @@
         jnp.zeros((mine.shape[0], width), full), mine, place * size, 1
     )
     mine = all_sum(mine)
-    input_own = after(input_own, outputs[3], outputs[1], pair_sums[2])
     expert_grad = expert_grad_sum(
-        group_finish(kept[0], [jnp.concatenate(pair_sums, 0), pair_last], member, group_count),
+        group_finish(kept[0], pair_sums, member, group_count),
         group_finish(kept[1], [jnp.concatenate(down_sums, 0)], member, group_count),
         hidden_size,
     )
@@ -875,8 +875,6 @@
     layer_out = tensor_gather(layer_own.astype(low)).astype(full)
     share = width // dp_count
     mine = lax.dynamic_slice_in_dim(mine, index * share, share, 1)
-    shards = after(shards, layer_out, input_grad, expert_grad).astype(full)
-    qkv_shard, out_shard = shards[:, : 3 * size], shards[:, 3 * size :]
     return (
         layer_out,
         input_grad,

time: 1040 us -> 1010 us (0.971)
  waiting for transfers between devices: 431 us -> 399 us
    ppermute x72 -> x70, waiting for transfers between devices: 303 us -> 270 us  [swap(): lax.ppermute(value, axis, [(i, i ^ distance) for i in range(lax.axis_size...]
    ppermute x72 -> x70, starting transfers between devices: 60.2 us -> 66 us  [swap(): lax.ppermute(value, axis, [(i, i ^ distance) for i in range(lax.axis_size...]
  transfers between devices with their start and end apart: 77 -> 76, of which waited for: 28 -> 30; matrix products, arithmetic and copies ran while one was open for 25% -> 25% of each run, Pallas kernels for 23% -> 24%
where the time goes in v9:
time: 1010 us; the launch traced here: 1000 us
  waiting for transfers between devices  399 us (40%)
  Pallas kernels  239 us (24%)
  matrix products  160 us (16%)
  other arithmetic  72 us (7%)
  starting transfers between devices  66.4 us (7%)
  local copies, waits for them, and re-layouts  53.1 us (5%)
  between operations  15.7 us (2%)
    ppermute x70, waiting for transfers between devices, swap(): lax.ppermute(value, axis, [(i, i ^ distance) for i in range(lax.axis_size...  270 us
    all_gather x1, waiting for transfers between devices, body(): lax.all_gather(jnp.concatenate([qkv_weight.reshape(-1, 3 * size), out_wei...  127 us
    dot_general x25, matrix products, contract(): lax.dot_general(left, right, (((left_dim,), (right_dim,)), ((), ())), pre...  126 us
    pallas_call x4, Pallas kernels, expert_pass(): pl.pallas_call(functools.partial(expert_kernel, count, len(carried)), gri...  120 us
    ppermute x70, starting transfers between devices, swap(): lax.ppermute(value, axis, [(i, i ^ distance) for i in range(lax.axis_size...  66 us
    pallas_call x2, Pallas kernels, down_pass(): pl.pallas_call(functools.partial(down_kernel, len(carried)), grid_spec=pl...  32.6 us
    pallas_call x1, Pallas kernels, up_pass(): pl.pallas_call(up_kernel, grid_spec=pltpu.PrefetchScalarGridSpec(num_scal...  26.8 us
  transfers between devices with their start and end apart: 76, of which 30 were waited for; matrix products, arithmetic and copies ran while one was open for 25% of the time, Pallas kernels for 24%

profile of v9, /device:TPU:0, one launch (start us, length us, event | category | flops | bytes accessed | tf_op | source)
XLA Modules:
  0.0 1004.7 jit_solution(4877942338997652090)
XLA Ops:
  21.8 5.9 slice_bitcast_fusion
  40.3 6.9 convolution_convert_fusion.3.rows
  47.2 127.2 %all-gather.4.cloned.1.call-done.right = bf16[2048,2176]{1,0:T(8,128)(2,1)} async-done(((bf16[256,2176]{1,0:T(8,128)(2,1)}), bf16[2048,2176]{1,0:T(8,128)(2,1)}) %all-gather.4.cloned.1.call-update) | async-done | bytes 8912912 | tf_op jit(solution)/shard_map/all_gather | solution.py:595
  184.8 11.7 %fusion.3.q_in.k_in.v_in = f32[1024,1536]{1,0:T(8,128)} fusion(bf16[1024,2048]{1,0:T(8,128)(2,1)} %fusion.2, bf16[2048,2176]{1,0:T(8,128)(2,1)} %all-gather.4.cloned.1.call-done.right), kind=kOutput, calls=%fused_computation.8 | convolution fusion | flops 6442450944 | bytes 16777216 | tf_op jit(solution)/shard_map/dot_general | solution.py:673
  200.8 12.9 %attention.1 = (bf16[1024,512]{1,0:T(8,128)(2,1)S(1)}, bf16[1024,512]{1,0:T(8,128)(2,1)S(1)}, bf16[1024,512]{1,0:T(8,128)(2,1)S(1)}, bf16[1024,512]{1,0:T(8,128)(2,1)S(1)}, f32[4,1024,1]{2,1,0:T(8,128)}) custom-call(f32[1024,1536]{1,0:T(8,128)} %fusion.3.q_in.k_in.v_in, f32[1024,1536]{1,0:T(8,128)} %fusion.3.q_in.k_in.v_in, ...), custom_call_target="tpu_custom_call" | custom-call | flops 1342177280 | bytes 10485760 | tf_op jit(solution)/shard_map/attention/pallas_call | solution.py:135
  217.4 5.5 spread.2
  236.7 11.0 %down.2 = (bf16[3072,2048]{1,0:T(8,128)(2,1)}, bf16[3072,1408]{1,0:T(8,128)(2,1)}) custom-call(s32[3]{0:T(128)S(1)} %pad_add_fusion.where, bf16[768,2048]{1,0:T(8,128)(2,1)} %convolution_convert_fusion.3.rows, bf16[1024,1408]{1,0:T(8,128)(2,1)S(1)} %get-tuple-element.236.own, bf16[1024,1408]{1,0:T(8,128)(2,1)} %collective-permute-done.came), custom_call_target="tpu_custom_call" | custom-call | flops 4429185024 | bytes 14221312 | tf_op jit(solution)/shard_map/down/pallas_call | solution.py:272
  247.7 12.1 %collective-permute-done.11 = bf16[1024,512]{1,0:T(8,128)(2,1)} collective-permute-done((bf16[1024,512]{1,0:T(8,128)(2,1)}, bf16[1024,512]{1,0:T(8,128)(2,1)}, u32[]{:S(2)}, u32[]{:S(2)}) %collective-permute-start.11) | collective-permute-done | bytes 1048608 | tf_op jit(solution)/shard_map/ppermute | solution.py:26
  289.6 33.5 %collective-permute-done.18.refs_2_ = bf16[768,512]{1,0:T(8,128)(2,1)S(1)} collective-permute-done((bf16[768,512]{1,0:T(8,128)(2,1)S(1)}, bf16[768,512]{1,0:T(8,128)(2,1)S(1)}, u32[]{:S(2)}, u32[]{:S(2)}) %collective-permute-start.18) | collective-permute-done | bytes 786464 | tf_op jit(solution)/shard_map/ppermute | solution.py:26
  329.7 20.3 %collective-permute-done.20.refs_10_ = bf16[1184,1408]{1,0:T(8,128)(2,1)S(1)} collective-permute-done((bf16[1184,1408]{1,0:T(8,128)(2,1)S(1)}, bf16[1184,1408]{1,0:T(8,128)(2,1)S(1)}, u32[]{:S(2)}, u32[]{:S(2)}) %collective-permute-start.20) | collective-permute-done | bytes 3334176 | tf_op jit(solution)/shard_map/ppermute | solution.py:26
  351.7 30.2 %expert.4 = (bf16[3072,2048]{1,0:T(8,128)(2,1)}, bf16[3072,1408]{1,0:T(8,128)(2,1)}, bf16[3072,2816]{1,0:T(8,128)(2,1)}, bf16[768,1024]{1,0:T(8,128)(2,1)}, bf16[768,1024]{1,0:T(8,128)(2,1)}, /*index=5*/f32[1,768]{1,0:T(1,128)}) custom-call(s32[3]{0:T(128)} %copy-done.9, bf16[768,512]{1,0:T(8,128)(2,1)} %copy-done.62, bf16[768,512]{1,0:T(8,128)(2,1)} %copy-done.64, ...), custom_call_target="tpu_custom_call" | custom-call | flops 17716740096 | bytes 32768000 | tf_op jit(solution)/shard_map/expert/pallas_call | solution.py:411
  383.6 21.5 %down.3 = (bf16[3072,2048]{1,0:T(8,128)(2,1)}, bf16[3072,1408]{1,0:T(8,128)(2,1)}) custom-call(s32[3]{0:T(128)S(1)} %copy-done.10, bf16[2304,2048]{1,0:T(8,128)(2,1)} %all-gather.8.cloned.1.call-done.rows, bf16[1024,1408]{1,0:T(8,128)(2,1)S(1)} %get-tuple-element.236.own, ...), custom_call_target="tpu_custom_call", output_to_operand_aliasing={{0}: (4, {}), {1}: (5, {})} | custom-call | flops 13287555072 | bytes 31129600 | tf_op jit(solution)/shard_map/down/pallas_call | solution.py:272
  405.1 29.9 %expert.5 = (bf16[3072,2048]{1,0:T(8,128)(2,1)}, bf16[3072,1408]{1,0:T(8,128)(2,1)}, bf16[3072,2816]{1,0:T(8,128)(2,1)}, bf16[768,1024]{1,0:T(8,128)(2,1)}, bf16[768,1024]{1,0:T(8,128)(2,1)}, /*index=5*/f32[1,768]{1,0:T(1,128)}) custom-call(s32[3]{0:T(128)} %copy-done.9, ...), custom_call_target="tpu_custom_call", output_to_operand_aliasing={{0}: (15, {}), {1}: (16, {}), {2}: (17, {})} | custom-call | flops 17716740096 | bytes 32768000 | tf_op jit(solution)/shard_map/expert/pallas_call | solution.py:411
  443.5 30.2 %expert.6 = (bf16[3072,2048]{1,0:T(8,128)(2,1)}, bf16[3072,1408]{1,0:T(8,128)(2,1)}, bf16[3072,2816]{1,0:T(8,128)(2,1)}, bf16[768,1024]{1,0:T(8,128)(2,1)}, bf16[768,1024]{1,0:T(8,128)(2,1)}, /*index=5*/f32[1,768]{1,0:T(1,128)}) custom-call(s32[3]{0:T(128)} %copy-done.9, ...), custom_call_target="tpu_custom_call", output_to_operand_aliasing={{0}: (15, {}), {1}: (16, {}), {2}: (17, {})} | custom-call | flops 17716740096 | bytes 32768000 | tf_op jit(solution)/shard_map/expert/pallas_call | solution.py:411
  485.2 29.8 %expert.7 = (bf16[3072,2048]{1,0:T(8,128)(2,1)}, bf16[3072,1408]{1,0:T(8,128)(2,1)}, bf16[3072,2816]{1,0:T(8,128)(2,1)}, bf16[768,1024]{1,0:T(8,128)(2,1)}, bf16[768,1024]{1,0:T(8,128)(2,1)}, /*index=5*/f32[1,768]{1,0:T(1,128)}) custom-call(s32[3]{0:T(128)} %copy-done.9, ...), custom_call_target="tpu_custom_call", output_to_operand_aliasing={{0}: (15, {}), {1}: (16, {}), {2}: (17, {})} | custom-call | flops 17716740096 | bytes 32768000 | tf_op jit(solution)/shard_map/expert/pallas_call | solution.py:411
  523.5 26.8 %up.1 = bf16[3072,2048]{1,0:T(8,128)(2,1)} custom-call(s32[3]{0:T(128)S(1)} %copy-done.11, bf16[3072,1408]{1,0:T(8,128)(2,1)} %get-tuple-element.184.act, bf16[1024,1408]{1,0:T(8,128)(2,1)S(1)} %get-tuple-element.236.own, bf16[1024,1408]{1,0:T(8,128)(2,1)} %collective-permute-done.came), custom_call_target="tpu_custom_call" | custom-call | flops 17716740096 | bytes 27000832 | tf_op jit(solution)/shard_map/up/pallas_call | solution.py:339
  567.7 18.0 %fusion.14 = bf16[1024,1408]{1,0:T(8,128)(2,1)} fusion(bf16[3072,1408]{1,0:T(8,128)(2,1)} %get-tuple-element.184.act, bf16[3072,2048]{1,0:T(8,128)(2,1)} %get-tuple-element.158, s32[]{:T(128)S(6)} %select_n.171), kind=kOutput, calls=%fused_computation.22 | convolution fusion | flops 8859811840 | bytes 17825796 | tf_op jit(solution)/shard_map/dot_general | solution.py:30
  610.2 16.5 %convolution_convert_fusion.2 = bf16[512,2816]{1,0:T(8,128)(2,1)} fusion(bf16[3072,2816]{1,0:T(8,128)(2,1)} %get-tuple-element.183, bf16[3072,2048]{1,0:T(8,128)(2,1)} %get-tuple-element.164, s32[]{:T(128)S(6)} %select_n.171), kind=kOutput, calls=%fused_computation.18 | convolution fusion | flops 8859811840 | bytes 23330820 | tf_op jit(solution)/shard_map/dot_general | solution.py:30
  626.7 11.9 %convolution_convert_fusion.1 = bf16[512,2816]{1,0:T(8,128)(2,1)} fusion(bf16[3072,2816]{1,0:T(8,128)(2,1)S(1)} %bitcast.151, bf16[3072,2048]{1,0:T(8,128)(2,1)} %get-tuple-element.164, s32[]{:T(128)S(6)} %select_n.173), kind=kOutput, calls=%fused_computation.17 | convolution fusion | flops 8859811840 | bytes 23330820 | tf_op jit(solution)/shard_map/dot_general | solution.py:30
  638.6 16.8 %collective-permute-done.47 = bf16[1024,512]{1,0:T(8,128)(2,1)S(1)} collective-permute-done((bf16[1024,512]{1,0:T(8,128)(2,1)S(1)}, bf16[1024,512]{1,0:T(8,128)(2,1)S(1)}, u32[]{:S(2)}, u32[]{:S(2)}) %collective-permute-start.47) | collective-permute-done | bytes 1048608 | tf_op jit(solution)/shard_map/ppermute | solution.py:26
  679.6 15.9 %attention_back.1.left = bf16[1024,1536]{1,0:T(8,128)(2,1)} custom-call(bf16[1024,512]{1,0:T(8,128)(2,1)S(1)} %copy-done.13, bf16[1024,512]{1,0:T(8,128)(2,1)S(1)} %copy-done.15, bf16[1024,512]{1,0:T(8,128)(2,1)S(1)} %copy-done.17, f32[4,1024,1]{2,1,0:T(8,128)} %get-tuple-element.175.logs, bf16[1024,512]{1,0:T(8,128)(2,1)S(1)} %copy-done.18, ...), custom_call_target="tpu_custom_call" | custom-call | flops 3355443200 | bytes 8388608 | tf_op jit(solution)/shard_map/attention_back/pallas_call | solution.py:188
  704.1 10.7 %convolution_convert_fusion = bf16[2048,1536]{1,0:T(8,128)(2,1)} fusion(bf16[1024,2048]{1,0:T(8,128)(2,1)S(1)} %copy-done.32, bf16[1024,1536]{1,0:T(8,128)(2,1)} %attention_back.1.left), kind=kOutput, calls=%fused_computation.7 | convolution fusion | flops 6445596672 | bytes 13631488 | tf_op jit(solution)/shard_map/dot_general | solution.py:30
  714.9 31.0 %collective-permute-done.50 = bf16[768,512]{1,0:T(8,128)(2,1)} collective-permute-done((bf16[768,512]{1,0:T(8,128)(2,1)S(1)}, bf16[768,512]{1,0:T(8,128)(2,1)}, u32[]{:S(2)}, u32[]{:S(2)}) %collective-permute-start.50) | collective-permute-done | bytes 786464 | tf_op jit(solution)/shard_map/ppermute | solution.py:26
  745.9 12.1 %spread.3 = (bf16[1024,1024]{1,0:T(8,128)(2,1)S(1)}, bf16[1024,1024]{1,0:T(8,128)(2,1)}) custom-call(s32[3]{0:T(128)S(1)} %copy-done.11, bf16[1024,1536]{1,0:T(8,128)(2,1)} %attention_back.1.left, bf16[2048,2176]{1,0:T(8,128)(2,1)} %all-gather.4.cloned.1.call-done.right), custom_call_target="tpu_custom_call" | custom-call | flops 6442450944 | bytes 13631488 | tf_op jit(solution)/shard_map/spread/pallas_call | solution.py:310
  761.9 17.0 %collective-permute-done.67 = bf16[256,1408]{1,0:T(8,128)(2,1)} collective-permute-done((bf16[256,1408]{1,0:T(8,128)(2,1)}, bf16[256,1408]{1,0:T(8,128)(2,1)}, u32[]{:S(2)}, u32[]{:S(2)}) %collective-permute-start.67) | collective-permute-done | bytes 720928 | tf_op jit(solution)/shard_map/ppermute | solution.py:26
  790.7 26.2 %fusion.11.refs_0_ = bf16[1024,2816]{1,0:T(8,128)(2,1)} fusion(bf16[3072,2816]{1,0:T(8,128)(2,1)} %get-tuple-element.183, bf16[3072,2048]{1,0:T(8,128)(2,1)} %get-tuple-element.164, s32[]{:T(128)S(6)} %select_n.186), kind=kOutput, calls=%fused_computation.16 | convolution fusion | flops 17719623680 | bytes 29360132 | tf_op jit(solution)/shard_map/dot_general | solution.py:30
  816.9 13.5 %fusion.17.refs_3_ = bf16[1024,1408]{1,0:T(8,128)(2,1)} fusion(bf16[3072,1408]{1,0:T(8,128)(2,1)S(1)} %bitcast.153, bf16[3072,2048]{1,0:T(8,128)(2,1)} %get-tuple-element.158, s32[]{:T(128)S(6)} %select_n.186), kind=kOutput, calls=%fused_computation.23 | convolution fusion | flops 8859811840 | bytes 17825796 | tf_op jit(solution)/shard_map/dot_general | solution.py:30
  830.5 24.4 %collective-permute-done.51 = bf16[768,512]{1,0:T(8,128)(2,1)S(1)} collective-permute-done((bf16[768,512]{1,0:T(8,128)(2,1)S(1)}, bf16[768,512]{1,0:T(8,128)(2,1)S(1)}, u32[]{:S(2)}, u32[]{:S(2)}) %collective-permute-start.51) | collective-permute-done | bytes 786464 | tf_op jit(solution)/shard_map/ppermute | solution.py:26
  866.9 20.3 %collective-permute-done.53 = bf16[1024,512]{1,0:T(8,128)(2,1)S(1)} collective-permute-done((bf16[1024,512]{1,0:T(8,128)(2,1)S(1)}, bf16[1024,512]{1,0:T(8,128)(2,1)S(1)}, u32[]{:S(2)}, u32[]{:S(2)}) %collective-permute-start.53) | collective-permute-done | bytes 1048608 | tf_op jit(solution)/shard_map/ppermute | solution.py:26
  890.3 20.0 %collective-permute-done.62 = f32[6,2048]{1,0:T(8,128)S(1)} collective-permute-done((f32[6,2048]{1,0:T(8,128)S(1)}, f32[6,2048]{1,0:T(8,128)S(1)}, u32[]{:S(2)}, u32[]{:S(2)}) %collective-permute-start.62) | collective-permute-done | bytes 49184 | tf_op jit(solution)/shard_map/ppermute | solution.py:26
  911.5 36.0 %collective-permute-done.63 = f32[6,2048]{1,0:T(8,128)S(1)} collective-permute-done((f32[6,2048]{1,0:T(8,128)S(1)}, f32[6,2048]{1,0:T(8,128)S(1)}, u32[]{:S(2)}, u32[]{:S(2)}) %collective-permute-start.63) | collective-permute-done | bytes 49184 | tf_op jit(solution)/shard_map/ppermute | solution.py:26
  971.8 13.0 %expert_grad_sum.1 = f32[3,1024,1408]{2,1,0:T(8,128)} custom-call(bf16[1024,2816]{1,0:T(8,128)(2,1)} %fusion.11.refs_0_, bf16[512,2816]{1,0:T(8,128)(2,1)} %collective-permute-done.68.refs_1_, bf16[512,2816]{1,0:T(8,128)(2,1)} %collective-permute-done.69.refs_2_, bf16[1024,1408]{1,0:T(8,128)(2,1)S(1)} %copy-done, ...), custom_call_target="tpu_custom_call" | custom-call | flops 4325376 | bytes 34603008 | tf_op jit(solution)/shard_map/expert_grad_sum/pallas_call | solution.py:495
  (451 shorter events, 270.4 us)
Async XLA Ops:
  7.2 167.2 %all-gather.4.cloned.1.call-start = ((), (), s32[]{:S(2)}) async-start(), calls=%async_computation.3 | async-start | bytes 10027008 | tf_op jit(solution)/shard_map/all_gather | solution.py:595
  10.3 256.4 %all-gather.6.cloned.1.call-start = ((), (), s32[]{:S(2)}) async-start(), calls=%async_computation.4 | async-start | bytes 5242880 | tf_op jit(solution)/shard_map/all_gather | solution.py:661
  14.0 162.8 %collective-permute-start.4 = (f32[1,768]{1,0:T(1,128)S(1)}, f32[1,768]{1,0:T(1,128)S(1)}, u32[]{:S(2)}, u32[]{:S(2)}) collective-permute-start(f32[1,768]{1,0:T(1,128)S(1)} %fusion.36), channel_id=1, source_target_pairs={{0,8},{4,12},{8,0},{12,4},{16,24},{20,28},{24,16},{28,20},{1,9},{5... | collective-permute-start | bytes 9224 | tf_op jit(solution)/shard_map/ppermute | solution.py:26
  17.7 160.7 %collective-permute-start.5 = (f32[1,768]{1,0:T(1,128)S(1)}, f32[1,768]{1,0:T(1,128)S(1)}, u32[]{:S(2)}, u32[]{:S(2)}) collective-permute-start(f32[1,768]{1,0:T(1,128)S(1)} %fusion.31), channel_id=1, source_target_pairs={{0,16},{4,20},{8,24},{12,28},{16,0},{20,4},{24,8},{28,12},{1,17},{... | collective-permute-start | bytes 9224 | tf_op jit(solution)/shard_map/ppermute | solution.py:26
  20.9 163.3 %collective-permute-start.6 = (f32[1,768]{1,0:T(1,128)S(1)}, f32[1,768]{1,0:T(1,128)S(1)}, u32[]{:S(2)}, u32[]{:S(2)}) collective-permute-start(f32[1,768]{1,0:T(1,128)S(1)} %fusion.26), channel_id=1, source_target_pairs={{0,24},{4,28},{8,16},{12,20},{16,8},{20,12},{24,0},{28,4},{1,25},{... | collective-permute-start | bytes 9224 | tf_op jit(solution)/shard_map/ppermute | solution.py:26
  20.9 163.3 %collective-permute-start.1 = (f32[1,1024]{1,0:T(1,128)S(1)}, f32[1,1024]{1,0:T(1,128)S(1)}, u32[]{:S(2)}, u32[]{:S(2)}) collective-permute-start(f32[1,1024]{1,0:T(1,128)S(1)} %get-tuple-element.273), channel_id=1, source_target_pairs={{0,8},{4,12},{8,0},{12,4},{16,24},{20,28},{24,16},{28,20},{1,9},{5... | collective-permute-start | bytes 12296 | tf_op jit(solution)/shard_map/ppermute | solution.py:26
  27.7 156.5 %collective-permute-start = (bf16[1024,1408]{1,0:T(8,128)(2,1)S(1)}, bf16[1024,1408]{1,0:T(8,128)(2,1)}, u32[]{:S(2)}, u32[]{:S(2)}) collective-permute-start(bf16[1024,1408]{1,0:T(8,128)(2,1)S(1)} %get-tuple-element.236.own), channel_id=1, source_target_pairs={{0,4},{4,0},{8,12},{12,8},{16,20},{20,16},{24,28},{28,24},{1,5},{5... | collective-permute-start | bytes 8650760 | tf_op jit(solution)/shard_map/ppermute | solution.py:26
  184.6 199.0 %all-gather.8.cloned.1.call-start = ((), (), s32[]{:S(2)}) async-start(), calls=%async_computation.5 | async-start | bytes 11796480 | tf_op jit(solution)/shard_map/all_gather | solution.py:697
  272.8 426.7 %reduce-scatter.4.cloned.1.call-start = ((), (), s32[]{:S(2)}) async-start(), calls=%async_computation.6 | async-start | bytes 15728640 | tf_op jit(solution)/shard_map/reduce_scatter | solution.py:788
  276.0 74.0 %collective-permute-start.20 = (bf16[1184,1408]{1,0:T(8,128)(2,1)S(1)}, bf16[1184,1408]{1,0:T(8,128)(2,1)S(1)}, u32[]{:S(2)}, u32[]{:S(2)}) collective-permute-start(bf16[1184,1408]{1,0:T(8,128)(2,1)S(1)} %pad_maximum_fusion.1), channel_id=1, source_target_pairs={{0,4},{4,0},{8,12},{12,8},{16,20},{20,16},{24,28},{28,24},{1,5},{5... | collective-permute-start | bytes 10002440 | tf_op jit(solution)/shard_map/ppermute | solution.py:26
  289.1 37.9 %collective-permute-start.15 = (bf16[768,512]{1,0:T(8,128)(2,1)S(1)}, bf16[768,512]{1,0:T(8,128)(2,1)}, u32[]{:S(2)}, u32[]{:S(2)}) collective-permute-start(bf16[768,512]{1,0:T(8,128)(2,1)S(1)} %fusion.101), channel_id=1, source_target_pairs={{0,16},{4,20},{8,24},{12,28},{16,0},{20,4},{24,8},{28,12},{1,17},{... | collective-permute-start | bytes 2359304 | tf_op jit(solution)/shard_map/ppermute | solution.py:26
  289.6 40.0 %collective-permute-start.17 = (bf16[768,512]{1,0:T(8,128)(2,1)S(1)}, bf16[768,512]{1,0:T(8,128)(2,1)S(1)}, u32[]{:S(2)}, u32[]{:S(2)}) collective-permute-start(bf16[768,512]{1,0:T(8,128)(2,1)S(1)} %fusion.99.refs_0_), channel_id=1, source_target_pairs={{0,1},{1,0},{2,3},{3,2},{4,5},{5,4},{6,7},{7,6},{8,9},{9,8},{10,11... | collective-permute-start | bytes 2359304 | tf_op jit(solution)/shard_map/ppermute | solution.py:26
  327.0 55.0 %collective-permute-start.16 = (bf16[768,512]{1,0:T(8,128)(2,1)}, bf16[768,512]{1,0:T(8,128)(2,1)}, u32[]{:S(2)}, u32[]{:S(2)}) collective-permute-start(bf16[768,512]{1,0:T(8,128)(2,1)} %fusion.102), channel_id=1, source_target_pairs={{0,24},{4,28},{8,16},{12,20},{16,8},{20,12},{24,0},{28,4},{1,25},{... | collective-permute-start | bytes 2359304 | tf_op jit(solution)/shard_map/ppermute | solution.py:26
  328.2 53.8 %collective-permute-start.27 = (bf16[768,512]{1,0:T(8,128)(2,1)}, bf16[768,512]{1,0:T(8,128)(2,1)}, u32[]{:S(2)}, u32[]{:S(2)}) collective-permute-start(bf16[768,512]{1,0:T(8,128)(2,1)} %collective-permute-done.15.refs_0_), channel_id=1, source_target_pairs={{0,2},{1,3},{2,0},{3,1},{4,6},{5,7},{6,4},{7,5},{8,10},{9,11},{10,... | collective-permute-start | bytes 2359304 | tf_op jit(solution)/shard_map/ppermute | solution.py:26
  329.6 75.5 %collective-permute-start.26 = (bf16[768,512]{1,0:T(8,128)(2,1)}, bf16[768,512]{1,0:T(8,128)(2,1)}, u32[]{:S(2)}, u32[]{:S(2)}) collective-permute-start(bf16[768,512]{1,0:T(8,128)(2,1)} %collective-permute-done.15.refs_0_), channel_id=1, source_target_pairs={{0,1},{1,0},{2,3},{3,2},{4,5},{5,4},{6,7},{7,6},{8,9},{9,8},{10,11... | collective-permute-start | bytes 2359304 | tf_op jit(solution)/shard_map/ppermute | solution.py:26
  382.0 53.1 %collective-permute-start.25 = (bf16[768,512]{1,0:T(8,128)(2,1)}, bf16[768,512]{1,0:T(8,128)(2,1)}, u32[]{:S(2)}, u32[]{:S(2)}) collective-permute-start(bf16[768,512]{1,0:T(8,128)(2,1)} %collective-permute-done.16.refs_0_), channel_id=1, source_target_pairs={{0,2},{1,3},{2,0},{3,1},{4,6},{5,7},{6,4},{7,5},{8,10},{9,11},{10,... | collective-permute-start | bytes 2359304 | tf_op jit(solution)/shard_map/ppermute | solution.py:26
  383.6 51.5 %collective-permute-start.21 = (bf16[768,512]{1,0:T(8,128)(2,1)}, bf16[768,512]{1,0:T(8,128)(2,1)}, u32[]{:S(2)}, u32[]{:S(2)}) collective-permute-start(bf16[768,512]{1,0:T(8,128)(2,1)} %fusion.100), channel_id=1, source_target_pairs={{0,8},{4,12},{8,0},{12,4},{16,24},{20,28},{24,16},{28,20},{1,9},{5... | collective-permute-start | bytes 2359304 | tf_op jit(solution)/shard_map/ppermute | solution.py:26
  435.9 37.9 %collective-permute-start.23 = (bf16[768,512]{1,0:T(8,128)(2,1)}, bf16[768,512]{1,0:T(8,128)(2,1)}, u32[]{:S(2)}, u32[]{:S(2)}) collective-permute-start(bf16[768,512]{1,0:T(8,128)(2,1)} %collective-permute-done.21.refs_0_), channel_id=1, source_target_pairs={{0,2},{1,3},{2,0},{3,1},{4,6},{5,7},{6,4},{7,5},{8,10},{9,11},{10,... | collective-permute-start | bytes 2359304 | tf_op jit(solution)/shard_map/ppermute | solution.py:26
  477.2 40.8 %collective-permute-start.35 = (bf16[768,512]{1,0:T(8,128)(2,1)}, bf16[768,512]{1,0:T(8,128)(2,1)}, u32[]{:S(2)}, u32[]{:S(2)}) collective-permute-start(bf16[768,512]{1,0:T(8,128)(2,1)} %add_convert_fusion.9), channel_id=1, source_target_pairs={{0,16},{4,20},{8,24},{12,28},{16,0},{20,4},{24,8},{28,12},{1,17},{... | collective-permute-start | bytes 2359304 | tf_op jit(solution)/shard_map/ppermute | solution.py:26
  552.3 410.3 %reduce-scatter.8.cloned.1.call-start = ((), (), s32[]{:S(2)}) async-start(), calls=%async_computation.8 | async-start | bytes 2359296 | tf_op jit(solution)/shard_map/reduce_scatter | solution.py:833
  607.5 47.9 %collective-permute-start.47 = (bf16[1024,512]{1,0:T(8,128)(2,1)S(1)}, bf16[1024,512]{1,0:T(8,128)(2,1)S(1)}, u32[]{:S(2)}, u32[]{:S(2)}) collective-permute-start(bf16[1024,512]{1,0:T(8,128)(2,1)S(1)} %get-tuple-element.296), channel_id=1, source_target_pairs={{0,2},{1,3},{2,0},{3,1},{4,6},{5,7},{6,4},{7,5},{8,10},{9,11},{10,... | collective-permute-start | bytes 3145736 | tf_op jit(solution)/shard_map/ppermute | solution.py:26
  609.0 46.4 %collective-permute-start.48 = (bf16[448,1408]{1,0:T(8,128)(2,1)S(1)}, bf16[448,1408]{1,0:T(8,128)(2,1)S(1)}, u32[]{:S(2)}, u32[]{:S(2)}) collective-permute-start(bf16[448,1408]{1,0:T(8,128)(2,1)S(1)} %copy-done.44), channel_id=1, source_target_pairs={{0,4},{4,0},{8,12},{12,8},{16,20},{20,16},{24,28},{28,24},{1,5},{5... | collective-permute-start | bytes 3784712 | tf_op jit(solution)/shard_map/ppermute | solution.py:26
  673.1 291.4 %reduce-scatter.6.cloned.1.call-start = ((), (), s32[]{:S(2)}) async-start(), calls=%async_computation.7 | async-start | bytes 7077888 | tf_op jit(solution)/shard_map/reduce_scatter | solution.py:841
  702.3 43.5 %collective-permute-start.50 = (bf16[768,512]{1,0:T(8,128)(2,1)S(1)}, bf16[768,512]{1,0:T(8,128)(2,1)}, u32[]{:S(2)}, u32[]{:S(2)}) collective-permute-start(bf16[768,512]{1,0:T(8,128)(2,1)S(1)} %get-tuple-element.169), channel_id=1, source_target_pairs={{0,16},{4,20},{8,24},{12,28},{16,0},{20,4},{24,8},{28,12},{1,17},{... | collective-permute-start | bytes 2359304 | tf_op jit(solution)/shard_map/ppermute | solution.py:26
  778.9 191.1 %collective-permute-start.69 = (bf16[512,2816]{1,0:T(8,128)(2,1)}, bf16[512,2816]{1,0:T(8,128)(2,1)}, u32[]{:S(2)}, u32[]{:S(2)}) collective-permute-start(bf16[512,2816]{1,0:T(8,128)(2,1)} %convolution_convert_fusion.1), channel_id=1, source_target_pairs={{0,4},{4,0},{8,12},{12,8},{16,20},{20,16},{24,28},{28,24},{1,5},{5... | collective-permute-start | bytes 8650760 | tf_op jit(solution)/shard_map/ppermute | solution.py:26
  779.7 190.3 %collective-permute-start.68 = (bf16[512,2816]{1,0:T(8,128)(2,1)}, bf16[512,2816]{1,0:T(8,128)(2,1)}, u32[]{:S(2)}, u32[]{:S(2)}) collective-permute-start(bf16[512,2816]{1,0:T(8,128)(2,1)} %convolution_convert_fusion.2), channel_id=1, source_target_pairs={{0,4},{4,0},{8,12},{12,8},{16,20},{20,16},{24,28},{28,24},{1,5},{5... | collective-permute-start | bytes 8650760 | tf_op jit(solution)/shard_map/ppermute | solution.py:26
  783.1 47.4 %collective-permute-start.52 = (bf16[768,512]{1,0:T(8,128)(2,1)S(1)}, bf16[768,512]{1,0:T(8,128)(2,1)S(1)}, u32[]{:S(2)}, u32[]{:S(2)}) collective-permute-start(bf16[768,512]{1,0:T(8,128)(2,1)S(1)} %copy-done.45), channel_id=1, source_target_pairs={{0,24},{4,28},{8,16},{12,20},{16,8},{20,12},{24,0},{28,4},{1,25},{... | collective-permute-start | bytes 2359304 | tf_op jit(solution)/shard_map/ppermute | solution.py:26
  785.3 69.6 %collective-permute-start.51 = (bf16[768,512]{1,0:T(8,128)(2,1)S(1)}, bf16[768,512]{1,0:T(8,128)(2,1)S(1)}, u32[]{:S(2)}, u32[]{:S(2)}) collective-permute-start(bf16[768,512]{1,0:T(8,128)(2,1)S(1)} %get-tuple-element.170), channel_id=1, source_target_pairs={{0,8},{4,12},{8,0},{12,4},{16,24},{20,28},{24,16},{28,20},{1,9},{5... | collective-permute-start | bytes 2359304 | tf_op jit(solution)/shard_map/ppermute | solution.py:26
  789.3 65.6 %collective-permute-start.57 = (bf16[1024,512]{1,0:T(8,128)(2,1)S(1)}, bf16[1024,512]{1,0:T(8,128)(2,1)S(1)}, u32[]{:S(2)}, u32[]{:S(2)}) collective-permute-start(bf16[1024,512]{1,0:T(8,128)(2,1)S(1)} %add_convert_fusion), channel_id=1, source_target_pairs={{0,2},{1,3},{2,0},{3,1},{4,6},{5,7},{6,4},{7,5},{8,10},{9,11},{10,... | collective-permute-start | bytes 3145736 | tf_op jit(solution)/shard_map/ppermute | solution.py:26
  865.2 92.6 %collective-permute-start.60 = (bf16[1024,512]{1,0:T(8,128)(2,1)S(1)}, bf16[1024,512]{1,0:T(8,128)(2,1)S(1)}, u32[]{:S(2)}, u32[]{:S(2)}) collective-permute-start(bf16[1024,512]{1,0:T(8,128)(2,1)S(1)} %get-tuple-element.240), channel_id=1, source_target_pairs={{0,2},{1,3},{2,0},{3,1},{4,6},{5,7},{6,4},{7,5},{8,10},{9,11},{10,... | collective-permute-start | bytes 3145736 | tf_op jit(solution)/shard_map/ppermute | solution.py:26
  889.4 96.7 %collective-permute-start.54 = (bf16[1024,1024]{1,0:T(8,128)(2,1)}, bf16[1024,1024]{1,0:T(8,128)(2,1)}, u32[]{:S(2)}, u32[]{:S(2)}) collective-permute-start(bf16[1024,1024]{1,0:T(8,128)(2,1)} %pad_maximum_fusion.5), channel_id=1, source_target_pairs={{0,1},{1,0},{2,3},{3,2},{4,5},{5,4},{6,7},{7,6},{8,9},{9,8},{10,11... | collective-permute-start | bytes 6291464 | tf_op jit(solution)/shard_map/ppermute | solution.py:26
  910.3 37.2 %collective-permute-start.63 = (f32[6,2048]{1,0:T(8,128)S(1)}, f32[6,2048]{1,0:T(8,128)S(1)}, u32[]{:S(2)}, u32[]{:S(2)}) collective-permute-start(f32[6,2048]{1,0:T(8,128)S(1)} %add.259), channel_id=1, source_target_pairs={{0,4},{4,0},{8,12},{12,8},{16,20},{20,16},{24,28},{28,24},{1,5},{5... | collective-permute-start | bytes 147464 | tf_op jit(solution)/shard_map/ppermute | solution.py:26
  (128 other events, 1705.5 us)
Sparse Core Ops, SparseCore 0:
  10.8 163.5 all-gather.3
  184.7 81.9 all-gather.5
  272.9 97.4 all-gather.7
  552.4 125.1 reduce-scatter.3
  681.0 86.9 reduce-scatter.7
  772.0 173.0 reduce-scatter.5

commit v10 on v9

--- a/solution.py
+++ b/solution.py
@@ -783,12 +783,18 @@
 
     unit = half // 128
     quarter = half // 2
-    expert_part = up_pass(where, after(activation, sums_sent[2], returned[1]), *down)
-    expert_part = after(expert_part, returned[2], came_home[3])
+    act_late = after(activation, sums_sent[2], returned[1])
+    down_given = term(grad_rows, act_late)(given_at, half)
+    down_sums = [group_send(down_given[: 56 * unit])]
+    expert_part = up_pass(
+        where, after(activation, down_given, returned[2], *gate_grad_near.values()), *down
+    )
+    expert_part = after(expert_part, down_sums[0], came_home[3], came_home[1])
     expert_own = lax.psum_scatter(expert_part, "tensor", scatter_dimension=1, tiled=True)
-    act_late = after(activation, expert_part, *gate_grad_near.values())
-    down_given = term(grad_rows, act_late)(given_at, half)
-    came_home = {s: after(v, down_given) for s, v in came_home.items()}
+    down_sums.append(group_send(down_given[56 * unit :], down_sums[0], expert_part))
+    pair_term = term(moe_rows, after(pre_grad, expert_part, came_home[0]))
+    pair_given = [pair_term(given_at + k * quarter, quarter) for k in range(2)]
+    came_home = {s: after(v, down_sums[1], *pair_given) for s, v in came_home.items()}
     back = unpacked([came_home[s] for s in range(EXPERTS)])
 
     gate_grad = jnp.concatenate(
@@ -816,18 +822,16 @@
     )
     router_grad = jnp.dot(logit_grad, moe_in, preferred_element_type=full)
     moe_gain_grad = jnp.sum(moe_grad * normed_two, axis=0)
-    pair_given = []
-    down_sums = []
     kept = []
-
-    def give_pair(sent):
-        down_sums.append(group_send(down_given[: 56 * unit], sent))
-        pair_term = term(moe_rows, after(pre_grad, sent))
-        pair_given.extend(pair_term(given_at + k * quarter, quarter) for k in range(2))
-        return (*pair_given, down_sums[0])
-
-    attn_grad = tensor_gather(hidden_grad.astype(low), give_pair)
-    down_sums.append(group_send(down_given[56 * unit : 96 * unit], down_sums[0], *pair_given))
+    pair_sums = []
+
+    def keep_pair(sent):
+        pair_sums.append(group_send(pair_given[0][: 27 * unit], down_sums[1], sent))
+        kept.append(term(moe_rows, after(pre_grad, sent))(mine_at, half))
+        return (kept[0], pair_sums[0])
+
+    attn_grad = tensor_gather(hidden_grad.astype(low), keep_pair)
+    pair_sums.append(group_send(pair_given[0][27 * unit : 48 * unit], pair_sums[0], kept[0]))
     context_grad = jnp.dot(attn_grad, out_full, preferred_element_type=full).astype(low)
     out_grad = contract(after(attn_grad, context_grad), context, 0, 0).astype(low)
     out_shard = lax.psum_scatter(out_grad, "dp", scatter_dimension=0, tiled=True).astype(full)
@@ -836,22 +840,21 @@
     outputs[2] = swap(part, "dp", 2 * group_count)
     context_grad = after(context_grad, out_grad)
     qkv_grad_rows = attention_back(query, keys, values, logs, context_grad, cosine, sine, scale)
-    qkv_grad_rows = after(qkv_grad_rows, down_sums[1])
+    qkv_grad_rows = after(qkv_grad_rows, pair_sums[1])
     qkv_grad = contract(normed_in, qkv_grad_rows, 0, 0).astype(low)
     qkv_shard = lax.psum_scatter(qkv_grad, "dp", scatter_dimension=0, tiled=True).astype(full)
-    down_sums.append(group_send(down_given[96 * unit :], down_sums[1], qkv_grad))
-    pair_sums = [group_send(v, down_sums[2]) for v in pair_given]
+    pair_sums.append(group_send(pair_given[0][48 * unit :], pair_sums[1], qkv_grad))
+    pair_last = group_send(pair_given[1], pair_sums[1], qkv_grad)
     for k in (2, 3):
         part = after(expert_own[k * MOST : (k + 1) * MOST], outputs[2])
         outputs[order[k]] = swap(part, "dp", order[k] * group_count)
 
     def keep(sent):
-        kept.append(term(moe_rows, after(pre_grad, sent))(mine_at, half))
-        kept.append(term(grad_rows, after(activation, kept[0]))(mine_at, half))
-        return (*kept, outputs[3], outputs[1])
+        kept.append(term(grad_rows, after(activation, sent))(mine_at, half))
+        return (kept[1], outputs[2], pair_sums[2])
 
     parts = spread_dot(
-        where, after(qkv_grad_rows, qkv_grad, outputs[2]), first, 0, tensor_count
+        where, after(qkv_grad_rows, qkv_grad), first, 0, tensor_count
     )
     normed_grad = near_reduce(*parts, [], filler=keep)
     normed_one = inputs_own * scale_one
@@ -865,11 +868,11 @@
     )
     mine = all_sum(mine)
     expert_grad = expert_grad_sum(
-        group_finish(kept[0], pair_sums, member, group_count),
+        group_finish(kept[0], [jnp.concatenate(pair_sums, 0), pair_last], member, group_count),
         group_finish(kept[1], [jnp.concatenate(down_sums, 0)], member, group_count),
         hidden_size,
     )
-    input_grad = tensor_gather(input_own.astype(low), lambda sent: (mine,))
+    input_grad = tensor_gather(input_own.astype(low), lambda sent: (mine, outputs[3], outputs[1]))
     input_grad = input_grad.astype(full)
     layer_own = hidden + unpacked([outputs[s] for s in range(EXPERTS)])
     layer_out = tensor_gather(layer_own.astype(low)).astype(full)

time: 1010 us -> 1040 us (1.030)
  waiting for transfers between devices: 399 us -> 424 us
    ppermute x70 -> x71, waiting for transfers between devices: 270 us -> 296 us  [swap(): lax.ppermute(value, axis, [(i, i ^ distance) for i in range(lax.axis_size...]
    ppermute x70 -> x71, starting transfers between devices: 66 us -> 61.1 us  [swap(): lax.ppermute(value, axis, [(i, i ^ distance) for i in range(lax.axis_size...]
    unnamed x171 -> x175, local copies, waits for them, and re-layouts: 19.8 us -> 22.4 us
  transfers between devices with their start and end apart: 76 -> 77, of which waited for: 30 -> 27; matrix products, arithmetic and copies ran while one was open for 25% -> 25% of each run, Pallas kernels for 24% -> 23%
where the time goes in v10:
time: 1040 us; the launch traced here: 1030 us
  waiting for transfers between devices  424 us (41%)
  Pallas kernels  237 us (23%)
  matrix products  159 us (15%)
  other arithmetic  73 us (7%)
  starting transfers between devices  61.6 us (6%)
  local copies, waits for them, and re-layouts  55.7 us (5%)
  between operations  16.1 us (2%)
    ppermute x71, waiting for transfers between devices, swap(): lax.ppermute(value, axis, [(i, i ^ distance) for i in range(lax.axis_size...  296 us
    all_gather x1, waiting for transfers between devices, body(): lax.all_gather(jnp.concatenate([qkv_weight.reshape(-1, 3 * size), out_wei...  127 us
    dot_general x25, matrix products, contract(): lax.dot_general(left, right, (((left_dim,), (right_dim,)), ((), ())), pre...  125 us
    pallas_call x4, Pallas kernels, expert_pass(): pl.pallas_call(functools.partial(expert_kernel, count, len(carried)), gri...  120 us
    ppermute x71, starting transfers between devices, swap(): lax.ppermute(value, axis, [(i, i ^ distance) for i in range(lax.axis_size...  61.1 us
    pallas_call x2, Pallas kernels, down_pass(): pl.pallas_call(functools.partial(down_kernel, len(carried)), grid_spec=pl...  32.8 us
    pallas_call x1, Pallas kernels, up_pass(): pl.pallas_call(up_kernel, grid_spec=pltpu.PrefetchScalarGridSpec(num_scal...  27 us
    unnamed x175, local copies, waits for them, and re-layouts  22.4 us
  transfers between devices with their start and end apart: 77, of which 27 were waited for; matrix products, arithmetic and copies ran while one was open for 25% of the time, Pallas kernels for 23%

profile of v10, /device:TPU:0, one launch (start us, length us, event | category | flops | bytes accessed | tf_op | source)
XLA Modules:
  0.0 1027.1 jit_solution(7800835709663363549)
XLA Ops:
  22.2 5.8 slice_bitcast_fusion
  40.1 6.9 convolution_convert_fusion.3.rows
  47.0 127.4 %all-gather.4.cloned.1.call-done.right = bf16[2048,2176]{1,0:T(8,128)(2,1)} async-done(((bf16[256,2176]{1,0:T(8,128)(2,1)}), bf16[2048,2176]{1,0:T(8,128)(2,1)}) %all-gather.4.cloned.1.call-update) | async-done | bytes 8912912 | tf_op jit(solution)/shard_map/all_gather | solution.py:595
  184.9 11.7 %fusion.3.q_in.k_in.v_in = f32[1024,1536]{1,0:T(8,128)} fusion(bf16[1024,2048]{1,0:T(8,128)(2,1)} %fusion.2, bf16[2048,2176]{1,0:T(8,128)(2,1)} %all-gather.4.cloned.1.call-done.right), kind=kOutput, calls=%fused_computation.8 | convolution fusion | flops 6442450944 | bytes 16777216 | tf_op jit(solution)/shard_map/dot_general | solution.py:673
  200.8 12.9 %attention.1 = (bf16[1024,512]{1,0:T(8,128)(2,1)S(1)}, bf16[1024,512]{1,0:T(8,128)(2,1)S(1)}, bf16[1024,512]{1,0:T(8,128)(2,1)S(1)}, bf16[1024,512]{1,0:T(8,128)(2,1)S(1)}, f32[4,1024,1]{2,1,0:T(8,128)}) custom-call(f32[1024,1536]{1,0:T(8,128)} %fusion.3.q_in.k_in.v_in, f32[1024,1536]{1,0:T(8,128)} %fusion.3.q_in.k_in.v_in, ...), custom_call_target="tpu_custom_call" | custom-call | flops 1342177280 | bytes 10485760 | tf_op jit(solution)/shard_map/attention/pallas_call | solution.py:135
  217.8 5.5 spread.2
  237.0 11.2 %down.2 = (bf16[3072,2048]{1,0:T(8,128)(2,1)}, bf16[3072,1408]{1,0:T(8,128)(2,1)}) custom-call(s32[3]{0:T(128)S(1)} %pad_add_fusion.where, bf16[768,2048]{1,0:T(8,128)(2,1)} %convolution_convert_fusion.3.rows, bf16[1024,1408]{1,0:T(8,128)(2,1)S(1)} %get-tuple-element.236.own, bf16[1024,1408]{1,0:T(8,128)(2,1)} %collective-permute-done.came), custom_call_target="tpu_custom_call" | custom-call | flops 4429185024 | bytes 14221312 | tf_op jit(solution)/shard_map/down/pallas_call | solution.py:272
  248.2 11.9 %collective-permute-done.11 = bf16[1024,512]{1,0:T(8,128)(2,1)} collective-permute-done((bf16[1024,512]{1,0:T(8,128)(2,1)}, bf16[1024,512]{1,0:T(8,128)(2,1)}, u32[]{:S(2)}, u32[]{:S(2)}) %collective-permute-start.11) | collective-permute-done | bytes 1048608 | tf_op jit(solution)/shard_map/ppermute | solution.py:26
  290.2 33.6 %collective-permute-done.18.refs_2_ = bf16[768,512]{1,0:T(8,128)(2,1)S(1)} collective-permute-done((bf16[768,512]{1,0:T(8,128)(2,1)S(1)}, bf16[768,512]{1,0:T(8,128)(2,1)S(1)}, u32[]{:S(2)}, u32[]{:S(2)}) %collective-permute-start.18) | collective-permute-done | bytes 786464 | tf_op jit(solution)/shard_map/ppermute | solution.py:26
  330.5 19.5 %collective-permute-done.20.refs_10_ = bf16[1184,1408]{1,0:T(8,128)(2,1)S(1)} collective-permute-done((bf16[1184,1408]{1,0:T(8,128)(2,1)S(1)}, bf16[1184,1408]{1,0:T(8,128)(2,1)S(1)}, u32[]{:S(2)}, u32[]{:S(2)}) %collective-permute-start.20) | collective-permute-done | bytes 3334176 | tf_op jit(solution)/shard_map/ppermute | solution.py:26
  351.7 30.0 %expert.4 = (bf16[3072,2048]{1,0:T(8,128)(2,1)}, bf16[3072,1408]{1,0:T(8,128)(2,1)}, bf16[3072,2816]{1,0:T(8,128)(2,1)}, bf16[768,1024]{1,0:T(8,128)(2,1)}, bf16[768,1024]{1,0:T(8,128)(2,1)}, /*index=5*/f32[1,768]{1,0:T(1,128)}) custom-call(s32[3]{0:T(128)} %copy-done.9, bf16[768,512]{1,0:T(8,128)(2,1)} %copy-done.67, bf16[768,512]{1,0:T(8,128)(2,1)} %copy-done.69, ...), custom_call_target="tpu_custom_call" | custom-call | flops 17716740096 | bytes 32768000 | tf_op jit(solution)/shard_map/expert/pallas_call | solution.py:411
  383.4 21.6 %down.3 = (bf16[3072,2048]{1,0:T(8,128)(2,1)}, bf16[3072,1408]{1,0:T(8,128)(2,1)}) custom-call(s32[3]{0:T(128)S(1)} %copy-done.10, bf16[2304,2048]{1,0:T(8,128)(2,1)} %all-gather.8.cloned.1.call-done.rows, bf16[1024,1408]{1,0:T(8,128)(2,1)S(1)} %get-tuple-element.236.own, ...), custom_call_target="tpu_custom_call", output_to_operand_aliasing={{0}: (4, {}), {1}: (5, {})} | custom-call | flops 13287555072 | bytes 31129600 | tf_op jit(solution)/shard_map/down/pallas_call | solution.py:272
  405.0 30.0 %expert.5 = (bf16[3072,2048]{1,0:T(8,128)(2,1)}, bf16[3072,1408]{1,0:T(8,128)(2,1)}, bf16[3072,2816]{1,0:T(8,128)(2,1)}, bf16[768,1024]{1,0:T(8,128)(2,1)}, bf16[768,1024]{1,0:T(8,128)(2,1)}, /*index=5*/f32[1,768]{1,0:T(1,128)}) custom-call(s32[3]{0:T(128)} %copy-done.9, ...), custom_call_target="tpu_custom_call", output_to_operand_aliasing={{0}: (15, {}), {1}: (16, {}), {2}: (17, {})} | custom-call | flops 17716740096 | bytes 32768000 | tf_op jit(solution)/shard_map/expert/pallas_call | solution.py:411
  443.4 30.2 %expert.6 = (bf16[3072,2048]{1,0:T(8,128)(2,1)}, bf16[3072,1408]{1,0:T(8,128)(2,1)}, bf16[3072,2816]{1,0:T(8,128)(2,1)}, bf16[768,1024]{1,0:T(8,128)(2,1)}, bf16[768,1024]{1,0:T(8,128)(2,1)}, /*index=5*/f32[1,768]{1,0:T(1,128)}) custom-call(s32[3]{0:T(128)} %copy-done.9, ...), custom_call_target="tpu_custom_call", output_to_operand_aliasing={{0}: (15, {}), {1}: (16, {}), {2}: (17, {})} | custom-call | flops 17716740096 | bytes 32768000 | tf_op jit(solution)/shard_map/expert/pallas_call | solution.py:411
  485.2 29.8 %expert.7 = (bf16[3072,2048]{1,0:T(8,128)(2,1)}, bf16[3072,1408]{1,0:T(8,128)(2,1)}, bf16[3072,2816]{1,0:T(8,128)(2,1)}, bf16[768,1024]{1,0:T(8,128)(2,1)}, bf16[768,1024]{1,0:T(8,128)(2,1)}, /*index=5*/f32[1,768]{1,0:T(1,128)}) custom-call(s32[3]{0:T(128)} %copy-done.9, ...), custom_call_target="tpu_custom_call", output_to_operand_aliasing={{0}: (15, {}), {1}: (16, {}), {2}: (17, {})} | custom-call | flops 17716740096 | bytes 32768000 | tf_op jit(solution)/shard_map/expert/pallas_call | solution.py:411
  526.8 14.1 %fusion.14 = bf16[1024,1408]{1,0:T(8,128)(2,1)S(1)} fusion(bf16[3072,1408]{1,0:T(8,128)(2,1)} %get-tuple-element.185.act, bf16[3072,2048]{1,0:T(8,128)(2,1)} %get-tuple-element.144, s32[]{:T(128)S(6)} %select_n.169), kind=kOutput, calls=%fused_computation.22 | convolution fusion | flops 8859811840 | bytes 17825796 | tf_op jit(solution)/shard_map/dot_general | solution.py:30
  549.7 27.0 %up.1 = bf16[3072,2048]{1,0:T(8,128)(2,1)} custom-call(s32[3]{0:T(128)S(1)} %copy-done.11, bf16[3072,1408]{1,0:T(8,128)(2,1)} %get-tuple-element.185.act, bf16[1024,1408]{1,0:T(8,128)(2,1)S(1)} %get-tuple-element.236.own, bf16[1024,1408]{1,0:T(8,128)(2,1)} %collective-permute-done.came), custom_call_target="tpu_custom_call" | custom-call | flops 17716740096 | bytes 27000832 | tf_op jit(solution)/shard_map/up/pallas_call | solution.py:339
  586.2 16.0 %collective-permute-done.45 = bf16[768,512]{1,0:T(8,128)(2,1)S(1)} collective-permute-done((bf16[768,512]{1,0:T(8,128)(2,1)S(1)}, bf16[768,512]{1,0:T(8,128)(2,1)S(1)}, u32[]{:S(2)}, u32[]{:S(2)}) %collective-permute-start.45) | collective-permute-done | bytes 786464 | tf_op jit(solution)/shard_map/ppermute | solution.py:26
  604.1 16.4 %convolution_convert_fusion.2 = bf16[512,2816]{1,0:T(8,128)(2,1)} fusion(bf16[3072,2816]{1,0:T(8,128)(2,1)} %get-tuple-element.168, bf16[3072,2048]{1,0:T(8,128)(2,1)} %get-tuple-element.161, s32[]{:T(128)S(6)} %select_n.169), kind=kOutput, calls=%fused_computation.18 | convolution fusion | flops 8859811840 | bytes 23330820 | tf_op jit(solution)/shard_map/dot_general | solution.py:30
  620.6 12.3 %convolution_convert_fusion.1 = bf16[512,2816]{1,0:T(8,128)(2,1)} fusion(bf16[3072,2816]{1,0:T(8,128)(2,1)S(1)} %bitcast.151, bf16[3072,2048]{1,0:T(8,128)(2,1)} %get-tuple-element.161, s32[]{:T(128)S(6)} %select_n.172), kind=kOutput, calls=%fused_computation.17 | convolution fusion | flops 8859811840 | bytes 23330820 | tf_op jit(solution)/shard_map/dot_general | solution.py:30
  656.2 26.3 %fusion.11.refs_0_ = bf16[1024,2816]{1,0:T(8,128)(2,1)} fusion(bf16[3072,2816]{1,0:T(8,128)(2,1)} %get-tuple-element.168, bf16[3072,2048]{1,0:T(8,128)(2,1)} %get-tuple-element.161, s32[]{:T(128)S(6)} %select_n.174), kind=kOutput, calls=%fused_computation.16 | convolution fusion | flops 17719623680 | bytes 29360132 | tf_op jit(solution)/shard_map/dot_general | solution.py:30
  682.5 13.4 %collective-permute-done.49 = bf16[1024,512]{1,0:T(8,128)(2,1)S(1)} collective-permute-done((bf16[1024,512]{1,0:T(8,128)(2,1)S(1)}, bf16[1024,512]{1,0:T(8,128)(2,1)S(1)}, u32[]{:S(2)}, u32[]{:S(2)}) %collective-permute-start.49) | collective-permute-done | bytes 1048608 | tf_op jit(solution)/shard_map/ppermute | solution.py:26
  720.1 15.6 %attention_back.1.left = bf16[1024,1536]{1,0:T(8,128)(2,1)} custom-call(bf16[1024,512]{1,0:T(8,128)(2,1)S(1)} %copy-done.13, bf16[1024,512]{1,0:T(8,128)(2,1)S(1)} %copy-done.15, bf16[1024,512]{1,0:T(8,128)(2,1)S(1)} %copy-done.17, f32[4,1024,1]{2,1,0:T(8,128)} %get-tuple-element.177.logs, bf16[1024,512]{1,0:T(8,128)(2,1)S(1)} %copy-done.18, ...), custom_call_target="tpu_custom_call" | custom-call | flops 3355443200 | bytes 8388608 | tf_op jit(solution)/shard_map/attention_back/pallas_call | solution.py:188
  735.8 7.8 collective-permute-done.57
  744.6 10.5 %convolution_convert_fusion = bf16[2048,1536]{1,0:T(8,128)(2,1)} fusion(bf16[1024,2048]{1,0:T(8,128)(2,1)S(1)} %copy-done.28, bf16[1024,1536]{1,0:T(8,128)(2,1)} %attention_back.1.left), kind=kOutput, calls=%fused_computation.7 | convolution fusion | flops 6445596672 | bytes 13631488 | tf_op jit(solution)/shard_map/dot_general | solution.py:30
  755.1 11.3 %spread.3 = (bf16[1024,1024]{1,0:T(8,128)(2,1)S(1)}, bf16[1024,1024]{1,0:T(8,128)(2,1)S(1)}) custom-call(s32[3]{0:T(128)S(1)} %copy-done.11, bf16[1024,1536]{1,0:T(8,128)(2,1)} %attention_back.1.left, bf16[2048,2176]{1,0:T(8,128)(2,1)} %all-gather.4.cloned.1.call-done.right), custom_call_target="tpu_custom_call" | custom-call | flops 6442450944 | bytes 13631488 | tf_op jit(solution)/shard_map/spread/pallas_call | solution.py:310
  779.6 15.9 %fusion.17.refs_3_ = bf16[1024,1408]{1,0:T(8,128)(2,1)} fusion(bf16[3072,1408]{1,0:T(8,128)(2,1)} %get-tuple-element.185.act, bf16[3072,2048]{1,0:T(8,128)(2,1)} %get-tuple-element.144, s32[]{:T(128)S(6)} %select_n.174), kind=kOutput, calls=%fused_computation.23 | convolution fusion | flops 8859811840 | bytes 17825796 | tf_op jit(solution)/shard_map/dot_general | solution.py:30
  795.5 75.2 %collective-permute-done.60 = bf16[128,2816]{1,0:T(8,128)(2,1)} collective-permute-done((bf16[128,2816]{1,0:T(8,128)(2,1)}, bf16[128,2816]{1,0:T(8,128)(2,1)}, u32[]{:S(2)}, u32[]{:S(2)}) %collective-permute-start.60) | collective-permute-done | bytes 720928 | tf_op jit(solution)/shard_map/ppermute | solution.py:26
  885.9 49.7 %collective-permute-done.53 = bf16[768,512]{1,0:T(8,128)(2,1)S(1)} collective-permute-done((bf16[768,512]{1,0:T(8,128)(2,1)S(1)}, bf16[768,512]{1,0:T(8,128)(2,1)S(1)}, u32[]{:S(2)}, u32[]{:S(2)}) %collective-permute-start.53) | collective-permute-done | bytes 786464 | tf_op jit(solution)/shard_map/ppermute | solution.py:26
  940.1 24.4 %collective-permute-done.65 = f32[6,2048]{1,0:T(8,128)S(1)} collective-permute-done((f32[6,2048]{1,0:T(8,128)S(1)}, f32[6,2048]{1,0:T(8,128)S(1)}, u32[]{:S(2)}, u32[]{:S(2)}) %collective-permute-start.65) | collective-permute-done | bytes 49184 | tf_op jit(solution)/shard_map/ppermute | solution.py:26
  973.2 5.6 collective-permute-done.68
  987.4 11.9 %expert_grad_sum.1 = f32[3,1024,1408]{2,1,0:T(8,128)} custom-call(bf16[1024,2816]{1,0:T(8,128)(2,1)} %fusion.11.refs_0_, bf16[512,2816]{1,0:T(8,128)(2,1)S(1)} %pad_maximum_fusion.2.refs_1_, bf16[512,2816]{1,0:T(8,128)(2,1)} %collective-permute-done.70.refs_2_, bf16[1024,1408]{1,0:T(8,128)(2,1)S(1)} %copy-done, bf16[1024,1408]{1,0:T(8,128)(2,1)S(1)} %pad_maximum_fusion.3.refs_4_), custom_call_target="tpu_custom_call" | custom-call | flops 4325376 | bytes 34603008 | tf_op jit(solution)/shard_map/expert_grad_sum/pallas_call | solution.py:495
  (459 shorter events, 269.6 us)
Async XLA Ops:
  7.2 167.2 %all-gather.4.cloned.1.call-start = ((), (), s32[]{:S(2)}) async-start(), calls=%async_computation.3 | async-start | bytes 10027008 | tf_op jit(solution)/shard_map/all_gather | solution.py:595
  10.3 256.4 %all-gather.6.cloned.1.call-start = ((), (), s32[]{:S(2)}) async-start(), calls=%async_computation.4 | async-start | bytes 5242880 | tf_op jit(solution)/shard_map/all_gather | solution.py:661
  14.5 162.3 %collective-permute-start.4 = (f32[1,768]{1,0:T(1,128)S(1)}, f32[1,768]{1,0:T(1,128)S(1)}, u32[]{:S(2)}, u32[]{:S(2)}) collective-permute-start(f32[1,768]{1,0:T(1,128)S(1)} %fusion.36), channel_id=1, source_target_pairs={{0,8},{4,12},{8,0},{12,4},{16,24},{20,28},{24,16},{28,20},{1,9},{5... | collective-permute-start | bytes 9224 | tf_op jit(solution)/shard_map/ppermute | solution.py:26
  18.1 160.3 %collective-permute-start.5 = (f32[1,768]{1,0:T(1,128)S(1)}, f32[1,768]{1,0:T(1,128)S(1)}, u32[]{:S(2)}, u32[]{:S(2)}) collective-permute-start(f32[1,768]{1,0:T(1,128)S(1)} %fusion.31), channel_id=1, source_target_pairs={{0,16},{4,20},{8,24},{12,28},{16,0},{20,4},{24,8},{28,12},{1,17},{... | collective-permute-start | bytes 9224 | tf_op jit(solution)/shard_map/ppermute | solution.py:26
  21.3 162.8 %collective-permute-start.6 = (f32[1,768]{1,0:T(1,128)S(1)}, f32[1,768]{1,0:T(1,128)S(1)}, u32[]{:S(2)}, u32[]{:S(2)}) collective-permute-start(f32[1,768]{1,0:T(1,128)S(1)} %fusion.26), channel_id=1, source_target_pairs={{0,24},{4,28},{8,16},{12,20},{16,8},{20,12},{24,0},{28,4},{1,25},{... | collective-permute-start | bytes 9224 | tf_op jit(solution)/shard_map/ppermute | solution.py:26
  21.3 162.8 %collective-permute-start.1 = (f32[1,1024]{1,0:T(1,128)S(1)}, f32[1,1024]{1,0:T(1,128)S(1)}, u32[]{:S(2)}, u32[]{:S(2)}) collective-permute-start(f32[1,1024]{1,0:T(1,128)S(1)} %get-tuple-element.273), channel_id=1, source_target_pairs={{0,8},{4,12},{8,0},{12,4},{16,24},{20,28},{24,16},{28,20},{1,9},{5... | collective-permute-start | bytes 12296 | tf_op jit(solution)/shard_map/ppermute | solution.py:26
  28.0 156.2 %collective-permute-start = (bf16[1024,1408]{1,0:T(8,128)(2,1)S(1)}, bf16[1024,1408]{1,0:T(8,128)(2,1)}, u32[]{:S(2)}, u32[]{:S(2)}) collective-permute-start(bf16[1024,1408]{1,0:T(8,128)(2,1)S(1)} %get-tuple-element.236.own), channel_id=1, source_target_pairs={{0,4},{4,0},{8,12},{12,8},{16,20},{20,16},{24,28},{28,24},{1,5},{5... | collective-permute-start | bytes 8650760 | tf_op jit(solution)/shard_map/ppermute | solution.py:26
  184.6 198.7 %all-gather.8.cloned.1.call-start = ((), (), s32[]{:S(2)}) async-start(), calls=%async_computation.5 | async-start | bytes 11796480 | tf_op jit(solution)/shard_map/all_gather | solution.py:697
  272.8 502.2 %reduce-scatter.4.cloned.1.call-start = ((), (), s32[]{:S(2)}) async-start(), calls=%async_computation.6 | async-start | bytes 15728640 | tf_op jit(solution)/shard_map/reduce_scatter | solution.py:793
  276.0 74.0 %collective-permute-start.20 = (bf16[1184,1408]{1,0:T(8,128)(2,1)S(1)}, bf16[1184,1408]{1,0:T(8,128)(2,1)S(1)}, u32[]{:S(2)}, u32[]{:S(2)}) collective-permute-start(bf16[1184,1408]{1,0:T(8,128)(2,1)S(1)} %pad_maximum_fusion.1), channel_id=1, source_target_pairs={{0,4},{4,0},{8,12},{12,8},{16,20},{20,16},{24,28},{28,24},{1,5},{5... | collective-permute-start | bytes 10002440 | tf_op jit(solution)/shard_map/ppermute | solution.py:26
  290.2 40.3 %collective-permute-start.17 = (bf16[768,512]{1,0:T(8,128)(2,1)S(1)}, bf16[768,512]{1,0:T(8,128)(2,1)S(1)}, u32[]{:S(2)}, u32[]{:S(2)}) collective-permute-start(bf16[768,512]{1,0:T(8,128)(2,1)S(1)} %fusion.99.refs_0_), channel_id=1, source_target_pairs={{0,1},{1,0},{2,3},{3,2},{4,5},{5,4},{6,7},{7,6},{8,9},{9,8},{10,11... | collective-permute-start | bytes 2359304 | tf_op jit(solution)/shard_map/ppermute | solution.py:26
  327.6 54.2 %collective-permute-start.16 = (bf16[768,512]{1,0:T(8,128)(2,1)}, bf16[768,512]{1,0:T(8,128)(2,1)}, u32[]{:S(2)}, u32[]{:S(2)}) collective-permute-start(bf16[768,512]{1,0:T(8,128)(2,1)} %fusion.102), channel_id=1, source_target_pairs={{0,24},{4,28},{8,16},{12,20},{16,8},{20,12},{24,0},{28,4},{1,25},{... | collective-permute-start | bytes 2359304 | tf_op jit(solution)/shard_map/ppermute | solution.py:26
  329.0 52.7 %collective-permute-start.27 = (bf16[768,512]{1,0:T(8,128)(2,1)}, bf16[768,512]{1,0:T(8,128)(2,1)}, u32[]{:S(2)}, u32[]{:S(2)}) collective-permute-start(bf16[768,512]{1,0:T(8,128)(2,1)} %collective-permute-done.15.refs_0_), channel_id=1, source_target_pairs={{0,2},{1,3},{2,0},{3,1},{4,6},{5,7},{6,4},{7,5},{8,10},{9,11},{10,... | collective-permute-start | bytes 2359304 | tf_op jit(solution)/shard_map/ppermute | solution.py:26
  330.5 74.5 %collective-permute-start.26 = (bf16[768,512]{1,0:T(8,128)(2,1)}, bf16[768,512]{1,0:T(8,128)(2,1)}, u32[]{:S(2)}, u32[]{:S(2)}) collective-permute-start(bf16[768,512]{1,0:T(8,128)(2,1)} %collective-permute-done.15.refs_0_), channel_id=1, source_target_pairs={{0,1},{1,0},{2,3},{3,2},{4,5},{5,4},{6,7},{7,6},{8,9},{9,8},{10,11... | collective-permute-start | bytes 2359304 | tf_op jit(solution)/shard_map/ppermute | solution.py:26
  381.8 53.2 %collective-permute-start.25 = (bf16[768,512]{1,0:T(8,128)(2,1)}, bf16[768,512]{1,0:T(8,128)(2,1)}, u32[]{:S(2)}, u32[]{:S(2)}) collective-permute-start(bf16[768,512]{1,0:T(8,128)(2,1)} %collective-permute-done.16.refs_0_), channel_id=1, source_target_pairs={{0,2},{1,3},{2,0},{3,1},{4,6},{5,7},{6,4},{7,5},{8,10},{9,11},{10,... | collective-permute-start | bytes 2359304 | tf_op jit(solution)/shard_map/ppermute | solution.py:26
  383.4 51.6 %collective-permute-start.21 = (bf16[768,512]{1,0:T(8,128)(2,1)}, bf16[768,512]{1,0:T(8,128)(2,1)}, u32[]{:S(2)}, u32[]{:S(2)}) collective-permute-start(bf16[768,512]{1,0:T(8,128)(2,1)} %fusion.100), channel_id=1, source_target_pairs={{0,8},{4,12},{8,0},{12,4},{16,24},{20,28},{24,16},{28,20},{1,9},{5... | collective-permute-start | bytes 2359304 | tf_op jit(solution)/shard_map/ppermute | solution.py:26
  477.1 40.7 %collective-permute-start.35 = (bf16[768,512]{1,0:T(8,128)(2,1)}, bf16[768,512]{1,0:T(8,128)(2,1)}, u32[]{:S(2)}, u32[]{:S(2)}) collective-permute-start(bf16[768,512]{1,0:T(8,128)(2,1)} %add_convert_fusion.9), channel_id=1, source_target_pairs={{0,16},{4,20},{8,24},{12,28},{16,0},{20,4},{24,8},{28,12},{1,17},{... | collective-permute-start | bytes 2359304 | tf_op jit(solution)/shard_map/ppermute | solution.py:26
  522.5 54.2 %collective-permute-start.42 = (bf16[768,512]{1,0:T(8,128)(2,1)}, bf16[768,512]{1,0:T(8,128)(2,1)}, u32[]{:S(2)}, u32[]{:S(2)}) collective-permute-start(bf16[768,512]{1,0:T(8,128)(2,1)} %add_convert_fusion.7), channel_id=1, source_target_pairs={{0,24},{4,28},{8,16},{12,20},{16,8},{20,12},{24,0},{28,4},{1,25},{... | collective-permute-start | bytes 2359304 | tf_op jit(solution)/shard_map/ppermute | solution.py:26
  576.8 422.6 %reduce-scatter.8.cloned.1.call-start = ((), (), s32[]{:S(2)}) async-start(), calls=%async_computation.8 | async-start | bytes 2359296 | tf_op jit(solution)/shard_map/reduce_scatter | solution.py:837
  585.1 47.8 %collective-permute-start.46 = (bf16[576,1408]{1,0:T(8,128)(2,1)S(1)}, bf16[576,1408]{1,0:T(8,128)(2,1)S(1)}, u32[]{:S(2)}, u32[]{:S(2)}) collective-permute-start(bf16[576,1408]{1,0:T(8,128)(2,1)S(1)} %slice.324), channel_id=1, source_target_pairs={{0,4},{4,0},{8,12},{12,8},{16,20},{20,16},{24,28},{28,24},{1,5},{5... | collective-permute-start | bytes 4866056 | tf_op jit(solution)/shard_map/ppermute | solution.py:26
  654.4 41.5 %collective-permute-start.49 = (bf16[1024,512]{1,0:T(8,128)(2,1)S(1)}, bf16[1024,512]{1,0:T(8,128)(2,1)S(1)}, u32[]{:S(2)}, u32[]{:S(2)}) collective-permute-start(bf16[1024,512]{1,0:T(8,128)(2,1)S(1)} %get-tuple-element.296), channel_id=1, source_target_pairs={{0,2},{1,3},{2,0},{3,1},{4,6},{5,7},{6,4},{7,5},{8,10},{9,11},{10,... | collective-permute-start | bytes 3145736 | tf_op jit(solution)/shard_map/ppermute | solution.py:26
  654.9 41.0 %collective-permute-start.50 = (bf16[216,2816]{1,0:T(8,128)(2,1)S(1)}, bf16[216,2816]{1,0:T(8,128)(2,1)S(1)}, u32[]{:S(2)}, u32[]{:S(2)}) collective-permute-start(bf16[216,2816]{1,0:T(8,128)(2,1)S(1)} %copy-done.41), channel_id=1, source_target_pairs={{0,4},{4,0},{8,12},{12,8},{16,20},{20,16},{24,28},{28,24},{1,5},{5... | collective-permute-start | bytes 3649544 | tf_op jit(solution)/shard_map/ppermute | solution.py:26
  713.5 287.7 %reduce-scatter.6.cloned.1.call-start = ((), (), s32[]{:S(2)}) async-start(), calls=%async_computation.7 | async-start | bytes 7077888 | tf_op jit(solution)/shard_map/reduce_scatter | solution.py:845
  769.9 216.9 %collective-permute-start.70 = (bf16[512,2816]{1,0:T(8,128)(2,1)}, bf16[512,2816]{1,0:T(8,128)(2,1)}, u32[]{:S(2)}, u32[]{:S(2)}) collective-permute-start(bf16[512,2816]{1,0:T(8,128)(2,1)} %convolution_convert_fusion.1), channel_id=1, source_target_pairs={{0,4},{4,0},{8,12},{12,8},{16,20},{20,16},{24,28},{28,24},{1,5},{5... | collective-permute-start | bytes 8650760 | tf_op jit(solution)/shard_map/ppermute | solution.py:26
  771.4 99.3 %collective-permute-start.60 = (bf16[128,2816]{1,0:T(8,128)(2,1)}, bf16[128,2816]{1,0:T(8,128)(2,1)}, u32[]{:S(2)}, u32[]{:S(2)}) collective-permute-start(bf16[128,2816]{1,0:T(8,128)(2,1)} %slice.337), channel_id=1, source_target_pairs={{0,4},{4,0},{8,12},{12,8},{16,20},{20,16},{24,28},{28,24},{1,5},{5... | collective-permute-start | bytes 2162696 | tf_op jit(solution)/shard_map/ppermute | solution.py:26
  774.8 96.0 %collective-permute-start.59 = (bf16[1024,512]{1,0:T(8,128)(2,1)}, bf16[1024,512]{1,0:T(8,128)(2,1)S(1)}, u32[]{:S(2)}, u32[]{:S(2)}) collective-permute-start(bf16[1024,512]{1,0:T(8,128)(2,1)} %add_convert_fusion), channel_id=1, source_target_pairs={{0,2},{1,3},{2,0},{3,1},{4,6},{5,7},{6,4},{7,5},{8,10},{9,11},{10,... | collective-permute-start | bytes 3145736 | tf_op jit(solution)/shard_map/ppermute | solution.py:26
  776.9 93.9 %collective-permute-start.52 = (bf16[768,512]{1,0:T(8,128)(2,1)S(1)}, bf16[768,512]{1,0:T(8,128)(2,1)S(1)}, u32[]{:S(2)}, u32[]{:S(2)}) collective-permute-start(bf16[768,512]{1,0:T(8,128)(2,1)S(1)} %get-tuple-element.171), channel_id=1, source_target_pairs={{0,16},{4,20},{8,24},{12,28},{16,0},{20,4},{24,8},{28,12},{1,17},{... | collective-permute-start | bytes 2359304 | tf_op jit(solution)/shard_map/ppermute | solution.py:26
  874.0 62.6 %collective-permute-start.54 = (bf16[768,512]{1,0:T(8,128)(2,1)S(1)}, bf16[768,512]{1,0:T(8,128)(2,1)S(1)}, u32[]{:S(2)}, u32[]{:S(2)}) collective-permute-start(bf16[768,512]{1,0:T(8,128)(2,1)S(1)} %get-tuple-element.173), channel_id=1, source_target_pairs={{0,24},{4,28},{8,16},{12,20},{16,8},{20,12},{24,0},{28,4},{1,25},{... | collective-permute-start | bytes 2359304 | tf_op jit(solution)/shard_map/ppermute | solution.py:26
  877.4 58.2 %collective-permute-start.53 = (bf16[768,512]{1,0:T(8,128)(2,1)S(1)}, bf16[768,512]{1,0:T(8,128)(2,1)S(1)}, u32[]{:S(2)}, u32[]{:S(2)}) collective-permute-start(bf16[768,512]{1,0:T(8,128)(2,1)S(1)} %get-tuple-element.172), channel_id=1, source_target_pairs={{0,8},{4,12},{8,0},{12,4},{16,24},{20,28},{24,16},{28,20},{1,9},{5... | collective-permute-start | bytes 2359304 | tf_op jit(solution)/shard_map/ppermute | solution.py:26
  884.3 54.8 %collective-permute-start.64 = (f32[6,2048]{1,0:T(8,128)S(1)}, f32[6,2048]{1,0:T(8,128)S(1)}, u32[]{:S(2)}, u32[]{:S(2)}) collective-permute-start(f32[6,2048]{1,0:T(8,128)S(1)} %fusion.121), channel_id=1, source_target_pairs={{0,1},{1,0},{2,3},{3,2},{4,5},{5,4},{6,7},{7,6},{8,9},{9,8},{10,11... | collective-permute-start | bytes 147464 | tf_op jit(solution)/shard_map/ppermute | solution.py:26
  884.4 94.4 %collective-permute-start.63 = (bf16[1024,512]{1,0:T(8,128)(2,1)S(1)}, bf16[1024,512]{1,0:T(8,128)(2,1)S(1)}, u32[]{:S(2)}, u32[]{:S(2)}) collective-permute-start(bf16[1024,512]{1,0:T(8,128)(2,1)S(1)} %get-tuple-element.240), channel_id=1, source_target_pairs={{0,2},{1,3},{2,0},{3,1},{4,6},{5,7},{6,4},{7,5},{8,10},{9,11},{10,... | collective-permute-start | bytes 3145736 | tf_op jit(solution)/shard_map/ppermute | solution.py:26
  937.9 42.8 %collective-permute-start.55 = (bf16[1024,512]{1,0:T(8,128)(2,1)S(1)}, bf16[1024,512]{1,0:T(8,128)(2,1)S(1)}, u32[]{:S(2)}, u32[]{:S(2)}) collective-permute-start(bf16[1024,512]{1,0:T(8,128)(2,1)S(1)} %add_convert_fusion.1), channel_id=1, source_target_pairs={{0,2},{1,3},{2,0},{3,1},{4,6},{5,7},{6,4},{7,5},{8,10},{9,11},{10,... | collective-permute-start | bytes 3145736 | tf_op jit(solution)/shard_map/ppermute | solution.py:26
  (131 other events, 1872.4 us)
Sparse Core Ops, SparseCore 0:
  10.8 163.5 all-gather.3
  184.8 81.9 all-gather.5
  273.0 97.7 all-gather.7
  576.9 114.9 reduce-scatter.3
  713.6 88.9 reduce-scatter.7
  806.6 132.5 reduce-scatter.5

commit v11 on v8

--- a/solution.py
+++ b/solution.py
@@ -735,9 +735,9 @@
             rows_raw = down_pass(where, after(grad_rest, even), *down, MOST, total, rows_raw)
             named_sum = after(named_sum, crossed[3])
         if step == 2:
-            named_sum = after(named_sum, crossed[1], *sums_sent)
+            named_sum = after(named_sum, crossed[1], sums_sent[0])
         if step == 3:
-            named_sum = after(named_sum, sums_sent[2])
+            named_sum = after(named_sum, sums_sent[1])
         moe_rows, activation, pre_grad, even, odd, gate_grad = expert_pass(
             step, where, arrived[step], pair, rows_raw[1], named_sum, router_block, carried
         )
@@ -754,9 +754,12 @@
         if step == 2:
             odd = after(odd, *returned, arrived[3][tensor_count // 2])
         if step == 3:
-            came_home[2] = swap(returned[1], "dp", 2 * group_count)
-            odd = after(odd, returned[2], came_home[2])
-        returned.append(near_reduce(even, odd, sums_sent).astype(low))
+            came_home[2] = swap(returned[0], "dp", 2 * group_count)
+            odd = after(odd, returned[1], came_home[2])
+        if step == 0:
+            own_parts = (even, odd)
+        else:
+            returned.append(near_reduce(even, odd, sums_sent).astype(low))
         gate_grads.append(gate_grad)
 
     def home(parts):
@@ -764,9 +767,10 @@
             s: swap(v, "dp", s * group_count) if s else v for s, v in zip(order, parts)
         }
 
-    came_home[0] = returned[0]
-    came_home[3] = swap(returned[2], "dp", 3 * group_count)
-    came_home[1] = swap(returned[3], "dp", group_count)
+    came_home[3] = swap(returned[1], "dp", 3 * group_count)
+    came_home[1] = swap(returned[2], "dp", group_count)
+    own_even, own_odd = own_parts
+    came_home[0] = near_reduce(own_even, after(own_odd, sums_sent[2]), []).astype(low)
     gate_grad_near = home([gate_grads[0]] + [after(v, even) for v in gate_grads[1:]])
     grad_rows = rows_raw[0]
 
@@ -779,13 +783,13 @@
 
     unit = half // 128
     quarter = half // 2
-    act_late = after(activation, sums_sent[3], returned[2])
+    act_late = after(activation, sums_sent[2], returned[1])
     down_given = term(grad_rows, act_late)(given_at, half)
     down_sums = [group_send(down_given[: 40 * unit])]
     expert_part = up_pass(
-        where, after(activation, down_given, returned[3], *gate_grad_near.values()), *down
-    )
-    expert_part = after(expert_part, down_sums[0], came_home[3], came_home[1])
+        where, after(activation, down_given, returned[2], *gate_grad_near.values()), *down
+    )
+    expert_part = after(expert_part, down_sums[0], *came_home.values())
     expert_own = lax.psum_scatter(expert_part, "tensor", scatter_dimension=1, tiled=True)
     down_sums.append(group_send(down_given[40 * unit : 80 * unit], down_sums[0]))
     came_home = {s: after(v, expert_part) for s, v in came_home.items()}
@@ -834,22 +838,20 @@
     qkv_grad = contract(normed_in, qkv_grad_rows, 0, 0).astype(low)
     grads_both = jnp.concatenate([qkv_grad, out_grad], 1)
     shards = lax.psum_scatter(grads_both, "dp", scatter_dimension=0, tiled=True)
-    pair_sums.append(group_send(pair_given[0][16 * unit : 32 * unit], pair_sums[0], grads_both))
-    pair_sums.append(group_send(pair_given[0][32 * unit :], pair_sums[1]))
-    pair_last = group_send(pair_given[1], pair_sums[2])
-    outputs = {}
+    pair_sums.append(group_send(pair_given[0][16 * unit :], pair_sums[0], grads_both))
+    pair_last = group_send(pair_given[1], pair_sums[0], grads_both)
+    outputs = {0: expert_own[:MOST]}
+    part = after(expert_own[MOST : 2 * MOST], grads_both)
+    outputs[2] = swap(part, "dp", 2 * group_count)
 
     def keep(sent):
-        part = after(expert_own[MOST : 2 * MOST], sent)
-        outputs[2] = swap(part, "dp", 2 * group_count)
         late = after(pre_grad, sent, expert_own)
         kept.append(term(moe_rows, late)(mine_at, half))
         kept.append(term(grad_rows, after(activation, kept[0]))(mine_at, half))
-        return (*kept, outputs[2], pair_sums[1])
+        return kept
 
     parts = spread_dot(where, after(qkv_grad_rows, grads_both), first, 0, tensor_count)
-    normed_grad = near_reduce(*parts, [], filler=keep)
-    outputs[0] = expert_own[:MOST]
+    normed_grad = near_reduce(*parts, [], outputs[2], filler=keep)
     for k in (2, 3):
         part = after(expert_own[k * MOST : (k + 1) * MOST], outputs[2])
         outputs[order[k]] = swap(part, "dp", order[k] * group_count)
@@ -863,19 +865,18 @@
         jnp.zeros((mine.shape[0], width), full), mine, place * size, 1
     )
     mine = all_sum(mine)
-    input_own = after(input_own, outputs[3], outputs[1], pair_sums[2])
     expert_grad = expert_grad_sum(
         group_finish(kept[0], [jnp.concatenate(pair_sums, 0), pair_last], member, group_count),
         group_finish(kept[1], [jnp.concatenate(down_sums, 0)], member, group_count),
         hidden_size,
     )
-    input_grad = tensor_gather(input_own.astype(low), lambda sent: (mine,))
+    input_grad = tensor_gather(input_own.astype(low), lambda sent: (mine, outputs[3], outputs[1]))
     input_grad = input_grad.astype(full)
     layer_own = hidden + unpacked([outputs[s] for s in range(EXPERTS)])
     layer_out = tensor_gather(layer_own.astype(low)).astype(full)
     share = width // dp_count
     mine = lax.dynamic_slice_in_dim(mine, index * share, share, 1)
-    shards = after(shards, layer_out, input_grad, expert_grad).astype(full)
+    shards = shards.astype(full)
     qkv_shard, out_shard = shards[:, : 3 * size], shards[:, 3 * size :]
     return (
         layer_out,

time: 1040 us -> 992 us (0.954)
  waiting for transfers between devices: 431 us -> 364 us
  starting transfers between devices: 61.1 us -> 73.4 us
    ppermute x72 -> x71, waiting for transfers between devices: 303 us -> 236 us  [swap(): lax.ppermute(value, axis, [(i, i ^ distance) for i in range(lax.axis_size...]
    ppermute x72 -> x71, starting transfers between devices: 60.2 us -> 72.7 us  [swap(): lax.ppermute(value, axis, [(i, i ^ distance) for i in range(lax.axis_size...]
  transfers between devices with their start and end apart: 77 -> 76, of which waited for: 28 -> 26; matrix products, arithmetic and copies ran while one was open for 25% -> 27% of each run, Pallas kernels for 23% -> 24%
where the time goes in v11:
time: 992 us; the launch traced here: 983 us
  waiting for transfers between devices  364 us (37%)
  Pallas kernels  238 us (24%)
  matrix products  155 us (16%)
  other arithmetic  81.8 us (8%)
  starting transfers between devices  73.4 us (7%)
  local copies, waits for them, and re-layouts  54.8 us (6%)
  between operations  15.8 us (2%)
    ppermute x71, waiting for transfers between devices, swap(): lax.ppermute(value, axis, [(i, i ^ distance) for i in range(lax.axis_size...  236 us
    all_gather x1, waiting for transfers between devices, body(): lax.all_gather(jnp.concatenate([qkv_weight.reshape(-1, 3 * size), out_wei...  127 us
    dot_general x25, matrix products, contract(): lax.dot_general(left, right, (((left_dim,), (right_dim,)), ((), ())), pre...  122 us
    pallas_call x4, Pallas kernels, expert_pass(): pl.pallas_call(functools.partial(expert_kernel, count, len(carried)), gri...  120 us
    ppermute x71, starting transfers between devices, swap(): lax.ppermute(value, axis, [(i, i ^ distance) for i in range(lax.axis_size...  72.7 us
    pallas_call x2, Pallas kernels, down_pass(): pl.pallas_call(functools.partial(down_kernel, len(carried)), grid_spec=pl...  32.6 us
    pallas_call x1, Pallas kernels, up_pass(): pl.pallas_call(up_kernel, grid_spec=pltpu.PrefetchScalarGridSpec(num_scal...  27 us
  transfers between devices with their start and end apart: 76, of which 26 were waited for; matrix products, arithmetic and copies ran while one was open for 27% of the time, Pallas kernels for 24%

profile of v11, /device:TPU:0, one launch (start us, length us, event | category | flops | bytes accessed | tf_op | source)
XLA Modules:
  0.0 982.8 jit_solution(14017374352669842270)
XLA Ops:
  21.8 5.9 slice_bitcast_fusion
  40.3 6.9 convolution_convert_fusion.3.rows
  47.2 127.2 %all-gather.4.cloned.1.call-done.right = bf16[2048,2176]{1,0:T(8,128)(2,1)} async-done(((bf16[256,2176]{1,0:T(8,128)(2,1)}), bf16[2048,2176]{1,0:T(8,128)(2,1)}) %all-gather.4.cloned.1.call-update) | async-done | bytes 8912912 | tf_op jit(solution)/shard_map/all_gather | solution.py:595
  185.1 11.7 %fusion.3.q_in.k_in.v_in = f32[1024,1536]{1,0:T(8,128)} fusion(bf16[1024,2048]{1,0:T(8,128)(2,1)} %fusion.2, bf16[2048,2176]{1,0:T(8,128)(2,1)} %all-gather.4.cloned.1.call-done.right), kind=kOutput, calls=%fused_computation.9 | convolution fusion | flops 6442450944 | bytes 16777216 | tf_op jit(solution)/shard_map/dot_general | solution.py:673
  201.0 12.8 %attention.1 = (bf16[1024,512]{1,0:T(8,128)(2,1)S(1)}, bf16[1024,512]{1,0:T(8,128)(2,1)S(1)}, bf16[1024,512]{1,0:T(8,128)(2,1)S(1)}, bf16[1024,512]{1,0:T(8,128)(2,1)S(1)}, f32[4,1024,1]{2,1,0:T(8,128)}) custom-call(f32[1024,1536]{1,0:T(8,128)} %fusion.3.q_in.k_in.v_in, f32[1024,1536]{1,0:T(8,128)} %fusion.3.q_in.k_in.v_in, ...), custom_call_target="tpu_custom_call" | custom-call | flops 1342177280 | bytes 10485760 | tf_op jit(solution)/shard_map/attention/pallas_call | solution.py:135
  217.7 5.5 spread.2
  236.9 11.0 %down.2 = (bf16[3072,2048]{1,0:T(8,128)(2,1)}, bf16[3072,1408]{1,0:T(8,128)(2,1)}) custom-call(s32[3]{0:T(128)S(1)} %pad_add_fusion.where, bf16[768,2048]{1,0:T(8,128)(2,1)} %convolution_convert_fusion.3.rows, bf16[1024,1408]{1,0:T(8,128)(2,1)S(1)} %get-tuple-element.236.own, bf16[1024,1408]{1,0:T(8,128)(2,1)} %collective-permute-done.came), custom_call_target="tpu_custom_call" | custom-call | flops 4429185024 | bytes 14221312 | tf_op jit(solution)/shard_map/down/pallas_call | solution.py:272
  247.9 12.1 %collective-permute-done.11 = bf16[1024,512]{1,0:T(8,128)(2,1)} collective-permute-done((bf16[1024,512]{1,0:T(8,128)(2,1)}, bf16[1024,512]{1,0:T(8,128)(2,1)}, u32[]{:S(2)}, u32[]{:S(2)}) %collective-permute-start.11) | collective-permute-done | bytes 1048608 | tf_op jit(solution)/shard_map/ppermute | solution.py:26
  289.5 33.7 %collective-permute-done.18.refs_2_ = bf16[768,512]{1,0:T(8,128)(2,1)S(1)} collective-permute-done((bf16[768,512]{1,0:T(8,128)(2,1)S(1)}, bf16[768,512]{1,0:T(8,128)(2,1)S(1)}, u32[]{:S(2)}, u32[]{:S(2)}) %collective-permute-start.18) | collective-permute-done | bytes 786464 | tf_op jit(solution)/shard_map/ppermute | solution.py:26
  329.8 20.1 %collective-permute-done.20.refs_10_ = bf16[1184,1408]{1,0:T(8,128)(2,1)S(1)} collective-permute-done((bf16[1184,1408]{1,0:T(8,128)(2,1)S(1)}, bf16[1184,1408]{1,0:T(8,128)(2,1)S(1)}, u32[]{:S(2)}, u32[]{:S(2)}) %collective-permute-start.20) | collective-permute-done | bytes 3334176 | tf_op jit(solution)/shard_map/ppermute | solution.py:26
  351.7 30.0 %expert.4 = (bf16[3072,2048]{1,0:T(8,128)(2,1)}, bf16[3072,1408]{1,0:T(8,128)(2,1)}, bf16[3072,2816]{1,0:T(8,128)(2,1)}, bf16[768,1024]{1,0:T(8,128)(2,1)}, bf16[768,1024]{1,0:T(8,128)(2,1)}, /*index=5*/f32[1,768]{1,0:T(1,128)}) custom-call(s32[3]{0:T(128)} %copy-done.10, bf16[768,512]{1,0:T(8,128)(2,1)} %copy-done.63, bf16[768,512]{1,0:T(8,128)(2,1)} %copy-done.65, ...), custom_call_target="tpu_custom_call" | custom-call | flops 17716740096 | bytes 32768000 | tf_op jit(solution)/shard_map/expert/pallas_call | solution.py:411
  383.4 21.6 %down.3 = (bf16[3072,2048]{1,0:T(8,128)(2,1)}, bf16[3072,1408]{1,0:T(8,128)(2,1)}) custom-call(s32[3]{0:T(128)S(1)} %copy-done.11, bf16[2304,2048]{1,0:T(8,128)(2,1)} %all-gather.8.cloned.1.call-done.rows, bf16[1024,1408]{1,0:T(8,128)(2,1)S(1)} %get-tuple-element.236.own, ...), custom_call_target="tpu_custom_call", output_to_operand_aliasing={{0}: (4, {}), {1}: (5, {})} | custom-call | flops 13287555072 | bytes 31129600 | tf_op jit(solution)/shard_map/down/pallas_call | solution.py:272
  405.0 30.2 %expert.5 = (bf16[3072,2048]{1,0:T(8,128)(2,1)}, bf16[3072,1408]{1,0:T(8,128)(2,1)}, bf16[3072,2816]{1,0:T(8,128)(2,1)}, bf16[768,1024]{1,0:T(8,128)(2,1)}, bf16[768,1024]{1,0:T(8,128)(2,1)}, /*index=5*/f32[1,768]{1,0:T(1,128)}) custom-call(s32[3]{0:T(128)} %copy-done.10, ...), custom_call_target="tpu_custom_call", output_to_operand_aliasing={{0}: (15, {}), {1}: (16, {}), {2}: (17, {})} | custom-call | flops 17716740096 | bytes 32768000 | tf_op jit(solution)/shard_map/expert/pallas_call | solution.py:411
  443.5 29.9 %expert.6 = (bf16[3072,2048]{1,0:T(8,128)(2,1)}, bf16[3072,1408]{1,0:T(8,128)(2,1)}, bf16[3072,2816]{1,0:T(8,128)(2,1)}, bf16[768,1024]{1,0:T(8,128)(2,1)}, bf16[768,1024]{1,0:T(8,128)(2,1)}, /*index=5*/f32[1,768]{1,0:T(1,128)}) custom-call(s32[3]{0:T(128)} %copy-done.10, ...), custom_call_target="tpu_custom_call", output_to_operand_aliasing={{0}: (15, {}), {1}: (16, {}), {2}: (17, {})} | custom-call | flops 17716740096 | bytes 32768000 | tf_op jit(solution)/shard_map/expert/pallas_call | solution.py:411
  485.1 29.8 %expert.7 = (bf16[3072,2048]{1,0:T(8,128)(2,1)}, bf16[3072,1408]{1,0:T(8,128)(2,1)}, bf16[3072,2816]{1,0:T(8,128)(2,1)}, bf16[768,1024]{1,0:T(8,128)(2,1)}, bf16[768,1024]{1,0:T(8,128)(2,1)}, /*index=5*/f32[1,768]{1,0:T(1,128)}) custom-call(s32[3]{0:T(128)} %copy-done.10, ...), custom_call_target="tpu_custom_call", output_to_operand_aliasing={{0}: (15, {}), {1}: (16, {}), {2}: (17, {})} | custom-call | flops 17716740096 | bytes 32768000 | tf_op jit(solution)/shard_map/expert/pallas_call | solution.py:411
  524.6 14.1 %fusion.14 = bf16[1024,1408]{1,0:T(8,128)(2,1)S(1)} fusion(bf16[3072,1408]{1,0:T(8,128)(2,1)} %get-tuple-element.185.act, bf16[3072,2048]{1,0:T(8,128)(2,1)} %get-tuple-element.144, s32[]{:T(128)S(6)} %select_n.169), kind=kOutput, calls=%fused_computation.23 | convolution fusion | flops 8859811840 | bytes 17825796 | tf_op jit(solution)/shard_map/dot_general | solution.py:30
  551.8 27.0 %up.1 = bf16[3072,2048]{1,0:T(8,128)(2,1)} custom-call(s32[3]{0:T(128)S(1)} %copy-done.12, bf16[3072,1408]{1,0:T(8,128)(2,1)} %get-tuple-element.185.act, bf16[1024,1408]{1,0:T(8,128)(2,1)S(1)} %get-tuple-element.236.own, bf16[1024,1408]{1,0:T(8,128)(2,1)} %collective-permute-done.came), custom_call_target="tpu_custom_call" | custom-call | flops 17716740096 | bytes 27000832 | tf_op jit(solution)/shard_map/up/pallas_call | solution.py:339
  606.4 15.0 %collective-permute-done.49 = bf16[320,1408]{1,0:T(8,128)(2,1)} collective-permute-done((bf16[320,1408]{1,0:T(8,128)(2,1)}, bf16[320,1408]{1,0:T(8,128)(2,1)}, u32[]{:S(2)}, u32[]{:S(2)}) %collective-permute-start.49) | collective-permute-done | bytes 901152 | tf_op jit(solution)/shard_map/ppermute | solution.py:26
  622.7 16.3 %convolution_convert_fusion.2 = bf16[512,2816]{1,0:T(8,128)(2,1)} fusion(bf16[3072,2816]{1,0:T(8,128)(2,1)} %get-tuple-element.184, bf16[3072,2048]{1,0:T(8,128)(2,1)} %get-tuple-element.168, s32[]{:T(128)S(6)} %select_n.169), kind=kOutput, calls=%fused_computation.19 | convolution fusion | flops 8859811840 | bytes 23330820 | tf_op jit(solution)/shard_map/dot_general | solution.py:30
  639.1 12.0 %convolution_convert_fusion.1 = bf16[512,2816]{1,0:T(8,128)(2,1)} fusion(bf16[3072,2816]{1,0:T(8,128)(2,1)S(1)} %bitcast.151, bf16[3072,2048]{1,0:T(8,128)(2,1)} %get-tuple-element.168, s32[]{:T(128)S(6)} %select_n.173), kind=kOutput, calls=%fused_computation.18 | convolution fusion | flops 8859811840 | bytes 23330820 | tf_op jit(solution)/shard_map/dot_general | solution.py:30
  664.8 15.8 %attention_back.1.left = bf16[1024,1536]{1,0:T(8,128)(2,1)} custom-call(bf16[1024,512]{1,0:T(8,128)(2,1)S(1)} %copy-done.14, bf16[1024,512]{1,0:T(8,128)(2,1)S(1)} %copy-done.16, bf16[1024,512]{1,0:T(8,128)(2,1)S(1)} %copy-done.18, f32[4,1024,1]{2,1,0:T(8,128)} %get-tuple-element.163.logs, bf16[1024,512]{1,0:T(8,128)(2,1)S(1)} %fusion.87.grad, ...), custom_call_target="tpu_custom_call" | custom-call | flops 3355443200 | bytes 8388608 | tf_op jit(solution)/shard_map/attention_back/pallas_call | solution.py:188
  684.3 8.7 convolution_convert_fusion
  693.1 7.8 pad_maximum_fusion
  700.9 12.2 %spread.3 = (bf16[1024,1024]{1,0:T(8,128)(2,1)S(1)}, bf16[1024,1024]{1,0:T(8,128)(2,1)}) custom-call(s32[3]{0:T(128)S(1)} %copy-done.12, bf16[1024,1536]{1,0:T(8,128)(2,1)} %attention_back.1.left, bf16[2048,2176]{1,0:T(8,128)(2,1)} %all-gather.4.cloned.1.call-done.right), custom_call_target="tpu_custom_call" | custom-call | flops 6442450944 | bytes 13631488 | tf_op jit(solution)/shard_map/spread/pallas_call | solution.py:310
  727.1 65.8 %collective-permute-done.53 = bf16[768,512]{1,0:T(8,128)(2,1)} collective-permute-done((bf16[768,512]{1,0:T(8,128)(2,1)}, bf16[768,512]{1,0:T(8,128)(2,1)}, u32[]{:S(2)}, u32[]{:S(2)}) %collective-permute-start.53) | collective-permute-done | bytes 786464 | tf_op jit(solution)/shard_map/ppermute | solution.py:26
  792.9 26.0 %fusion.11.refs_0_ = bf16[1024,2816]{1,0:T(8,128)(2,1)} fusion(bf16[3072,2816]{1,0:T(8,128)(2,1)} %get-tuple-element.184, bf16[3072,2048]{1,0:T(8,128)(2,1)} %get-tuple-element.168, s32[]{:T(128)S(6)} %select_n.186), kind=kOutput, calls=%fused_computation.17 | convolution fusion | flops 17719623680 | bytes 29360132 | tf_op jit(solution)/shard_map/dot_general | solution.py:30
  818.9 13.4 %fusion.17.refs_3_ = bf16[1024,1408]{1,0:T(8,128)(2,1)} fusion(bf16[3072,1408]{1,0:T(8,128)(2,1)S(1)} %bitcast.153, bf16[3072,2048]{1,0:T(8,128)(2,1)} %get-tuple-element.144, s32[]{:T(128)S(6)} %select_n.186), kind=kOutput, calls=%fused_computation.24 | convolution fusion | flops 8859811840 | bytes 17825796 | tf_op jit(solution)/shard_map/dot_general | solution.py:30
  838.2 16.7 %collective-permute-done.54 = bf16[768,512]{1,0:T(8,128)(2,1)S(1)} collective-permute-done((bf16[768,512]{1,0:T(8,128)(2,1)S(1)}, bf16[768,512]{1,0:T(8,128)(2,1)S(1)}, u32[]{:S(2)}, u32[]{:S(2)}) %collective-permute-start.54) | collective-permute-done | bytes 786464 | tf_op jit(solution)/shard_map/ppermute | solution.py:26
  865.0 20.2 %collective-permute-done.56 = bf16[1024,512]{1,0:T(8,128)(2,1)S(1)} collective-permute-done((bf16[1024,512]{1,0:T(8,128)(2,1)S(1)}, bf16[1024,512]{1,0:T(8,128)(2,1)S(1)}, u32[]{:S(2)}, u32[]{:S(2)}) %collective-permute-start.56) | collective-permute-done | bytes 1048608 | tf_op jit(solution)/shard_map/ppermute | solution.py:26
  887.6 15.7 %collective-permute-done.64 = f32[6,2048]{1,0:T(8,128)S(1)} collective-permute-done((f32[6,2048]{1,0:T(8,128)S(1)}, f32[6,2048]{1,0:T(8,128)S(1)}, u32[]{:S(2)}, u32[]{:S(2)}) %collective-permute-start.64) | collective-permute-done | bytes 49184 | tf_op jit(solution)/shard_map/ppermute | solution.py:26
  907.6 16.6 %collective-permute-start.66 = (f32[6,2048]{1,0:T(8,128)S(1)}, f32[6,2048]{1,0:T(8,128)S(1)}, u32[]{:S(2)}, u32[]{:S(2)}) collective-permute-start(f32[6,2048]{1,0:T(8,128)S(1)} %add.258), channel_id=1, source_target_pairs={{0,8},{4,12},{8,0},{12,4},{16,24},{20,28},{24,16},{28,20},{1,9},{5... | collective-permute-start | bytes 147464 | tf_op jit(solution)/shard_map/ppermute | solution.py:26
  951.0 12.0 %expert_grad_sum.1 = f32[3,1024,1408]{2,1,0:T(8,128)} custom-call(bf16[1024,2816]{1,0:T(8,128)(2,1)} %fusion.11.refs_0_, bf16[512,2816]{1,0:T(8,128)(2,1)S(1)} %copy-done, bf16[512,2816]{1,0:T(8,128)(2,1)} %collective-permute-done.70.refs_2_, bf16[1024,1408]{1,0:T(8,128)(2,1)S(1)} %copy-done.1, bf16[1024,1408]{1,0:T(8,128)(2,1)S(1)} %pad_maximum_fusion.4.refs_4_), custom_call_target="tpu_custom_call" | custom-call | flops 4325376 | bytes 34603008 | tf_op jit(solution)/shard_map/expert_grad_sum/pallas_call | solution.py:495
  (458 shorter events, 263.1 us)
Async XLA Ops:
  7.2 167.2 %all-gather.4.cloned.1.call-start = ((), (), s32[]{:S(2)}) async-start(), calls=%async_computation.2 | async-start | bytes 10027008 | tf_op jit(solution)/shard_map/all_gather | solution.py:595
  10.3 256.4 %all-gather.6.cloned.1.call-start = ((), (), s32[]{:S(2)}) async-start(), calls=%async_computation.3 | async-start | bytes 5242880 | tf_op jit(solution)/shard_map/all_gather | solution.py:661
  14.0 162.8 %collective-permute-start.4 = (f32[1,768]{1,0:T(1,128)S(1)}, f32[1,768]{1,0:T(1,128)S(1)}, u32[]{:S(2)}, u32[]{:S(2)}) collective-permute-start(f32[1,768]{1,0:T(1,128)S(1)} %fusion.36), channel_id=1, source_target_pairs={{0,8},{4,12},{8,0},{12,4},{16,24},{20,28},{24,16},{28,20},{1,9},{5... | collective-permute-start | bytes 9224 | tf_op jit(solution)/shard_map/ppermute | solution.py:26
  17.7 160.7 %collective-permute-start.5 = (f32[1,768]{1,0:T(1,128)S(1)}, f32[1,768]{1,0:T(1,128)S(1)}, u32[]{:S(2)}, u32[]{:S(2)}) collective-permute-start(f32[1,768]{1,0:T(1,128)S(1)} %fusion.31), channel_id=1, source_target_pairs={{0,16},{4,20},{8,24},{12,28},{16,0},{20,4},{24,8},{28,12},{1,17},{... | collective-permute-start | bytes 9224 | tf_op jit(solution)/shard_map/ppermute | solution.py:26
  20.9 163.3 %collective-permute-start.6 = (f32[1,768]{1,0:T(1,128)S(1)}, f32[1,768]{1,0:T(1,128)S(1)}, u32[]{:S(2)}, u32[]{:S(2)}) collective-permute-start(f32[1,768]{1,0:T(1,128)S(1)} %fusion.26), channel_id=1, source_target_pairs={{0,24},{4,28},{8,16},{12,20},{16,8},{20,12},{24,0},{28,4},{1,25},{... | collective-permute-start | bytes 9224 | tf_op jit(solution)/shard_map/ppermute | solution.py:26
  20.9 163.3 %collective-permute-start.1 = (f32[1,1024]{1,0:T(1,128)S(1)}, f32[1,1024]{1,0:T(1,128)S(1)}, u32[]{:S(2)}, u32[]{:S(2)}) collective-permute-start(f32[1,1024]{1,0:T(1,128)S(1)} %get-tuple-element.275), channel_id=1, source_target_pairs={{0,8},{4,12},{8,0},{12,4},{16,24},{20,28},{24,16},{28,20},{1,9},{5... | collective-permute-start | bytes 12296 | tf_op jit(solution)/shard_map/ppermute | solution.py:26
  27.7 156.5 %collective-permute-start = (bf16[1024,1408]{1,0:T(8,128)(2,1)S(1)}, bf16[1024,1408]{1,0:T(8,128)(2,1)}, u32[]{:S(2)}, u32[]{:S(2)}) collective-permute-start(bf16[1024,1408]{1,0:T(8,128)(2,1)S(1)} %get-tuple-element.236.own), channel_id=1, source_target_pairs={{0,4},{4,0},{8,12},{12,8},{16,20},{20,16},{24,28},{28,24},{1,5},{5... | collective-permute-start | bytes 8650760 | tf_op jit(solution)/shard_map/ppermute | solution.py:26
  184.6 198.8 %all-gather.8.cloned.1.call-start = ((), (), s32[]{:S(2)}) async-start(), calls=%async_computation.4 | async-start | bytes 11796480 | tf_op jit(solution)/shard_map/all_gather | solution.py:697
  272.8 440.6 %reduce-scatter.3.cloned.1.call-start = ((), (), s32[]{:S(2)}) async-start(), calls=%async_computation.5 | async-start | bytes 15728640 | tf_op jit(solution)/shard_map/reduce_scatter | solution.py:793
  276.0 74.0 %collective-permute-start.20 = (bf16[1184,1408]{1,0:T(8,128)(2,1)S(1)}, bf16[1184,1408]{1,0:T(8,128)(2,1)S(1)}, u32[]{:S(2)}, u32[]{:S(2)}) collective-permute-start(bf16[1184,1408]{1,0:T(8,128)(2,1)S(1)} %pad_maximum_fusion.2), channel_id=1, source_target_pairs={{0,4},{4,0},{8,12},{12,8},{16,20},{20,16},{24,28},{28,24},{1,5},{5... | collective-permute-start | bytes 10002440 | tf_op jit(solution)/shard_map/ppermute | solution.py:26
  286.6 36.6 %collective-permute-start.18 = (bf16[768,512]{1,0:T(8,128)(2,1)S(1)}, bf16[768,512]{1,0:T(8,128)(2,1)S(1)}, u32[]{:S(2)}, u32[]{:S(2)}) collective-permute-start(bf16[768,512]{1,0:T(8,128)(2,1)S(1)} %fusion.99.refs_0_), channel_id=1, source_target_pairs={{0,2},{1,3},{2,0},{3,1},{4,6},{5,7},{6,4},{7,5},{8,10},{9,11},{10,... | collective-permute-start | bytes 2359304 | tf_op jit(solution)/shard_map/ppermute | solution.py:26
  289.0 38.0 %collective-permute-start.15 = (bf16[768,512]{1,0:T(8,128)(2,1)S(1)}, bf16[768,512]{1,0:T(8,128)(2,1)}, u32[]{:S(2)}, u32[]{:S(2)}) collective-permute-start(bf16[768,512]{1,0:T(8,128)(2,1)S(1)} %fusion.101), channel_id=1, source_target_pairs={{0,16},{4,20},{8,24},{12,28},{16,0},{20,4},{24,8},{28,12},{1,17},{... | collective-permute-start | bytes 2359304 | tf_op jit(solution)/shard_map/ppermute | solution.py:26
  289.5 40.3 %collective-permute-start.17 = (bf16[768,512]{1,0:T(8,128)(2,1)S(1)}, bf16[768,512]{1,0:T(8,128)(2,1)S(1)}, u32[]{:S(2)}, u32[]{:S(2)}) collective-permute-start(bf16[768,512]{1,0:T(8,128)(2,1)S(1)} %fusion.99.refs_0_), channel_id=1, source_target_pairs={{0,1},{1,0},{2,3},{3,2},{4,5},{5,4},{6,7},{7,6},{8,9},{9,8},{10,11... | collective-permute-start | bytes 2359304 | tf_op jit(solution)/shard_map/ppermute | solution.py:26
  327.0 54.8 %collective-permute-start.16 = (bf16[768,512]{1,0:T(8,128)(2,1)}, bf16[768,512]{1,0:T(8,128)(2,1)}, u32[]{:S(2)}, u32[]{:S(2)}) collective-permute-start(bf16[768,512]{1,0:T(8,128)(2,1)} %fusion.102), channel_id=1, source_target_pairs={{0,24},{4,28},{8,16},{12,20},{16,8},{20,12},{24,0},{28,4},{1,25},{... | collective-permute-start | bytes 2359304 | tf_op jit(solution)/shard_map/ppermute | solution.py:26
  328.3 53.4 %collective-permute-start.27 = (bf16[768,512]{1,0:T(8,128)(2,1)}, bf16[768,512]{1,0:T(8,128)(2,1)}, u32[]{:S(2)}, u32[]{:S(2)}) collective-permute-start(bf16[768,512]{1,0:T(8,128)(2,1)} %collective-permute-done.15.refs_0_), channel_id=1, source_target_pairs={{0,2},{1,3},{2,0},{3,1},{4,6},{5,7},{6,4},{7,5},{8,10},{9,11},{10,... | collective-permute-start | bytes 2359304 | tf_op jit(solution)/shard_map/ppermute | solution.py:26
  329.8 75.1 %collective-permute-start.26 = (bf16[768,512]{1,0:T(8,128)(2,1)}, bf16[768,512]{1,0:T(8,128)(2,1)}, u32[]{:S(2)}, u32[]{:S(2)}) collective-permute-start(bf16[768,512]{1,0:T(8,128)(2,1)} %collective-permute-done.15.refs_0_), channel_id=1, source_target_pairs={{0,1},{1,0},{2,3},{3,2},{4,5},{5,4},{6,7},{7,6},{8,9},{9,8},{10,11... | collective-permute-start | bytes 2359304 | tf_op jit(solution)/shard_map/ppermute | solution.py:26
  381.8 53.4 %collective-permute-start.25 = (bf16[768,512]{1,0:T(8,128)(2,1)}, bf16[768,512]{1,0:T(8,128)(2,1)}, u32[]{:S(2)}, u32[]{:S(2)}) collective-permute-start(bf16[768,512]{1,0:T(8,128)(2,1)} %collective-permute-done.16.refs_0_), channel_id=1, source_target_pairs={{0,2},{1,3},{2,0},{3,1},{4,6},{5,7},{6,4},{7,5},{8,10},{9,11},{10,... | collective-permute-start | bytes 2359304 | tf_op jit(solution)/shard_map/ppermute | solution.py:26
  383.3 51.8 %collective-permute-start.21 = (bf16[768,512]{1,0:T(8,128)(2,1)}, bf16[768,512]{1,0:T(8,128)(2,1)}, u32[]{:S(2)}, u32[]{:S(2)}) collective-permute-start(bf16[768,512]{1,0:T(8,128)(2,1)} %fusion.100), channel_id=1, source_target_pairs={{0,8},{4,12},{8,0},{12,4},{16,24},{20,28},{24,16},{28,20},{1,9},{5... | collective-permute-start | bytes 2359304 | tf_op jit(solution)/shard_map/ppermute | solution.py:26
  435.9 37.5 %collective-permute-start.23 = (bf16[768,512]{1,0:T(8,128)(2,1)}, bf16[768,512]{1,0:T(8,128)(2,1)}, u32[]{:S(2)}, u32[]{:S(2)}) collective-permute-start(bf16[768,512]{1,0:T(8,128)(2,1)} %collective-permute-done.21.refs_0_), channel_id=1, source_target_pairs={{0,2},{1,3},{2,0},{3,1},{4,6},{5,7},{6,4},{7,5},{8,10},{9,11},{10,... | collective-permute-start | bytes 2359304 | tf_op jit(solution)/shard_map/ppermute | solution.py:26
  477.0 40.7 %collective-permute-start.35 = (bf16[768,512]{1,0:T(8,128)(2,1)}, bf16[768,512]{1,0:T(8,128)(2,1)}, u32[]{:S(2)}, u32[]{:S(2)}) collective-permute-start(bf16[768,512]{1,0:T(8,128)(2,1)} %add_convert_fusion.9), channel_id=1, source_target_pairs={{0,16},{4,20},{8,24},{12,28},{16,0},{20,4},{24,8},{28,12},{1,17},{... | collective-permute-start | bytes 2359304 | tf_op jit(solution)/shard_map/ppermute | solution.py:26
  543.4 37.3 %collective-permute-start.42 = (bf16[768,512]{1,0:T(8,128)(2,1)}, bf16[768,512]{1,0:T(8,128)(2,1)}, u32[]{:S(2)}, u32[]{:S(2)}) collective-permute-start(bf16[768,512]{1,0:T(8,128)(2,1)} %add_convert_fusion.7), channel_id=1, source_target_pairs={{0,24},{4,28},{8,16},{12,20},{16,8},{20,12},{24,0},{28,4},{1,25},{... | collective-permute-start | bytes 2359304 | tf_op jit(solution)/shard_map/ppermute | solution.py:26
  548.3 32.4 %collective-permute-start.41 = (bf16[320,1408]{1,0:T(8,128)(2,1)}, bf16[320,1408]{1,0:T(8,128)(2,1)}, u32[]{:S(2)}, u32[]{:S(2)}) collective-permute-start(bf16[320,1408]{1,0:T(8,128)(2,1)} %get-tuple-element.257), channel_id=1, source_target_pairs={{0,4},{4,0},{8,12},{12,8},{16,20},{20,16},{24,28},{28,24},{1,5},{5... | collective-permute-start | bytes 2703368 | tf_op jit(solution)/shard_map/ppermute | solution.py:26
  580.9 359.0 %reduce-scatter.5.cloned.1.call-start = ((), (), s32[]{:S(2)}) async-start(), calls=%async_computation.6 | async-start | bytes 9437184 | tf_op jit(solution)/shard_map/reduce_scatter | solution.py:840
  605.8 46.0 %collective-permute-start.48 = (bf16[1024,512]{1,0:T(8,128)(2,1)S(1)}, bf16[1024,512]{1,0:T(8,128)(2,1)S(1)}, u32[]{:S(2)}, u32[]{:S(2)}) collective-permute-start(bf16[1024,512]{1,0:T(8,128)(2,1)S(1)} %get-tuple-element.298), channel_id=1, source_target_pairs={{0,2},{1,3},{2,0},{3,1},{4,6},{5,7},{6,4},{7,5},{8,10},{9,11},{10,... | collective-permute-start | bytes 3145736 | tf_op jit(solution)/shard_map/ppermute | solution.py:26
  716.3 76.6 %collective-permute-start.53 = (bf16[768,512]{1,0:T(8,128)(2,1)}, bf16[768,512]{1,0:T(8,128)(2,1)}, u32[]{:S(2)}, u32[]{:S(2)}) collective-permute-start(bf16[768,512]{1,0:T(8,128)(2,1)} %get-tuple-element.177), channel_id=1, source_target_pairs={{0,16},{4,20},{8,24},{12,28},{16,0},{20,4},{24,8},{28,12},{1,17},{... | collective-permute-start | bytes 2359304 | tf_op jit(solution)/shard_map/ppermute | solution.py:26
  721.1 226.3 %collective-permute-start.70 = (bf16[512,2816]{1,0:T(8,128)(2,1)}, bf16[512,2816]{1,0:T(8,128)(2,1)}, u32[]{:S(2)}, u32[]{:S(2)}) collective-permute-start(bf16[512,2816]{1,0:T(8,128)(2,1)} %convolution_convert_fusion.1), channel_id=1, source_target_pairs={{0,4},{4,0},{8,12},{12,8},{16,20},{20,16},{24,28},{28,24},{1,5},{5... | collective-permute-start | bytes 8650760 | tf_op jit(solution)/shard_map/ppermute | solution.py:26
  721.8 214.6 %collective-permute-start.69 = (bf16[384,2816]{1,0:T(8,128)(2,1)}, bf16[384,2816]{1,0:T(8,128)(2,1)}, u32[]{:S(2)}, u32[]{:S(2)}) collective-permute-start(bf16[384,2816]{1,0:T(8,128)(2,1)} %slice.349), channel_id=1, source_target_pairs={{0,4},{4,0},{8,12},{12,8},{16,20},{20,16},{24,28},{28,24},{1,5},{5... | collective-permute-start | bytes 6488072 | tf_op jit(solution)/shard_map/ppermute | solution.py:26
  792.9 43.0 %collective-permute-start.59 = (bf16[1024,512]{1,0:T(8,128)(2,1)S(1)}, bf16[1024,512]{1,0:T(8,128)(2,1)S(1)}, u32[]{:S(2)}, u32[]{:S(2)}) collective-permute-start(bf16[1024,512]{1,0:T(8,128)(2,1)S(1)} %add_convert_fusion), channel_id=1, source_target_pairs={{0,2},{1,3},{2,0},{3,1},{4,6},{5,7},{6,4},{7,5},{8,10},{9,11},{10,... | collective-permute-start | bytes 3145736 | tf_op jit(solution)/shard_map/ppermute | solution.py:26
  818.9 36.0 %collective-permute-start.54 = (bf16[768,512]{1,0:T(8,128)(2,1)S(1)}, bf16[768,512]{1,0:T(8,128)(2,1)S(1)}, u32[]{:S(2)}, u32[]{:S(2)}) collective-permute-start(bf16[768,512]{1,0:T(8,128)(2,1)S(1)} %copy-done.47), channel_id=1, source_target_pairs={{0,8},{4,12},{8,0},{12,4},{16,24},{20,28},{24,16},{28,20},{1,9},{5... | collective-permute-start | bytes 2359304 | tf_op jit(solution)/shard_map/ppermute | solution.py:26
  862.9 68.8 %collective-permute-start.62 = (bf16[1024,512]{1,0:T(8,128)(2,1)S(1)}, bf16[1024,512]{1,0:T(8,128)(2,1)S(1)}, u32[]{:S(2)}, u32[]{:S(2)}) collective-permute-start(bf16[1024,512]{1,0:T(8,128)(2,1)S(1)} %get-tuple-element.240), channel_id=1, source_target_pairs={{0,2},{1,3},{2,0},{3,1},{4,6},{5,7},{6,4},{7,5},{8,10},{9,11},{10,... | collective-permute-start | bytes 3145736 | tf_op jit(solution)/shard_map/ppermute | solution.py:26
  887.2 77.1 %collective-permute-start.57 = (bf16[1024,1024]{1,0:T(8,128)(2,1)}, bf16[1024,1024]{1,0:T(8,128)(2,1)}, u32[]{:S(2)}, u32[]{:S(2)}) collective-permute-start(bf16[1024,1024]{1,0:T(8,128)(2,1)} %pad_maximum_fusion.7), channel_id=1, source_target_pairs={{0,1},{1,0},{2,3},{3,2},{4,5},{5,4},{6,7},{7,6},{8,9},{9,8},{10,11... | collective-permute-start | bytes 6291464 | tf_op jit(solution)/shard_map/ppermute | solution.py:26
  934.4 35.7 %collective-permute-start.68 = (bf16[1024,1024]{1,0:T(8,128)(2,1)}, bf16[1024,1024]{1,0:T(8,128)(2,1)}, u32[]{:S(2)}, u32[]{:S(2)}) collective-permute-start(bf16[1024,1024]{1,0:T(8,128)(2,1)} %pad_maximum_fusion.8), channel_id=1, source_target_pairs={{0,1},{1,0},{2,3},{3,2},{4,5},{5,4},{6,7},{7,6},{8,9},{9,8},{10,11... | collective-permute-start | bytes 6291464 | tf_op jit(solution)/shard_map/ppermute | solution.py:26
  (130 other events, 2041.4 us)
Sparse Core Ops, SparseCore 0:
  10.8 163.5 all-gather.3
  184.7 81.9 all-gather.5
  272.9 97.7 all-gather.7
  581.0 118.5 reduce-scatter.2
  703.7 206.1 reduce-scatter.4

commit v12 on v11

--- a/solution.py
+++ b/solution.py
@@ -785,13 +785,12 @@
     quarter = half // 2
     act_late = after(activation, sums_sent[2], returned[1])
     down_given = term(grad_rows, act_late)(given_at, half)
-    down_sums = [group_send(down_given[: 40 * unit])]
+    down_sums = [group_send(down_given[: 56 * unit])]
     expert_part = up_pass(
         where, after(activation, down_given, returned[2], *gate_grad_near.values()), *down
     )
     expert_part = after(expert_part, down_sums[0], *came_home.values())
     expert_own = lax.psum_scatter(expert_part, "tensor", scatter_dimension=1, tiled=True)
-    down_sums.append(group_send(down_given[40 * unit : 80 * unit], down_sums[0]))
     came_home = {s: after(v, expert_part) for s, v in came_home.items()}
     back = unpacked([came_home[s] for s in range(EXPERTS)])
 
@@ -824,21 +823,22 @@
     kept = []
 
     def give_pair(sent):
-        down_sums.append(group_send(down_given[80 * unit :], down_sums[1], sent))
-        pair_term = term(moe_rows, after(pre_grad, sent, down_sums[1]))
+        down_sums.append(group_send(down_given[56 * unit : 112 * unit], down_sums[0], sent))
+        pair_term = term(moe_rows, after(pre_grad, sent))
         pair_given.extend(pair_term(given_at + k * quarter, quarter) for k in range(2))
-        return (*pair_given, down_sums[2])
+        return (*pair_given, down_sums[1])
 
     attn_grad = tensor_gather(hidden_grad.astype(low), give_pair)
-    pair_sums = [group_send(pair_given[0][: 16 * unit], down_sums[2])]
+    down_sums.append(group_send(down_given[112 * unit :], down_sums[1]))
+    pair_sums = [group_send(pair_given[0][: 12 * unit], down_sums[1])]
     context_grad = jnp.dot(attn_grad, out_full, preferred_element_type=full).astype(low)
     out_grad = contract(after(attn_grad, context_grad), context, 0, 0).astype(low)
     qkv_grad_rows = attention_back(query, keys, values, logs, context_grad, cosine, sine, scale)
-    qkv_grad_rows = after(qkv_grad_rows, pair_sums[0], out_grad)
+    qkv_grad_rows = after(qkv_grad_rows, pair_sums[0], down_sums[2], out_grad)
     qkv_grad = contract(normed_in, qkv_grad_rows, 0, 0).astype(low)
     grads_both = jnp.concatenate([qkv_grad, out_grad], 1)
     shards = lax.psum_scatter(grads_both, "dp", scatter_dimension=0, tiled=True)
-    pair_sums.append(group_send(pair_given[0][16 * unit :], pair_sums[0], grads_both))
+    pair_sums.append(group_send(pair_given[0][12 * unit :], pair_sums[0], grads_both))
     pair_last = group_send(pair_given[1], pair_sums[0], grads_both)
     outputs = {0: expert_own[:MOST]}
     part = after(expert_own[MOST : 2 * MOST], grads_both)
@@ -847,11 +847,11 @@
     def keep(sent):
         late = after(pre_grad, sent, expert_own)
         kept.append(term(moe_rows, late)(mine_at, half))
-        kept.append(term(grad_rows, after(activation, kept[0]))(mine_at, half))
+        kept.append(term(grad_rows, after(activation, kept[0], outputs[2]))(mine_at, half))
         return kept
 
     parts = spread_dot(where, after(qkv_grad_rows, grads_both), first, 0, tensor_count)
-    normed_grad = near_reduce(*parts, [], outputs[2], filler=keep)
+    normed_grad = near_reduce(*parts, [], filler=keep)
     for k in (2, 3):
         part = after(expert_own[k * MOST : (k + 1) * MOST], outputs[2])
         outputs[order[k]] = swap(part, "dp", order[k] * group_count)

time: 992 us -> 983 us (level)
  starting transfers between devices: 73.4 us -> 61.7 us
    ppermute x71, starting transfers between devices: 72.7 us -> 61.1 us  [swap(): lax.ppermute(value, axis, [(i, i ^ distance) for i in range(lax.axis_size...]
  transfers between devices with their start and end apart: 76 -> 76, of which waited for: 26 -> 24; matrix products, arithmetic and copies ran while one was open for 27% -> 27% of each run, Pallas kernels for 24% -> 24%
where the time goes in v12:
time: 983 us; the launch traced here: 974 us
  waiting for transfers between devices  365 us (37%)
  Pallas kernels  238 us (24%)
  matrix products  156 us (16%)
  other arithmetic  83.5 us (8%)
  starting transfers between devices  61.7 us (6%)
  local copies, waits for them, and re-layouts  53.4 us (5%)
  between operations  15.7 us (2%)
    ppermute x71, waiting for transfers between devices, swap(): lax.ppermute(value, axis, [(i, i ^ distance) for i in range(lax.axis_size...  238 us
    all_gather x1, waiting for transfers between devices, body(): lax.all_gather(jnp.concatenate([qkv_weight.reshape(-1, 3 * size), out_wei...  127 us
    dot_general x25, matrix products, contract(): lax.dot_general(left, right, (((left_dim,), (right_dim,)), ((), ())), pre...  122 us
    pallas_call x4, Pallas kernels, expert_pass(): pl.pallas_call(functools.partial(expert_kernel, count, len(carried)), gri...  120 us
    ppermute x71, starting transfers between devices, swap(): lax.ppermute(value, axis, [(i, i ^ distance) for i in range(lax.axis_size...  61.1 us
    pallas_call x2, Pallas kernels, down_pass(): pl.pallas_call(functools.partial(down_kernel, len(carried)), grid_spec=pl...  32.5 us
    pallas_call x1, Pallas kernels, up_pass(): pl.pallas_call(up_kernel, grid_spec=pltpu.PrefetchScalarGridSpec(num_scal...  27 us
  transfers between devices with their start and end apart: 76, of which 24 were waited for; matrix products, arithmetic and copies ran while one was open for 27% of the time, Pallas kernels for 24%

profile of v12, /device:TPU:0, one launch (start us, length us, event | category | flops | bytes accessed | tf_op | source)
XLA Modules:
  0.0 974.0 jit_solution(11965617045443034768)
XLA Ops:
  21.8 5.9 slice_bitcast_fusion
  40.3 6.9 convolution_convert_fusion.3.rows
  47.2 127.2 %all-gather.4.cloned.1.call-done.right = bf16[2048,2176]{1,0:T(8,128)(2,1)} async-done(((bf16[256,2176]{1,0:T(8,128)(2,1)}), bf16[2048,2176]{1,0:T(8,128)(2,1)}) %all-gather.4.cloned.1.call-update) | async-done | bytes 8912912 | tf_op jit(solution)/shard_map/all_gather | solution.py:595
  178.9 5.2 fusion.2
  185.1 11.7 %fusion.3.q_in.k_in.v_in = f32[1024,1536]{1,0:T(8,128)} fusion(bf16[1024,2048]{1,0:T(8,128)(2,1)} %fusion.2, bf16[2048,2176]{1,0:T(8,128)(2,1)} %all-gather.4.cloned.1.call-done.right), kind=kOutput, calls=%fused_computation.9 | convolution fusion | flops 6442450944 | bytes 16777216 | tf_op jit(solution)/shard_map/dot_general | solution.py:673
  201.0 12.9 %attention.1 = (bf16[1024,512]{1,0:T(8,128)(2,1)S(1)}, bf16[1024,512]{1,0:T(8,128)(2,1)S(1)}, bf16[1024,512]{1,0:T(8,128)(2,1)S(1)}, bf16[1024,512]{1,0:T(8,128)(2,1)S(1)}, f32[4,1024,1]{2,1,0:T(8,128)}) custom-call(f32[1024,1536]{1,0:T(8,128)} %fusion.3.q_in.k_in.v_in, f32[1024,1536]{1,0:T(8,128)} %fusion.3.q_in.k_in.v_in, ...), custom_call_target="tpu_custom_call" | custom-call | flops 1342177280 | bytes 10485760 | tf_op jit(solution)/shard_map/attention/pallas_call | solution.py:135
  217.7 5.5 spread.2
  229.1 5.0 collective-permute-done.10.refs_8_
  237.0 11.0 %down.2 = (bf16[3072,2048]{1,0:T(8,128)(2,1)}, bf16[3072,1408]{1,0:T(8,128)(2,1)}) custom-call(s32[3]{0:T(128)S(1)} %pad_add_fusion.where, bf16[768,2048]{1,0:T(8,128)(2,1)} %convolution_convert_fusion.3.rows, bf16[1024,1408]{1,0:T(8,128)(2,1)S(1)} %get-tuple-element.234.own, bf16[1024,1408]{1,0:T(8,128)(2,1)} %collective-permute-done.came), custom_call_target="tpu_custom_call" | custom-call | flops 4429185024 | bytes 14221312 | tf_op jit(solution)/shard_map/down/pallas_call | solution.py:272
  247.9 12.1 %collective-permute-done.11 = bf16[1024,512]{1,0:T(8,128)(2,1)} collective-permute-done((bf16[1024,512]{1,0:T(8,128)(2,1)}, bf16[1024,512]{1,0:T(8,128)(2,1)}, u32[]{:S(2)}, u32[]{:S(2)}) %collective-permute-start.11) | collective-permute-done | bytes 1048608 | tf_op jit(solution)/shard_map/ppermute | solution.py:26
  289.5 33.7 %collective-permute-done.18.refs_2_ = bf16[768,512]{1,0:T(8,128)(2,1)S(1)} collective-permute-done((bf16[768,512]{1,0:T(8,128)(2,1)S(1)}, bf16[768,512]{1,0:T(8,128)(2,1)S(1)}, u32[]{:S(2)}, u32[]{:S(2)}) %collective-permute-start.18) | collective-permute-done | bytes 786464 | tf_op jit(solution)/shard_map/ppermute | solution.py:26
  329.9 20.0 %collective-permute-done.20.refs_10_ = bf16[1184,1408]{1,0:T(8,128)(2,1)S(1)} collective-permute-done((bf16[1184,1408]{1,0:T(8,128)(2,1)S(1)}, bf16[1184,1408]{1,0:T(8,128)(2,1)S(1)}, u32[]{:S(2)}, u32[]{:S(2)}) %collective-permute-start.20) | collective-permute-done | bytes 3334176 | tf_op jit(solution)/shard_map/ppermute | solution.py:26
  351.7 30.0 %expert.4 = (bf16[3072,2048]{1,0:T(8,128)(2,1)}, bf16[3072,1408]{1,0:T(8,128)(2,1)}, bf16[3072,2816]{1,0:T(8,128)(2,1)}, bf16[768,1024]{1,0:T(8,128)(2,1)}, bf16[768,1024]{1,0:T(8,128)(2,1)}, /*index=5*/f32[1,768]{1,0:T(1,128)}) custom-call(s32[3]{0:T(128)} %copy-done.10, bf16[768,512]{1,0:T(8,128)(2,1)} %copy-done.60, bf16[768,512]{1,0:T(8,128)(2,1)} %copy-done.62, ...), custom_call_target="tpu_custom_call" | custom-call | flops 17716740096 | bytes 32768000 | tf_op jit(solution)/shard_map/expert/pallas_call | solution.py:411
  383.4 21.5 %down.3 = (bf16[3072,2048]{1,0:T(8,128)(2,1)}, bf16[3072,1408]{1,0:T(8,128)(2,1)}) custom-call(s32[3]{0:T(128)S(1)} %copy-done.11, bf16[2304,2048]{1,0:T(8,128)(2,1)} %all-gather.8.cloned.1.call-done.rows, bf16[1024,1408]{1,0:T(8,128)(2,1)S(1)} %get-tuple-element.234.own, ...), custom_call_target="tpu_custom_call", output_to_operand_aliasing={{0}: (4, {}), {1}: (5, {})} | custom-call | flops 13287555072 | bytes 31129600 | tf_op jit(solution)/shard_map/down/pallas_call | solution.py:272
  405.0 30.2 %expert.5 = (bf16[3072,2048]{1,0:T(8,128)(2,1)}, bf16[3072,1408]{1,0:T(8,128)(2,1)}, bf16[3072,2816]{1,0:T(8,128)(2,1)}, bf16[768,1024]{1,0:T(8,128)(2,1)}, bf16[768,1024]{1,0:T(8,128)(2,1)}, /*index=5*/f32[1,768]{1,0:T(1,128)}) custom-call(s32[3]{0:T(128)} %copy-done.10, ...), custom_call_target="tpu_custom_call", output_to_operand_aliasing={{0}: (15, {}), {1}: (16, {}), {2}: (17, {})} | custom-call | flops 17716740096 | bytes 32768000 | tf_op jit(solution)/shard_map/expert/pallas_call | solution.py:411
  443.9 29.9 %expert.6 = (bf16[3072,2048]{1,0:T(8,128)(2,1)}, bf16[3072,1408]{1,0:T(8,128)(2,1)}, bf16[3072,2816]{1,0:T(8,128)(2,1)}, bf16[768,1024]{1,0:T(8,128)(2,1)}, bf16[768,1024]{1,0:T(8,128)(2,1)}, /*index=5*/f32[1,768]{1,0:T(1,128)}) custom-call(s32[3]{0:T(128)} %copy-done.10, ...), custom_call_target="tpu_custom_call", output_to_operand_aliasing={{0}: (15, {}), {1}: (16, {}), {2}: (17, {})} | custom-call | flops 17716740096 | bytes 32768000 | tf_op jit(solution)/shard_map/expert/pallas_call | solution.py:411
  485.4 29.8 %expert.7 = (bf16[3072,2048]{1,0:T(8,128)(2,1)}, bf16[3072,1408]{1,0:T(8,128)(2,1)}, bf16[3072,2816]{1,0:T(8,128)(2,1)}, bf16[768,1024]{1,0:T(8,128)(2,1)}, bf16[768,1024]{1,0:T(8,128)(2,1)}, /*index=5*/f32[1,768]{1,0:T(1,128)}) custom-call(s32[3]{0:T(128)} %copy-done.10, ...), custom_call_target="tpu_custom_call", output_to_operand_aliasing={{0}: (15, {}), {1}: (16, {}), {2}: (17, {})} | custom-call | flops 17716740096 | bytes 32768000 | tf_op jit(solution)/shard_map/expert/pallas_call | solution.py:411
  524.6 14.1 %fusion.14 = bf16[1024,1408]{1,0:T(8,128)(2,1)S(1)} fusion(bf16[3072,1408]{1,0:T(8,128)(2,1)} %get-tuple-element.183.act, bf16[3072,2048]{1,0:T(8,128)(2,1)} %get-tuple-element.143, s32[]{:T(128)S(6)} %select_n.169), kind=kOutput, calls=%fused_computation.23 | convolution fusion | flops 8859811840 | bytes 17825796 | tf_op jit(solution)/shard_map/dot_general | solution.py:30
  551.8 27.0 %up.1 = bf16[3072,2048]{1,0:T(8,128)(2,1)} custom-call(s32[3]{0:T(128)S(1)} %copy-done.12, bf16[3072,1408]{1,0:T(8,128)(2,1)} %get-tuple-element.183.act, bf16[1024,1408]{1,0:T(8,128)(2,1)S(1)} %get-tuple-element.234.own, bf16[1024,1408]{1,0:T(8,128)(2,1)} %collective-permute-done.came), custom_call_target="tpu_custom_call" | custom-call | flops 17716740096 | bytes 27000832 | tf_op jit(solution)/shard_map/up/pallas_call | solution.py:339
  607.5 17.3 %convolution_convert_fusion.2 = bf16[512,2816]{1,0:T(8,128)(2,1)} fusion(bf16[3072,2816]{1,0:T(8,128)(2,1)} %get-tuple-element.182, bf16[3072,2048]{1,0:T(8,128)(2,1)} %get-tuple-element.167, s32[]{:T(128)S(6)} %select_n.169), kind=kOutput, calls=%fused_computation.19 | convolution fusion | flops 8859811840 | bytes 23330820 | tf_op jit(solution)/shard_map/dot_general | solution.py:30
  624.8 12.0 %convolution_convert_fusion.1 = bf16[512,2816]{1,0:T(8,128)(2,1)} fusion(bf16[3072,2816]{1,0:T(8,128)(2,1)S(1)} %bitcast.151, bf16[3072,2048]{1,0:T(8,128)(2,1)} %get-tuple-element.167, s32[]{:T(128)S(6)} %select_n.173), kind=kOutput, calls=%fused_computation.18 | convolution fusion | flops 8859811840 | bytes 23330820 | tf_op jit(solution)/shard_map/dot_general | solution.py:30
  636.8 12.3 %collective-permute-done.48 = bf16[1024,512]{1,0:T(8,128)(2,1)S(1)} collective-permute-done((bf16[1024,512]{1,0:T(8,128)(2,1)S(1)}, bf16[1024,512]{1,0:T(8,128)(2,1)S(1)}, u32[]{:S(2)}, u32[]{:S(2)}) %collective-permute-start.48) | collective-permute-done | bytes 1048608 | tf_op jit(solution)/shard_map/ppermute | solution.py:26
  665.1 15.8 %attention_back.1.left = bf16[1024,1536]{1,0:T(8,128)(2,1)} custom-call(bf16[1024,512]{1,0:T(8,128)(2,1)S(1)} %copy-done.14, bf16[1024,512]{1,0:T(8,128)(2,1)S(1)} %copy-done.16, bf16[1024,512]{1,0:T(8,128)(2,1)S(1)} %copy-done.18, f32[4,1024,1]{2,1,0:T(8,128)} %get-tuple-element.162.logs, bf16[1024,512]{1,0:T(8,128)(2,1)S(1)} %fusion.87.grad, ...), custom_call_target="tpu_custom_call" | custom-call | flops 3355443200 | bytes 8388608 | tf_op jit(solution)/shard_map/attention_back/pallas_call | solution.py:188
  680.8 10.5 %convolution_convert_fusion = bf16[2048,1536]{0,1:T(8,128)(2,1)} fusion(bf16[1024,2048]{1,0:T(8,128)(2,1)S(1)} %copy-done.32, bf16[1024,1536]{1,0:T(8,128)(2,1)} %attention_back.1.left), kind=kOutput, calls=%fused_computation.8 | convolution fusion | flops 6445596672 | bytes 13631488 | tf_op jit(solution)/shard_map/dot_general | solution.py:30
  691.4 7.8 pad_maximum_fusion
  699.2 12.2 %spread.3 = (bf16[1024,1024]{1,0:T(8,128)(2,1)S(1)}, bf16[1024,1024]{1,0:T(8,128)(2,1)}) custom-call(s32[3]{0:T(128)S(1)} %copy-done.12, bf16[1024,1536]{1,0:T(8,128)(2,1)} %attention_back.1.left, bf16[2048,2176]{1,0:T(8,128)(2,1)} %all-gather.4.cloned.1.call-done.right), custom_call_target="tpu_custom_call" | custom-call | flops 6442450944 | bytes 13631488 | tf_op jit(solution)/shard_map/spread/pallas_call | solution.py:310
  726.8 26.4 %fusion.11.refs_0_ = bf16[1024,2816]{1,0:T(8,128)(2,1)} fusion(bf16[3072,2816]{1,0:T(8,128)(2,1)} %get-tuple-element.182, bf16[3072,2048]{1,0:T(8,128)(2,1)} %get-tuple-element.167, s32[]{:T(128)S(6)} %select_n.186), kind=kOutput, calls=%fused_computation.17 | convolution fusion | flops 17719623680 | bytes 29360132 | tf_op jit(solution)/shard_map/dot_general | solution.py:30
  753.2 48.6 %collective-permute-done.53 = bf16[768,512]{1,0:T(8,128)(2,1)S(1)} collective-permute-done((bf16[768,512]{1,0:T(8,128)(2,1)S(1)}, bf16[768,512]{1,0:T(8,128)(2,1)S(1)}, u32[]{:S(2)}, u32[]{:S(2)}) %collective-permute-start.53) | collective-permute-done | bytes 786464 | tf_op jit(solution)/shard_map/ppermute | solution.py:26
  801.8 13.5 %fusion.17.refs_3_ = bf16[1024,1408]{1,0:T(8,128)(2,1)} fusion(bf16[3072,1408]{1,0:T(8,128)(2,1)S(1)} %bitcast.153, bf16[3072,2048]{1,0:T(8,128)(2,1)} %get-tuple-element.143, s32[]{:T(128)S(6)} %select_n.186), kind=kOutput, calls=%fused_computation.24 | convolution fusion | flops 8859811840 | bytes 17825796 | tf_op jit(solution)/shard_map/dot_general | solution.py:30
  827.3 29.7 %collective-permute-done.54 = bf16[768,512]{1,0:T(8,128)(2,1)S(1)} collective-permute-done((bf16[768,512]{1,0:T(8,128)(2,1)S(1)}, bf16[768,512]{1,0:T(8,128)(2,1)S(1)}, u32[]{:S(2)}, u32[]{:S(2)}) %collective-permute-start.54) | collective-permute-done | bytes 786464 | tf_op jit(solution)/shard_map/ppermute | solution.py:26
  862.3 43.4 %collective-permute-done.64 = f32[6,2048]{1,0:T(8,128)S(1)} collective-permute-done((f32[6,2048]{1,0:T(8,128)S(1)}, f32[6,2048]{1,0:T(8,128)S(1)}, u32[]{:S(2)}, u32[]{:S(2)}) %collective-permute-start.64) | collective-permute-done | bytes 49184 | tf_op jit(solution)/shard_map/ppermute | solution.py:26
  942.1 12.0 %expert_grad_sum.1 = f32[3,1024,1408]{2,1,0:T(8,128)} custom-call(bf16[1024,2816]{1,0:T(8,128)(2,1)} %fusion.11.refs_0_, bf16[512,2816]{1,0:T(8,128)(2,1)S(1)} %copy-done, bf16[512,2816]{1,0:T(8,128)(2,1)} %collective-permute-done.70.refs_2_, bf16[1024,1408]{1,0:T(8,128)(2,1)S(1)} %copy-done.1, bf16[1024,1408]{1,0:T(8,128)(2,1)S(1)} %pad_maximum_fusion.4.refs_4_), custom_call_target="tpu_custom_call" | custom-call | flops 4325376 | bytes 34603008 | tf_op jit(solution)/shard_map/expert_grad_sum/pallas_call | solution.py:495
  (450 shorter events, 256.9 us)
Async XLA Ops:
  7.2 167.2 %all-gather.4.cloned.1.call-start = ((), (), s32[]{:S(2)}) async-start(), calls=%async_computation.2 | async-start | bytes 10027008 | tf_op jit(solution)/shard_map/all_gather | solution.py:595
  10.3 256.4 %all-gather.6.cloned.1.call-start = ((), (), s32[]{:S(2)}) async-start(), calls=%async_computation.3 | async-start | bytes 5242880 | tf_op jit(solution)/shard_map/all_gather | solution.py:661
  14.0 162.8 %collective-permute-start.4 = (f32[1,768]{1,0:T(1,128)S(1)}, f32[1,768]{1,0:T(1,128)S(1)}, u32[]{:S(2)}, u32[]{:S(2)}) collective-permute-start(f32[1,768]{1,0:T(1,128)S(1)} %fusion.36), channel_id=1, source_target_pairs={{0,8},{4,12},{8,0},{12,4},{16,24},{20,28},{24,16},{28,20},{1,9},{5... | collective-permute-start | bytes 9224 | tf_op jit(solution)/shard_map/ppermute | solution.py:26
  17.7 160.7 %collective-permute-start.5 = (f32[1,768]{1,0:T(1,128)S(1)}, f32[1,768]{1,0:T(1,128)S(1)}, u32[]{:S(2)}, u32[]{:S(2)}) collective-permute-start(f32[1,768]{1,0:T(1,128)S(1)} %fusion.31), channel_id=1, source_target_pairs={{0,16},{4,20},{8,24},{12,28},{16,0},{20,4},{24,8},{28,12},{1,17},{... | collective-permute-start | bytes 9224 | tf_op jit(solution)/shard_map/ppermute | solution.py:26
  20.9 163.3 %collective-permute-start.6 = (f32[1,768]{1,0:T(1,128)S(1)}, f32[1,768]{1,0:T(1,128)S(1)}, u32[]{:S(2)}, u32[]{:S(2)}) collective-permute-start(f32[1,768]{1,0:T(1,128)S(1)} %fusion.26), channel_id=1, source_target_pairs={{0,24},{4,28},{8,16},{12,20},{16,8},{20,12},{24,0},{28,4},{1,25},{... | collective-permute-start | bytes 9224 | tf_op jit(solution)/shard_map/ppermute | solution.py:26
  20.9 163.3 %collective-permute-start.1 = (f32[1,1024]{1,0:T(1,128)S(1)}, f32[1,1024]{1,0:T(1,128)S(1)}, u32[]{:S(2)}, u32[]{:S(2)}) collective-permute-start(f32[1,1024]{1,0:T(1,128)S(1)} %get-tuple-element.273), channel_id=1, source_target_pairs={{0,8},{4,12},{8,0},{12,4},{16,24},{20,28},{24,16},{28,20},{1,9},{5... | collective-permute-start | bytes 12296 | tf_op jit(solution)/shard_map/ppermute | solution.py:26
  27.7 156.5 %collective-permute-start = (bf16[1024,1408]{1,0:T(8,128)(2,1)S(1)}, bf16[1024,1408]{1,0:T(8,128)(2,1)}, u32[]{:S(2)}, u32[]{:S(2)}) collective-permute-start(bf16[1024,1408]{1,0:T(8,128)(2,1)S(1)} %get-tuple-element.234.own), channel_id=1, source_target_pairs={{0,4},{4,0},{8,12},{12,8},{16,20},{20,16},{24,28},{28,24},{1,5},{5... | collective-permute-start | bytes 8650760 | tf_op jit(solution)/shard_map/ppermute | solution.py:26
  184.6 198.8 %all-gather.8.cloned.1.call-start = ((), (), s32[]{:S(2)}) async-start(), calls=%async_computation.4 | async-start | bytes 11796480 | tf_op jit(solution)/shard_map/all_gather | solution.py:697
  272.8 451.5 %reduce-scatter.3.cloned.1.call-start = ((), (), s32[]{:S(2)}) async-start(), calls=%async_computation.5 | async-start | bytes 15728640 | tf_op jit(solution)/shard_map/reduce_scatter | solution.py:793
  276.0 74.0 %collective-permute-start.20 = (bf16[1184,1408]{1,0:T(8,128)(2,1)S(1)}, bf16[1184,1408]{1,0:T(8,128)(2,1)S(1)}, u32[]{:S(2)}, u32[]{:S(2)}) collective-permute-start(bf16[1184,1408]{1,0:T(8,128)(2,1)S(1)} %pad_maximum_fusion.2), channel_id=1, source_target_pairs={{0,4},{4,0},{8,12},{12,8},{16,20},{20,16},{24,28},{28,24},{1,5},{5... | collective-permute-start | bytes 10002440 | tf_op jit(solution)/shard_map/ppermute | solution.py:26
  289.0 38.1 %collective-permute-start.15 = (bf16[768,512]{1,0:T(8,128)(2,1)S(1)}, bf16[768,512]{1,0:T(8,128)(2,1)}, u32[]{:S(2)}, u32[]{:S(2)}) collective-permute-start(bf16[768,512]{1,0:T(8,128)(2,1)S(1)} %fusion.101), channel_id=1, source_target_pairs={{0,16},{4,20},{8,24},{12,28},{16,0},{20,4},{24,8},{28,12},{1,17},{... | collective-permute-start | bytes 2359304 | tf_op jit(solution)/shard_map/ppermute | solution.py:26
  289.5 40.4 %collective-permute-start.17 = (bf16[768,512]{1,0:T(8,128)(2,1)S(1)}, bf16[768,512]{1,0:T(8,128)(2,1)S(1)}, u32[]{:S(2)}, u32[]{:S(2)}) collective-permute-start(bf16[768,512]{1,0:T(8,128)(2,1)S(1)} %fusion.99.refs_0_), channel_id=1, source_target_pairs={{0,1},{1,0},{2,3},{3,2},{4,5},{5,4},{6,7},{7,6},{8,9},{9,8},{10,11... | collective-permute-start | bytes 2359304 | tf_op jit(solution)/shard_map/ppermute | solution.py:26
  327.1 54.8 %collective-permute-start.16 = (bf16[768,512]{1,0:T(8,128)(2,1)}, bf16[768,512]{1,0:T(8,128)(2,1)}, u32[]{:S(2)}, u32[]{:S(2)}) collective-permute-start(bf16[768,512]{1,0:T(8,128)(2,1)} %fusion.102), channel_id=1, source_target_pairs={{0,24},{4,28},{8,16},{12,20},{16,8},{20,12},{24,0},{28,4},{1,25},{... | collective-permute-start | bytes 2359304 | tf_op jit(solution)/shard_map/ppermute | solution.py:26
  328.4 53.3 %collective-permute-start.27 = (bf16[768,512]{1,0:T(8,128)(2,1)}, bf16[768,512]{1,0:T(8,128)(2,1)}, u32[]{:S(2)}, u32[]{:S(2)}) collective-permute-start(bf16[768,512]{1,0:T(8,128)(2,1)} %collective-permute-done.15.refs_0_), channel_id=1, source_target_pairs={{0,2},{1,3},{2,0},{3,1},{4,6},{5,7},{6,4},{7,5},{8,10},{9,11},{10,... | collective-permute-start | bytes 2359304 | tf_op jit(solution)/shard_map/ppermute | solution.py:26
  329.9 75.0 %collective-permute-start.26 = (bf16[768,512]{1,0:T(8,128)(2,1)}, bf16[768,512]{1,0:T(8,128)(2,1)}, u32[]{:S(2)}, u32[]{:S(2)}) collective-permute-start(bf16[768,512]{1,0:T(8,128)(2,1)} %collective-permute-done.15.refs_0_), channel_id=1, source_target_pairs={{0,1},{1,0},{2,3},{3,2},{4,5},{5,4},{6,7},{7,6},{8,9},{9,8},{10,11... | collective-permute-start | bytes 2359304 | tf_op jit(solution)/shard_map/ppermute | solution.py:26
  381.8 53.3 %collective-permute-start.25 = (bf16[768,512]{1,0:T(8,128)(2,1)}, bf16[768,512]{1,0:T(8,128)(2,1)}, u32[]{:S(2)}, u32[]{:S(2)}) collective-permute-start(bf16[768,512]{1,0:T(8,128)(2,1)} %collective-permute-done.16.refs_0_), channel_id=1, source_target_pairs={{0,2},{1,3},{2,0},{3,1},{4,6},{5,7},{6,4},{7,5},{8,10},{9,11},{10,... | collective-permute-start | bytes 2359304 | tf_op jit(solution)/shard_map/ppermute | solution.py:26
  383.4 51.8 %collective-permute-start.21 = (bf16[768,512]{1,0:T(8,128)(2,1)}, bf16[768,512]{1,0:T(8,128)(2,1)}, u32[]{:S(2)}, u32[]{:S(2)}) collective-permute-start(bf16[768,512]{1,0:T(8,128)(2,1)} %fusion.100), channel_id=1, source_target_pairs={{0,8},{4,12},{8,0},{12,4},{16,24},{20,28},{24,16},{28,20},{1,9},{5... | collective-permute-start | bytes 2359304 | tf_op jit(solution)/shard_map/ppermute | solution.py:26
  435.9 38.0 %collective-permute-start.23 = (bf16[768,512]{1,0:T(8,128)(2,1)}, bf16[768,512]{1,0:T(8,128)(2,1)}, u32[]{:S(2)}, u32[]{:S(2)}) collective-permute-start(bf16[768,512]{1,0:T(8,128)(2,1)} %collective-permute-done.21.refs_0_), channel_id=1, source_target_pairs={{0,2},{1,3},{2,0},{3,1},{4,6},{5,7},{6,4},{7,5},{8,10},{9,11},{10,... | collective-permute-start | bytes 2359304 | tf_op jit(solution)/shard_map/ppermute | solution.py:26
  477.4 40.7 %collective-permute-start.35 = (bf16[768,512]{1,0:T(8,128)(2,1)}, bf16[768,512]{1,0:T(8,128)(2,1)}, u32[]{:S(2)}, u32[]{:S(2)}) collective-permute-start(bf16[768,512]{1,0:T(8,128)(2,1)} %add_convert_fusion.9), channel_id=1, source_target_pairs={{0,16},{4,20},{8,24},{12,28},{16,0},{20,4},{24,8},{28,12},{1,17},{... | collective-permute-start | bytes 2359304 | tf_op jit(solution)/shard_map/ppermute | solution.py:26
  543.4 37.3 %collective-permute-start.42 = (bf16[768,512]{1,0:T(8,128)(2,1)}, bf16[768,512]{1,0:T(8,128)(2,1)}, u32[]{:S(2)}, u32[]{:S(2)}) collective-permute-start(bf16[768,512]{1,0:T(8,128)(2,1)} %add_convert_fusion.7), channel_id=1, source_target_pairs={{0,24},{4,28},{8,16},{12,20},{16,8},{20,12},{24,0},{28,4},{1,25},{... | collective-permute-start | bytes 2359304 | tf_op jit(solution)/shard_map/ppermute | solution.py:26
  581.0 350.1 %reduce-scatter.5.cloned.1.call-start = ((), (), s32[]{:S(2)}) async-start(), calls=%async_computation.6 | async-start | bytes 9437184 | tf_op jit(solution)/shard_map/reduce_scatter | solution.py:840
  604.8 44.4 %collective-permute-start.48 = (bf16[1024,512]{1,0:T(8,128)(2,1)S(1)}, bf16[1024,512]{1,0:T(8,128)(2,1)S(1)}, u32[]{:S(2)}, u32[]{:S(2)}) collective-permute-start(bf16[1024,512]{1,0:T(8,128)(2,1)S(1)} %get-tuple-element.296), channel_id=1, source_target_pairs={{0,2},{1,3},{2,0},{3,1},{4,6},{5,7},{6,4},{7,5},{8,10},{9,11},{10,... | collective-permute-start | bytes 3145736 | tf_op jit(solution)/shard_map/ppermute | solution.py:26
  606.1 43.0 %collective-permute-start.49 = (bf16[448,1408]{1,0:T(8,128)(2,1)S(1)}, bf16[448,1408]{1,0:T(8,128)(2,1)S(1)}, u32[]{:S(2)}, u32[]{:S(2)}) collective-permute-start(bf16[448,1408]{1,0:T(8,128)(2,1)S(1)} %copy-done.43), channel_id=1, source_target_pairs={{0,4},{4,0},{8,12},{12,8},{16,20},{20,16},{24,28},{28,24},{1,5},{5... | collective-permute-start | bytes 3784712 | tf_op jit(solution)/shard_map/ppermute | solution.py:26
  717.3 221.2 %collective-permute-start.70 = (bf16[512,2816]{1,0:T(8,128)(2,1)}, bf16[512,2816]{1,0:T(8,128)(2,1)}, u32[]{:S(2)}, u32[]{:S(2)}) collective-permute-start(bf16[512,2816]{1,0:T(8,128)(2,1)} %convolution_convert_fusion.1), channel_id=1, source_target_pairs={{0,4},{4,0},{8,12},{12,8},{16,20},{20,16},{24,28},{28,24},{1,5},{5... | collective-permute-start | bytes 8650760 | tf_op jit(solution)/shard_map/ppermute | solution.py:26
  718.2 209.3 %collective-permute-start.69 = (bf16[416,2816]{1,0:T(8,128)(2,1)}, bf16[416,2816]{1,0:T(8,128)(2,1)}, u32[]{:S(2)}, u32[]{:S(2)}) collective-permute-start(bf16[416,2816]{1,0:T(8,128)(2,1)} %slice.349), channel_id=1, source_target_pairs={{0,4},{4,0},{8,12},{12,8},{16,20},{20,16},{24,28},{28,24},{1,5},{5... | collective-permute-start | bytes 7028744 | tf_op jit(solution)/shard_map/ppermute | solution.py:26
  721.9 93.3 %collective-permute-start.59 = (bf16[1024,512]{1,0:T(8,128)(2,1)}, bf16[1024,512]{1,0:T(8,128)(2,1)}, u32[]{:S(2)}, u32[]{:S(2)}) collective-permute-start(bf16[1024,512]{1,0:T(8,128)(2,1)} %add_convert_fusion), channel_id=1, source_target_pairs={{0,2},{1,3},{2,0},{3,1},{4,6},{5,7},{6,4},{7,5},{8,10},{9,11},{10,... | collective-permute-start | bytes 3145736 | tf_op jit(solution)/shard_map/ppermute | solution.py:26
  726.1 75.6 %collective-permute-start.53 = (bf16[768,512]{1,0:T(8,128)(2,1)S(1)}, bf16[768,512]{1,0:T(8,128)(2,1)S(1)}, u32[]{:S(2)}, u32[]{:S(2)}) collective-permute-start(bf16[768,512]{1,0:T(8,128)(2,1)S(1)} %get-tuple-element.176), channel_id=1, source_target_pairs={{0,16},{4,20},{8,24},{12,28},{16,0},{20,4},{24,8},{28,12},{1,17},{... | collective-permute-start | bytes 2359304 | tf_op jit(solution)/shard_map/ppermute | solution.py:26
  820.0 38.9 %collective-permute-start.55 = (bf16[768,512]{1,0:T(8,128)(2,1)S(1)}, bf16[768,512]{1,0:T(8,128)(2,1)S(1)}, u32[]{:S(2)}, u32[]{:S(2)}) collective-permute-start(bf16[768,512]{1,0:T(8,128)(2,1)S(1)} %get-tuple-element.178), channel_id=1, source_target_pairs={{0,24},{4,28},{8,16},{12,20},{16,8},{20,12},{24,0},{28,4},{1,25},{... | collective-permute-start | bytes 2359304 | tf_op jit(solution)/shard_map/ppermute | solution.py:26
  820.3 36.7 %collective-permute-start.54 = (bf16[768,512]{1,0:T(8,128)(2,1)S(1)}, bf16[768,512]{1,0:T(8,128)(2,1)S(1)}, u32[]{:S(2)}, u32[]{:S(2)}) collective-permute-start(bf16[768,512]{1,0:T(8,128)(2,1)S(1)} %get-tuple-element.177), channel_id=1, source_target_pairs={{0,8},{4,12},{8,0},{12,4},{16,24},{20,28},{24,16},{28,20},{1,9},{5... | collective-permute-start | bytes 2359304 | tf_op jit(solution)/shard_map/ppermute | solution.py:26
  857.0 63.2 %collective-permute-start.62 = (bf16[1024,512]{1,0:T(8,128)(2,1)S(1)}, bf16[1024,512]{1,0:T(8,128)(2,1)S(1)}, u32[]{:S(2)}, u32[]{:S(2)}) collective-permute-start(bf16[1024,512]{1,0:T(8,128)(2,1)S(1)} %get-tuple-element.238), channel_id=1, source_target_pairs={{0,2},{1,3},{2,0},{3,1},{4,6},{5,7},{6,4},{7,5},{8,10},{9,11},{10,... | collective-permute-start | bytes 3145736 | tf_op jit(solution)/shard_map/ppermute | solution.py:26
  860.1 62.2 %collective-permute-start.56 = (bf16[1024,512]{1,0:T(8,128)(2,1)S(1)}, bf16[1024,512]{1,0:T(8,128)(2,1)S(1)}, u32[]{:S(2)}, u32[]{:S(2)}) collective-permute-start(bf16[1024,512]{1,0:T(8,128)(2,1)S(1)} %add_convert_fusion.1), channel_id=1, source_target_pairs={{0,2},{1,3},{2,0},{3,1},{4,6},{5,7},{6,4},{7,5},{8,10},{9,11},{10,... | collective-permute-start | bytes 3145736 | tf_op jit(solution)/shard_map/ppermute | solution.py:26
  861.4 44.3 %collective-permute-start.64 = (f32[6,2048]{1,0:T(8,128)S(1)}, f32[6,2048]{1,0:T(8,128)S(1)}, u32[]{:S(2)}, u32[]{:S(2)}) collective-permute-start(f32[6,2048]{1,0:T(8,128)S(1)} %add_dynamic-update-slice_fusion), channel_id=1, source_target_pairs={{0,2},{1,3},{2,0},{3,1},{4,6},{5,7},{6,4},{7,5},{8,10},{9,11},{10,... | collective-permute-start | bytes 147464 | tf_op jit(solution)/shard_map/ppermute | solution.py:26
  (126 other events, 1868.0 us)
Sparse Core Ops, SparseCore 0:
  10.8 163.5 all-gather.3
  184.7 81.9 all-gather.5
  272.9 97.7 all-gather.7
  581.1 116.8 reduce-scatter.2
  702.0 207.5 reduce-scatter.4

commit v13 on v12

--- a/solution.py
+++ b/solution.py
@@ -864,18 +864,23 @@
     mine = lax.dynamic_update_slice_in_dim(
         jnp.zeros((mine.shape[0], width), full), mine, place * size, 1
     )
-    mine = all_sum(mine)
     expert_grad = expert_grad_sum(
         group_finish(kept[0], [jnp.concatenate(pair_sums, 0), pair_last], member, group_count),
         group_finish(kept[1], [jnp.concatenate(down_sums, 0)], member, group_count),
         hidden_size,
     )
-    input_grad = tensor_gather(input_own.astype(low), lambda sent: (mine, outputs[3], outputs[1]))
+    small_sums = []
+
+    def sum_small(sent):
+        small_sums.append(all_sum(after(mine, sent)))
+        return (small_sums[0], outputs[3], outputs[1])
+
+    input_grad = tensor_gather(input_own.astype(low), sum_small)
     input_grad = input_grad.astype(full)
     layer_own = hidden + unpacked([outputs[s] for s in range(EXPERTS)])
     layer_out = tensor_gather(layer_own.astype(low)).astype(full)
     share = width // dp_count
-    mine = lax.dynamic_slice_in_dim(mine, index * share, share, 1)
+    mine = lax.dynamic_slice_in_dim(small_sums[0], index * share, share, 1)
     shards = shards.astype(full)
     qkv_shard, out_shard = shards[:, : 3 * size], shards[:, 3 * size :]
     return (

time: 983 us -> 974 us (level)
  transfers between devices with their start and end apart: 76 -> 76, of which waited for: 24 -> 24; matrix products, arithmetic and copies ran while one was open for 27% -> 27% of each run, Pallas kernels for 24% -> 25%
where the time goes in v13:
time: 974 us; the launch traced here: 965 us
  waiting for transfers between devices  359 us (37%)
  Pallas kernels  238 us (24%)
  matrix products  156 us (16%)
  other arithmetic  83.4 us (9%)
  starting transfers between devices  59.1 us (6%)
  local copies, waits for them, and re-layouts  53.5 us (5%)
  between operations  15.7 us (2%)
    ppermute x71, waiting for transfers between devices, swap(): lax.ppermute(value, axis, [(i, i ^ distance) for i in range(lax.axis_size...  231 us
    all_gather x1, waiting for transfers between devices, body(): lax.all_gather(jnp.concatenate([qkv_weight.reshape(-1, 3 * size), out_wei...  127 us
    dot_general x25, matrix products, contract(): lax.dot_general(left, right, (((left_dim,), (right_dim,)), ((), ())), pre...  122 us
    pallas_call x4, Pallas kernels, expert_pass(): pl.pallas_call(functools.partial(expert_kernel, count, len(carried)), gri...  120 us
    ppermute x71, starting transfers between devices, swap(): lax.ppermute(value, axis, [(i, i ^ distance) for i in range(lax.axis_size...  58.5 us
    pallas_call x2, Pallas kernels, down_pass(): pl.pallas_call(functools.partial(down_kernel, len(carried)), grid_spec=pl...  32.5 us
    pallas_call x1, Pallas kernels, up_pass(): pl.pallas_call(up_kernel, grid_spec=pltpu.PrefetchScalarGridSpec(num_scal...  27 us
  transfers between devices with their start and end apart: 76, of which 24 were waited for; matrix products, arithmetic and copies ran while one was open for 27% of the time, Pallas kernels for 25%

profile of v13, /device:TPU:0, one launch (start us, length us, event | category | flops | bytes accessed | tf_op | source)
XLA Modules:
  0.0 964.8 jit_solution(89439885306994967)
XLA Ops:
  21.8 5.9 slice_bitcast_fusion
  40.3 6.9 convolution_convert_fusion.3.rows
  47.2 127.2 %all-gather.4.cloned.1.call-done.right = bf16[2048,2176]{1,0:T(8,128)(2,1)} async-done(((bf16[256,2176]{1,0:T(8,128)(2,1)}), bf16[2048,2176]{1,0:T(8,128)(2,1)}) %all-gather.4.cloned.1.call-update) | async-done | bytes 8912912 | tf_op jit(solution)/shard_map/all_gather | solution.py:595
  185.1 11.7 %fusion.3.q_in.k_in.v_in = f32[1024,1536]{1,0:T(8,128)} fusion(bf16[1024,2048]{1,0:T(8,128)(2,1)} %fusion.2, bf16[2048,2176]{1,0:T(8,128)(2,1)} %all-gather.4.cloned.1.call-done.right), kind=kOutput, calls=%fused_computation.9 | convolution fusion | flops 6442450944 | bytes 16777216 | tf_op jit(solution)/shard_map/dot_general | solution.py:673
  201.0 12.9 %attention.1 = (bf16[1024,512]{1,0:T(8,128)(2,1)S(1)}, bf16[1024,512]{1,0:T(8,128)(2,1)S(1)}, bf16[1024,512]{1,0:T(8,128)(2,1)S(1)}, bf16[1024,512]{1,0:T(8,128)(2,1)S(1)}, f32[4,1024,1]{2,1,0:T(8,128)}) custom-call(f32[1024,1536]{1,0:T(8,128)} %fusion.3.q_in.k_in.v_in, f32[1024,1536]{1,0:T(8,128)} %fusion.3.q_in.k_in.v_in, ...), custom_call_target="tpu_custom_call" | custom-call | flops 1342177280 | bytes 10485760 | tf_op jit(solution)/shard_map/attention/pallas_call | solution.py:135
  217.7 5.5 spread.2
  237.0 11.0 %down.2 = (bf16[3072,2048]{1,0:T(8,128)(2,1)}, bf16[3072,1408]{1,0:T(8,128)(2,1)}) custom-call(s32[3]{0:T(128)S(1)} %pad_add_fusion.where, bf16[768,2048]{1,0:T(8,128)(2,1)} %convolution_convert_fusion.3.rows, bf16[1024,1408]{1,0:T(8,128)(2,1)S(1)} %get-tuple-element.236.own, bf16[1024,1408]{1,0:T(8,128)(2,1)} %collective-permute-done.came), custom_call_target="tpu_custom_call" | custom-call | flops 4429185024 | bytes 14221312 | tf_op jit(solution)/shard_map/down/pallas_call | solution.py:272
  247.9 12.1 %collective-permute-done.11 = bf16[1024,512]{1,0:T(8,128)(2,1)} collective-permute-done((bf16[1024,512]{1,0:T(8,128)(2,1)}, bf16[1024,512]{1,0:T(8,128)(2,1)}, u32[]{:S(2)}, u32[]{:S(2)}) %collective-permute-start.11) | collective-permute-done | bytes 1048608 | tf_op jit(solution)/shard_map/ppermute | solution.py:26
  289.5 33.7 %collective-permute-done.18.refs_2_ = bf16[768,512]{1,0:T(8,128)(2,1)S(1)} collective-permute-done((bf16[768,512]{1,0:T(8,128)(2,1)S(1)}, bf16[768,512]{1,0:T(8,128)(2,1)S(1)}, u32[]{:S(2)}, u32[]{:S(2)}) %collective-permute-start.18) | collective-permute-done | bytes 786464 | tf_op jit(solution)/shard_map/ppermute | solution.py:26
  329.9 20.0 %collective-permute-done.20.refs_10_ = bf16[1184,1408]{1,0:T(8,128)(2,1)S(1)} collective-permute-done((bf16[1184,1408]{1,0:T(8,128)(2,1)S(1)}, bf16[1184,1408]{1,0:T(8,128)(2,1)S(1)}, u32[]{:S(2)}, u32[]{:S(2)}) %collective-permute-start.20) | collective-permute-done | bytes 3334176 | tf_op jit(solution)/shard_map/ppermute | solution.py:26
  351.7 30.0 %expert.4 = (bf16[3072,2048]{1,0:T(8,128)(2,1)}, bf16[3072,1408]{1,0:T(8,128)(2,1)}, bf16[3072,2816]{1,0:T(8,128)(2,1)}, bf16[768,1024]{1,0:T(8,128)(2,1)}, bf16[768,1024]{1,0:T(8,128)(2,1)}, /*index=5*/f32[1,768]{1,0:T(1,128)}) custom-call(s32[3]{0:T(128)} %copy-done.10, bf16[768,512]{1,0:T(8,128)(2,1)} %copy-done.60, bf16[768,512]{1,0:T(8,128)(2,1)} %copy-done.62, ...), custom_call_target="tpu_custom_call" | custom-call | flops 17716740096 | bytes 32768000 | tf_op jit(solution)/shard_map/expert/pallas_call | solution.py:411
  383.4 21.5 %down.3 = (bf16[3072,2048]{1,0:T(8,128)(2,1)}, bf16[3072,1408]{1,0:T(8,128)(2,1)}) custom-call(s32[3]{0:T(128)S(1)} %copy-done.11, bf16[2304,2048]{1,0:T(8,128)(2,1)} %all-gather.8.cloned.1.call-done.rows, bf16[1024,1408]{1,0:T(8,128)(2,1)S(1)} %get-tuple-element.236.own, ...), custom_call_target="tpu_custom_call", output_to_operand_aliasing={{0}: (4, {}), {1}: (5, {})} | custom-call | flops 13287555072 | bytes 31129600 | tf_op jit(solution)/shard_map/down/pallas_call | solution.py:272
  405.0 30.2 %expert.5 = (bf16[3072,2048]{1,0:T(8,128)(2,1)}, bf16[3072,1408]{1,0:T(8,128)(2,1)}, bf16[3072,2816]{1,0:T(8,128)(2,1)}, bf16[768,1024]{1,0:T(8,128)(2,1)}, bf16[768,1024]{1,0:T(8,128)(2,1)}, /*index=5*/f32[1,768]{1,0:T(1,128)}) custom-call(s32[3]{0:T(128)} %copy-done.10, ...), custom_call_target="tpu_custom_call", output_to_operand_aliasing={{0}: (15, {}), {1}: (16, {}), {2}: (17, {})} | custom-call | flops 17716740096 | bytes 32768000 | tf_op jit(solution)/shard_map/expert/pallas_call | solution.py:411
  443.9 29.9 %expert.6 = (bf16[3072,2048]{1,0:T(8,128)(2,1)}, bf16[3072,1408]{1,0:T(8,128)(2,1)}, bf16[3072,2816]{1,0:T(8,128)(2,1)}, bf16[768,1024]{1,0:T(8,128)(2,1)}, bf16[768,1024]{1,0:T(8,128)(2,1)}, /*index=5*/f32[1,768]{1,0:T(1,128)}) custom-call(s32[3]{0:T(128)} %copy-done.10, ...), custom_call_target="tpu_custom_call", output_to_operand_aliasing={{0}: (15, {}), {1}: (16, {}), {2}: (17, {})} | custom-call | flops 17716740096 | bytes 32768000 | tf_op jit(solution)/shard_map/expert/pallas_call | solution.py:411
  485.4 29.8 %expert.7 = (bf16[3072,2048]{1,0:T(8,128)(2,1)}, bf16[3072,1408]{1,0:T(8,128)(2,1)}, bf16[3072,2816]{1,0:T(8,128)(2,1)}, bf16[768,1024]{1,0:T(8,128)(2,1)}, bf16[768,1024]{1,0:T(8,128)(2,1)}, /*index=5*/f32[1,768]{1,0:T(1,128)}) custom-call(s32[3]{0:T(128)} %copy-done.10, ...), custom_call_target="tpu_custom_call", output_to_operand_aliasing={{0}: (15, {}), {1}: (16, {}), {2}: (17, {})} | custom-call | flops 17716740096 | bytes 32768000 | tf_op jit(solution)/shard_map/expert/pallas_call | solution.py:411
  524.6 14.1 %fusion.14 = bf16[1024,1408]{1,0:T(8,128)(2,1)S(1)} fusion(bf16[3072,1408]{1,0:T(8,128)(2,1)} %get-tuple-element.184.act, bf16[3072,2048]{1,0:T(8,128)(2,1)} %get-tuple-element.144, s32[]{:T(128)S(6)} %select_n.169), kind=kOutput, calls=%fused_computation.23 | convolution fusion | flops 8859811840 | bytes 17825796 | tf_op jit(solution)/shard_map/dot_general | solution.py:30
  551.8 27.0 %up.1 = bf16[3072,2048]{1,0:T(8,128)(2,1)} custom-call(s32[3]{0:T(128)S(1)} %copy-done.12, bf16[3072,1408]{1,0:T(8,128)(2,1)} %get-tuple-element.184.act, bf16[1024,1408]{1,0:T(8,128)(2,1)S(1)} %get-tuple-element.236.own, bf16[1024,1408]{1,0:T(8,128)(2,1)} %collective-permute-done.came), custom_call_target="tpu_custom_call" | custom-call | flops 17716740096 | bytes 27000832 | tf_op jit(solution)/shard_map/up/pallas_call | solution.py:339
  607.5 17.3 %convolution_convert_fusion.2 = bf16[512,2816]{1,0:T(8,128)(2,1)} fusion(bf16[3072,2816]{1,0:T(8,128)(2,1)} %get-tuple-element.183, bf16[3072,2048]{1,0:T(8,128)(2,1)} %get-tuple-element.168, s32[]{:T(128)S(6)} %select_n.169), kind=kOutput, calls=%fused_computation.19 | convolution fusion | flops 8859811840 | bytes 23330820 | tf_op jit(solution)/shard_map/dot_general | solution.py:30
  624.8 12.0 %convolution_convert_fusion.1 = bf16[512,2816]{1,0:T(8,128)(2,1)} fusion(bf16[3072,2816]{1,0:T(8,128)(2,1)S(1)} %bitcast.149, bf16[3072,2048]{1,0:T(8,128)(2,1)} %get-tuple-element.168, s32[]{:T(128)S(6)} %select_n.173), kind=kOutput, calls=%fused_computation.18 | convolution fusion | flops 8859811840 | bytes 23330820 | tf_op jit(solution)/shard_map/dot_general | solution.py:30
  636.8 12.3 %collective-permute-done.48 = bf16[1024,512]{1,0:T(8,128)(2,1)S(1)} collective-permute-done((bf16[1024,512]{1,0:T(8,128)(2,1)S(1)}, bf16[1024,512]{1,0:T(8,128)(2,1)S(1)}, u32[]{:S(2)}, u32[]{:S(2)}) %collective-permute-start.48) | collective-permute-done | bytes 1048608 | tf_op jit(solution)/shard_map/ppermute | solution.py:26
  665.1 15.8 %attention_back.1.left = bf16[1024,1536]{1,0:T(8,128)(2,1)} custom-call(bf16[1024,512]{1,0:T(8,128)(2,1)S(1)} %copy-done.14, bf16[1024,512]{1,0:T(8,128)(2,1)S(1)} %copy-done.16, bf16[1024,512]{1,0:T(8,128)(2,1)S(1)} %copy-done.18, f32[4,1024,1]{2,1,0:T(8,128)} %get-tuple-element.163.logs, bf16[1024,512]{1,0:T(8,128)(2,1)S(1)} %fusion.87.grad, ...), custom_call_target="tpu_custom_call" | custom-call | flops 3355443200 | bytes 8388608 | tf_op jit(solution)/shard_map/attention_back/pallas_call | solution.py:188
  680.8 10.5 %convolution_convert_fusion = bf16[2048,1536]{0,1:T(8,128)(2,1)} fusion(bf16[1024,2048]{1,0:T(8,128)(2,1)S(1)} %copy-done.32, bf16[1024,1536]{1,0:T(8,128)(2,1)} %attention_back.1.left), kind=kOutput, calls=%fused_computation.8 | convolution fusion | flops 6445596672 | bytes 13631488 | tf_op jit(solution)/shard_map/dot_general | solution.py:30
  691.4 7.8 pad_maximum_fusion
  699.2 12.2 %spread.3 = (bf16[1024,1024]{1,0:T(8,128)(2,1)S(1)}, bf16[1024,1024]{1,0:T(8,128)(2,1)}) custom-call(s32[3]{0:T(128)S(1)} %copy-done.12, bf16[1024,1536]{1,0:T(8,128)(2,1)} %attention_back.1.left, bf16[2048,2176]{1,0:T(8,128)(2,1)} %all-gather.4.cloned.1.call-done.right), custom_call_target="tpu_custom_call" | custom-call | flops 6442450944 | bytes 13631488 | tf_op jit(solution)/shard_map/spread/pallas_call | solution.py:310
  726.8 26.4 %fusion.11.refs_0_ = bf16[1024,2816]{1,0:T(8,128)(2,1)} fusion(bf16[3072,2816]{1,0:T(8,128)(2,1)} %get-tuple-element.183, bf16[3072,2048]{1,0:T(8,128)(2,1)} %get-tuple-element.168, s32[]{:T(128)S(6)} %select_n.186), kind=kOutput, calls=%fused_computation.17 | convolution fusion | flops 17719623680 | bytes 29360132 | tf_op jit(solution)/shard_map/dot_general | solution.py:30
  753.2 48.6 %collective-permute-done.53 = bf16[768,512]{1,0:T(8,128)(2,1)S(1)} collective-permute-done((bf16[768,512]{1,0:T(8,128)(2,1)S(1)}, bf16[768,512]{1,0:T(8,128)(2,1)S(1)}, u32[]{:S(2)}, u32[]{:S(2)}) %collective-permute-start.53) | collective-permute-done | bytes 786464 | tf_op jit(solution)/shard_map/ppermute | solution.py:26
  801.8 13.5 %fusion.17.refs_3_ = bf16[1024,1408]{1,0:T(8,128)(2,1)} fusion(bf16[3072,1408]{1,0:T(8,128)(2,1)S(1)} %bitcast.151, bf16[3072,2048]{1,0:T(8,128)(2,1)} %get-tuple-element.144, s32[]{:T(128)S(6)} %select_n.186), kind=kOutput, calls=%fused_computation.24 | convolution fusion | flops 8859811840 | bytes 17825796 | tf_op jit(solution)/shard_map/dot_general | solution.py:30
  828.1 28.9 %collective-permute-done.54 = bf16[768,512]{1,0:T(8,128)(2,1)S(1)} collective-permute-done((bf16[768,512]{1,0:T(8,128)(2,1)S(1)}, bf16[768,512]{1,0:T(8,128)(2,1)S(1)}, u32[]{:S(2)}, u32[]{:S(2)}) %collective-permute-start.54) | collective-permute-done | bytes 786464 | tf_op jit(solution)/shard_map/ppermute | solution.py:26
  861.4 24.9 %collective-permute-done.64 = f32[6,2048]{1,0:T(8,128)S(1)} collective-permute-done((f32[6,2048]{1,0:T(8,128)S(1)}, f32[6,2048]{1,0:T(8,128)S(1)}, u32[]{:S(2)}, u32[]{:S(2)}) %collective-permute-start.64) | collective-permute-done | bytes 49184 | tf_op jit(solution)/shard_map/ppermute | solution.py:26
  891.0 9.5 collective-permute-done.66
  900.6 10.5 %collective-permute-done.67 = f32[6,2048]{1,0:T(8,128)S(1)} collective-permute-done((f32[6,2048]{1,0:T(8,128)S(1)}, f32[6,2048]{1,0:T(8,128)S(1)}, u32[]{:S(2)}, u32[]{:S(2)}) %collective-permute-start.67) | collective-permute-done | bytes 49184 | tf_op jit(solution)/shard_map/ppermute | solution.py:26
  933.0 12.0 %expert_grad_sum.1 = f32[3,1024,1408]{2,1,0:T(8,128)} custom-call(bf16[1024,2816]{1,0:T(8,128)(2,1)} %fusion.11.refs_0_, bf16[512,2816]{1,0:T(8,128)(2,1)S(1)} %copy-done, bf16[512,2816]{1,0:T(8,128)(2,1)} %collective-permute-done.70.refs_2_, bf16[1024,1408]{1,0:T(8,128)(2,1)S(1)} %copy-done.1, bf16[1024,1408]{1,0:T(8,128)(2,1)S(1)} %pad_maximum_fusion.4.refs_4_), custom_call_target="tpu_custom_call" | custom-call | flops 4325376 | bytes 34603008 | tf_op jit(solution)/shard_map/expert_grad_sum/pallas_call | solution.py:495
  (450 shorter events, 257.4 us)
Async XLA Ops:
  7.2 167.2 %all-gather.4.cloned.1.call-start = ((), (), s32[]{:S(2)}) async-start(), calls=%async_computation.2 | async-start | bytes 10027008 | tf_op jit(solution)/shard_map/all_gather | solution.py:595
  10.3 256.4 %all-gather.6.cloned.1.call-start = ((), (), s32[]{:S(2)}) async-start(), calls=%async_computation.3 | async-start | bytes 5242880 | tf_op jit(solution)/shard_map/all_gather | solution.py:661
  14.0 162.8 %collective-permute-start.4 = (f32[1,768]{1,0:T(1,128)S(1)}, f32[1,768]{1,0:T(1,128)S(1)}, u32[]{:S(2)}, u32[]{:S(2)}) collective-permute-start(f32[1,768]{1,0:T(1,128)S(1)} %fusion.36), channel_id=1, source_target_pairs={{0,8},{4,12},{8,0},{12,4},{16,24},{20,28},{24,16},{28,20},{1,9},{5... | collective-permute-start | bytes 9224 | tf_op jit(solution)/shard_map/ppermute | solution.py:26
  17.7 160.7 %collective-permute-start.5 = (f32[1,768]{1,0:T(1,128)S(1)}, f32[1,768]{1,0:T(1,128)S(1)}, u32[]{:S(2)}, u32[]{:S(2)}) collective-permute-start(f32[1,768]{1,0:T(1,128)S(1)} %fusion.31), channel_id=1, source_target_pairs={{0,16},{4,20},{8,24},{12,28},{16,0},{20,4},{24,8},{28,12},{1,17},{... | collective-permute-start | bytes 9224 | tf_op jit(solution)/shard_map/ppermute | solution.py:26
  20.9 163.3 %collective-permute-start.6 = (f32[1,768]{1,0:T(1,128)S(1)}, f32[1,768]{1,0:T(1,128)S(1)}, u32[]{:S(2)}, u32[]{:S(2)}) collective-permute-start(f32[1,768]{1,0:T(1,128)S(1)} %fusion.26), channel_id=1, source_target_pairs={{0,24},{4,28},{8,16},{12,20},{16,8},{20,12},{24,0},{28,4},{1,25},{... | collective-permute-start | bytes 9224 | tf_op jit(solution)/shard_map/ppermute | solution.py:26
  20.9 163.3 %collective-permute-start.1 = (f32[1,1024]{1,0:T(1,128)S(1)}, f32[1,1024]{1,0:T(1,128)S(1)}, u32[]{:S(2)}, u32[]{:S(2)}) collective-permute-start(f32[1,1024]{1,0:T(1,128)S(1)} %get-tuple-element.275), channel_id=1, source_target_pairs={{0,8},{4,12},{8,0},{12,4},{16,24},{20,28},{24,16},{28,20},{1,9},{5... | collective-permute-start | bytes 12296 | tf_op jit(solution)/shard_map/ppermute | solution.py:26
  27.7 156.5 %collective-permute-start = (bf16[1024,1408]{1,0:T(8,128)(2,1)S(1)}, bf16[1024,1408]{1,0:T(8,128)(2,1)}, u32[]{:S(2)}, u32[]{:S(2)}) collective-permute-start(bf16[1024,1408]{1,0:T(8,128)(2,1)S(1)} %get-tuple-element.236.own), channel_id=1, source_target_pairs={{0,4},{4,0},{8,12},{12,8},{16,20},{20,16},{24,28},{28,24},{1,5},{5... | collective-permute-start | bytes 8650760 | tf_op jit(solution)/shard_map/ppermute | solution.py:26
  184.6 198.8 %all-gather.8.cloned.1.call-start = ((), (), s32[]{:S(2)}) async-start(), calls=%async_computation.4 | async-start | bytes 11796480 | tf_op jit(solution)/shard_map/all_gather | solution.py:697
  272.8 451.5 %reduce-scatter.3.cloned.1.call-start = ((), (), s32[]{:S(2)}) async-start(), calls=%async_computation.5 | async-start | bytes 15728640 | tf_op jit(solution)/shard_map/reduce_scatter | solution.py:793
  276.0 74.0 %collective-permute-start.20 = (bf16[1184,1408]{1,0:T(8,128)(2,1)S(1)}, bf16[1184,1408]{1,0:T(8,128)(2,1)S(1)}, u32[]{:S(2)}, u32[]{:S(2)}) collective-permute-start(bf16[1184,1408]{1,0:T(8,128)(2,1)S(1)} %pad_maximum_fusion.2), channel_id=1, source_target_pairs={{0,4},{4,0},{8,12},{12,8},{16,20},{20,16},{24,28},{28,24},{1,5},{5... | collective-permute-start | bytes 10002440 | tf_op jit(solution)/shard_map/ppermute | solution.py:26
  286.6 36.6 %collective-permute-start.18 = (bf16[768,512]{1,0:T(8,128)(2,1)S(1)}, bf16[768,512]{1,0:T(8,128)(2,1)S(1)}, u32[]{:S(2)}, u32[]{:S(2)}) collective-permute-start(bf16[768,512]{1,0:T(8,128)(2,1)S(1)} %fusion.99.refs_0_), channel_id=1, source_target_pairs={{0,2},{1,3},{2,0},{3,1},{4,6},{5,7},{6,4},{7,5},{8,10},{9,11},{10,... | collective-permute-start | bytes 2359304 | tf_op jit(solution)/shard_map/ppermute | solution.py:26
  289.0 38.1 %collective-permute-start.15 = (bf16[768,512]{1,0:T(8,128)(2,1)S(1)}, bf16[768,512]{1,0:T(8,128)(2,1)}, u32[]{:S(2)}, u32[]{:S(2)}) collective-permute-start(bf16[768,512]{1,0:T(8,128)(2,1)S(1)} %fusion.101), channel_id=1, source_target_pairs={{0,16},{4,20},{8,24},{12,28},{16,0},{20,4},{24,8},{28,12},{1,17},{... | collective-permute-start | bytes 2359304 | tf_op jit(solution)/shard_map/ppermute | solution.py:26
  289.5 40.4 %collective-permute-start.17 = (bf16[768,512]{1,0:T(8,128)(2,1)S(1)}, bf16[768,512]{1,0:T(8,128)(2,1)S(1)}, u32[]{:S(2)}, u32[]{:S(2)}) collective-permute-start(bf16[768,512]{1,0:T(8,128)(2,1)S(1)} %fusion.99.refs_0_), channel_id=1, source_target_pairs={{0,1},{1,0},{2,3},{3,2},{4,5},{5,4},{6,7},{7,6},{8,9},{9,8},{10,11... | collective-permute-start | bytes 2359304 | tf_op jit(solution)/shard_map/ppermute | solution.py:26
  327.1 54.8 %collective-permute-start.16 = (bf16[768,512]{1,0:T(8,128)(2,1)}, bf16[768,512]{1,0:T(8,128)(2,1)}, u32[]{:S(2)}, u32[]{:S(2)}) collective-permute-start(bf16[768,512]{1,0:T(8,128)(2,1)} %fusion.102), channel_id=1, source_target_pairs={{0,24},{4,28},{8,16},{12,20},{16,8},{20,12},{24,0},{28,4},{1,25},{... | collective-permute-start | bytes 2359304 | tf_op jit(solution)/shard_map/ppermute | solution.py:26
  328.4 53.3 %collective-permute-start.27 = (bf16[768,512]{1,0:T(8,128)(2,1)}, bf16[768,512]{1,0:T(8,128)(2,1)}, u32[]{:S(2)}, u32[]{:S(2)}) collective-permute-start(bf16[768,512]{1,0:T(8,128)(2,1)} %collective-permute-done.15.refs_0_), channel_id=1, source_target_pairs={{0,2},{1,3},{2,0},{3,1},{4,6},{5,7},{6,4},{7,5},{8,10},{9,11},{10,... | collective-permute-start | bytes 2359304 | tf_op jit(solution)/shard_map/ppermute | solution.py:26
  329.9 75.0 %collective-permute-start.26 = (bf16[768,512]{1,0:T(8,128)(2,1)}, bf16[768,512]{1,0:T(8,128)(2,1)}, u32[]{:S(2)}, u32[]{:S(2)}) collective-permute-start(bf16[768,512]{1,0:T(8,128)(2,1)} %collective-permute-done.15.refs_0_), channel_id=1, source_target_pairs={{0,1},{1,0},{2,3},{3,2},{4,5},{5,4},{6,7},{7,6},{8,9},{9,8},{10,11... | collective-permute-start | bytes 2359304 | tf_op jit(solution)/shard_map/ppermute | solution.py:26
  381.8 53.3 %collective-permute-start.25 = (bf16[768,512]{1,0:T(8,128)(2,1)}, bf16[768,512]{1,0:T(8,128)(2,1)}, u32[]{:S(2)}, u32[]{:S(2)}) collective-permute-start(bf16[768,512]{1,0:T(8,128)(2,1)} %collective-permute-done.16.refs_0_), channel_id=1, source_target_pairs={{0,2},{1,3},{2,0},{3,1},{4,6},{5,7},{6,4},{7,5},{8,10},{9,11},{10,... | collective-permute-start | bytes 2359304 | tf_op jit(solution)/shard_map/ppermute | solution.py:26
  383.4 51.8 %collective-permute-start.21 = (bf16[768,512]{1,0:T(8,128)(2,1)}, bf16[768,512]{1,0:T(8,128)(2,1)}, u32[]{:S(2)}, u32[]{:S(2)}) collective-permute-start(bf16[768,512]{1,0:T(8,128)(2,1)} %fusion.100), channel_id=1, source_target_pairs={{0,8},{4,12},{8,0},{12,4},{16,24},{20,28},{24,16},{28,20},{1,9},{5... | collective-permute-start | bytes 2359304 | tf_op jit(solution)/shard_map/ppermute | solution.py:26
  435.9 38.0 %collective-permute-start.23 = (bf16[768,512]{1,0:T(8,128)(2,1)}, bf16[768,512]{1,0:T(8,128)(2,1)}, u32[]{:S(2)}, u32[]{:S(2)}) collective-permute-start(bf16[768,512]{1,0:T(8,128)(2,1)} %collective-permute-done.21.refs_0_), channel_id=1, source_target_pairs={{0,2},{1,3},{2,0},{3,1},{4,6},{5,7},{6,4},{7,5},{8,10},{9,11},{10,... | collective-permute-start | bytes 2359304 | tf_op jit(solution)/shard_map/ppermute | solution.py:26
  477.4 40.7 %collective-permute-start.35 = (bf16[768,512]{1,0:T(8,128)(2,1)}, bf16[768,512]{1,0:T(8,128)(2,1)}, u32[]{:S(2)}, u32[]{:S(2)}) collective-permute-start(bf16[768,512]{1,0:T(8,128)(2,1)} %add_convert_fusion.9), channel_id=1, source_target_pairs={{0,16},{4,20},{8,24},{12,28},{16,0},{20,4},{24,8},{28,12},{1,17},{... | collective-permute-start | bytes 2359304 | tf_op jit(solution)/shard_map/ppermute | solution.py:26
  543.4 37.3 %collective-permute-start.42 = (bf16[768,512]{1,0:T(8,128)(2,1)}, bf16[768,512]{1,0:T(8,128)(2,1)}, u32[]{:S(2)}, u32[]{:S(2)}) collective-permute-start(bf16[768,512]{1,0:T(8,128)(2,1)} %add_convert_fusion.7), channel_id=1, source_target_pairs={{0,24},{4,28},{8,16},{12,20},{16,8},{20,12},{24,0},{28,4},{1,25},{... | collective-permute-start | bytes 2359304 | tf_op jit(solution)/shard_map/ppermute | solution.py:26
  581.0 341.0 %reduce-scatter.5.cloned.1.call-start = ((), (), s32[]{:S(2)}) async-start(), calls=%async_computation.6 | async-start | bytes 9437184 | tf_op jit(solution)/shard_map/reduce_scatter | solution.py:840
  604.8 44.4 %collective-permute-start.48 = (bf16[1024,512]{1,0:T(8,128)(2,1)S(1)}, bf16[1024,512]{1,0:T(8,128)(2,1)S(1)}, u32[]{:S(2)}, u32[]{:S(2)}) collective-permute-start(bf16[1024,512]{1,0:T(8,128)(2,1)S(1)} %get-tuple-element.298), channel_id=1, source_target_pairs={{0,2},{1,3},{2,0},{3,1},{4,6},{5,7},{6,4},{7,5},{8,10},{9,11},{10,... | collective-permute-start | bytes 3145736 | tf_op jit(solution)/shard_map/ppermute | solution.py:26
  606.1 43.0 %collective-permute-start.49 = (bf16[448,1408]{1,0:T(8,128)(2,1)S(1)}, bf16[448,1408]{1,0:T(8,128)(2,1)S(1)}, u32[]{:S(2)}, u32[]{:S(2)}) collective-permute-start(bf16[448,1408]{1,0:T(8,128)(2,1)S(1)} %copy-done.43), channel_id=1, source_target_pairs={{0,4},{4,0},{8,12},{12,8},{16,20},{20,16},{24,28},{28,24},{1,5},{5... | collective-permute-start | bytes 3784712 | tf_op jit(solution)/shard_map/ppermute | solution.py:26
  717.3 212.0 %collective-permute-start.70 = (bf16[512,2816]{1,0:T(8,128)(2,1)}, bf16[512,2816]{1,0:T(8,128)(2,1)}, u32[]{:S(2)}, u32[]{:S(2)}) collective-permute-start(bf16[512,2816]{1,0:T(8,128)(2,1)} %convolution_convert_fusion.1), channel_id=1, source_target_pairs={{0,4},{4,0},{8,12},{12,8},{16,20},{20,16},{24,28},{28,24},{1,5},{5... | collective-permute-start | bytes 8650760 | tf_op jit(solution)/shard_map/ppermute | solution.py:26
  718.2 200.2 %collective-permute-start.69 = (bf16[416,2816]{1,0:T(8,128)(2,1)}, bf16[416,2816]{1,0:T(8,128)(2,1)}, u32[]{:S(2)}, u32[]{:S(2)}) collective-permute-start(bf16[416,2816]{1,0:T(8,128)(2,1)} %slice.349), channel_id=1, source_target_pairs={{0,4},{4,0},{8,12},{12,8},{16,20},{20,16},{24,28},{28,24},{1,5},{5... | collective-permute-start | bytes 7028744 | tf_op jit(solution)/shard_map/ppermute | solution.py:26
  721.9 93.3 %collective-permute-start.59 = (bf16[1024,512]{1,0:T(8,128)(2,1)}, bf16[1024,512]{1,0:T(8,128)(2,1)}, u32[]{:S(2)}, u32[]{:S(2)}) collective-permute-start(bf16[1024,512]{1,0:T(8,128)(2,1)} %add_convert_fusion), channel_id=1, source_target_pairs={{0,2},{1,3},{2,0},{3,1},{4,6},{5,7},{6,4},{7,5},{8,10},{9,11},{10,... | collective-permute-start | bytes 3145736 | tf_op jit(solution)/shard_map/ppermute | solution.py:26
  726.1 75.6 %collective-permute-start.53 = (bf16[768,512]{1,0:T(8,128)(2,1)S(1)}, bf16[768,512]{1,0:T(8,128)(2,1)S(1)}, u32[]{:S(2)}, u32[]{:S(2)}) collective-permute-start(bf16[768,512]{1,0:T(8,128)(2,1)S(1)} %get-tuple-element.177), channel_id=1, source_target_pairs={{0,16},{4,20},{8,24},{12,28},{16,0},{20,4},{24,8},{28,12},{1,17},{... | collective-permute-start | bytes 2359304 | tf_op jit(solution)/shard_map/ppermute | solution.py:26
  820.0 38.0 %collective-permute-start.55 = (bf16[768,512]{1,0:T(8,128)(2,1)S(1)}, bf16[768,512]{1,0:T(8,128)(2,1)S(1)}, u32[]{:S(2)}, u32[]{:S(2)}) collective-permute-start(bf16[768,512]{1,0:T(8,128)(2,1)S(1)} %get-tuple-element.179), channel_id=1, source_target_pairs={{0,24},{4,28},{8,16},{12,20},{16,8},{20,12},{24,0},{28,4},{1,25},{... | collective-permute-start | bytes 2359304 | tf_op jit(solution)/shard_map/ppermute | solution.py:26
  820.3 36.7 %collective-permute-start.54 = (bf16[768,512]{1,0:T(8,128)(2,1)S(1)}, bf16[768,512]{1,0:T(8,128)(2,1)S(1)}, u32[]{:S(2)}, u32[]{:S(2)}) collective-permute-start(bf16[768,512]{1,0:T(8,128)(2,1)S(1)} %get-tuple-element.178), channel_id=1, source_target_pairs={{0,8},{4,12},{8,0},{12,4},{16,24},{20,28},{24,16},{28,20},{1,9},{5... | collective-permute-start | bytes 2359304 | tf_op jit(solution)/shard_map/ppermute | solution.py:26
  827.2 83.9 %collective-permute-start.62 = (bf16[1024,512]{1,0:T(8,128)(2,1)S(1)}, bf16[1024,512]{1,0:T(8,128)(2,1)S(1)}, u32[]{:S(2)}, u32[]{:S(2)}) collective-permute-start(bf16[1024,512]{1,0:T(8,128)(2,1)S(1)} %get-tuple-element.240), channel_id=1, source_target_pairs={{0,2},{1,3},{2,0},{3,1},{4,6},{5,7},{6,4},{7,5},{8,10},{9,11},{10,... | collective-permute-start | bytes 3145736 | tf_op jit(solution)/shard_map/ppermute | solution.py:26
  859.3 54.0 %collective-permute-start.56 = (bf16[1024,512]{1,0:T(8,128)(2,1)S(1)}, bf16[1024,512]{1,0:T(8,128)(2,1)S(1)}, u32[]{:S(2)}, u32[]{:S(2)}) collective-permute-start(bf16[1024,512]{1,0:T(8,128)(2,1)S(1)} %add_convert_fusion.1), channel_id=1, source_target_pairs={{0,2},{1,3},{2,0},{3,1},{4,6},{5,7},{6,4},{7,5},{8,10},{9,11},{10,... | collective-permute-start | bytes 3145736 | tf_op jit(solution)/shard_map/ppermute | solution.py:26
  (126 other events, 1836.8 us)
Sparse Core Ops, SparseCore 0:
  10.8 163.5 all-gather.3
  184.7 81.9 all-gather.5
  272.9 97.7 all-gather.7
  581.1 116.8 reduce-scatter.2
  702.0 210.3 reduce-scatter.4

commit v14 on v13

--- a/solution.py
+++ b/solution.py
@@ -881,7 +881,7 @@
     layer_out = tensor_gather(layer_own.astype(low)).astype(full)
     share = width // dp_count
     mine = lax.dynamic_slice_in_dim(small_sums[0], index * share, share, 1)
-    shards = shards.astype(full)
+    shards = after(shards, expert_grad).astype(full)
     qkv_shard, out_shard = shards[:, : 3 * size], shards[:, 3 * size :]
     return (
         layer_out,

time: 974 us -> 968 us (level)
  no operation moved by 1% of the time
where the time goes in v14:
time: 968 us; the launch traced here: 959 us
  waiting for transfers between devices  359 us (37%)
  Pallas kernels  238 us (25%)
  matrix products  156 us (16%)
  other arithmetic  82.8 us (9%)
  starting transfers between devices  59.2 us (6%)
  local copies, waits for them, and re-layouts  48.4 us (5%)
  between operations  15.7 us (2%)
    ppermute x71, waiting for transfers between devices, swap(): lax.ppermute(value, axis, [(i, i ^ distance) for i in range(lax.axis_size...  231 us
    all_gather x1, waiting for transfers between devices, body(): lax.all_gather(jnp.concatenate([qkv_weight.reshape(-1, 3 * size), out_wei...  127 us
    dot_general x25, matrix products, contract(): lax.dot_general(left, right, (((left_dim,), (right_dim,)), ((), ())), pre...  122 us
    pallas_call x4, Pallas kernels, expert_pass(): pl.pallas_call(functools.partial(expert_kernel, count, len(carried)), gri...  120 us
    ppermute x71, starting transfers between devices, swap(): lax.ppermute(value, axis, [(i, i ^ distance) for i in range(lax.axis_size...  58.5 us
    pallas_call x2, Pallas kernels, down_pass(): pl.pallas_call(functools.partial(down_kernel, len(carried)), grid_spec=pl...  32.5 us
    pallas_call x1, Pallas kernels, up_pass(): pl.pallas_call(up_kernel, grid_spec=pltpu.PrefetchScalarGridSpec(num_scal...  27 us
  transfers between devices with their start and end apart: 76, of which 24 were waited for; matrix products, arithmetic and copies ran while one was open for 27% of the time, Pallas kernels for 25%

profile of v14, /device:TPU:0, one launch (start us, length us, event | category | flops | bytes accessed | tf_op | source)
XLA Modules:
  0.0 958.9 jit_solution(7517096989668062162)
XLA Ops:
  21.8 5.9 slice_bitcast_fusion
  40.4 6.9 convolution_convert_fusion.3.rows
  47.3 127.2 %all-gather.4.cloned.1.call-done.right = bf16[2048,2176]{1,0:T(8,128)(2,1)} async-done(((bf16[256,2176]{1,0:T(8,128)(2,1)}), bf16[2048,2176]{1,0:T(8,128)(2,1)}) %all-gather.4.cloned.1.call-update) | async-done | bytes 8912912 | tf_op jit(solution)/shard_map/all_gather | solution.py:595
  185.1 11.7 %fusion.3.q_in.k_in.v_in = f32[1024,1536]{1,0:T(8,128)} fusion(bf16[1024,2048]{1,0:T(8,128)(2,1)} %fusion.2, bf16[2048,2176]{1,0:T(8,128)(2,1)} %all-gather.4.cloned.1.call-done.right), kind=kOutput, calls=%fused_computation.9 | convolution fusion | flops 6442450944 | bytes 16777216 | tf_op jit(solution)/shard_map/dot_general | solution.py:673
  201.0 12.9 %attention.1 = (bf16[1024,512]{1,0:T(8,128)(2,1)S(1)}, bf16[1024,512]{1,0:T(8,128)(2,1)S(1)}, bf16[1024,512]{1,0:T(8,128)(2,1)S(1)}, bf16[1024,512]{1,0:T(8,128)(2,1)S(1)}, f32[4,1024,1]{2,1,0:T(8,128)}) custom-call(f32[1024,1536]{1,0:T(8,128)} %fusion.3.q_in.k_in.v_in, f32[1024,1536]{1,0:T(8,128)} %fusion.3.q_in.k_in.v_in, ...), custom_call_target="tpu_custom_call" | custom-call | flops 1342177280 | bytes 10485760 | tf_op jit(solution)/shard_map/attention/pallas_call | solution.py:135
  217.7 5.5 spread.2
  237.0 11.0 %down.2 = (bf16[3072,2048]{1,0:T(8,128)(2,1)}, bf16[3072,1408]{1,0:T(8,128)(2,1)}) custom-call(s32[3]{0:T(128)S(1)} %pad_add_fusion.where, bf16[768,2048]{1,0:T(8,128)(2,1)} %convolution_convert_fusion.3.rows, bf16[1024,1408]{1,0:T(8,128)(2,1)S(1)} %get-tuple-element.238.own, bf16[1024,1408]{1,0:T(8,128)(2,1)} %collective-permute-done.came), custom_call_target="tpu_custom_call" | custom-call | flops 4429185024 | bytes 14221312 | tf_op jit(solution)/shard_map/down/pallas_call | solution.py:272
  247.9 12.1 %collective-permute-done.11 = bf16[1024,512]{1,0:T(8,128)(2,1)} collective-permute-done((bf16[1024,512]{1,0:T(8,128)(2,1)}, bf16[1024,512]{1,0:T(8,128)(2,1)}, u32[]{:S(2)}, u32[]{:S(2)}) %collective-permute-start.11) | collective-permute-done | bytes 1048608 | tf_op jit(solution)/shard_map/ppermute | solution.py:26
  289.5 33.7 %collective-permute-done.18.refs_2_ = bf16[768,512]{1,0:T(8,128)(2,1)S(1)} collective-permute-done((bf16[768,512]{1,0:T(8,128)(2,1)S(1)}, bf16[768,512]{1,0:T(8,128)(2,1)S(1)}, u32[]{:S(2)}, u32[]{:S(2)}) %collective-permute-start.18) | collective-permute-done | bytes 786464 | tf_op jit(solution)/shard_map/ppermute | solution.py:26
  330.0 20.0 %collective-permute-done.20.refs_10_ = bf16[1184,1408]{1,0:T(8,128)(2,1)S(1)} collective-permute-done((bf16[1184,1408]{1,0:T(8,128)(2,1)S(1)}, bf16[1184,1408]{1,0:T(8,128)(2,1)S(1)}, u32[]{:S(2)}, u32[]{:S(2)}) %collective-permute-start.20) | collective-permute-done | bytes 3334176 | tf_op jit(solution)/shard_map/ppermute | solution.py:26
  351.7 30.1 %expert.4 = (bf16[3072,2048]{1,0:T(8,128)(2,1)}, bf16[3072,1408]{1,0:T(8,128)(2,1)}, bf16[3072,2816]{1,0:T(8,128)(2,1)}, bf16[768,1024]{1,0:T(8,128)(2,1)}, bf16[768,1024]{1,0:T(8,128)(2,1)}, /*index=5*/f32[1,768]{1,0:T(1,128)}) custom-call(s32[3]{0:T(128)} %copy-done.9, bf16[768,512]{1,0:T(8,128)(2,1)} %copy-done.54, bf16[768,512]{1,0:T(8,128)(2,1)} %copy-done.56, ...), custom_call_target="tpu_custom_call" | custom-call | flops 17716740096 | bytes 32768000 | tf_op jit(solution)/shard_map/expert/pallas_call | solution.py:411
  383.4 21.5 %down.3 = (bf16[3072,2048]{1,0:T(8,128)(2,1)}, bf16[3072,1408]{1,0:T(8,128)(2,1)}) custom-call(s32[3]{0:T(128)S(1)} %copy-done.10, bf16[2304,2048]{1,0:T(8,128)(2,1)} %all-gather.8.cloned.1.call-done.rows, bf16[1024,1408]{1,0:T(8,128)(2,1)S(1)} %get-tuple-element.238.own, ...), custom_call_target="tpu_custom_call", output_to_operand_aliasing={{0}: (4, {}), {1}: (5, {})} | custom-call | flops 13287555072 | bytes 31129600 | tf_op jit(solution)/shard_map/down/pallas_call | solution.py:272
  405.0 30.2 %expert.5 = (bf16[3072,2048]{1,0:T(8,128)(2,1)}, bf16[3072,1408]{1,0:T(8,128)(2,1)}, bf16[3072,2816]{1,0:T(8,128)(2,1)}, bf16[768,1024]{1,0:T(8,128)(2,1)}, bf16[768,1024]{1,0:T(8,128)(2,1)}, /*index=5*/f32[1,768]{1,0:T(1,128)}) custom-call(s32[3]{0:T(128)} %copy-done.9, ...), custom_call_target="tpu_custom_call", output_to_operand_aliasing={{0}: (15, {}), {1}: (16, {}), {2}: (17, {})} | custom-call | flops 17716740096 | bytes 32768000 | tf_op jit(solution)/shard_map/expert/pallas_call | solution.py:411
  443.9 29.9 %expert.6 = (bf16[3072,2048]{1,0:T(8,128)(2,1)}, bf16[3072,1408]{1,0:T(8,128)(2,1)}, bf16[3072,2816]{1,0:T(8,128)(2,1)}, bf16[768,1024]{1,0:T(8,128)(2,1)}, bf16[768,1024]{1,0:T(8,128)(2,1)}, /*index=5*/f32[1,768]{1,0:T(1,128)}) custom-call(s32[3]{0:T(128)} %copy-done.9, ...), custom_call_target="tpu_custom_call", output_to_operand_aliasing={{0}: (15, {}), {1}: (16, {}), {2}: (17, {})} | custom-call | flops 17716740096 | bytes 32768000 | tf_op jit(solution)/shard_map/expert/pallas_call | solution.py:411
  485.6 29.8 %expert.7 = (bf16[3072,2048]{1,0:T(8,128)(2,1)}, bf16[3072,1408]{1,0:T(8,128)(2,1)}, bf16[3072,2816]{1,0:T(8,128)(2,1)}, bf16[768,1024]{1,0:T(8,128)(2,1)}, bf16[768,1024]{1,0:T(8,128)(2,1)}, /*index=5*/f32[1,768]{1,0:T(1,128)}) custom-call(s32[3]{0:T(128)} %copy-done.9, ...), custom_call_target="tpu_custom_call", output_to_operand_aliasing={{0}: (15, {}), {1}: (16, {}), {2}: (17, {})} | custom-call | flops 17716740096 | bytes 32768000 | tf_op jit(solution)/shard_map/expert/pallas_call | solution.py:411
  524.6 14.1 %fusion.14 = bf16[1024,1408]{1,0:T(8,128)(2,1)S(1)} fusion(bf16[3072,1408]{1,0:T(8,128)(2,1)} %get-tuple-element.185.act, bf16[3072,2048]{1,0:T(8,128)(2,1)} %get-tuple-element.145, s32[]{:T(128)S(6)} %select_n.169), kind=kOutput, calls=%fused_computation.23 | convolution fusion | flops 8859811840 | bytes 17825796 | tf_op jit(solution)/shard_map/dot_general | solution.py:30
  551.8 27.0 %up.1 = bf16[3072,2048]{1,0:T(8,128)(2,1)} custom-call(s32[3]{0:T(128)S(1)} %copy-done.11, bf16[3072,1408]{1,0:T(8,128)(2,1)} %get-tuple-element.185.act, bf16[1024,1408]{1,0:T(8,128)(2,1)S(1)} %get-tuple-element.238.own, bf16[1024,1408]{1,0:T(8,128)(2,1)} %collective-permute-done.came), custom_call_target="tpu_custom_call" | custom-call | flops 17716740096 | bytes 27000832 | tf_op jit(solution)/shard_map/up/pallas_call | solution.py:339
  607.4 17.4 %convolution_convert_fusion.2 = bf16[512,2816]{1,0:T(8,128)(2,1)} fusion(bf16[3072,2816]{1,0:T(8,128)(2,1)} %get-tuple-element.184, bf16[3072,2048]{1,0:T(8,128)(2,1)} %get-tuple-element.169, s32[]{:T(128)S(6)} %select_n.169), kind=kOutput, calls=%fused_computation.19 | convolution fusion | flops 8859811840 | bytes 23330820 | tf_op jit(solution)/shard_map/dot_general | solution.py:30
  624.8 12.0 %convolution_convert_fusion.1 = bf16[512,2816]{1,0:T(8,128)(2,1)} fusion(bf16[3072,2816]{1,0:T(8,128)(2,1)S(1)} %bitcast.149, bf16[3072,2048]{1,0:T(8,128)(2,1)} %get-tuple-element.169, s32[]{:T(128)S(6)} %select_n.173), kind=kOutput, calls=%fused_computation.18 | convolution fusion | flops 8859811840 | bytes 23330820 | tf_op jit(solution)/shard_map/dot_general | solution.py:30
  636.8 12.3 %collective-permute-done.48 = bf16[1024,512]{1,0:T(8,128)(2,1)S(1)} collective-permute-done((bf16[1024,512]{1,0:T(8,128)(2,1)S(1)}, bf16[1024,512]{1,0:T(8,128)(2,1)S(1)}, u32[]{:S(2)}, u32[]{:S(2)}) %collective-permute-start.48) | collective-permute-done | bytes 1048608 | tf_op jit(solution)/shard_map/ppermute | solution.py:26
  665.1 15.7 %attention_back.1.left = bf16[1024,1536]{1,0:T(8,128)(2,1)} custom-call(bf16[1024,512]{1,0:T(8,128)(2,1)S(1)} %copy-done.13, bf16[1024,512]{1,0:T(8,128)(2,1)S(1)} %copy-done.15, bf16[1024,512]{1,0:T(8,128)(2,1)S(1)} %copy-done.17, f32[4,1024,1]{2,1,0:T(8,128)} %get-tuple-element.164.logs, bf16[1024,512]{1,0:T(8,128)(2,1)S(1)} %fusion.87.grad, ...), custom_call_target="tpu_custom_call" | custom-call | flops 3355443200 | bytes 8388608 | tf_op jit(solution)/shard_map/attention_back/pallas_call | solution.py:188
  680.8 10.5 %convolution_convert_fusion = bf16[2048,1536]{0,1:T(8,128)(2,1)} fusion(bf16[1024,2048]{1,0:T(8,128)(2,1)S(1)} %copy-done.26, bf16[1024,1536]{1,0:T(8,128)(2,1)} %attention_back.1.left), kind=kOutput, calls=%fused_computation.8 | convolution fusion | flops 6445596672 | bytes 13631488 | tf_op jit(solution)/shard_map/dot_general | solution.py:30
  691.3 7.8 pad_maximum_fusion
  699.2 12.2 %spread.3 = (bf16[1024,1024]{1,0:T(8,128)(2,1)S(1)}, bf16[1024,1024]{1,0:T(8,128)(2,1)}) custom-call(s32[3]{0:T(128)S(1)} %copy-done.11, bf16[1024,1536]{1,0:T(8,128)(2,1)} %attention_back.1.left, bf16[2048,2176]{1,0:T(8,128)(2,1)} %all-gather.4.cloned.1.call-done.right), custom_call_target="tpu_custom_call" | custom-call | flops 6442450944 | bytes 13631488 | tf_op jit(solution)/shard_map/spread/pallas_call | solution.py:310
  726.7 26.4 %fusion.11.refs_0_ = bf16[1024,2816]{1,0:T(8,128)(2,1)} fusion(bf16[3072,2816]{1,0:T(8,128)(2,1)} %get-tuple-element.184, bf16[3072,2048]{1,0:T(8,128)(2,1)} %get-tuple-element.169, s32[]{:T(128)S(6)} %select_n.186), kind=kOutput, calls=%fused_computation.17 | convolution fusion | flops 17719623680 | bytes 29360132 | tf_op jit(solution)/shard_map/dot_general | solution.py:30
  753.1 48.5 %collective-permute-done.53 = bf16[768,512]{1,0:T(8,128)(2,1)S(1)} collective-permute-done((bf16[768,512]{1,0:T(8,128)(2,1)S(1)}, bf16[768,512]{1,0:T(8,128)(2,1)S(1)}, u32[]{:S(2)}, u32[]{:S(2)}) %collective-permute-start.53) | collective-permute-done | bytes 786464 | tf_op jit(solution)/shard_map/ppermute | solution.py:26
  801.7 13.5 %fusion.17.refs_3_ = bf16[1024,1408]{1,0:T(8,128)(2,1)} fusion(bf16[3072,1408]{1,0:T(8,128)(2,1)S(1)} %bitcast.151, bf16[3072,2048]{1,0:T(8,128)(2,1)} %get-tuple-element.145, s32[]{:T(128)S(6)} %select_n.186), kind=kOutput, calls=%fused_computation.24 | convolution fusion | flops 8859811840 | bytes 17825796 | tf_op jit(solution)/shard_map/dot_general | solution.py:30
  828.0 28.8 %collective-permute-done.54 = bf16[768,512]{1,0:T(8,128)(2,1)S(1)} collective-permute-done((bf16[768,512]{1,0:T(8,128)(2,1)S(1)}, bf16[768,512]{1,0:T(8,128)(2,1)S(1)}, u32[]{:S(2)}, u32[]{:S(2)}) %collective-permute-start.54) | collective-permute-done | bytes 786464 | tf_op jit(solution)/shard_map/ppermute | solution.py:26
  861.3 24.9 %collective-permute-done.64 = f32[6,2048]{1,0:T(8,128)S(1)} collective-permute-done((f32[6,2048]{1,0:T(8,128)S(1)}, f32[6,2048]{1,0:T(8,128)S(1)}, u32[]{:S(2)}, u32[]{:S(2)}) %collective-permute-start.64) | collective-permute-done | bytes 49184 | tf_op jit(solution)/shard_map/ppermute | solution.py:26
  890.9 9.5 collective-permute-done.66
  900.5 10.4 %collective-permute-done.67 = f32[6,2048]{1,0:T(8,128)S(1)} collective-permute-done((f32[6,2048]{1,0:T(8,128)S(1)}, f32[6,2048]{1,0:T(8,128)S(1)}, u32[]{:S(2)}, u32[]{:S(2)}) %collective-permute-start.67) | collective-permute-done | bytes 49184 | tf_op jit(solution)/shard_map/ppermute | solution.py:26
  920.1 11.9 %expert_grad_sum.1 = f32[3,1024,1408]{2,1,0:T(8,128)} custom-call(bf16[1024,2816]{1,0:T(8,128)(2,1)} %fusion.11.refs_0_, bf16[512,2816]{1,0:T(8,128)(2,1)S(1)} %pad_maximum_fusion.3.refs_1_, bf16[512,2816]{1,0:T(8,128)(2,1)} %collective-permute-done.70.refs_2_, bf16[1024,1408]{1,0:T(8,128)(2,1)S(1)} %copy-done, bf16[1024,1408]{1,0:T(8,128)(2,1)S(1)} %pad_maximum_fusion.4.refs_4_), custom_call_target="tpu_custom_call" | custom-call | flops 4325376 | bytes 34603008 | tf_op jit(solution)/shard_map/expert_grad_sum/pallas_call | solution.py:495
  (438 shorter events, 251.9 us)
Async XLA Ops:
  7.2 167.2 %all-gather.4.cloned.1.call-start = ((), (), s32[]{:S(2)}) async-start(), calls=%async_computation.2 | async-start | bytes 10027008 | tf_op jit(solution)/shard_map/all_gather | solution.py:595
  10.3 256.4 %all-gather.6.cloned.1.call-start = ((), (), s32[]{:S(2)}) async-start(), calls=%async_computation.3 | async-start | bytes 5242880 | tf_op jit(solution)/shard_map/all_gather | solution.py:661
  14.0 162.8 %collective-permute-start.4 = (f32[1,768]{1,0:T(1,128)S(1)}, f32[1,768]{1,0:T(1,128)S(1)}, u32[]{:S(2)}, u32[]{:S(2)}) collective-permute-start(f32[1,768]{1,0:T(1,128)S(1)} %fusion.36), channel_id=1, source_target_pairs={{0,8},{4,12},{8,0},{12,4},{16,24},{20,28},{24,16},{28,20},{1,9},{5... | collective-permute-start | bytes 9224 | tf_op jit(solution)/shard_map/ppermute | solution.py:26
  17.7 160.7 %collective-permute-start.5 = (f32[1,768]{1,0:T(1,128)S(1)}, f32[1,768]{1,0:T(1,128)S(1)}, u32[]{:S(2)}, u32[]{:S(2)}) collective-permute-start(f32[1,768]{1,0:T(1,128)S(1)} %fusion.31), channel_id=1, source_target_pairs={{0,16},{4,20},{8,24},{12,28},{16,0},{20,4},{24,8},{28,12},{1,17},{... | collective-permute-start | bytes 9224 | tf_op jit(solution)/shard_map/ppermute | solution.py:26
  20.9 163.3 %collective-permute-start.6 = (f32[1,768]{1,0:T(1,128)S(1)}, f32[1,768]{1,0:T(1,128)S(1)}, u32[]{:S(2)}, u32[]{:S(2)}) collective-permute-start(f32[1,768]{1,0:T(1,128)S(1)} %fusion.26), channel_id=1, source_target_pairs={{0,24},{4,28},{8,16},{12,20},{16,8},{20,12},{24,0},{28,4},{1,25},{... | collective-permute-start | bytes 9224 | tf_op jit(solution)/shard_map/ppermute | solution.py:26
  20.9 163.3 %collective-permute-start.1 = (f32[1,1024]{1,0:T(1,128)S(1)}, f32[1,1024]{1,0:T(1,128)S(1)}, u32[]{:S(2)}, u32[]{:S(2)}) collective-permute-start(f32[1,1024]{1,0:T(1,128)S(1)} %get-tuple-element.277), channel_id=1, source_target_pairs={{0,8},{4,12},{8,0},{12,4},{16,24},{20,28},{24,16},{28,20},{1,9},{5... | collective-permute-start | bytes 12296 | tf_op jit(solution)/shard_map/ppermute | solution.py:26
  27.7 156.5 %collective-permute-start = (bf16[1024,1408]{1,0:T(8,128)(2,1)S(1)}, bf16[1024,1408]{1,0:T(8,128)(2,1)}, u32[]{:S(2)}, u32[]{:S(2)}) collective-permute-start(bf16[1024,1408]{1,0:T(8,128)(2,1)S(1)} %get-tuple-element.238.own), channel_id=1, source_target_pairs={{0,4},{4,0},{8,12},{12,8},{16,20},{20,16},{24,28},{28,24},{1,5},{5... | collective-permute-start | bytes 8650760 | tf_op jit(solution)/shard_map/ppermute | solution.py:26
  184.6 198.8 %all-gather.8.cloned.1.call-start = ((), (), s32[]{:S(2)}) async-start(), calls=%async_computation.4 | async-start | bytes 11796480 | tf_op jit(solution)/shard_map/all_gather | solution.py:697
  272.8 451.5 %reduce-scatter.3.cloned.1.call-start = ((), (), s32[]{:S(2)}) async-start(), calls=%async_computation.5 | async-start | bytes 15728640 | tf_op jit(solution)/shard_map/reduce_scatter | solution.py:793
  276.0 74.0 %collective-permute-start.20 = (bf16[1184,1408]{1,0:T(8,128)(2,1)S(1)}, bf16[1184,1408]{1,0:T(8,128)(2,1)S(1)}, u32[]{:S(2)}, u32[]{:S(2)}) collective-permute-start(bf16[1184,1408]{1,0:T(8,128)(2,1)S(1)} %pad_maximum_fusion.2), channel_id=1, source_target_pairs={{0,4},{4,0},{8,12},{12,8},{16,20},{20,16},{24,28},{28,24},{1,5},{5... | collective-permute-start | bytes 10002440 | tf_op jit(solution)/shard_map/ppermute | solution.py:26
  286.6 36.6 %collective-permute-start.18 = (bf16[768,512]{1,0:T(8,128)(2,1)S(1)}, bf16[768,512]{1,0:T(8,128)(2,1)S(1)}, u32[]{:S(2)}, u32[]{:S(2)}) collective-permute-start(bf16[768,512]{1,0:T(8,128)(2,1)S(1)} %fusion.99.refs_0_), channel_id=1, source_target_pairs={{0,2},{1,3},{2,0},{3,1},{4,6},{5,7},{6,4},{7,5},{8,10},{9,11},{10,... | collective-permute-start | bytes 2359304 | tf_op jit(solution)/shard_map/ppermute | solution.py:26
  289.0 38.0 %collective-permute-start.15 = (bf16[768,512]{1,0:T(8,128)(2,1)S(1)}, bf16[768,512]{1,0:T(8,128)(2,1)}, u32[]{:S(2)}, u32[]{:S(2)}) collective-permute-start(bf16[768,512]{1,0:T(8,128)(2,1)S(1)} %fusion.101), channel_id=1, source_target_pairs={{0,16},{4,20},{8,24},{12,28},{16,0},{20,4},{24,8},{28,12},{1,17},{... | collective-permute-start | bytes 2359304 | tf_op jit(solution)/shard_map/ppermute | solution.py:26
  289.5 40.4 %collective-permute-start.17 = (bf16[768,512]{1,0:T(8,128)(2,1)S(1)}, bf16[768,512]{1,0:T(8,128)(2,1)S(1)}, u32[]{:S(2)}, u32[]{:S(2)}) collective-permute-start(bf16[768,512]{1,0:T(8,128)(2,1)S(1)} %fusion.99.refs_0_), channel_id=1, source_target_pairs={{0,1},{1,0},{2,3},{3,2},{4,5},{5,4},{6,7},{7,6},{8,9},{9,8},{10,11... | collective-permute-start | bytes 2359304 | tf_op jit(solution)/shard_map/ppermute | solution.py:26
  327.1 54.7 %collective-permute-start.16 = (bf16[768,512]{1,0:T(8,128)(2,1)}, bf16[768,512]{1,0:T(8,128)(2,1)}, u32[]{:S(2)}, u32[]{:S(2)}) collective-permute-start(bf16[768,512]{1,0:T(8,128)(2,1)} %fusion.102), channel_id=1, source_target_pairs={{0,24},{4,28},{8,16},{12,20},{16,8},{20,12},{24,0},{28,4},{1,25},{... | collective-permute-start | bytes 2359304 | tf_op jit(solution)/shard_map/ppermute | solution.py:26
  328.5 53.3 %collective-permute-start.27 = (bf16[768,512]{1,0:T(8,128)(2,1)}, bf16[768,512]{1,0:T(8,128)(2,1)}, u32[]{:S(2)}, u32[]{:S(2)}) collective-permute-start(bf16[768,512]{1,0:T(8,128)(2,1)} %collective-permute-done.15.refs_0_), channel_id=1, source_target_pairs={{0,2},{1,3},{2,0},{3,1},{4,6},{5,7},{6,4},{7,5},{8,10},{9,11},{10,... | collective-permute-start | bytes 2359304 | tf_op jit(solution)/shard_map/ppermute | solution.py:26
  329.9 75.0 %collective-permute-start.26 = (bf16[768,512]{1,0:T(8,128)(2,1)}, bf16[768,512]{1,0:T(8,128)(2,1)}, u32[]{:S(2)}, u32[]{:S(2)}) collective-permute-start(bf16[768,512]{1,0:T(8,128)(2,1)} %collective-permute-done.15.refs_0_), channel_id=1, source_target_pairs={{0,1},{1,0},{2,3},{3,2},{4,5},{5,4},{6,7},{7,6},{8,9},{9,8},{10,11... | collective-permute-start | bytes 2359304 | tf_op jit(solution)/shard_map/ppermute | solution.py:26
  381.8 53.3 %collective-permute-start.25 = (bf16[768,512]{1,0:T(8,128)(2,1)}, bf16[768,512]{1,0:T(8,128)(2,1)}, u32[]{:S(2)}, u32[]{:S(2)}) collective-permute-start(bf16[768,512]{1,0:T(8,128)(2,1)} %collective-permute-done.16.refs_0_), channel_id=1, source_target_pairs={{0,2},{1,3},{2,0},{3,1},{4,6},{5,7},{6,4},{7,5},{8,10},{9,11},{10,... | collective-permute-start | bytes 2359304 | tf_op jit(solution)/shard_map/ppermute | solution.py:26
  383.4 51.8 %collective-permute-start.21 = (bf16[768,512]{1,0:T(8,128)(2,1)}, bf16[768,512]{1,0:T(8,128)(2,1)}, u32[]{:S(2)}, u32[]{:S(2)}) collective-permute-start(bf16[768,512]{1,0:T(8,128)(2,1)} %fusion.100), channel_id=1, source_target_pairs={{0,8},{4,12},{8,0},{12,4},{16,24},{20,28},{24,16},{28,20},{1,9},{5... | collective-permute-start | bytes 2359304 | tf_op jit(solution)/shard_map/ppermute | solution.py:26
  435.9 38.0 %collective-permute-start.23 = (bf16[768,512]{1,0:T(8,128)(2,1)}, bf16[768,512]{1,0:T(8,128)(2,1)}, u32[]{:S(2)}, u32[]{:S(2)}) collective-permute-start(bf16[768,512]{1,0:T(8,128)(2,1)} %collective-permute-done.21.refs_0_), channel_id=1, source_target_pairs={{0,2},{1,3},{2,0},{3,1},{4,6},{5,7},{6,4},{7,5},{8,10},{9,11},{10,... | collective-permute-start | bytes 2359304 | tf_op jit(solution)/shard_map/ppermute | solution.py:26
  477.4 40.9 %collective-permute-start.35 = (bf16[768,512]{1,0:T(8,128)(2,1)}, bf16[768,512]{1,0:T(8,128)(2,1)}, u32[]{:S(2)}, u32[]{:S(2)}) collective-permute-start(bf16[768,512]{1,0:T(8,128)(2,1)} %add_convert_fusion.9), channel_id=1, source_target_pairs={{0,16},{4,20},{8,24},{12,28},{16,0},{20,4},{24,8},{28,12},{1,17},{... | collective-permute-start | bytes 2359304 | tf_op jit(solution)/shard_map/ppermute | solution.py:26
  543.4 37.3 %collective-permute-start.42 = (bf16[768,512]{1,0:T(8,128)(2,1)}, bf16[768,512]{1,0:T(8,128)(2,1)}, u32[]{:S(2)}, u32[]{:S(2)}) collective-permute-start(bf16[768,512]{1,0:T(8,128)(2,1)} %add_convert_fusion.7), channel_id=1, source_target_pairs={{0,24},{4,28},{8,16},{12,20},{16,8},{20,12},{24,0},{28,4},{1,25},{... | collective-permute-start | bytes 2359304 | tf_op jit(solution)/shard_map/ppermute | solution.py:26
  580.9 351.1 %reduce-scatter.5.cloned.1.call-start = ((), (), s32[]{:S(2)}) async-start(), calls=%async_computation.6 | async-start | bytes 9437184 | tf_op jit(solution)/shard_map/reduce_scatter | solution.py:840
  604.7 44.4 %collective-permute-start.48 = (bf16[1024,512]{1,0:T(8,128)(2,1)S(1)}, bf16[1024,512]{1,0:T(8,128)(2,1)S(1)}, u32[]{:S(2)}, u32[]{:S(2)}) collective-permute-start(bf16[1024,512]{1,0:T(8,128)(2,1)S(1)} %get-tuple-element.300), channel_id=1, source_target_pairs={{0,2},{1,3},{2,0},{3,1},{4,6},{5,7},{6,4},{7,5},{8,10},{9,11},{10,... | collective-permute-start | bytes 3145736 | tf_op jit(solution)/shard_map/ppermute | solution.py:26
  606.1 43.0 %collective-permute-start.49 = (bf16[448,1408]{1,0:T(8,128)(2,1)S(1)}, bf16[448,1408]{1,0:T(8,128)(2,1)S(1)}, u32[]{:S(2)}, u32[]{:S(2)}) collective-permute-start(bf16[448,1408]{1,0:T(8,128)(2,1)S(1)} %copy-done.37), channel_id=1, source_target_pairs={{0,4},{4,0},{8,12},{12,8},{16,20},{20,16},{24,28},{28,24},{1,5},{5... | collective-permute-start | bytes 3784712 | tf_op jit(solution)/shard_map/ppermute | solution.py:26
  717.3 202.2 %collective-permute-start.70 = (bf16[512,2816]{1,0:T(8,128)(2,1)}, bf16[512,2816]{1,0:T(8,128)(2,1)}, u32[]{:S(2)}, u32[]{:S(2)}) collective-permute-start(bf16[512,2816]{1,0:T(8,128)(2,1)} %convolution_convert_fusion.1), channel_id=1, source_target_pairs={{0,4},{4,0},{8,12},{12,8},{16,20},{20,16},{24,28},{28,24},{1,5},{5... | collective-permute-start | bytes 8650760 | tf_op jit(solution)/shard_map/ppermute | solution.py:26
  718.2 199.2 %collective-permute-start.69 = (bf16[416,2816]{1,0:T(8,128)(2,1)}, bf16[416,2816]{1,0:T(8,128)(2,1)}, u32[]{:S(2)}, u32[]{:S(2)}) collective-permute-start(bf16[416,2816]{1,0:T(8,128)(2,1)} %slice.347), channel_id=1, source_target_pairs={{0,4},{4,0},{8,12},{12,8},{16,20},{20,16},{24,28},{28,24},{1,5},{5... | collective-permute-start | bytes 7028744 | tf_op jit(solution)/shard_map/ppermute | solution.py:26
  721.9 93.3 %collective-permute-start.59 = (bf16[1024,512]{1,0:T(8,128)(2,1)}, bf16[1024,512]{1,0:T(8,128)(2,1)}, u32[]{:S(2)}, u32[]{:S(2)}) collective-permute-start(bf16[1024,512]{1,0:T(8,128)(2,1)} %add_convert_fusion), channel_id=1, source_target_pairs={{0,2},{1,3},{2,0},{3,1},{4,6},{5,7},{6,4},{7,5},{8,10},{9,11},{10,... | collective-permute-start | bytes 3145736 | tf_op jit(solution)/shard_map/ppermute | solution.py:26
  726.1 75.6 %collective-permute-start.53 = (bf16[768,512]{1,0:T(8,128)(2,1)S(1)}, bf16[768,512]{1,0:T(8,128)(2,1)S(1)}, u32[]{:S(2)}, u32[]{:S(2)}) collective-permute-start(bf16[768,512]{1,0:T(8,128)(2,1)S(1)} %get-tuple-element.178), channel_id=1, source_target_pairs={{0,16},{4,20},{8,24},{12,28},{16,0},{20,4},{24,8},{28,12},{1,17},{... | collective-permute-start | bytes 2359304 | tf_op jit(solution)/shard_map/ppermute | solution.py:26
  819.9 38.0 %collective-permute-start.55 = (bf16[768,512]{1,0:T(8,128)(2,1)S(1)}, bf16[768,512]{1,0:T(8,128)(2,1)S(1)}, u32[]{:S(2)}, u32[]{:S(2)}) collective-permute-start(bf16[768,512]{1,0:T(8,128)(2,1)S(1)} %get-tuple-element.180), channel_id=1, source_target_pairs={{0,24},{4,28},{8,16},{12,20},{16,8},{20,12},{24,0},{28,4},{1,25},{... | collective-permute-start | bytes 2359304 | tf_op jit(solution)/shard_map/ppermute | solution.py:26
  820.3 36.6 %collective-permute-start.54 = (bf16[768,512]{1,0:T(8,128)(2,1)S(1)}, bf16[768,512]{1,0:T(8,128)(2,1)S(1)}, u32[]{:S(2)}, u32[]{:S(2)}) collective-permute-start(bf16[768,512]{1,0:T(8,128)(2,1)S(1)} %get-tuple-element.179), channel_id=1, source_target_pairs={{0,8},{4,12},{8,0},{12,4},{16,24},{20,28},{24,16},{28,20},{1,9},{5... | collective-permute-start | bytes 2359304 | tf_op jit(solution)/shard_map/ppermute | solution.py:26
  827.2 83.8 %collective-permute-start.62 = (bf16[1024,512]{1,0:T(8,128)(2,1)S(1)}, bf16[1024,512]{1,0:T(8,128)(2,1)S(1)}, u32[]{:S(2)}, u32[]{:S(2)}) collective-permute-start(bf16[1024,512]{1,0:T(8,128)(2,1)S(1)} %get-tuple-element.242), channel_id=1, source_target_pairs={{0,2},{1,3},{2,0},{3,1},{4,6},{5,7},{6,4},{7,5},{8,10},{9,11},{10,... | collective-permute-start | bytes 3145736 | tf_op jit(solution)/shard_map/ppermute | solution.py:26
  859.2 53.9 %collective-permute-start.56 = (bf16[1024,512]{1,0:T(8,128)(2,1)S(1)}, bf16[1024,512]{1,0:T(8,128)(2,1)S(1)}, u32[]{:S(2)}, u32[]{:S(2)}) collective-permute-start(bf16[1024,512]{1,0:T(8,128)(2,1)S(1)} %add_convert_fusion.1), channel_id=1, source_target_pairs={{0,2},{1,3},{2,0},{3,1},{4,6},{5,7},{6,4},{7,5},{8,10},{9,11},{10,... | collective-permute-start | bytes 3145736 | tf_op jit(solution)/shard_map/ppermute | solution.py:26
  (120 other events, 1788.9 us)
Sparse Core Ops, SparseCore 0:
  10.8 163.5 all-gather.3
  184.7 81.9 all-gather.5
  272.9 97.8 all-gather.7
  581.0 116.8 reduce-scatter.2
  702.0 210.2 reduce-scatter.4
